TPU v7x, 256 devices: a whole 4x4x8 slice. The times are simulated.
256 devices in a mesh: blk: 128 (over x, z, y), pipe: 2 (over core).
Axes of the slice: x: 4, y: 4, z: 8, core: 2. Of those that a mesh axis runs over, the one named last changes fastest.
Arguments:
- endpoints: bfloat16 [2, 2, 12, 16384, 128], P('pipe', None, None, 'blk'), may hold values from -6 to 6
- row_counts: int32 [2], replicated, may hold values from 1 to 12, as said below
- layer_order: int32 [4], replicated, may hold values from 0 to 3, each once
- depth_weight: float32 [4, 3, 3, 128], replicated, may hold values from -2 to 2
- point_weight: bfloat16 [4, 128, 128], replicated, may hold values from -0.5 to 0.5
- point_bias: float32 [4, 128], replicated, may hold values from -3 to 3
Outputs:
- endpoints_out: bfloat16 [2, 2, 12, 16384, 128], P('pipe', None, None, 'blk')
- grad_depth: float32 [4, 3, 3, 128], replicated
- grad_point: float32 [4, 128, 128], replicated
- grad_bias: float32 [4, 128], replicated
Inputs may be any that keep to these rules, and one draw needn't show every extreme that they name: `row_counts`: one of the two counts is 12. `layer_order`: a permutation of the layers.
All inputs are finite; a program needn't handle non-finite values.
Results may differ from a plain program's by a relative error of at most 0.013.
Values may be sent and summed in bfloat16 or wider, within the bound.
A program may use at most 64 MiB of HBM per device.

v0:
```python
import math

import jax
import jax.numpy as jnp
from jax import lax
from jax.sharding import PartitionSpec as P

root_half = 0.7071067811865476
density_norm = 0.3989422804014327


def padded_2(x, sides, width):
    for axis, dim in sides:
        size, length = (lax.axis_size(axis), x.shape[dim])
        up = [(i, (i + 1) % size) for i in range(size)]
        down = [(j, i) for i, j in up]
        last = lax.slice_in_dim(x, length - width, length, axis=dim)
        first = lax.slice_in_dim(x, 0, width, axis=dim)
        before = lax.ppermute(last, axis, up)
        after = lax.ppermute(first, axis, down)
        x = jnp.concatenate([before, x, after], axis=dim)
    return x


def passed_along(value, axis, steps):
    count = lax.axis_size(axis)
    first, last = (max(0, -steps), min(count, count - steps))
    return lax.ppermute(value, axis, [(source, source + steps) for source in range(first, last)])


def gelu_pair(preact):
    normal_cdf = 0.5 * (1.0 + lax.erf(preact * root_half))
    normal_pdf = density_norm * jnp.exp(-0.5 * preact * preact)
    return (preact * normal_cdf, normal_cdf + preact * normal_pdf)


def select_row(table, chosen):
    return lax.dynamic_index_in_dim(table, chosen, 0, keepdims=False)


def row_mask(row_counts, chosen, height):
    return (jnp.arange(height)[:, None, None] < select_row(row_counts, chosen)).astype(jnp.float32)


def rim_one(activation):
    return padded_2(activation, (("blk", 1),), 1)


def widen(activation):
    return jnp.pad(rim_one(activation), ((1, 1), (0, 0), (0, 0)))


def widen_back(back_mix):
    rimmed = padded_2(back_mix, (("blk", 1),), 1)
    return jnp.pad(rimmed, ((1, 1), (0, 0), (0, 0)))


def mixing(padded, depth, point, offset_vec):
    height = padded.shape[0] - 2
    breadth = padded.shape[1] - 2
    channels = padded.shape[2]
    depthwise = jnp.zeros((height, breadth, channels), jnp.float32)
    for row_off in range(3):
        for col_off in range(3):
            depthwise = depthwise + depth[row_off, col_off] * padded[
                row_off : row_off + height, col_off : col_off + breadth
            ].astype(jnp.float32)
    mixed_bf = depthwise.astype(jnp.bfloat16)
    preact = jnp.dot(
        mixed_bf.reshape(height * breadth, channels), point, preferred_element_type=jnp.float32
    )
    preact = preact.reshape(height, breadth, channels) + offset_vec
    return (mixed_bf, preact)


def layer_weights(layer_id, depth_weight, point_weight, point_bias):
    return (
        select_row(depth_weight, layer_id),
        select_row(point_weight, layer_id),
        select_row(point_bias, layer_id),
    )


def advance(wide, live_rows, weights, breadth):
    padded_full = jnp.pad(wide, ((1, 1), (0, 0), (0, 0)))
    mixed_full, preact_full = mixing(padded_full, weights[0], weights[1], weights[2])
    following = (
        (wide[:, 1:-1].astype(jnp.float32) + gelu_pair(preact_full)[0]) * live_rows
    ).astype(jnp.bfloat16)
    margin = (wide.shape[1] - breadth) // 2
    kept = (wide[:, margin : margin + breadth],)
    return (following, kept)


def restore(kept, weights):
    padded = widen(kept[0])
    mixed_bf, preact = mixing(padded, weights[0], weights[1], weights[2])
    return (padded, mixed_bf, preact)


def run_layers(activation, live_rows, layer_ids, weight_args, breadth, on_kept):
    count = len(layer_ids)
    for layer_pos in range(count):
        weights = layer_weights(
            layer_ids[layer_pos], weight_args[0], weight_args[1], weight_args[2]
        )
        wide = rim_one(activation)
        following, kept = advance(wide, live_rows, weights, breadth)
        on_kept(layer_pos, kept)
        activation = following
        wide = following
    return activation


def retreat(cotangent, live_rows, weights, padded, mixed_bf, preact):
    depth, point = (weights[0], weights[1])
    height = padded.shape[0] - 2
    breadth = padded.shape[1] - 2
    channels = padded.shape[2]
    masked_grad = cotangent.astype(jnp.float32) * live_rows
    gated = (masked_grad * gelu_pair(preact)[1]).astype(jnp.bfloat16)
    flat_mix = mixed_bf.reshape(height * breadth, channels)
    flat_gate = gated.reshape(height * breadth, channels)
    point_term = lax.dot_general(
        flat_mix, flat_gate, (((0,), (0,)), ((), ())), preferred_element_type=jnp.float32
    )
    bias_term = jnp.sum(gated.astype(jnp.float32), axis=(0, 1))
    back_mix = lax.dot_general(
        flat_gate, point, (((1,), (1,)), ((), ())), preferred_element_type=jnp.float32
    )
    back_mix = back_mix.reshape(height, breadth, channels).astype(jnp.bfloat16)
    spread = widen_back(back_mix)
    back_float = back_mix.astype(jnp.float32)
    earlier = jnp.zeros((height, breadth, channels), jnp.float32)
    kernel_rows = []
    for row_off in range(3):
        kernel_row = []
        for col_off in range(3):
            kernel_row.append(
                jnp.sum(
                    back_float
                    * padded[row_off : row_off + height, col_off : col_off + breadth].astype(
                        jnp.float32
                    ),
                    axis=(0, 1),
                )
            )
            earlier = earlier + depth[row_off, col_off] * spread[
                2 - row_off : 2 - row_off + height, 2 - col_off : 2 - col_off + breadth
            ].astype(jnp.float32)
        kernel_rows.append(jnp.stack(kernel_row))
    previous = ((masked_grad + earlier) * live_rows).astype(jnp.bfloat16)
    return (previous, (jnp.stack(kernel_rows), point_term, bias_term))


def add_terms(totals, layer_id, pieces, weight_on):
    return tuple(
        (whole.at[layer_id].add(piece * weight_on) for whole, piece in zip(totals, pieces))
    )


def store_at(buffers, kept, chosen, active):
    return tuple(
        (
            buf.at[chosen].set(jnp.where(active, item, select_row(buf, chosen)))
            for buf, item in zip(buffers, kept)
        )
    )


def fetch_at(buffers, chosen):
    return tuple((select_row(buf, chosen) for buf in buffers))


def shards(endpoints, row_counts, layer_order, depth_weight, point_weight, point_bias):
    held = endpoints[0]
    batches = held.shape[0]
    height = held.shape[1]
    breadth = held.shape[2]
    channels = held.shape[3]
    sections = lax.axis_size("pipe")
    section = lax.axis_index("pipe")
    layers = layer_order.shape[0]
    per_section = layers // sections
    weight_args = (depth_weight, point_weight, point_bias)
    totals = (
        jnp.zeros(depth_weight.shape, jnp.float32),
        jnp.zeros(point_weight.shape, jnp.float32),
        jnp.zeros(point_bias.shape, jnp.float32),
    )
    moments = batches + sections - 1
    stores = [None] * per_section
    received = jnp.zeros((height, breadth, channels), jnp.bfloat16)
    outcomes = jnp.zeros(held.shape, jnp.bfloat16)
    layer_ids = [
        select_row(layer_order, section * per_section + layer_pos)
        for layer_pos in range(per_section)
    ]
    for moment in range(moments):
        offset = moment - section
        active = (offset >= 0) & (offset < batches)
        chosen = jnp.clip(offset, 0, batches - 1)
        live_rows = row_mask(row_counts, chosen, height)
        first_in = (select_row(held, chosen).astype(jnp.float32) * live_rows).astype(jnp.bfloat16)
        activation = jnp.where(section == 0, first_in, received)

        def keep_moment(layer_pos, kept):
            if stores[layer_pos] is None:
                stores[layer_pos] = tuple(
                    (jnp.zeros((batches,) + item.shape, item.dtype) for item in kept)
                )
            stores[layer_pos] = store_at(stores[layer_pos], kept, chosen, active)

        activation = run_layers(activation, live_rows, layer_ids, weight_args, breadth, keep_moment)
        outcomes = store_at((outcomes,), (activation,), chosen, active & (section == sections - 1))[
            0
        ]
        if moment < batches:
            received = passed_along(activation, "pipe", 1)
    returned = jnp.zeros((height, breadth, channels), jnp.bfloat16)
    input_grads = jnp.zeros(held.shape, jnp.bfloat16)
    for moment in range(moments):
        offset = moment - (sections - 1 - section)
        active = (offset >= 0) & (offset < batches)
        weight_on = active.astype(jnp.float32)
        chosen = jnp.clip(offset, 0, batches - 1)
        live_rows = row_mask(row_counts, chosen, height)
        cotangent = jnp.where(section == sections - 1, select_row(held, chosen), returned)
        for layer_pos in range(per_section - 1, -1, -1):
            layer_id = layer_ids[layer_pos]
            weights = layer_weights(layer_id, depth_weight, point_weight, point_bias)
            padded, mixed_bf, preact = restore(fetch_at(stores[layer_pos], chosen), weights)
            cotangent, pieces = retreat(cotangent, live_rows, weights, padded, mixed_bf, preact)
            totals = add_terms(totals, layer_id, pieces, weight_on)
        input_grads = store_at((input_grads,), (cotangent,), chosen, active & (section == 0))[0]
        if moment < batches:
            returned = passed_along(cotangent, "pipe", -1)
    result = jnp.where(section == 0, input_grads, outcomes)[None]
    summed = lax.psum(totals, ("blk", "pipe"))
    factor = 1.0 / math.sqrt(batches * height * breadth * lax.axis_size("blk"))
    return (result, summed[0] * factor, summed[1] * factor, summed[2] * factor)


def solution(mesh):
    in_specs = (P("pipe", None, None, "blk", None), P(), P(), P(), P(), P())
    out_specs = (P("pipe", None, None, "blk", None), P(), P(), P())
    return jax.shard_map(shards, mesh=mesh, in_specs=in_specs, out_specs=out_specs, check_vma=False)
```

profile of v0, /device:TPU:1, one launch (start us, length us, event | category | flops | bytes accessed | tf_op | source)
XLA Modules:
  0.0 507.2 jit_solution(1982061927999604369)
XLA Ops:
  9.2 1.2 fusion.322
  10.4 2.2 collective-permute-start
  12.6 9.0 %collective-permute-start.1 = (bf16[12,1,128]{2,1,0:T(2,128)(2,1)S(1)}, bf16[12,1,128]{2,1,0:T(2,128)(2,1)S(1)}, u32[]{:S(2)}, u32[]{:S(2)}) collective-permute-start(bf16[12,1,128]{2,1,0:T(2,128)(2,1)S(1)} %get-tuple-element.507), channel_id=1, source_target_pairs={{2,0},{4,2},{6,4},{8,6},{10,8},{12,10},{14,12},{16,14},{18,16},{20... | collective-permute-start | bytes 9224 | tf_op jit(solution)/shard_map/ppermute | solution.py:20
  34.2 2.1 bitcast_dynamic-update-slice_fusion.2
  36.4 6.9 %collective-permute-start.3 = (bf16[12,1,128]{2,1,0:T(2,128)(2,1)S(1)}, bf16[12,1,128]{2,1,0:T(2,128)(2,1)S(1)}, u32[]{:S(2)}, u32[]{:S(2)}) collective-permute-start(bf16[12,1,128]{2,1,0:T(2,128)(2,1)S(1)} %get-tuple-element.505), channel_id=1, source_target_pairs={{2,0},{4,2},{6,4},{8,6},{10,8},{12,10},{14,12},{16,14},{18,16},{20... | collective-permute-start | bytes 9224 | tf_op jit(solution)/shard_map/ppermute | solution.py:20
  45.5 2.7 bitcast_dynamic-update-slice_fusion
  48.2 1.4 collective-permute-start.4
  49.6 1.2 compare_convert_fusion.1
  54.1 7.2 %collective-permute-start.6 = (bf16[12,1,128]{2,1,0:T(2,128)(2,1)S(1)}, bf16[12,1,128]{2,1,0:T(2,128)(2,1)S(1)}, u32[]{:S(2)}, u32[]{:S(2)}) collective-permute-start(bf16[12,1,128]{2,1,0:T(2,128)(2,1)S(1)} %get-tuple-element.503), channel_id=1, source_target_pairs={{2,0},{4,2},{6,4},{8,6},{10,8},{12,10},{14,12},{16,14},{18,16},{20... | collective-permute-start | bytes 9224 | tf_op jit(solution)/shard_map/ppermute | solution.py:20
  62.4 2.1 fusion.377
  64.9 7.0 %collective-permute-start.8 = (bf16[12,1,128]{2,1,0:T(2,128)(2,1)S(1)}, bf16[12,1,128]{2,1,0:T(2,128)(2,1)S(1)}, u32[]{:S(2)}, u32[]{:S(2)}) collective-permute-start(bf16[12,1,128]{2,1,0:T(2,128)(2,1)S(1)} %get-tuple-element.501), channel_id=1, source_target_pairs={{2,0},{4,2},{6,4},{8,6},{10,8},{12,10},{14,12},{16,14},{18,16},{20... | collective-permute-start | bytes 9224 | tf_op jit(solution)/shard_map/ppermute | solution.py:20
  73.1 2.8 fusion.371
  75.9 1.3 collective-permute-start.9
  77.2 1.1 compare_convert_fusion
  79.4 2.1 collective-permute-done.9
  82.6 7.3 %collective-permute-start.11 = (bf16[12,1,128]{2,1,0:T(2,128)(2,1)S(1)}, bf16[12,1,128]{2,1,0:T(2,128)(2,1)S(1)}, u32[]{:S(2)}, u32[]{:S(2)}) collective-permute-start(bf16[12,1,128]{2,1,0:T(2,128)(2,1)S(1)} %get-tuple-element.497), channel_id=1, source_target_pairs={{2,0},{4,2},{6,4},{8,6},{10,8},{12,10},{14,12},{16,14},{18,16},{20... | collective-permute-start | bytes 9224 | tf_op jit(solution)/shard_map/ppermute | solution.py:20
  90.2 6.9 %collective-permute-start.17 = (bf16[12,1,128]{2,1,0:T(2,128)(2,1)S(1)}, bf16[12,1,128]{2,1,0:T(2,128)(2,1)S(1)}, u32[]{:S(2)}, u32[]{:S(2)}) collective-permute-start(bf16[12,1,128]{2,1,0:T(2,128)(2,1)S(1)} %get-tuple-element.499), channel_id=1, source_target_pairs={{2,0},{4,2},{6,4},{8,6},{10,8},{12,10},{14,12},{16,14},{18,16},{20... | collective-permute-start | bytes 9224 | tf_op jit(solution)/shard_map/ppermute | solution.py:20
  97.2 7.0 %collective-permute-start.26 = (bf16[12,1,128]{2,1,0:T(2,128)(2,1)S(1)}, bf16[12,1,128]{2,1,0:T(2,128)(2,1)S(1)}, u32[]{:S(2)}, u32[]{:S(2)}) collective-permute-start(bf16[12,1,128]{2,1,0:T(2,128)(2,1)S(1)} %get-tuple-element.489), channel_id=1, source_target_pairs={{2,0},{4,2},{6,4},{8,6},{10,8},{12,10},{14,12},{16,14},{18,16},{20... | collective-permute-start | bytes 9224 | tf_op jit(solution)/shard_map/ppermute | solution.py:20
  104.3 2.1 fusion.376
  106.6 7.0 %collective-permute-start.35 = (bf16[12,1,128]{2,1,0:T(2,128)(2,1)S(1)}, bf16[12,1,128]{2,1,0:T(2,128)(2,1)S(1)}, u32[]{:S(2)}, u32[]{:S(2)}) collective-permute-start(bf16[12,1,128]{2,1,0:T(2,128)(2,1)S(1)} %get-tuple-element.481), channel_id=1, source_target_pairs={{2,0},{4,2},{6,4},{8,6},{10,8},{12,10},{14,12},{16,14},{18,16},{20... | collective-permute-start | bytes 9224 | tf_op jit(solution)/shard_map/ppermute | solution.py:20
  114.1 1.7 fusion.87
  115.8 7.0 %collective-permute-start.13 = (bf16[12,1,128]{2,1,0:T(2,128)(2,1)S(1)}, bf16[12,1,128]{2,1,0:T(2,128)(2,1)S(1)}, u32[]{:S(2)}, u32[]{:S(2)}) collective-permute-start(bf16[12,1,128]{2,1,0:T(2,128)(2,1)S(1)} %get-tuple-element.495), channel_id=1, source_target_pairs={{2,0},{4,2},{6,4},{8,6},{10,8},{12,10},{14,12},{16,14},{18,16},{20... | collective-permute-start | bytes 9224 | tf_op jit(solution)/shard_map/ppermute | solution.py:20
  122.9 1.7 fusion.105
  124.7 7.0 %collective-permute-start.22 = (bf16[12,1,128]{2,1,0:T(2,128)(2,1)S(1)}, bf16[12,1,128]{2,1,0:T(2,128)(2,1)S(1)}, u32[]{:S(2)}, u32[]{:S(2)}) collective-permute-start(bf16[12,1,128]{2,1,0:T(2,128)(2,1)S(1)} %get-tuple-element.487), channel_id=1, source_target_pairs={{2,0},{4,2},{6,4},{8,6},{10,8},{12,10},{14,12},{16,14},{18,16},{20... | collective-permute-start | bytes 9224 | tf_op jit(solution)/shard_map/ppermute | solution.py:20
  131.8 1.7 fusion.123
  133.6 7.0 %collective-permute-start.31 = (bf16[12,1,128]{2,1,0:T(2,128)(2,1)S(1)}, bf16[12,1,128]{2,1,0:T(2,128)(2,1)S(1)}, u32[]{:S(2)}, u32[]{:S(2)}) collective-permute-start(bf16[12,1,128]{2,1,0:T(2,128)(2,1)S(1)} %get-tuple-element.479), channel_id=1, source_target_pairs={{2,0},{4,2},{6,4},{8,6},{10,8},{12,10},{14,12},{16,14},{18,16},{20... | collective-permute-start | bytes 9224 | tf_op jit(solution)/shard_map/ppermute | solution.py:20
  142.3 1.1 fusion.180
  144.8 1.6 fusion.13
  146.3 1.1 fusion.451
  147.5 7.0 %collective-permute-start.39 = (bf16[12,1,128]{2,1,0:T(2,128)(2,1)S(1)}, bf16[12,1,128]{2,1,0:T(2,128)(2,1)S(1)}, u32[]{:S(2)}, u32[]{:S(2)}) collective-permute-start(bf16[12,1,128]{2,1,0:T(2,128)(2,1)S(1)} %get-tuple-element.473), channel_id=1, source_target_pairs={{2,0},{4,2},{6,4},{8,6},{10,8},{12,10},{14,12},{16,14},{18,16},{20... | collective-permute-start | bytes 9224 | tf_op jit(solution)/shard_map/ppermute | solution.py:20
  154.8 1.7 fusion.96
  156.5 7.0 %collective-permute-start.15 = (bf16[12,1,128]{2,1,0:T(2,128)(2,1)}, bf16[12,1,128]{2,1,0:T(2,128)(2,1)S(1)}, u32[]{:S(2)}, u32[]{:S(2)}) collective-permute-start(bf16[12,1,128]{2,1,0:T(2,128)(2,1)} %get-tuple-element.493), channel_id=1, source_target_pairs={{2,0},{4,2},{6,4},{8,6},{10,8},{12,10},{14,12},{16,14},{18,16},{20... | collective-permute-start | bytes 9224 | tf_op jit(solution)/shard_map/ppermute | solution.py:20
  163.6 1.7 fusion.114
  166.0 2.7 fusion.279
  170.0 1.2 select_maximum_fusion.22
  171.2 1.2 fusion.179
  173.4 1.1 fusion.197
  174.6 6.9 %collective-permute-start.19 = (bf16[12,1,128]{2,1,0:T(2,128)(2,1)S(1)}, bf16[12,1,128]{2,1,0:T(2,128)(2,1)S(1)}, u32[]{:S(2)}, u32[]{:S(2)}) collective-permute-start(bf16[12,1,128]{2,1,0:T(2,128)(2,1)S(1)} %get-tuple-element.491), channel_id=1, source_target_pairs={{2,0},{4,2},{6,4},{8,6},{10,8},{12,10},{14,12},{16,14},{18,16},{20... | collective-permute-start | bytes 9224 | tf_op jit(solution)/shard_map/ppermute | solution.py:20
  182.8 2.5 bitcast_dynamic-update-slice_fusion.1
  186.2 8.9 %collective-permute-start.20 = (bf16[12,128,128]{2,1,0:T(8,128)(2,1)}, bf16[12,128,128]{2,1,0:T(8,128)(2,1)S(1)}, u32[]{:S(2)}, u32[]{:S(2)}) collective-permute-start(bf16[12,128,128]{2,1,0:T(8,128)(2,1)} %get-tuple-element.461), channel_id=1, source_target_pairs={{1,0},{3,2},{5,4},{7,6},{9,8},{11,10},{13,12},{15,14},{17,16},{19,... | collective-permute-start | bytes 1179656 | tf_op jit(solution)/shard_map/ppermute | solution.py:28
  195.9 2.8 fusion.16
  200.6 1.1 fusion.214
  201.8 7.2 %collective-permute-start.24 = (bf16[12,1,128]{2,1,0:T(2,128)(2,1)S(1)}, bf16[12,1,128]{2,1,0:T(2,128)(2,1)S(1)}, u32[]{:S(2)}, u32[]{:S(2)}) collective-permute-start(bf16[12,1,128]{2,1,0:T(2,128)(2,1)S(1)} %get-tuple-element.485), channel_id=1, source_target_pairs={{2,0},{4,2},{6,4},{8,6},{10,8},{12,10},{14,12},{16,14},{18,16},{20... | collective-permute-start | bytes 9224 | tf_op jit(solution)/shard_map/ppermute | solution.py:20
  209.0 2.4 fusion.19
  212.8 1.2 select_maximum_fusion.14
  214.1 1.1 fusion.213
  216.2 1.1 fusion.231
  217.4 6.9 %collective-permute-start.28 = (bf16[12,1,128]{2,1,0:T(2,128)(2,1)S(1)}, bf16[12,1,128]{2,1,0:T(2,128)(2,1)S(1)}, u32[]{:S(2)}, u32[]{:S(2)}) collective-permute-start(bf16[12,1,128]{2,1,0:T(2,128)(2,1)S(1)} %get-tuple-element.483), channel_id=1, source_target_pairs={{2,0},{4,2},{6,4},{8,6},{10,8},{12,10},{14,12},{16,14},{18,16},{20... | collective-permute-start | bytes 9224 | tf_op jit(solution)/shard_map/ppermute | solution.py:20
  225.5 2.5 fusion.373
  228.0 2.7 collective-permute-start.29
  231.4 2.7 fusion.22
  236.0 1.1 fusion.248
  237.5 7.2 %collective-permute-start.33 = (bf16[12,1,128]{2,1,0:T(2,128)(2,1)S(1)}, bf16[12,1,128]{2,1,0:T(2,128)(2,1)S(1)}, u32[]{:S(2)}, u32[]{:S(2)}) collective-permute-start(bf16[12,1,128]{2,1,0:T(2,128)(2,1)S(1)} %get-tuple-element.477), channel_id=1, source_target_pairs={{2,0},{4,2},{6,4},{8,6},{10,8},{12,10},{14,12},{16,14},{18,16},{20... | collective-permute-start | bytes 9224 | tf_op jit(solution)/shard_map/ppermute | solution.py:20
  244.7 2.4 fusion.25
  248.5 1.2 select_maximum_fusion.6
  249.7 1.1 fusion.247
  251.6 2.5 fusion.28
  254.8 1.1 fusion.265
  256.6 75.0 %all-reduce.18 = (f32[4,3,3,128]{3,2,1,0:T(4,128)S(1)}, f32[4,128]{1,0:T(4,128)S(1)}) all-reduce(f32[4,3,3,128]{3,2,1,0:T(4,128)S(1)} %constant_dynamic-update-slice_fusion, f32[4,128]{1,0:T(4,128)S(1)} %scatter-add.89), channel_id=1, replica_groups=mesh['blk'=128,'pipe'=2] {'blk','pipe'}, use_global_device_ids=true, to_apply=%region_62.63 | all-reduce | flops 5120 | bytes 40960 | tf_op jit(solution)/shard_map/psum | solution.py:239
  331.7 6.9 %collective-permute-start.37 = (bf16[12,1,128]{2,1,0:T(2,128)(2,1)S(1)}, bf16[12,1,128]{2,1,0:T(2,128)(2,1)S(1)}, u32[]{:S(2)}, u32[]{:S(2)}) collective-permute-start(bf16[12,1,128]{2,1,0:T(2,128)(2,1)S(1)} %get-tuple-element.475), channel_id=1, source_target_pairs={{2,0},{4,2},{6,4},{8,6},{10,8},{12,10},{14,12},{16,14},{18,16},{20... | collective-permute-start | bytes 9224 | tf_op jit(solution)/shard_map/ppermute | solution.py:20
  340.9 1.9 fusion.372
  342.7 2.1 select_bitcast_fusion
  344.8 153.4 %all-reduce.21.cloned.1.call-done = f32[4,128,128]{2,1,0:T(8,128)} async-done(((f32[4,128,128]{2,1,0:T(8,128)}), f32[4,128,128]{2,1,0:T(8,128)}) %all-reduce.21.cloned.1.call-update) | async-done | bytes 262160 | tf_op jit(solution)/shard_map/psum | solution.py:239
  498.3 1.7 broadcast_multiply_fusion
  (283 shorter events, 46.2 us)
Async XLA Ops:
  7.2 27.1 %copy-start = (bf16[4,128,128]{2,1,0:T(8,128)(2,1)S(1)}, bf16[4,128,128]{2,1,0:T(8,128)(2,1)}, u32[]{:S(2)}) copy-start(bf16[4,128,128]{2,1,0:T(8,128)(2,1)} %param.70) | copy-start | bytes 393220
  7.2 491.1 %all-reduce.21.cloned.1.call-start = ((), (), s32[]{:S(2)}) async-start(), calls=%async_computation | async-start | bytes 524288 | tf_op jit(solution)/shard_map/psum | solution.py:239
  10.4 11.2 %copy-start.40 = (s32[4]{0:T(128)S(1)}, s32[4]{0:T(128)}, u32[]{:S(2)}) copy-start(s32[4]{0:T(128)} %param.68) | copy-start | bytes 52
  10.4 23.5 %collective-permute-start = (bf16[12,1,128]{2,1,0:T(2,128)(2,1)S(1)}, bf16[12,1,128]{2,1,0:T(2,128)(2,1)S(1)}, u32[]{:S(2)}, u32[]{:S(2)}) collective-permute-start(bf16[12,1,128]{2,1,0:T(2,128)(2,1)S(1)} %get-tuple-element.506), channel_id=1, source_target_pairs={{0,2},{2,4},{4,6},{6,8},{8,10},{10,12},{12,14},{14,16},{16,18},{18... | collective-permute-start | bytes 9224 | tf_op jit(solution)/shard_map/ppermute | solution.py:19
  12.6 21.3 %collective-permute-start.1 = (bf16[12,1,128]{2,1,0:T(2,128)(2,1)S(1)}, bf16[12,1,128]{2,1,0:T(2,128)(2,1)S(1)}, u32[]{:S(2)}, u32[]{:S(2)}) collective-permute-start(bf16[12,1,128]{2,1,0:T(2,128)(2,1)S(1)} %get-tuple-element.507), channel_id=1, source_target_pairs={{2,0},{4,2},{6,4},{8,6},{10,8},{12,10},{14,12},{16,14},{18,16},{20... | collective-permute-start | bytes 9224 | tf_op jit(solution)/shard_map/ppermute | solution.py:20
  21.6 4.3 copy-start.37
  26.7 77.6 %copy-start.45 = (f32[128]{0:T(128)}, f32[128]{0:T(128)S(1)}, u32[]{:S(2)}) copy-start(f32[128]{0:T(128)S(1)} %get-tuple-element.529) | copy-start | bytes 1540
  26.7 114.9 %copy-start.48 = (f32[128]{0:T(128)}, f32[128]{0:T(128)S(1)}, u32[]{:S(2)}) copy-start(f32[128]{0:T(128)S(1)} %get-tuple-element.528) | copy-start | bytes 1540
  36.3 8.0 %collective-permute-start.2 = (bf16[12,1,128]{2,1,0:T(2,128)(2,1)S(1)}, bf16[12,1,128]{2,1,0:T(2,128)(2,1)S(1)}, u32[]{:S(2)}, u32[]{:S(2)}) collective-permute-start(bf16[12,1,128]{2,1,0:T(2,128)(2,1)S(1)} %get-tuple-element.504), channel_id=1, source_target_pairs={{0,2},{2,4},{4,6},{6,8},{8,10},{10,12},{12,14},{14,16},{16,18},{18... | collective-permute-start | bytes 9224 | tf_op jit(solution)/shard_map/ppermute | solution.py:19
  36.4 7.9 %collective-permute-start.3 = (bf16[12,1,128]{2,1,0:T(2,128)(2,1)S(1)}, bf16[12,1,128]{2,1,0:T(2,128)(2,1)S(1)}, u32[]{:S(2)}, u32[]{:S(2)}) collective-permute-start(bf16[12,1,128]{2,1,0:T(2,128)(2,1)S(1)} %get-tuple-element.505), channel_id=1, source_target_pairs={{2,0},{4,2},{6,4},{8,6},{10,8},{12,10},{14,12},{16,14},{18,16},{20... | collective-permute-start | bytes 9224 | tf_op jit(solution)/shard_map/ppermute | solution.py:20
  44.0 97.6 %copy-start.42 = (f32[12]{0:T(128)}, f32[12]{0:T(128)S(1)}, u32[]{:S(2)}) copy-start(f32[12]{0:T(128)S(1)} %compare_convert_fusion.5) | copy-start | bytes 148
  48.2 2.8 copy-start.1
  48.2 4.7 collective-permute-start.4
  54.0 8.3 %collective-permute-start.5 = (bf16[12,1,128]{2,1,0:T(2,128)(2,1)S(1)}, bf16[12,1,128]{2,1,0:T(2,128)(2,1)S(1)}, u32[]{:S(2)}, u32[]{:S(2)}) collective-permute-start(bf16[12,1,128]{2,1,0:T(2,128)(2,1)S(1)} %get-tuple-element.502), channel_id=1, source_target_pairs={{0,2},{2,4},{4,6},{6,8},{8,10},{10,12},{12,14},{14,16},{16,18},{18... | collective-permute-start | bytes 9224 | tf_op jit(solution)/shard_map/ppermute | solution.py:19
  54.1 8.2 %collective-permute-start.6 = (bf16[12,1,128]{2,1,0:T(2,128)(2,1)S(1)}, bf16[12,1,128]{2,1,0:T(2,128)(2,1)S(1)}, u32[]{:S(2)}, u32[]{:S(2)}) collective-permute-start(bf16[12,1,128]{2,1,0:T(2,128)(2,1)S(1)} %get-tuple-element.503), channel_id=1, source_target_pairs={{2,0},{4,2},{6,4},{8,6},{10,8},{12,10},{14,12},{16,14},{18,16},{20... | collective-permute-start | bytes 9224 | tf_op jit(solution)/shard_map/ppermute | solution.py:20
  64.6 8.4 %collective-permute-start.7 = (bf16[12,1,128]{2,1,0:T(2,128)(2,1)S(1)}, bf16[12,1,128]{2,1,0:T(2,128)(2,1)S(1)}, u32[]{:S(2)}, u32[]{:S(2)}) collective-permute-start(bf16[12,1,128]{2,1,0:T(2,128)(2,1)S(1)} %get-tuple-element.500), channel_id=1, source_target_pairs={{0,2},{2,4},{4,6},{6,8},{8,10},{10,12},{12,14},{14,16},{16,18},{18... | collective-permute-start | bytes 9224 | tf_op jit(solution)/shard_map/ppermute | solution.py:19
  64.9 8.1 %collective-permute-start.8 = (bf16[12,1,128]{2,1,0:T(2,128)(2,1)S(1)}, bf16[12,1,128]{2,1,0:T(2,128)(2,1)S(1)}, u32[]{:S(2)}, u32[]{:S(2)}) collective-permute-start(bf16[12,1,128]{2,1,0:T(2,128)(2,1)S(1)} %get-tuple-element.501), channel_id=1, source_target_pairs={{2,0},{4,2},{6,4},{8,6},{10,8},{12,10},{14,12},{16,14},{18,16},{20... | collective-permute-start | bytes 9224 | tf_op jit(solution)/shard_map/ppermute | solution.py:20
  75.9 5.5 %collective-permute-start.9 = (bf16[12,128,128]{2,1,0:T(8,128)(2,1)S(1)}, bf16[12,128,128]{2,1,0:T(8,128)(2,1)S(1)}, u32[]{:S(2)}, u32[]{:S(2)}) collective-permute-start(bf16[12,128,128]{2,1,0:T(8,128)(2,1)S(1)} %get-tuple-element.547), channel_id=1, source_target_pairs={{0,1},{2,3},{4,5},{6,7},{8,9},{10,11},{12,13},{14,15},{16,17},{18,... | collective-permute-start | bytes 1179656 | tf_op jit(solution)/shard_map/ppermute | solution.py:28
  82.5 14.7 %collective-permute-start.10 = (bf16[12,1,128]{2,1,0:T(2,128)(2,1)S(1)}, bf16[12,1,128]{2,1,0:T(2,128)(2,1)S(1)}, u32[]{:S(2)}, u32[]{:S(2)}) collective-permute-start(bf16[12,1,128]{2,1,0:T(2,128)(2,1)S(1)} %get-tuple-element.496), channel_id=1, source_target_pairs={{0,2},{2,4},{4,6},{6,8},{8,10},{10,12},{12,14},{14,16},{16,18},{18... | collective-permute-start | bytes 9224 | tf_op jit(solution)/shard_map/ppermute | solution.py:19
  82.6 21.6 %collective-permute-start.11 = (bf16[12,1,128]{2,1,0:T(2,128)(2,1)S(1)}, bf16[12,1,128]{2,1,0:T(2,128)(2,1)S(1)}, u32[]{:S(2)}, u32[]{:S(2)}) collective-permute-start(bf16[12,1,128]{2,1,0:T(2,128)(2,1)S(1)} %get-tuple-element.497), channel_id=1, source_target_pairs={{2,0},{4,2},{6,4},{8,6},{10,8},{12,10},{14,12},{16,14},{18,16},{20... | collective-permute-start | bytes 9224 | tf_op jit(solution)/shard_map/ppermute | solution.py:20
  90.0 24.1 %copy-start.13 = (bf16[12,128,128]{2,1,0:T(8,128)(2,1)}, bf16[12,128,128]{2,1,0:T(8,128)(2,1)S(1)}, u32[]{:S(2)}) copy-start(bf16[12,128,128]{2,1,0:T(8,128)(2,1)S(1)} %get-tuple-element.471) | copy-start | bytes 1179652
  90.0 32.9 %copy-start.9 = (bf16[12,128,128]{2,1,0:T(8,128)(2,1)}, bf16[12,128,128]{2,1,0:T(8,128)(2,1)S(1)}, u32[]{:S(2)}) copy-start(bf16[12,128,128]{2,1,0:T(8,128)(2,1)S(1)} %get-tuple-element.470) | copy-start | bytes 1179652
  90.0 41.8 %copy-start.5 = (bf16[12,128,128]{2,1,0:T(8,128)(2,1)}, bf16[12,128,128]{2,1,0:T(8,128)(2,1)S(1)}, u32[]{:S(2)}) copy-start(bf16[12,128,128]{2,1,0:T(8,128)(2,1)S(1)} %get-tuple-element.469) | copy-start | bytes 1179652
  90.1 16.5 %collective-permute-start.16 = (bf16[12,1,128]{2,1,0:T(2,128)(2,1)S(1)}, bf16[12,1,128]{2,1,0:T(2,128)(2,1)S(1)}, u32[]{:S(2)}, u32[]{:S(2)}) collective-permute-start(bf16[12,1,128]{2,1,0:T(2,128)(2,1)S(1)} %get-tuple-element.498), channel_id=1, source_target_pairs={{0,2},{2,4},{4,6},{6,8},{8,10},{10,12},{12,14},{14,16},{16,18},{18... | collective-permute-start | bytes 9224 | tf_op jit(solution)/shard_map/ppermute | solution.py:19
  90.2 23.4 %collective-permute-start.17 = (bf16[12,1,128]{2,1,0:T(2,128)(2,1)S(1)}, bf16[12,1,128]{2,1,0:T(2,128)(2,1)S(1)}, u32[]{:S(2)}, u32[]{:S(2)}) collective-permute-start(bf16[12,1,128]{2,1,0:T(2,128)(2,1)S(1)} %get-tuple-element.499), channel_id=1, source_target_pairs={{2,0},{4,2},{6,4},{8,6},{10,8},{12,10},{14,12},{16,14},{18,16},{20... | collective-permute-start | bytes 9224 | tf_op jit(solution)/shard_map/ppermute | solution.py:20
  97.1 18.8 %collective-permute-start.25 = (bf16[12,1,128]{2,1,0:T(2,128)(2,1)S(1)}, bf16[12,1,128]{2,1,0:T(2,128)(2,1)S(1)}, u32[]{:S(2)}, u32[]{:S(2)}) collective-permute-start(bf16[12,1,128]{2,1,0:T(2,128)(2,1)S(1)} %get-tuple-element.488), channel_id=1, source_target_pairs={{0,2},{2,4},{4,6},{6,8},{8,10},{10,12},{12,14},{14,16},{16,18},{18... | collective-permute-start | bytes 9224 | tf_op jit(solution)/shard_map/ppermute | solution.py:19
  97.2 25.6 %collective-permute-start.26 = (bf16[12,1,128]{2,1,0:T(2,128)(2,1)S(1)}, bf16[12,1,128]{2,1,0:T(2,128)(2,1)S(1)}, u32[]{:S(2)}, u32[]{:S(2)}) collective-permute-start(bf16[12,1,128]{2,1,0:T(2,128)(2,1)S(1)} %get-tuple-element.489), channel_id=1, source_target_pairs={{2,0},{4,2},{6,4},{8,6},{10,8},{12,10},{14,12},{16,14},{18,16},{20... | collective-permute-start | bytes 9224 | tf_op jit(solution)/shard_map/ppermute | solution.py:20
  104.1 20.5 %collective-permute-start.34 = (bf16[12,1,128]{2,1,0:T(2,128)(2,1)S(1)}, bf16[12,1,128]{2,1,0:T(2,128)(2,1)S(1)}, u32[]{:S(2)}, u32[]{:S(2)}) collective-permute-start(bf16[12,1,128]{2,1,0:T(2,128)(2,1)S(1)} %get-tuple-element.480), channel_id=1, source_target_pairs={{0,2},{2,4},{4,6},{6,8},{8,10},{10,12},{12,14},{14,16},{16,18},{18... | collective-permute-start | bytes 9224 | tf_op jit(solution)/shard_map/ppermute | solution.py:19
  106.5 48.2 %copy-start.11 = (bf16[12,128,128]{2,1,0:T(8,128)(2,1)}, bf16[12,128,128]{2,1,0:T(8,128)(2,1)S(1)}, u32[]{:S(2)}) copy-start(bf16[12,128,128]{2,1,0:T(8,128)(2,1)S(1)} %get-tuple-element.467) | copy-start | bytes 1179652
  106.5 57.0 %copy-start.7 = (bf16[12,128,128]{2,1,0:T(8,128)(2,1)}, bf16[12,128,128]{2,1,0:T(8,128)(2,1)S(1)}, u32[]{:S(2)}) copy-start(bf16[12,128,128]{2,1,0:T(8,128)(2,1)S(1)} %get-tuple-element.466) | copy-start | bytes 1179652
  106.6 25.1 %collective-permute-start.35 = (bf16[12,1,128]{2,1,0:T(2,128)(2,1)S(1)}, bf16[12,1,128]{2,1,0:T(2,128)(2,1)S(1)}, u32[]{:S(2)}, u32[]{:S(2)}) collective-permute-start(bf16[12,1,128]{2,1,0:T(2,128)(2,1)S(1)} %get-tuple-element.481), channel_id=1, source_target_pairs={{2,0},{4,2},{6,4},{8,6},{10,8},{12,10},{14,12},{16,14},{18,16},{20... | collective-permute-start | bytes 9224 | tf_op jit(solution)/shard_map/ppermute | solution.py:20
  113.6 20.0 %collective-permute-start.12 = (bf16[12,1,128]{2,1,0:T(2,128)(2,1)S(1)}, bf16[12,1,128]{2,1,0:T(2,128)(2,1)S(1)}, u32[]{:S(2)}, u32[]{:S(2)}) collective-permute-start(bf16[12,1,128]{2,1,0:T(2,128)(2,1)S(1)} %get-tuple-element.494), channel_id=1, source_target_pairs={{0,2},{2,4},{4,6},{6,8},{8,10},{10,12},{12,14},{14,16},{16,18},{18... | collective-permute-start | bytes 9224 | tf_op jit(solution)/shard_map/ppermute | solution.py:19
  115.8 24.7 %collective-permute-start.13 = (bf16[12,1,128]{2,1,0:T(2,128)(2,1)S(1)}, bf16[12,1,128]{2,1,0:T(2,128)(2,1)S(1)}, u32[]{:S(2)}, u32[]{:S(2)}) collective-permute-start(bf16[12,1,128]{2,1,0:T(2,128)(2,1)S(1)} %get-tuple-element.495), channel_id=1, source_target_pairs={{2,0},{4,2},{6,4},{8,6},{10,8},{12,10},{14,12},{16,14},{18,16},{20... | collective-permute-start | bytes 9224 | tf_op jit(solution)/shard_map/ppermute | solution.py:20
  122.8 24.7 %collective-permute-start.21 = (bf16[12,1,128]{2,1,0:T(2,128)(2,1)S(1)}, bf16[12,1,128]{2,1,0:T(2,128)(2,1)S(1)}, u32[]{:S(2)}, u32[]{:S(2)}) collective-permute-start(bf16[12,1,128]{2,1,0:T(2,128)(2,1)S(1)} %get-tuple-element.486), channel_id=1, source_target_pairs={{0,2},{2,4},{4,6},{6,8},{8,10},{10,12},{12,14},{14,16},{16,18},{18... | collective-permute-start | bytes 9224 | tf_op jit(solution)/shard_map/ppermute | solution.py:19
  124.7 29.8 %collective-permute-start.22 = (bf16[12,1,128]{2,1,0:T(2,128)(2,1)S(1)}, bf16[12,1,128]{2,1,0:T(2,128)(2,1)S(1)}, u32[]{:S(2)}, u32[]{:S(2)}) collective-permute-start(bf16[12,1,128]{2,1,0:T(2,128)(2,1)S(1)} %get-tuple-element.487), channel_id=1, source_target_pairs={{2,0},{4,2},{6,4},{8,6},{10,8},{12,10},{14,12},{16,14},{18,16},{20... | collective-permute-start | bytes 9224 | tf_op jit(solution)/shard_map/ppermute | solution.py:20
  131.7 24.8 %collective-permute-start.30 = (bf16[12,1,128]{2,1,0:T(2,128)(2,1)S(1)}, bf16[12,1,128]{2,1,0:T(2,128)(2,1)S(1)}, u32[]{:S(2)}, u32[]{:S(2)}) collective-permute-start(bf16[12,1,128]{2,1,0:T(2,128)(2,1)S(1)} %get-tuple-element.478), channel_id=1, source_target_pairs={{0,2},{2,4},{4,6},{6,8},{8,10},{10,12},{12,14},{14,16},{16,18},{18... | collective-permute-start | bytes 9224 | tf_op jit(solution)/shard_map/ppermute | solution.py:19
  133.6 29.9 %collective-permute-start.31 = (bf16[12,1,128]{2,1,0:T(2,128)(2,1)S(1)}, bf16[12,1,128]{2,1,0:T(2,128)(2,1)S(1)}, u32[]{:S(2)}, u32[]{:S(2)}) collective-permute-start(bf16[12,1,128]{2,1,0:T(2,128)(2,1)S(1)} %get-tuple-element.479), channel_id=1, source_target_pairs={{2,0},{4,2},{6,4},{8,6},{10,8},{12,10},{14,12},{16,14},{18,16},{20... | collective-permute-start | bytes 9224 | tf_op jit(solution)/shard_map/ppermute | solution.py:20
  140.5 24.8 %collective-permute-start.38 = (bf16[12,1,128]{2,1,0:T(2,128)(2,1)S(1)}, bf16[12,1,128]{2,1,0:T(2,128)(2,1)S(1)}, u32[]{:S(2)}, u32[]{:S(2)}) collective-permute-start(bf16[12,1,128]{2,1,0:T(2,128)(2,1)S(1)} %get-tuple-element.472), channel_id=1, source_target_pairs={{0,2},{2,4},{4,6},{6,8},{8,10},{10,12},{12,14},{14,16},{16,18},{18... | collective-permute-start | bytes 9224 | tf_op jit(solution)/shard_map/ppermute | solution.py:19
  143.4 3.0 copy-start.15
  147.5 17.8 %collective-permute-start.39 = (bf16[12,1,128]{2,1,0:T(2,128)(2,1)S(1)}, bf16[12,1,128]{2,1,0:T(2,128)(2,1)S(1)}, u32[]{:S(2)}, u32[]{:S(2)}) collective-permute-start(bf16[12,1,128]{2,1,0:T(2,128)(2,1)S(1)} %get-tuple-element.473), channel_id=1, source_target_pairs={{2,0},{4,2},{6,4},{8,6},{10,8},{12,10},{14,12},{16,14},{18,16},{20... | collective-permute-start | bytes 9224 | tf_op jit(solution)/shard_map/ppermute | solution.py:20
  154.5 15.5 %collective-permute-start.14 = (bf16[12,1,128]{2,1,0:T(2,128)(2,1)}, bf16[12,1,128]{2,1,0:T(2,128)(2,1)S(1)}, u32[]{:S(2)}, u32[]{:S(2)}) collective-permute-start(bf16[12,1,128]{2,1,0:T(2,128)(2,1)} %get-tuple-element.492), channel_id=1, source_target_pairs={{0,2},{2,4},{4,6},{6,8},{8,10},{10,12},{12,14},{14,16},{16,18},{18... | collective-permute-start | bytes 9224 | tf_op jit(solution)/shard_map/ppermute | solution.py:19
  156.5 13.5 %collective-permute-start.15 = (bf16[12,1,128]{2,1,0:T(2,128)(2,1)}, bf16[12,1,128]{2,1,0:T(2,128)(2,1)S(1)}, u32[]{:S(2)}, u32[]{:S(2)}) collective-permute-start(bf16[12,1,128]{2,1,0:T(2,128)(2,1)} %get-tuple-element.493), channel_id=1, source_target_pairs={{2,0},{4,2},{6,4},{8,6},{10,8},{12,10},{14,12},{16,14},{18,16},{20... | collective-permute-start | bytes 9224 | tf_op jit(solution)/shard_map/ppermute | solution.py:20
  173.0 1.5 copy-start.34
  174.5 8.0 %collective-permute-start.18 = (bf16[12,1,128]{2,1,0:T(2,128)(2,1)S(1)}, bf16[12,1,128]{2,1,0:T(2,128)(2,1)S(1)}, u32[]{:S(2)}, u32[]{:S(2)}) collective-permute-start(bf16[12,1,128]{2,1,0:T(2,128)(2,1)S(1)} %get-tuple-element.490), channel_id=1, source_target_pairs={{0,2},{2,4},{4,6},{6,8},{8,10},{10,12},{12,14},{14,16},{16,18},{18... | collective-permute-start | bytes 9224 | tf_op jit(solution)/shard_map/ppermute | solution.py:19
  174.6 7.9 %collective-permute-start.19 = (bf16[12,1,128]{2,1,0:T(2,128)(2,1)S(1)}, bf16[12,1,128]{2,1,0:T(2,128)(2,1)S(1)}, u32[]{:S(2)}, u32[]{:S(2)}) collective-permute-start(bf16[12,1,128]{2,1,0:T(2,128)(2,1)S(1)} %get-tuple-element.491), channel_id=1, source_target_pairs={{2,0},{4,2},{6,4},{8,6},{10,8},{12,10},{14,12},{16,14},{18,16},{20... | collective-permute-start | bytes 9224 | tf_op jit(solution)/shard_map/ppermute | solution.py:20
  186.2 13.3 %collective-permute-start.20 = (bf16[12,128,128]{2,1,0:T(8,128)(2,1)}, bf16[12,128,128]{2,1,0:T(8,128)(2,1)S(1)}, u32[]{:S(2)}, u32[]{:S(2)}) collective-permute-start(bf16[12,128,128]{2,1,0:T(8,128)(2,1)} %get-tuple-element.461), channel_id=1, source_target_pairs={{1,0},{3,2},{5,4},{7,6},{9,8},{11,10},{13,12},{15,14},{17,16},{19,... | collective-permute-start | bytes 1179656 | tf_op jit(solution)/shard_map/ppermute | solution.py:28
  195.9 2.8 copy-start.3
  201.7 9.8 %copy-start.19 = (bf16[12,128,128]{2,1,0:T(8,128)(2,1)}, bf16[12,128,128]{2,1,0:T(8,128)(2,1)S(1)}, u32[]{:S(2)}) copy-start(bf16[12,128,128]{2,1,0:T(8,128)(2,1)S(1)} %get-tuple-element.550) | copy-start | bytes 1179652
  201.7 11.1 %collective-permute-start.23 = (bf16[12,1,128]{2,1,0:T(2,128)(2,1)S(1)}, bf16[12,1,128]{2,1,0:T(2,128)(2,1)S(1)}, u32[]{:S(2)}, u32[]{:S(2)}) collective-permute-start(bf16[12,1,128]{2,1,0:T(2,128)(2,1)S(1)} %get-tuple-element.484), channel_id=1, source_target_pairs={{0,2},{2,4},{4,6},{6,8},{8,10},{10,12},{12,14},{14,16},{16,18},{18... | collective-permute-start | bytes 9224 | tf_op jit(solution)/shard_map/ppermute | solution.py:19
  201.8 11.0 %collective-permute-start.24 = (bf16[12,1,128]{2,1,0:T(2,128)(2,1)S(1)}, bf16[12,1,128]{2,1,0:T(2,128)(2,1)S(1)}, u32[]{:S(2)}, u32[]{:S(2)}) collective-permute-start(bf16[12,1,128]{2,1,0:T(2,128)(2,1)S(1)} %get-tuple-element.485), channel_id=1, source_target_pairs={{2,0},{4,2},{6,4},{8,6},{10,8},{12,10},{14,12},{16,14},{18,16},{20... | collective-permute-start | bytes 9224 | tf_op jit(solution)/shard_map/ppermute | solution.py:20
  212.8 1.2 copy-start.33
  215.8 1.5 copy-start.35
  216.2 9.3 %copy-start.21 = (bf16[1,12,128,128]{3,2,1,0:T(8,128)(2,1)S(1)}, bf16[1,12,128,128]{3,2,1,0:T(8,128)(2,1)}, u32[]{:S(2)}) copy-start(bf16[1,12,128,128]{3,2,1,0:T(8,128)(2,1)} %constant_dynamic-slice_fusion.13) | copy-start | bytes 1179652
  217.3 8.2 %copy-start.4 = (bf16[2,12,128,128]{3,2,1,0:T(8,128)(2,1)S(1)}, bf16[2,12,128,128]{3,2,1,0:T(8,128)(2,1)}, u32[]{:S(2)}) copy-start(bf16[2,12,128,128]{3,2,1,0:T(8,128)(2,1)} %copy-done.2) | copy-start | bytes 2359300
  217.3 8.0 %collective-permute-start.27 = (bf16[12,1,128]{2,1,0:T(2,128)(2,1)S(1)}, bf16[12,1,128]{2,1,0:T(2,128)(2,1)S(1)}, u32[]{:S(2)}, u32[]{:S(2)}) collective-permute-start(bf16[12,1,128]{2,1,0:T(2,128)(2,1)S(1)} %get-tuple-element.482), channel_id=1, source_target_pairs={{0,2},{2,4},{4,6},{6,8},{8,10},{10,12},{12,14},{14,16},{16,18},{18... | collective-permute-start | bytes 9224 | tf_op jit(solution)/shard_map/ppermute | solution.py:19
  217.4 7.9 %collective-permute-start.28 = (bf16[12,1,128]{2,1,0:T(2,128)(2,1)S(1)}, bf16[12,1,128]{2,1,0:T(2,128)(2,1)S(1)}, u32[]{:S(2)}, u32[]{:S(2)}) collective-permute-start(bf16[12,1,128]{2,1,0:T(2,128)(2,1)S(1)} %get-tuple-element.483), channel_id=1, source_target_pairs={{2,0},{4,2},{6,4},{8,6},{10,8},{12,10},{14,12},{16,14},{18,16},{20... | collective-permute-start | bytes 9224 | tf_op jit(solution)/shard_map/ppermute | solution.py:20
  228.0 6.8 %collective-permute-start.29 = (bf16[12,128,128]{2,1,0:T(8,128)(2,1)}, bf16[12,128,128]{2,1,0:T(8,128)(2,1)S(1)}, u32[]{:S(2)}, u32[]{:S(2)}) collective-permute-start(bf16[12,128,128]{2,1,0:T(8,128)(2,1)} %get-tuple-element.459), channel_id=1, source_target_pairs={{1,0},{3,2},{5,4},{7,6},{9,8},{11,10},{13,12},{15,14},{17,16},{19,... | collective-permute-start | bytes 1179656 | tf_op jit(solution)/shard_map/ppermute | solution.py:28
  237.1 10.0 %copy-start.17 = (bf16[12,128,128]{2,1,0:T(8,128)(2,1)}, bf16[12,128,128]{2,1,0:T(8,128)(2,1)S(1)}, u32[]{:S(2)}) copy-start(bf16[12,128,128]{2,1,0:T(8,128)(2,1)S(1)} %get-tuple-element.552) | copy-start | bytes 1179652
  237.1 11.3 %collective-permute-start.32 = (bf16[12,1,128]{2,1,0:T(2,128)(2,1)S(1)}, bf16[12,1,128]{2,1,0:T(2,128)(2,1)S(1)}, u32[]{:S(2)}, u32[]{:S(2)}) collective-permute-start(bf16[12,1,128]{2,1,0:T(2,128)(2,1)S(1)} %get-tuple-element.476), channel_id=1, source_target_pairs={{0,2},{2,4},{4,6},{6,8},{8,10},{10,12},{12,14},{14,16},{16,18},{18... | collective-permute-start | bytes 9224 | tf_op jit(solution)/shard_map/ppermute | solution.py:19
  237.5 11.0 %collective-permute-start.33 = (bf16[12,1,128]{2,1,0:T(2,128)(2,1)S(1)}, bf16[12,1,128]{2,1,0:T(2,128)(2,1)S(1)}, u32[]{:S(2)}, u32[]{:S(2)}) collective-permute-start(bf16[12,1,128]{2,1,0:T(2,128)(2,1)S(1)} %get-tuple-element.477), channel_id=1, source_target_pairs={{2,0},{4,2},{6,4},{8,6},{10,8},{12,10},{14,12},{16,14},{18,16},{20... | collective-permute-start | bytes 9224 | tf_op jit(solution)/shard_map/ppermute | solution.py:20
  248.5 1.2 copy-start.31
  251.6 3.2 copy-start.6
  331.6 8.2 %collective-permute-start.36 = (bf16[12,1,128]{2,1,0:T(2,128)(2,1)S(1)}, bf16[12,1,128]{2,1,0:T(2,128)(2,1)S(1)}, u32[]{:S(2)}, u32[]{:S(2)}) collective-permute-start(bf16[12,1,128]{2,1,0:T(2,128)(2,1)S(1)} %get-tuple-element.474), channel_id=1, source_target_pairs={{0,2},{2,4},{4,6},{6,8},{8,10},{10,12},{12,14},{14,16},{16,18},{18... | collective-permute-start | bytes 9224 | tf_op jit(solution)/shard_map/ppermute | solution.py:19
  331.7 8.1 %collective-permute-start.37 = (bf16[12,1,128]{2,1,0:T(2,128)(2,1)S(1)}, bf16[12,1,128]{2,1,0:T(2,128)(2,1)S(1)}, u32[]{:S(2)}, u32[]{:S(2)}) collective-permute-start(bf16[12,1,128]{2,1,0:T(2,128)(2,1)S(1)} %get-tuple-element.475), channel_id=1, source_target_pairs={{2,0},{4,2},{6,4},{8,6},{10,8},{12,10},{14,12},{16,14},{18,16},{20... | collective-permute-start | bytes 9224 | tf_op jit(solution)/shard_map/ppermute | solution.py:20
  (32 other events, 31.9 us)
Sparse Core Ops, SparseCore 0:
  254.2 243.9 all-reduce.20
where the time goes:
time: 517 us; the launch traced here: 507 us
  waiting for transfers between devices  158 us (31%)
  starting transfers between devices  147 us (28%)
  blocking collectives  75 us (15%)
  other arithmetic  51.4 us (10%)
  matrix products  39.2 us (8%)
  between operations  19.5 us (4%)
  local copies, waits for them, and re-layouts  17 us (3%)
    psum x1, waiting for transfers between devices, shards(): summed = lax.psum(totals, ('blk', 'pipe'))  153 us
    ppermute x18, starting transfers between devices, padded_2(): after = lax.ppermute(first, axis, down)  128 us
    psum x1, blocking collectives, shards(): summed = lax.psum(totals, ('blk', 'pipe'))  75 us
    dot_general x12, matrix products, mixing(): jnp.dot(mixed_bf.reshape(height * breadth, channels), point, preferred_el...  18.3 us
    dot_general x6, matrix products, retreat(): lax.dot_general(flat_mix, flat_gate, (((0,), (0,)), ((), ())), preferred_...  14.3 us
    ppermute x4, starting transfers between devices, passed_along(): lax.ppermute(value, axis, [(source, source + steps) for source in range(f...  14.2 us
  transfers between devices with their start and end apart: 41, of which 7 were waited for; matrix products, arithmetic and copies ran while one was open for 12% of the time, Pallas kernels for 0%

commit v1 on v0

v1 whole, which is shorter than its diff:
```python
import math

import jax
import jax.numpy as jnp
from jax import lax
from jax.sharding import PartitionSpec as P

root_half = 0.7071067811865476
density_norm = 0.3989422804014327

X_HALO = 8
G_HALO = 4


def gelu_pair(preact):
    normal_cdf = 0.5 * (1.0 + lax.erf(preact * root_half))
    normal_pdf = density_norm * jnp.exp(-0.5 * preact * preact)
    return (preact * normal_cdf, normal_cdf + preact * normal_pdf)


def select_row(table, chosen):
    return lax.dynamic_index_in_dim(table, chosen, 0, keepdims=False)


def pad_rows(x):
    return jnp.pad(x, ((1, 1), (0, 0), (0, 0)))


def conv_forward(padded, depth):
    height = padded.shape[0] - 2
    breadth = padded.shape[1] - 2
    acc = jnp.zeros((height, breadth, padded.shape[2]), jnp.float32)
    for i in range(3):
        for j in range(3):
            acc = acc + depth[i, j] * padded[i : i + height, j : j + breadth].astype(jnp.float32)
    return acc


def conv_backward(spread, depth):
    height = spread.shape[0] - 2
    breadth = spread.shape[1] - 2
    acc = jnp.zeros((height, breadth, spread.shape[2]), jnp.float32)
    for i in range(3):
        for j in range(3):
            acc = acc + depth[i, j] * spread[
                2 - i : 2 - i + height, 2 - j : 2 - j + breadth
            ].astype(jnp.float32)
    return acc


def shards(endpoints, row_counts, layer_order, depth_weight, point_weight, point_bias):
    held = endpoints[0]
    height = held.shape[1]
    breadth = held.shape[2]
    channels = held.shape[3]
    layers = layer_order.shape[0]
    core = lax.axis_index("pipe")

    swap = [(0, 1), (1, 0)]
    sent = select_row(held, 1 - core)
    received = lax.ppermute(sent, "pipe", swap)
    mine = select_row(held, core)
    x_in = jnp.where(core == 0, mine, received)
    g_in = jnp.where(core == 0, received, mine)

    edge_x_hi = x_in[:, breadth - X_HALO :]
    edge_x_lo = x_in[:, :X_HALO]
    edge_g_hi = g_in[:, breadth - G_HALO :]
    edge_g_lo = g_in[:, :G_HALO]
    size = lax.axis_size("blk")
    up = [(i, (i + 1) % size) for i in range(size)]
    down = [(j, i) for i, j in up]
    from_left = lax.ppermute(jnp.concatenate([edge_x_hi, edge_g_hi], axis=1), "blk", up)
    from_right = lax.ppermute(jnp.concatenate([edge_x_lo, edge_g_lo], axis=1), "blk", down)
    x_wide = jnp.concatenate([from_left[:, :X_HALO], x_in, from_right[:, :X_HALO]], axis=1)
    g_wide = jnp.concatenate([from_left[:, X_HALO:], g_in, from_right[:, X_HALO:]], axis=1)

    live = (jnp.arange(height)[:, None, None] < select_row(row_counts, core)).astype(jnp.float32)

    weights = []
    for p in range(layers):
        w = layer_order[p]
        weights.append(
            (select_row(depth_weight, w), select_row(point_weight, w), select_row(point_bias, w))
        )

    activation = (x_wide.astype(jnp.float32) * live).astype(jnp.bfloat16)
    acts, mixes, preacts = [], [], []
    for p in range(layers):
        depth, point, offset_vec = weights[p]
        acts.append(activation)
        mixed = conv_forward(pad_rows(activation), depth).astype(jnp.bfloat16)
        rows, span = mixed.shape[0], mixed.shape[1]
        preact = jnp.dot(
            mixed.reshape(rows * span, channels), point, preferred_element_type=jnp.float32
        ).reshape(rows, span, channels) + offset_vec
        mixes.append(mixed)
        preacts.append(preact)
        activation = (
            (activation[:, 1:-1].astype(jnp.float32) + gelu_pair(preact)[0]) * live
        ).astype(jnp.bfloat16)
    final_halo = X_HALO - layers
    outcome = activation[:, final_halo : final_halo + breadth]

    cotangent = g_wide
    depth_terms, point_terms, bias_terms = [None] * layers, [None] * layers, [None] * layers
    for p in range(layers - 1, -1, -1):
        depth, point, _ = weights[p]
        halo_c = (cotangent.shape[1] - breadth) // 2
        halo_p = (preacts[p].shape[1] - breadth) // 2
        shift = halo_p - halo_c
        span = cotangent.shape[1]
        preact = preacts[p][:, shift : shift + span]
        masked = cotangent.astype(jnp.float32) * live
        gated = (masked * gelu_pair(preact)[1]).astype(jnp.bfloat16)
        back_mix = lax.dot_general(
            gated.reshape(height * span, channels),
            point,
            (((1,), (1,)), ((), ())),
            preferred_element_type=jnp.float32,
        ).reshape(height, span, channels).astype(jnp.bfloat16)

        gate_in = gated[:, halo_c : halo_c + breadth].reshape(height * breadth, channels)
        mix_in = mixes[p][:, halo_p : halo_p + breadth].reshape(height * breadth, channels)
        point_terms[p] = lax.dot_general(
            mix_in, gate_in, (((0,), (0,)), ((), ())), preferred_element_type=jnp.float32
        )
        bias_terms[p] = jnp.sum(gate_in.astype(jnp.float32), axis=0)
        back_in = back_mix[:, halo_c : halo_c + breadth].astype(jnp.float32)
        padded = pad_rows(acts[p])
        halo_a = (acts[p].shape[1] - breadth) // 2
        rows_k = []
        for i in range(3):
            row_k = []
            for j in range(3):
                start = halo_a - 1 + j
                row_k.append(
                    jnp.sum(
                        back_in * padded[i : i + height, start : start + breadth].astype(jnp.float32),
                        axis=(0, 1),
                    )
                )
            rows_k.append(jnp.stack(row_k))
        depth_terms[p] = jnp.stack(rows_k)

        earlier = conv_backward(pad_rows(back_mix), depth)
        cotangent = ((masked[:, 1:-1] + earlier) * live).astype(jnp.bfloat16)
    input_grad = cotangent

    got_outcome = lax.ppermute(outcome, "pipe", [(0, 1)])
    got_grad = lax.ppermute(input_grad, "pipe", [(1, 0)])
    first = jnp.where(core == 0, input_grad, got_outcome)
    second = jnp.where(core == 0, got_grad, outcome)
    result = jnp.stack([first, second])[None]

    totals = (jnp.stack(depth_terms), jnp.stack(point_terms), jnp.stack(bias_terms))
    summed = lax.psum(totals, ("blk", "pipe"))
    inverse = jnp.zeros((layers,), jnp.int32).at[layer_order].set(jnp.arange(layers, dtype=jnp.int32))
    factor = 1.0 / math.sqrt(held.shape[0] * height * breadth * lax.axis_size("blk"))
    ordered = tuple(jnp.take(s, inverse, axis=0) * factor for s in summed)
    return (result, ordered[0], ordered[1], ordered[2])


def solution(mesh):
    in_specs = (P("pipe", None, None, "blk", None), P(), P(), P(), P(), P())
    out_specs = (P("pipe", None, None, "blk", None), P(), P(), P())
    return jax.shard_map(shards, mesh=mesh, in_specs=in_specs, out_specs=out_specs, check_vma=False)
```

time: 517 us -> 390 us (0.75); the launches traced: 507 us -> 389 us
  starting transfers between devices: 147 us -> 15.9 us
  waiting for transfers between devices: 158 us -> 246 us
  other arithmetic: 51.4 us -> 17.2 us
  matrix products: 39.2 us -> 5.41 us
  local copies, waits for them, and re-layouts: 17 us -> 9.03 us
    ppermute x40 -> x5, starting transfers between devices: 147 us -> 15.9 us  [the longest x1 8.56 us: shards(): lax.ppermute(jnp.concatenate([edge_x_lo, edge_g_lo], axis=1), 'blk', down)]
    psum x1, waiting for transfers between devices: 153 us -> 239 us  [shards(): summed = lax.psum(totals, ('blk', 'pipe'))]
    dot_general x24 -> x12, matrix products: 39.2 us -> 5.41 us  [the longest x4 2.54 us: shards(): jnp.dot(mixed.reshape(rows * span, channels), point, preferred_element_ty...]
    scatter x6 -> x0, other arithmetic: 9.87 us -> none  [store_at(): buf.at[chosen].set(jnp.where(active, item, select_row(buf, chosen)))]
    convert_element_type x15 -> x11, other arithmetic: 17.7 us -> 8.57 us  [the longest x3 4.58 us: shards(): gated = (masked * gelu_pair(preact)[1]).astype(jnp.bfloat16)]
    another operation x30 -> x21, other arithmetic: 9.15 us -> 1.87 us  [the longest x2 0.99 us: shards(): result = jnp.stack([first, second])[None]]
    concatenate x18 -> x2, other arithmetic: 5.55 us -> 0.03 us  [the longest x1 0.01 us: shards(): jnp.concatenate([edge_x_lo, edge_g_lo], axis=1)]
  transfers between devices with their start and end apart: 41 -> 6, of which waited for: 7 -> 3; matrix products, arithmetic and copies ran while one was open for 12% -> 3% of each run, Pallas kernels for 0% -> 0%
where the time goes in v1:
time: 390 us; the launch traced here: 389 us
  waiting for transfers between devices  246 us (63%)
  blocking collectives  72.5 us (19%)
  between operations  22.4 us (6%)
  other arithmetic  17.2 us (4%)
  starting transfers between devices  15.9 us (4%)
  local copies, waits for them, and re-layouts  9.03 us (2%)
  matrix products  5.41 us (1%)
    psum x1, waiting for transfers between devices, shards(): summed = lax.psum(totals, ('blk', 'pipe'))  239 us
    psum x1, blocking collectives, shards(): summed = lax.psum(totals, ('blk', 'pipe'))  72.5 us
    ppermute x1, starting transfers between devices, shards(): lax.ppermute(jnp.concatenate([edge_x_lo, edge_g_lo], axis=1), 'blk', down)  8.56 us
  transfers between devices with their start and end apart: 6, of which 3 were waited for; matrix products, arithmetic and copies ran while one was open for 3% of the time, Pallas kernels for 0%

profile of v1, /device:TPU:1, one launch (start us, length us, event | category | flops | bytes accessed | tf_op | source)
XLA Modules:
  0.0 388.8 jit_solution(9636832579034243003)
XLA Ops:
  7.2 0.0 copy-start
  7.2 0.0 all-reduce.11.cloned.1.call-start
  7.2 1.1 dynamic-slice_bitcast_fusion
  8.3 3.3 collective-permute-start
  11.7 0.7 copy-done.5
  12.3 0.6 fusion.141
  14.2 0.0 copy-start.4
  20.9 0.6 scatter_custom_fusion
  21.5 0.6 copy-done.7
  22.2 0.6 dynamic_slice.52
  22.8 0.1 bitcast_select_fusion.1
  22.9 8.6 %collective-permute-start.2 = (bf16[12,12,128]{2,1,0:T(8,128)(2,1)S(1)}, bf16[12,12,128]{2,1,0:T(8,128)(2,1)S(1)}, u32[]{:S(2)}, u32[]{:S(2)}) collective-permute-start(bf16[12,12,128]{2,1,0:T(8,128)(2,1)S(1)} %pad_maximum_fusion.2), channel_id=1, source_target_pairs={{2,0},{4,2},{6,4},{8,6},{10,8},{12,10},{14,12},{16,14},{18,16},{20... | collective-permute-start | bytes 110600 | tf_op jit(solution)/shard_map/ppermute | solution.py:74
  31.5 0.1 collective-permute-start.1
  31.6 0.7 compare_convert_fusion
  32.3 0.4 collective-permute-done.2
  32.7 0.6 copy-done.2
  33.3 6.7 %collective-permute-done.1 = bf16[12,12,128]{2,1,0:T(8,128)(2,1)S(1)} collective-permute-done((bf16[12,12,128]{2,1,0:T(8,128)(2,1)S(1)}, bf16[12,12,128]{2,1,0:T(8,128)(2,1)S(1)}, u32[]{:S(2)}, u32[]{:S(2)}) %collective-permute-start.1) | collective-permute-done | bytes 36896 | tf_op jit(solution)/shard_map/ppermute | solution.py:73
  40.0 0.7 slice-done
  40.7 0.2 multiply_convert_fusion
  40.9 0.7 fusion.5
  41.6 0.5 fusion.7
  42.1 0.7 fusion.13
  42.8 0.5 fusion.15
  43.3 0.7 fusion.21
  44.0 0.5 fusion.23
  44.6 0.1 slice_convert_fusion
  44.7 0.7 add_convert_fusion
  45.3 0.1 copy-done.3
  45.5 1.0 fusion.29
  46.5 0.4 convolution_convert_fusion.3
  46.9 0.2 convert_reduce_fusion
  47.1 0.9 fusion.72
  48.0 1.5 fusion.35
  49.5 0.4 convolution_convert_fusion.2
  49.9 0.2 convert_reduce_fusion.1
  50.1 0.9 fusion.63
  50.9 1.5 fusion.41
  52.5 0.4 convolution_convert_fusion.1
  52.9 0.2 convert_reduce_fusion.2
  53.1 0.7 fusion.54
  53.8 1.5 fusion.47
  55.3 0.4 convolution_convert_fusion
  55.7 0.2 convert_reduce_fusion.3
  56.0 0.3 convolution_bitcast_fusion
  56.3 0.3 convolution_bitcast_fusion.1
  56.7 0.3 convolution_bitcast_fusion.2
  57.0 0.3 fusion.99
  57.3 1.3 collective-permute-start.3
  58.6 0.9 fusion.89
  59.7 72.5 %all-reduce.8 = (f32[4,3,3,128]{3,2,1,0:T(4,128)S(1)}, f32[4,128]{1,0:T(4,128)S(1)}) all-reduce(f32[4,3,3,128]{3,2,1,0:T(4,128)S(1)} %pad_maximum_fusion.3, f32[4,128]{1,0:T(4,128)S(1)} %pad_maximum_fusion.4), channel_id=1, replica_groups=mesh['blk'=128,'pipe'=2] {'blk','pipe'}, use_global_device_ids=true, to_apply=%region_37.38 | all-reduce | flops 5120 | bytes 40960 | tf_op jit(solution)/shard_map/psum | solution.py:157
  132.2 0.6 gather_fusion
  132.7 0.1 select_multiply_fusion.1
  132.8 0.6 copy.19
  133.4 0.3 convolution_bitcast_fusion.3
  133.8 0.7 pad_maximum_fusion
  134.5 0.0 all-reduce.11.cloned.1.call-update
  134.5 0.6 gather_fusion.2
  135.1 0.9 select_bitcast_fusion.1
  136.0 2.6 collective-permute-start.4
  138.7 0.7 select_multiply_fusion.2
  139.3 239.3 %all-reduce.11.cloned.1.call-done = f32[4,128,128]{2,1,0:T(8,128)} async-done(((f32[4,128,128]{2,1,0:T(8,128)}), f32[4,128,128]{2,1,0:T(8,128)}) %all-reduce.11.cloned.1.call-update) | async-done | bytes 262160 | tf_op jit(solution)/shard_map/psum | solution.py:157
  378.6 1.5 gather_fusion.1
  380.2 0.8 select_multiply_fusion
  381.0 0.9 maximum_bitcast_fusion
  (53 shorter events, 0.4 us)
Async XLA Ops:
  7.2 34.4 %copy-start = (bf16[4,128,128]{2,1,0:T(8,128)(2,1)S(1)}, bf16[4,128,128]{2,1,0:T(8,128)(2,1)}, u32[]{:S(2)}) copy-start(bf16[4,128,128]{2,1,0:T(8,128)(2,1)} %param.10) | copy-start | bytes 393220
  7.2 15.6 %copy-start.1 = (bf16[1,2,12,128,128]{4,3,2,1,0:T(8,128)(2,1)S(1)}, bf16[1,2,12,128,128]{4,3,2,1,0:T(8,128)(2,1)}, u32[]{:S(2)}) copy-start(bf16[1,2,12,128,128]{4,3,2,1,0:T(8,128)(2,1)} %param.6) | copy-start | bytes 2359300
  7.2 371.4 %all-reduce.11.cloned.1.call-start = ((), (), s32[]{:S(2)}) async-start(), calls=%async_computation | async-start | bytes 524288 | tf_op jit(solution)/shard_map/psum | solution.py:157
  8.3 14.4 %collective-permute-start = (bf16[12,128,128]{2,1,0:T(8,128)(2,1)S(1)}, bf16[12,128,128]{2,1,0:T(8,128)(2,1)S(1)}, u32[]{:S(2)}, u32[]{:S(2)}) collective-permute-start(bf16[12,128,128]{2,1,0:T(8,128)(2,1)S(1)} %dynamic-slice_bitcast_fusion), channel_id=1, source_target_pairs={{0,1},{1,0},{2,3},{3,2},{4,5},{5,4},{6,7},{7,6},{8,9},{9,8},{10,11... | collective-permute-start | bytes 1179656 | tf_op jit(solution)/shard_map/ppermute | solution.py:61
  11.7 0.7 copy-start.5
  14.2 6.6 %copy-start.4 = (f32[4,3,3,128]{3,0,2,1:T(4,128)S(1)}, f32[4,3,3,128]{3,0,2,1:T(4,128)}, u32[]{:S(2)}) copy-start(f32[4,3,3,128]{3,0,2,1:T(4,128)} %param.9) | copy-start | bytes 55300
  19.4 1.3 copy-start.6
  21.5 0.7 copy-start.7
  22.9 9.7 %collective-permute-start.2 = (bf16[12,12,128]{2,1,0:T(8,128)(2,1)S(1)}, bf16[12,12,128]{2,1,0:T(8,128)(2,1)S(1)}, u32[]{:S(2)}, u32[]{:S(2)}) collective-permute-start(bf16[12,12,128]{2,1,0:T(8,128)(2,1)S(1)} %pad_maximum_fusion.2), channel_id=1, source_target_pairs={{2,0},{4,2},{6,4},{8,6},{10,8},{12,10},{14,12},{16,14},{18,16},{20... | collective-permute-start | bytes 110600 | tf_op jit(solution)/shard_map/ppermute | solution.py:74
  31.5 8.4 %collective-permute-start.1 = (bf16[12,12,128]{2,1,0:T(8,128)(2,1)S(1)}, bf16[12,12,128]{2,1,0:T(8,128)(2,1)S(1)}, u32[]{:S(2)}, u32[]{:S(2)}) collective-permute-start(bf16[12,12,128]{2,1,0:T(8,128)(2,1)S(1)} %pad_maximum_fusion.1), channel_id=1, source_target_pairs={{0,2},{2,4},{4,6},{6,8},{8,10},{10,12},{12,14},{14,16},{16,18},{18... | collective-permute-start | bytes 110600 | tf_op jit(solution)/shard_map/ppermute | solution.py:73
  32.7 0.6 copy-start.2
  40.0 0.7 slice-start
  44.6 0.8 copy-start.3
  57.3 77.8 %collective-permute-start.3 = (bf16[12,128,128]{2,1,0:T(8,128)(2,1)S(1)}, bf16[12,128,128]{2,1,0:T(8,128)(2,1)S(1)}, u32[]{:S(2)}, u32[]{:S(2)}) collective-permute-start(bf16[12,128,128]{2,1,0:T(8,128)(2,1)S(1)} %fusion.99), channel_id=1, source_target_pairs={{0,1},{2,3},{4,5},{6,7},{8,9},{10,11},{12,13},{14,15},{16,17},{18,... | collective-permute-start | bytes 1179656 | tf_op jit(solution)/shard_map/ppermute | solution.py:150
  136.0 244.9 %collective-permute-start.4 = (bf16[12,128,128]{2,1,0:T(8,128)(2,1)S(1)}, bf16[12,128,128]{2,1,0:T(8,128)(2,1)S(1)}, u32[]{:S(2)}, u32[]{:S(2)}) collective-permute-start(bf16[12,128,128]{2,1,0:T(8,128)(2,1)S(1)} %get-tuple-element.51), channel_id=1, source_target_pairs={{1,0},{3,2},{5,4},{7,6},{9,8},{11,10},{13,12},{15,14},{17,16},{19,... | collective-permute-start | bytes 1179656 | tf_op jit(solution)/shard_map/ppermute | solution.py:151
Sparse Core Ops, SparseCore 0:
  134.6 243.9 all-reduce.10

commit v2 on v1

--- a/solution.py
+++ b/solution.py
@@ -3,13 +3,23 @@
 import jax
 import jax.numpy as jnp
 from jax import lax
-from jax.sharding import PartitionSpec as P
+from jax.sharding import Mesh, PartitionSpec as P
 
 root_half = 0.7071067811865476
 density_norm = 0.3989422804014327
 
 X_HALO = 8
 G_HALO = 4
+
+
+BLK_AXES = ("x", "z", "y")
+
+
+def blk_count():
+    count = 1
+    for axis in BLK_AXES:
+        count *= lax.axis_size(axis)
+    return count
 
 
 def gelu_pair(preact):
@@ -67,11 +77,11 @@
     edge_x_lo = x_in[:, :X_HALO]
     edge_g_hi = g_in[:, breadth - G_HALO :]
     edge_g_lo = g_in[:, :G_HALO]
-    size = lax.axis_size("blk")
+    size = blk_count()
     up = [(i, (i + 1) % size) for i in range(size)]
     down = [(j, i) for i, j in up]
-    from_left = lax.ppermute(jnp.concatenate([edge_x_hi, edge_g_hi], axis=1), "blk", up)
-    from_right = lax.ppermute(jnp.concatenate([edge_x_lo, edge_g_lo], axis=1), "blk", down)
+    from_left = lax.ppermute(jnp.concatenate([edge_x_hi, edge_g_hi], axis=1), BLK_AXES, up)
+    from_right = lax.ppermute(jnp.concatenate([edge_x_lo, edge_g_lo], axis=1), BLK_AXES, down)
     x_wide = jnp.concatenate([from_left[:, :X_HALO], x_in, from_right[:, :X_HALO]], axis=1)
     g_wide = jnp.concatenate([from_left[:, X_HALO:], g_in, from_right[:, X_HALO:]], axis=1)
 
@@ -153,15 +163,30 @@
     second = jnp.where(core == 0, got_grad, outcome)
     result = jnp.stack([first, second])[None]
 
-    totals = (jnp.stack(depth_terms), jnp.stack(point_terms), jnp.stack(bias_terms))
-    summed = lax.psum(totals, ("blk", "pipe"))
+    pieces = (jnp.stack(depth_terms), jnp.stack(point_terms), jnp.stack(bias_terms))
+    flat = jnp.concatenate([piece.reshape(layers, -1) for piece in pieces], axis=1)
+    for axis in ("pipe",) + BLK_AXES:
+        flat = lax.psum(flat, axis)
     inverse = jnp.zeros((layers,), jnp.int32).at[layer_order].set(jnp.arange(layers, dtype=jnp.int32))
-    factor = 1.0 / math.sqrt(held.shape[0] * height * breadth * lax.axis_size("blk"))
-    ordered = tuple(jnp.take(s, inverse, axis=0) * factor for s in summed)
+    factor = 1.0 / math.sqrt(held.shape[0] * height * breadth * blk_count())
+    flat = jnp.take(flat, inverse, axis=0) * factor
+    ordered, at = [], 0
+    for piece in pieces:
+        width = piece[0].size
+        ordered.append(flat[:, at : at + width].reshape(piece.shape))
+        at += width
     return (result, ordered[0], ordered[1], ordered[2])
 
 
 def solution(mesh):
-    in_specs = (P("pipe", None, None, "blk", None), P(), P(), P(), P(), P())
-    out_specs = (P("pipe", None, None, "blk", None), P(), P(), P())
-    return jax.shard_map(shards, mesh=mesh, in_specs=in_specs, out_specs=out_specs, check_vma=False)
+    devices = mesh.devices
+    blk = devices.shape[0]
+    y_size = 4 if blk % 4 == 0 else 1
+    rest = blk // y_size
+    z_size = 8 if rest % 8 == 0 else rest
+    x_size = rest // z_size
+    torus = Mesh(devices.reshape(x_size, z_size, y_size, devices.shape[1]), BLK_AXES + ("pipe",))
+    spec = P("pipe", None, None, BLK_AXES, None)
+    in_specs = (spec, P(), P(), P(), P(), P())
+    out_specs = (spec, P(), P(), P())
+    return jax.shard_map(shards, mesh=torus, in_specs=in_specs, out_specs=out_specs, check_vma=False)

time: 390 us -> 269 us (0.69)
  blocking collectives: 72.5 us -> 0 us
  waiting for transfers between devices: 246 us -> 196 us
    psum x1 -> x0, blocking collectives: 72.5 us -> none  [shards(): summed = lax.psum(totals, ('blk', 'pipe'))]
    psum x1 -> x4, waiting for transfers between devices: 239 us -> 188 us  [shards(): flat = lax.psum(flat, axis)]
  transfers between devices with their start and end apart: 6 -> 9, of which waited for: 3 -> 6; matrix products, arithmetic and copies ran while one was open for 3% -> 2% of each run, Pallas kernels for 0% -> 0%
where the time goes in v2:
time: 269 us; the launch traced here: 267 us
  waiting for transfers between devices  196 us (73%)
  between operations  22.1 us (8%)
  other arithmetic  16 us (6%)
  starting transfers between devices  15.6 us (6%)
  local copies, waits for them, and re-layouts  12.4 us (5%)
  matrix products  5.42 us (2%)
    psum x4, waiting for transfers between devices, shards(): flat = lax.psum(flat, axis)  188 us
    ppermute x1, starting transfers between devices, shards(): lax.ppermute(jnp.concatenate([edge_x_lo, edge_g_lo], axis=1), BLK_AXES, d...  8.56 us
    ppermute x1, waiting for transfers between devices, shards(): lax.ppermute(jnp.concatenate([edge_x_hi, edge_g_hi], axis=1), BLK_AXES, up)  6.67 us
  transfers between devices with their start and end apart: 9, of which 6 were waited for; matrix products, arithmetic and copies ran while one was open for 2% of the time, Pallas kernels for 0%

profile of v2, /device:TPU:1, one launch (start us, length us, event | category | flops | bytes accessed | tf_op | source)
XLA Modules:
  0.0 267.2 jit_solution(16909377268215459945)
XLA Ops:
  7.2 0.0 all-reduce.13.cloned.1.call-start
  7.2 1.1 dynamic-slice_bitcast_fusion
  8.3 3.3 %collective-permute-start = (bf16[12,128,128]{2,1,0:T(8,128)(2,1)S(1)}, bf16[12,128,128]{2,1,0:T(8,128)(2,1)S(1)}, u32[]{:S(2)}, u32[]{:S(2)}) collective-permute-start(bf16[12,128,128]{2,1,0:T(8,128)(2,1)S(1)} %dynamic-slice_bitcast_fusion), channel_id=1, source_target_pairs={{0,1},{1,0},{2,3},{3,2},{4,5},{5,4},{6,7},{7,6},{8,9},{9,8},{10,11... | collective-permute-start | bytes 1179656 | tf_op jit(solution)/shard_map/ppermute | solution.py:71
  11.7 0.7 copy-done.5
  12.3 0.6 fusion.145
  20.9 0.6 copy-done.7
  21.5 0.6 dynamic_slice.52
  22.1 0.1 bitcast_select_fusion.1
  22.3 8.6 %collective-permute-start.2 = (bf16[12,12,128]{2,1,0:T(8,128)(2,1)S(1)}, bf16[12,12,128]{2,1,0:T(8,128)(2,1)S(1)}, u32[]{:S(2)}, u32[]{:S(2)}) collective-permute-start(bf16[12,12,128]{2,1,0:T(8,128)(2,1)S(1)} %pad_maximum_fusion.1), channel_id=1, source_target_pairs={{2,0},{4,2},{6,4},{8,6},{10,8},{12,10},{14,12},{16,14},{18,16},{20... | collective-permute-start | bytes 110600 | tf_op jit(solution)/shard_map/ppermute | solution.py:84
  30.8 0.1 collective-permute-start.1
  30.9 0.7 compare_convert_fusion
  31.6 0.4 collective-permute-done.2
  32.0 0.6 copy-done.2
  32.6 6.7 %collective-permute-done.1 = bf16[12,12,128]{2,1,0:T(8,128)(2,1)S(1)} collective-permute-done((bf16[12,12,128]{2,1,0:T(8,128)(2,1)S(1)}, bf16[12,12,128]{2,1,0:T(8,128)(2,1)S(1)}, u32[]{:S(2)}, u32[]{:S(2)}) %collective-permute-start.1) | collective-permute-done | bytes 36896 | tf_op jit(solution)/shard_map/ppermute | solution.py:83
  39.3 0.7 slice-done
  40.0 0.2 multiply_convert_fusion
  40.2 0.7 fusion.5
  40.9 0.5 fusion.7
  41.4 0.7 fusion.13
  42.1 0.5 fusion.15
  42.7 0.7 fusion.21
  43.4 0.5 fusion.23
  43.9 0.1 slice_convert_fusion
  44.0 0.7 add_convert_fusion
  44.7 0.1 copy-done.3
  44.8 1.0 fusion.29
  45.8 0.4 convolution_convert_fusion.3
  46.2 0.2 convert_reduce_fusion
  46.4 1.5 fusion.35
  48.0 0.4 convolution_convert_fusion.2
  48.4 0.2 convert_reduce_fusion.1
  48.6 1.5 fusion.41
  50.1 0.4 convolution_convert_fusion.1
  50.5 0.2 convert_reduce_fusion.2
  50.7 1.5 fusion.47
  52.2 0.4 convolution_convert_fusion
  52.6 0.2 convert_reduce_fusion.3
  52.8 0.3 fusion.100
  53.2 0.3 fusion.102
  53.5 0.3 fusion.104
  53.9 0.3 fusion.106
  54.2 0.9 fusion.72
  55.1 0.9 fusion.63
  56.0 0.7 fusion.54
  56.7 0.3 fusion.99
  57.0 1.3 collective-permute-start.3
  58.5 0.8 fusion.89
  59.4 1.0 maximum_maximum_fusion
  60.4 0.0 all-reduce.15.cloned.1.call-start
  60.5 0.6 scatter_custom_fusion
  61.1 21.7 %all-reduce.13.cloned.1.call-done = f32[4,17664]{1,0:T(4,128)} async-done(((f32[4,17664]{1,0:T(4,128)}), f32[4,17664]{1,0:T(4,128)}) %all-reduce.13.cloned.1.call-update) | async-done | bytes 282640 | tf_op jit(solution)/shard_map/psum | solution.py:169
  82.9 0.0 all-reduce.17.cloned.1.call-start
  82.9 1.0 select_bitcast_fusion.1
  83.9 2.1 collective-permute-start.4
  86.0 44.6 %all-reduce.15.cloned.1.call-done = f32[4,17664]{1,0:T(4,128)} async-done(((f32[4,17664]{1,0:T(4,128)}), f32[4,17664]{1,0:T(4,128)}) %all-reduce.15.cloned.1.call-update) | async-done | bytes 282640 | tf_op jit(solution)/shard_map/psum | solution.py:169
  130.6 0.0 all-reduce.19.cloned.1.call-start
  130.7 73.4 %all-reduce.17.cloned.1.call-done = f32[4,17664]{1,0:T(4,128)} async-done(((f32[4,17664]{1,0:T(4,128)}), f32[4,17664]{1,0:T(4,128)}) %all-reduce.17.cloned.1.call-update) | async-done | bytes 282640 | tf_op jit(solution)/shard_map/psum | solution.py:169
  204.2 0.9 maximum_bitcast_fusion
  205.1 48.8 %all-reduce.19.cloned.1.call-done = f32[4,17664]{1,0:T(4,128)} async-done(((f32[4,17664]{1,0:T(4,128)}), f32[4,17664]{1,0:T(4,128)}) %all-reduce.19.cloned.1.call-update) | async-done | bytes 282640 | tf_op jit(solution)/shard_map/psum | solution.py:169
  253.9 4.6 %gather_fusion = f32[4,17664]{1,0:T(4,128)S(1)} fusion(f32[4,17664]{1,0:T(4,128)} %all-reduce.19.cloned.1.call-done, s32[1024]{0:T(1024)S(1)} %pad_clamp_fusion), kind=kCustom, calls=%fused_computation | custom fusion | bytes 565264 | tf_op jit(solution)/shard_map/jit(_take)/gather | solution.py:172
  258.5 0.2 select_multiply_fusion
  258.7 0.6 slice.892
  259.3 0.6 slice.894
  259.9 0.7 copy.33
  (62 shorter events, 0.5 us)
Async XLA Ops:
  7.2 33.7 %copy-start = (bf16[4,128,128]{2,1,0:T(8,128)(2,1)S(1)}, bf16[4,128,128]{2,1,0:T(8,128)(2,1)}, u32[]{:S(2)}) copy-start(bf16[4,128,128]{2,1,0:T(8,128)(2,1)} %param.10) | copy-start | bytes 393220
  7.2 15.0 %copy-start.1 = (bf16[1,2,12,128,128]{4,3,2,1,0:T(8,128)(2,1)S(1)}, bf16[1,2,12,128,128]{4,3,2,1,0:T(8,128)(2,1)}, u32[]{:S(2)}) copy-start(bf16[1,2,12,128,128]{4,3,2,1,0:T(8,128)(2,1)} %param.6) | copy-start | bytes 2359300
  7.2 75.6 %all-reduce.13.cloned.1.call-start = ((), (), s32[]{:S(2)}) async-start(), calls=%async_computation | async-start | bytes 565248 | tf_op jit(solution)/shard_map/psum | solution.py:169
  8.3 13.8 %collective-permute-start = (bf16[12,128,128]{2,1,0:T(8,128)(2,1)S(1)}, bf16[12,128,128]{2,1,0:T(8,128)(2,1)S(1)}, u32[]{:S(2)}, u32[]{:S(2)}) collective-permute-start(bf16[12,128,128]{2,1,0:T(8,128)(2,1)S(1)} %dynamic-slice_bitcast_fusion), channel_id=1, source_target_pairs={{0,1},{1,0},{2,3},{3,2},{4,5},{5,4},{6,7},{7,6},{8,9},{9,8},{10,11... | collective-permute-start | bytes 1179656 | tf_op jit(solution)/shard_map/ppermute | solution.py:71
  11.7 0.7 copy-start.5
  14.2 6.6 %copy-start.4 = (f32[4,3,3,128]{3,0,2,1:T(4,128)S(1)}, f32[4,3,3,128]{3,0,2,1:T(4,128)}, u32[]{:S(2)}) copy-start(f32[4,3,3,128]{3,0,2,1:T(4,128)} %param.9) | copy-start | bytes 55300
  19.4 1.3 copy-start.6
  20.9 0.7 copy-start.7
  22.3 9.7 %collective-permute-start.2 = (bf16[12,12,128]{2,1,0:T(8,128)(2,1)S(1)}, bf16[12,12,128]{2,1,0:T(8,128)(2,1)S(1)}, u32[]{:S(2)}, u32[]{:S(2)}) collective-permute-start(bf16[12,12,128]{2,1,0:T(8,128)(2,1)S(1)} %pad_maximum_fusion.1), channel_id=1, source_target_pairs={{2,0},{4,2},{6,4},{8,6},{10,8},{12,10},{14,12},{16,14},{18,16},{20... | collective-permute-start | bytes 110600 | tf_op jit(solution)/shard_map/ppermute | solution.py:84
  30.8 8.4 %collective-permute-start.1 = (bf16[12,12,128]{2,1,0:T(8,128)(2,1)S(1)}, bf16[12,12,128]{2,1,0:T(8,128)(2,1)S(1)}, u32[]{:S(2)}, u32[]{:S(2)}) collective-permute-start(bf16[12,12,128]{2,1,0:T(8,128)(2,1)S(1)} %pad_maximum_fusion), channel_id=1, source_target_pairs={{0,2},{2,4},{4,6},{6,8},{8,10},{10,12},{12,14},{14,16},{16,18},{18... | collective-permute-start | bytes 110600 | tf_op jit(solution)/shard_map/ppermute | solution.py:83
  32.0 0.6 copy-start.2
  39.3 0.7 slice-start
  44.0 0.8 copy-start.3
  57.0 25.9 %collective-permute-start.3 = (bf16[12,128,128]{2,1,0:T(8,128)(2,1)S(1)}, bf16[12,128,128]{2,1,0:T(8,128)(2,1)S(1)}, u32[]{:S(2)}, u32[]{:S(2)}) collective-permute-start(bf16[12,128,128]{2,1,0:T(8,128)(2,1)S(1)} %fusion.99), channel_id=1, source_target_pairs={{0,1},{2,3},{4,5},{6,7},{8,9},{10,11},{12,13},{14,15},{16,17},{18,... | collective-permute-start | bytes 1179656 | tf_op jit(solution)/shard_map/ppermute | solution.py:160
  60.4 70.2 %all-reduce.15.cloned.1.call-start = ((), (), s32[]{:S(2)}) async-start(), calls=%async_computation.1 | async-start | bytes 565248 | tf_op jit(solution)/shard_map/psum | solution.py:169
  82.9 121.2 %all-reduce.17.cloned.1.call-start = ((), (), s32[]{:S(2)}) async-start(), calls=%async_computation.2 | async-start | bytes 565248 | tf_op jit(solution)/shard_map/psum | solution.py:169
  83.9 120.3 %collective-permute-start.4 = (bf16[12,128,128]{2,1,0:T(8,128)(2,1)S(1)}, bf16[12,128,128]{2,1,0:T(8,128)(2,1)S(1)}, u32[]{:S(2)}, u32[]{:S(2)}) collective-permute-start(bf16[12,128,128]{2,1,0:T(8,128)(2,1)S(1)} %get-tuple-element.45), channel_id=1, source_target_pairs={{1,0},{3,2},{5,4},{7,6},{9,8},{11,10},{13,12},{15,14},{17,16},{19,... | collective-permute-start | bytes 1179656 | tf_op jit(solution)/shard_map/ppermute | solution.py:161
  130.6 123.3 %all-reduce.19.cloned.1.call-start = ((), (), s32[]{:S(2)}) async-start(), calls=%async_computation.3 | async-start | bytes 565248 | tf_op jit(solution)/shard_map/psum | solution.py:169
Sparse Core Ops, SparseCore 0:
  60.5 22.2 all-reduce.12
  85.2 45.3 all-reduce.14
  132.9 71.0 all-reduce.16
  206.4 47.4 all-reduce.18

commit v3 on v2

--- a/solution.py
+++ b/solution.py
@@ -56,6 +56,25 @@
                 2 - i : 2 - i + height, 2 - j : 2 - j + breadth
             ].astype(jnp.float32)
     return acc
+
+
+def all_reduce(flat, core):
+    half = flat.shape[1] // 2
+    swap = [(0, 1), (1, 0)]
+    mine = lax.dynamic_slice_in_dim(flat, core * half, half, axis=1)
+    other = lax.dynamic_slice_in_dim(flat, (1 - core) * half, half, axis=1)
+    acc = mine + lax.ppermute(other, "pipe", swap)
+    for axis in ("y", "z", "x"):
+        size = lax.axis_size(axis)
+        bit = 1
+        while bit < size:
+            pairs = [(i, i ^ bit) for i in range(size)]
+            acc = acc + lax.ppermute(acc, axis, pairs)
+            bit *= 2
+    theirs = lax.ppermute(acc, "pipe", swap)
+    low = jnp.where(core == 0, acc, theirs)
+    high = jnp.where(core == 0, theirs, acc)
+    return jnp.concatenate([low, high], axis=1)
 
 
 def shards(endpoints, row_counts, layer_order, depth_weight, point_weight, point_bias):
@@ -165,8 +184,7 @@
 
     pieces = (jnp.stack(depth_terms), jnp.stack(point_terms), jnp.stack(bias_terms))
     flat = jnp.concatenate([piece.reshape(layers, -1) for piece in pieces], axis=1)
-    for axis in ("pipe",) + BLK_AXES:
-        flat = lax.psum(flat, axis)
+    flat = all_reduce(flat, core)
     inverse = jnp.zeros((layers,), jnp.int32).at[layer_order].set(jnp.arange(layers, dtype=jnp.int32))
     factor = 1.0 / math.sqrt(held.shape[0] * height * breadth * blk_count())
     flat = jnp.take(flat, inverse, axis=0) * factor

time: 269 us -> 110 us (0.41)
  waiting for transfers between devices: 196 us -> 35.7 us
  starting transfers between devices: 15.6 us -> 34.6 us
  between operations: 22.1 us -> 9.1 us
  local copies, waits for them, and re-layouts: 12.4 us -> 8.48 us
    psum x4 -> x0, waiting for transfers between devices: 188 us -> none  [shards(): flat = lax.psum(flat, axis)]
    ppermute x0 -> x9, waiting for transfers between devices: none -> 28.6 us  [the longest x7 27.6 us: all_reduce(): acc = acc + lax.ppermute(acc, axis, pairs)]
    ppermute x0 -> x9, starting transfers between devices: none -> 10.5 us  [the longest x1 8.14 us: all_reduce(): theirs = lax.ppermute(acc, 'pipe', swap)]
    ppermute x1, starting transfers between devices: 2.14 us -> 10.8 us  [shards(): got_grad = lax.ppermute(input_grad, 'pipe', [(1, 0)])]
    gather x1, local copies, waits for them, and re-layouts: 4.64 us -> 0.69 us  [shards(): flat = jnp.take(flat, inverse, axis=0) * factor]
  transfers between devices with their start and end apart: 9 -> 14, of which waited for: 6 -> 9; matrix products, arithmetic and copies ran while one was open for 2% -> 5% of each run, Pallas kernels for 0% -> 0%
where the time goes in v3:
time: 110 us
  waiting for transfers between devices  35.7 us (32%)
  starting transfers between devices  34.6 us (31%)
  other arithmetic  15.9 us (14%)
  between operations  9.1 us (8%)
  local copies, waits for them, and re-layouts  8.48 us (8%)
  matrix products  5.96 us (5%)
    ppermute x7, waiting for transfers between devices, all_reduce(): acc = acc + lax.ppermute(acc, axis, pairs)  27.6 us
    ppermute x1, starting transfers between devices, shards(): got_grad = lax.ppermute(input_grad, 'pipe', [(1, 0)])  10.8 us
    ppermute x1, starting transfers between devices, shards(): lax.ppermute(jnp.concatenate([edge_x_lo, edge_g_lo], axis=1), BLK_AXES, d...  8.56 us
    ppermute x1, starting transfers between devices, all_reduce(): theirs = lax.ppermute(acc, 'pipe', swap)  8.14 us
    ppermute x1, waiting for transfers between devices, shards(): lax.ppermute(jnp.concatenate([edge_x_hi, edge_g_hi], axis=1), BLK_AXES, up)  6.67 us
    convert_element_type x3, other arithmetic, shards(): gated = (masked * gelu_pair(preact)[1]).astype(jnp.bfloat16)  4.75 us
    ppermute x1, starting transfers between devices, shards(): received = lax.ppermute(sent, 'pipe', swap)  3.33 us
    reduce_sum x4, other arithmetic, shards(): jnp.sum(back_in * padded[i:i + height, start:start + breadth].astype(jnp....  3.28 us
  transfers between devices with their start and end apart: 14, of which 9 were waited for; matrix products, arithmetic and copies ran while one was open for 5% of the time, Pallas kernels for 0%

profile of v3, /device:TPU:1, one launch (start us, length us, event | category | flops | bytes accessed | tf_op | source)
XLA Modules:
  0.0 109.8 jit_solution(11966202695052193147)
XLA Ops:
  0.7 1.1 %dynamic-slice_bitcast_fusion = bf16[12,128,128]{2,1,0:T(8,128)(2,1)S(1)} fusion(bf16[1,2,12,128,128]{4,3,2,1,0:T(8,128)(2,1)} %param.6, s32[]{:T(128)S(6)} %select_n.84), kind=kLoop, calls=%fused_computation.200 | loop fusion | bytes 786436 | tf_op jit(solution)/shard_map/jit(dynamic_index_in_dim)/squeeze | solution.py:32
  1.8 3.3 %collective-permute-start = (bf16[12,128,128]{2,1,0:T(8,128)(2,1)S(1)}, bf16[12,128,128]{2,1,0:T(8,128)(2,1)S(1)}, u32[]{:S(2)}, u32[]{:S(2)}) collective-permute-start(bf16[12,128,128]{2,1,0:T(8,128)(2,1)S(1)} %dynamic-slice_bitcast_fusion), channel_id=1, source_target_pairs={{0,1},{1,0},{2,3},{3,2},{4,5},{5,4},{6,7},{7,6},{8,9},{9,8},{10,11... | collective-permute-start | bytes 1179656 | tf_op jit(solution)/shard_map/ppermute | solution.py:90
  5.1 0.7 copy-done.6
  5.8 0.6 fusion.145
  14.3 0.6 copy-done.8
  15.0 0.6 dynamic_slice.58
  15.7 8.6 %collective-permute-start.2 = (bf16[12,12,128]{2,1,0:T(8,128)(2,1)S(1)}, bf16[12,12,128]{2,1,0:T(8,128)(2,1)S(1)}, u32[]{:S(2)}, u32[]{:S(2)}) collective-permute-start(bf16[12,12,128]{2,1,0:T(8,128)(2,1)S(1)} %pad_maximum_fusion.2), channel_id=1, source_target_pairs={{2,0},{4,2},{6,4},{8,6},{10,8},{12,10},{14,12},{16,14},{18,16},{20... | collective-permute-start | bytes 110600 | tf_op jit(solution)/shard_map/ppermute | solution.py:103
  24.4 0.7 compare_convert_fusion
  25.0 0.4 collective-permute-done.2
  25.4 0.6 copy-done.3
  26.1 6.7 %collective-permute-done.1 = bf16[12,12,128]{2,1,0:T(8,128)(2,1)S(1)} collective-permute-done((bf16[12,12,128]{2,1,0:T(8,128)(2,1)S(1)}, bf16[12,12,128]{2,1,0:T(8,128)(2,1)S(1)}, u32[]{:S(2)}, u32[]{:S(2)}) %collective-permute-start.1) | collective-permute-done | bytes 36896 | tf_op jit(solution)/shard_map/ppermute | solution.py:102
  32.7 0.7 slice-done
  33.5 0.2 multiply_convert_fusion
  33.6 0.7 fusion.5
  34.3 0.5 fusion.7
  34.9 0.7 fusion.13
  35.6 0.5 fusion.15
  36.1 0.7 fusion.21
  36.8 0.5 fusion.23
  37.3 0.7 add_convert_fusion
  38.0 0.1 copy-done.4
  38.2 1.6 %fusion.29 = (bf16[12,136,128]{2,1,0:T(8,128)(2,1)S(1)}, f32[12,136,128]{2,1,0:T(8,128)S(1)}, f32[12,136,128]{2,1,0:T(8,128)S(1)}, f32[12,136,128]{2,1,0:T(8,128)}) fusion(f32[12]{0:T(128)S(1)} %compare_convert_fusion, bf16[12,4,128]{2,1,0:T(4,128)(2,1)S(1)} %slice.796, bf16[12,128,128]{2,1,0:T(8,128)(2,1)S(1)} %get-tuple-element.55, ...), kind=kOutput, calls=%fused_computation.87 | convolution fusion | flops 57237504 | bytes 3793924 | tf_op jit(solution)/shard_map/dot_general | solution.py:123
  39.7 0.4 convolution_convert_fusion.3
  40.1 0.2 convert_reduce_fusion
  40.3 1.7 %fusion.35 = (bf16[12,134,128]{2,1,0:T(8,128)(2,1)S(1)}, f32[12,134,128]{2,1,0:T(8,128)S(1)}) fusion(f32[12,138,128]{2,1,0:T(8,128)S(1)} %get-tuple-element.116, f32[12]{0:T(128)S(1)} %compare_convert_fusion, f32[128]{0:T(128)S(1)} %get-tuple-element.68, f32[128]{0:T(128)S(1)} %get-tuple-element.69, f32[128]{0:T(128)S(1)} %get-tuple-element.70, ...), kind=kLoop, calls=%fused_computation.93 | loop fusion | flops 8438784 | bytes 4582400 | tf_op jit(solution)/shard_map/convert_element_type | solution.py:144
  42.0 0.4 convolution_convert_fusion.2
  42.4 0.2 convert_reduce_fusion.1
  42.6 1.5 %fusion.41 = (bf16[12,132,128]{2,1,0:T(8,128)(2,1)S(1)}, f32[12,132,128]{2,1,0:T(8,128)S(1)}) fusion(f32[12,140,128]{2,1,0:T(8,128)S(1)} %get-tuple-element.114, f32[12]{0:T(128)S(1)} %compare_convert_fusion, f32[128]{0:T(128)S(1)} %get-tuple-element.77, f32[128]{0:T(128)S(1)} %get-tuple-element.78, f32[128]{0:T(128)S(1)} %get-tuple-element.79, ...), kind=kLoop, calls=%fused_computation.99 | loop fusion | flops 8312832 | bytes 4563968 | tf_op jit(solution)/shard_map/convert_element_type | solution.py:144
  44.2 0.4 convolution_convert_fusion.1
  44.5 0.2 convert_reduce_fusion.2
  44.8 1.5 %fusion.47 = (bf16[12,130,128]{2,1,0:T(8,128)(2,1)S(1)}, f32[12,130,128]{2,1,0:T(8,128)S(1)}) fusion(f32[12,142,128]{2,1,0:T(8,128)S(1)} %get-tuple-element.112, f32[12]{0:T(128)S(1)} %compare_convert_fusion, f32[128]{0:T(128)S(1)} %get-tuple-element.86, f32[128]{0:T(128)S(1)} %get-tuple-element.87, f32[128]{0:T(128)S(1)} %get-tuple-element.88, ...), kind=kLoop, calls=%fused_computation.105 | loop fusion | flops 8186880 | bytes 4545536 | tf_op jit(solution)/shard_map/convert_element_type | solution.py:144
  46.3 0.4 convolution_convert_fusion
  46.7 0.2 convert_reduce_fusion.3
  46.9 0.3 fusion.100
  47.2 0.3 fusion.102
  47.6 0.3 fusion.104
  47.9 0.3 fusion.106
  48.3 0.9 fusion.72
  49.1 0.9 fusion.63
  50.0 0.7 fusion.54
  51.0 0.8 fusion.89
  51.9 0.3 maximum_maximum_fusion
  52.2 1.5 %collective-permute-start.5 = (f32[4,8832]{1,0:T(4,128)S(1)}, f32[4,8832]{1,0:T(4,128)S(1)}, u32[]{:S(2)}, u32[]{:S(2)}) collective-permute-start(f32[4,8832]{1,0:T(4,128)S(1)} %constant_dynamic-slice_fusion), channel_id=1, source_target_pairs={{0,1},{1,0},{2,3},{3,2},{4,5},{5,4},{6,7},{7,6},{8,9},{9,8},{10,11... | collective-permute-start | bytes 423944 | tf_op jit(solution)/shard_map/ppermute | solution.py:66
  53.7 1.0 collective-permute-done.5
  55.0 4.8 %collective-permute-done.6 = f32[4,8832]{1,0:T(4,128)S(1)} collective-permute-done((f32[4,8832]{1,0:T(4,128)S(1)}, f32[4,8832]{1,0:T(4,128)S(1)}, u32[]{:S(2)}, u32[]{:S(2)}) %collective-permute-start.6) | collective-permute-done | bytes 141344 | tf_op jit(solution)/shard_map/ppermute | solution.py:72
  59.9 0.3 fusion.99
  60.2 1.3 %collective-permute-start.3 = (bf16[12,128,128]{2,1,0:T(8,128)(2,1)S(1)}, bf16[12,128,128]{2,1,0:T(8,128)(2,1)S(1)}, u32[]{:S(2)}, u32[]{:S(2)}) collective-permute-start(bf16[12,128,128]{2,1,0:T(8,128)(2,1)S(1)} %fusion.99), channel_id=1, source_target_pairs={{0,1},{2,3},{4,5},{6,7},{8,9},{10,11},{12,13},{14,15},{16,17},{18,... | collective-permute-start | bytes 1179656 | tf_op jit(solution)/shard_map/ppermute | solution.py:179
  61.5 3.8 %collective-permute-done.7 = f32[4,8832]{1,0:T(4,128)S(1)} collective-permute-done((f32[4,8832]{1,0:T(4,128)S(1)}, f32[4,8832]{1,0:T(4,128)S(1)}, u32[]{:S(2)}, u32[]{:S(2)}) %collective-permute-start.7) | collective-permute-done | bytes 141344 | tf_op jit(solution)/shard_map/ppermute | solution.py:72
  65.4 0.1 collective-permute-start.8
  65.5 3.9 %collective-permute-done.8 = f32[4,8832]{1,0:T(4,128)S(1)} collective-permute-done((f32[4,8832]{1,0:T(4,128)S(1)}, f32[4,8832]{1,0:T(4,128)S(1)}, u32[]{:S(2)}, u32[]{:S(2)}) %collective-permute-start.8) | collective-permute-done | bytes 141344 | tf_op jit(solution)/shard_map/ppermute | solution.py:72
  69.4 0.3 collective-permute-start.9
  69.8 0.6 scatter_custom_fusion
  70.4 5.4 %collective-permute-done.9 = f32[4,8832]{1,0:T(4,128)S(1)} collective-permute-done((f32[4,8832]{1,0:T(4,128)S(1)}, f32[4,8832]{1,0:T(4,128)S(1)}, u32[]{:S(2)}, u32[]{:S(2)}) %collective-permute-start.9) | collective-permute-done | bytes 141344 | tf_op jit(solution)/shard_map/ppermute | solution.py:72
  76.0 1.0 select_bitcast_fusion.1
  76.9 10.8 %collective-permute-start.4 = (bf16[12,128,128]{2,1,0:T(8,128)(2,1)S(1)}, bf16[12,128,128]{2,1,0:T(8,128)(2,1)S(1)}, u32[]{:S(2)}, u32[]{:S(2)}) collective-permute-start(bf16[12,128,128]{2,1,0:T(8,128)(2,1)S(1)} %get-tuple-element.45), channel_id=1, source_target_pairs={{1,0},{3,2},{5,4},{7,6},{9,8},{11,10},{13,12},{15,14},{17,16},{19,... | collective-permute-start | bytes 1179656 | tf_op jit(solution)/shard_map/ppermute | solution.py:180
  87.9 4.2 %collective-permute-done.11 = f32[4,8832]{1,0:T(4,128)S(1)} collective-permute-done((f32[4,8832]{1,0:T(4,128)S(1)}, f32[4,8832]{1,0:T(4,128)S(1)}, u32[]{:S(2)}, u32[]{:S(2)}) %collective-permute-start.11) | collective-permute-done | bytes 141344 | tf_op jit(solution)/shard_map/ppermute | solution.py:72
  92.3 5.4 %collective-permute-done.12 = f32[4,8832]{1,0:T(4,128)S(1)} collective-permute-done((f32[4,8832]{1,0:T(4,128)S(1)}, f32[4,8832]{1,0:T(4,128)S(1)}, u32[]{:S(2)}, u32[]{:S(2)}) %collective-permute-start.12) | collective-permute-done | bytes 141344 | tf_op jit(solution)/shard_map/ppermute | solution.py:72
  97.7 8.1 %collective-permute-start.13 = (f32[4,8832]{1,0:T(4,128)S(1)}, f32[4,8832]{1,0:T(4,128)S(1)}, u32[]{:S(2)}, u32[]{:S(2)}) collective-permute-start(f32[4,8832]{1,0:T(4,128)S(1)} %add.512), channel_id=1, source_target_pairs={{0,1},{1,0},{2,3},{3,2},{4,5},{5,4},{6,7},{7,6},{8,9},{9,8},{10,11... | collective-permute-start | bytes 423944 | tf_op jit(solution)/shard_map/ppermute | solution.py:74
  105.9 0.9 maximum_bitcast_fusion
  107.0 0.7 gather_fusion
  107.7 0.2 select_multiply_fusion
  107.9 0.6 slice.892
  108.5 0.6 slice.894
  109.1 0.7 copy.33
  (81 shorter events, 1.6 us)
Async XLA Ops:
  0.6 33.7 %copy-start = (bf16[4,128,128]{2,1,0:T(8,128)(2,1)S(1)}, bf16[4,128,128]{2,1,0:T(8,128)(2,1)}, u32[]{:S(2)}) copy-start(bf16[4,128,128]{2,1,0:T(8,128)(2,1)} %param.10) | copy-start | bytes 393220
  0.6 14.9 %copy-start.2 = (bf16[1,2,12,128,128]{4,3,2,1,0:T(8,128)(2,1)S(1)}, bf16[1,2,12,128,128]{4,3,2,1,0:T(8,128)(2,1)}, u32[]{:S(2)}) copy-start(bf16[1,2,12,128,128]{4,3,2,1,0:T(8,128)(2,1)} %param.6) | copy-start | bytes 2359300
  1.8 13.8 %collective-permute-start = (bf16[12,128,128]{2,1,0:T(8,128)(2,1)S(1)}, bf16[12,128,128]{2,1,0:T(8,128)(2,1)S(1)}, u32[]{:S(2)}, u32[]{:S(2)}) collective-permute-start(bf16[12,128,128]{2,1,0:T(8,128)(2,1)S(1)} %dynamic-slice_bitcast_fusion), channel_id=1, source_target_pairs={{0,1},{1,0},{2,3},{3,2},{4,5},{5,4},{6,7},{7,6},{8,9},{9,8},{10,11... | collective-permute-start | bytes 1179656 | tf_op jit(solution)/shard_map/ppermute | solution.py:90
  5.1 0.7 copy-start.6
  7.6 6.6 %copy-start.5 = (f32[4,3,3,128]{3,0,2,1:T(4,128)S(1)}, f32[4,3,3,128]{3,0,2,1:T(4,128)}, u32[]{:S(2)}) copy-start(f32[4,3,3,128]{3,0,2,1:T(4,128)} %param.9) | copy-start | bytes 55300
  12.8 1.3 %copy-start.7 = (f32[4,128]{1,0:T(4,128)S(1)}, f32[4,128]{1,0:T(4,128)}, u32[]{:S(2)}) copy-start(f32[4,128]{1,0:T(4,128)} %param.11) | copy-start | bytes 6148
  14.3 0.7 copy-start.8
  15.7 9.7 %collective-permute-start.2 = (bf16[12,12,128]{2,1,0:T(8,128)(2,1)S(1)}, bf16[12,12,128]{2,1,0:T(8,128)(2,1)S(1)}, u32[]{:S(2)}, u32[]{:S(2)}) collective-permute-start(bf16[12,12,128]{2,1,0:T(8,128)(2,1)S(1)} %pad_maximum_fusion.2), channel_id=1, source_target_pairs={{2,0},{4,2},{6,4},{8,6},{10,8},{12,10},{14,12},{16,14},{18,16},{20... | collective-permute-start | bytes 110600 | tf_op jit(solution)/shard_map/ppermute | solution.py:103
  24.3 8.4 %collective-permute-start.1 = (bf16[12,12,128]{2,1,0:T(8,128)(2,1)S(1)}, bf16[12,12,128]{2,1,0:T(8,128)(2,1)S(1)}, u32[]{:S(2)}, u32[]{:S(2)}) collective-permute-start(bf16[12,12,128]{2,1,0:T(8,128)(2,1)S(1)} %pad_maximum_fusion.1), channel_id=1, source_target_pairs={{0,2},{2,4},{4,6},{6,8},{8,10},{10,12},{12,14},{14,16},{16,18},{18... | collective-permute-start | bytes 110600 | tf_op jit(solution)/shard_map/ppermute | solution.py:102
  25.4 0.6 copy-start.3
  32.7 0.7 slice-start
  37.3 0.8 copy-start.4
  52.2 2.5 %collective-permute-start.5 = (f32[4,8832]{1,0:T(4,128)S(1)}, f32[4,8832]{1,0:T(4,128)S(1)}, u32[]{:S(2)}, u32[]{:S(2)}) collective-permute-start(f32[4,8832]{1,0:T(4,128)S(1)} %constant_dynamic-slice_fusion), channel_id=1, source_target_pairs={{0,1},{1,0},{2,3},{3,2},{4,5},{5,4},{6,7},{7,6},{8,9},{9,8},{10,11... | collective-permute-start | bytes 423944 | tf_op jit(solution)/shard_map/ppermute | solution.py:66
  54.8 5.2 %copy-start.1 = (f32[12,136,128]{2,1,0:T(8,128)S(1)}, f32[12,136,128]{2,1,0:T(8,128)}, u32[]{:S(2)}) copy-start(f32[12,136,128]{2,1,0:T(8,128)} %get-tuple-element.117) | copy-start | bytes 2506756
  54.8 5.0 %collective-permute-start.6 = (f32[4,8832]{1,0:T(4,128)S(1)}, f32[4,8832]{1,0:T(4,128)S(1)}, u32[]{:S(2)}, u32[]{:S(2)}) collective-permute-start(f32[4,8832]{1,0:T(4,128)S(1)} %dynamic-slice_add_fusion), channel_id=1, source_target_pairs={{0,2},{2,0},{4,6},{6,4},{1,3},{3,1},{5,7},{7,5},{8,10},{10,8},{12,... | collective-permute-start | bytes 423944 | tf_op jit(solution)/shard_map/ppermute | solution.py:72
  59.8 5.5 %collective-permute-start.7 = (f32[4,8832]{1,0:T(4,128)S(1)}, f32[4,8832]{1,0:T(4,128)S(1)}, u32[]{:S(2)}, u32[]{:S(2)}) collective-permute-start(f32[4,8832]{1,0:T(4,128)S(1)} %add.506), channel_id=1, source_target_pairs={{0,4},{2,6},{4,0},{6,2},{1,5},{3,7},{5,1},{7,3},{8,12},{10,14},{12... | collective-permute-start | bytes 423944 | tf_op jit(solution)/shard_map/ppermute | solution.py:72
  60.2 15.7 %collective-permute-start.3 = (bf16[12,128,128]{2,1,0:T(8,128)(2,1)S(1)}, bf16[12,128,128]{2,1,0:T(8,128)(2,1)S(1)}, u32[]{:S(2)}, u32[]{:S(2)}) collective-permute-start(bf16[12,128,128]{2,1,0:T(8,128)(2,1)S(1)} %fusion.99), channel_id=1, source_target_pairs={{0,1},{2,3},{4,5},{6,7},{8,9},{10,11},{12,13},{14,15},{16,17},{18,... | collective-permute-start | bytes 1179656 | tf_op jit(solution)/shard_map/ppermute | solution.py:179
  65.4 4.0 %collective-permute-start.8 = (f32[4,8832]{1,0:T(4,128)S(1)}, f32[4,8832]{1,0:T(4,128)S(1)}, u32[]{:S(2)}, u32[]{:S(2)}) collective-permute-start(f32[4,8832]{1,0:T(4,128)S(1)} %add.507), channel_id=1, source_target_pairs={{0,8},{8,0},{16,24},{24,16},{32,40},{40,32},{48,56},{56,48},{1,9},... | collective-permute-start | bytes 423944 | tf_op jit(solution)/shard_map/ppermute | solution.py:72
  69.4 6.4 %collective-permute-start.9 = (f32[4,8832]{1,0:T(4,128)S(1)}, f32[4,8832]{1,0:T(4,128)S(1)}, u32[]{:S(2)}, u32[]{:S(2)}) collective-permute-start(f32[4,8832]{1,0:T(4,128)S(1)} %add.508), channel_id=1, source_target_pairs={{0,16},{8,24},{16,0},{24,8},{32,48},{40,56},{48,32},{56,40},{1,17}... | collective-permute-start | bytes 423944 | tf_op jit(solution)/shard_map/ppermute | solution.py:72
  75.9 11.9 %collective-permute-start.10 = (f32[4,8832]{1,0:T(4,128)S(1)}, f32[4,8832]{1,0:T(4,128)S(1)}, u32[]{:S(2)}, u32[]{:S(2)}) collective-permute-start(f32[4,8832]{1,0:T(4,128)S(1)} %add.509), channel_id=1, source_target_pairs={{0,32},{8,40},{16,48},{24,56},{32,0},{40,8},{48,16},{56,24},{1,33}... | collective-permute-start | bytes 423944 | tf_op jit(solution)/shard_map/ppermute | solution.py:72
  76.9 29.0 %collective-permute-start.4 = (bf16[12,128,128]{2,1,0:T(8,128)(2,1)S(1)}, bf16[12,128,128]{2,1,0:T(8,128)(2,1)S(1)}, u32[]{:S(2)}, u32[]{:S(2)}) collective-permute-start(bf16[12,128,128]{2,1,0:T(8,128)(2,1)S(1)} %get-tuple-element.45), channel_id=1, source_target_pairs={{1,0},{3,2},{5,4},{7,6},{9,8},{11,10},{13,12},{15,14},{17,16},{19,... | collective-permute-start | bytes 1179656 | tf_op jit(solution)/shard_map/ppermute | solution.py:180
  87.8 4.3 %collective-permute-start.11 = (f32[4,8832]{1,0:T(4,128)S(1)}, f32[4,8832]{1,0:T(4,128)S(1)}, u32[]{:S(2)}, u32[]{:S(2)}) collective-permute-start(f32[4,8832]{1,0:T(4,128)S(1)} %add.510), channel_id=1, source_target_pairs={{0,64},{64,0},{128,192},{192,128},{1,65},{65,1},{129,193},{193,129... | collective-permute-start | bytes 423944 | tf_op jit(solution)/shard_map/ppermute | solution.py:72
  92.2 5.5 %collective-permute-start.12 = (f32[4,8832]{1,0:T(4,128)S(1)}, f32[4,8832]{1,0:T(4,128)S(1)}, u32[]{:S(2)}, u32[]{:S(2)}) collective-permute-start(f32[4,8832]{1,0:T(4,128)S(1)} %add.511), channel_id=1, source_target_pairs={{0,128},{64,192},{128,0},{192,64},{1,129},{65,193},{129,1},{193,65... | collective-permute-start | bytes 423944 | tf_op jit(solution)/shard_map/ppermute | solution.py:72
  97.7 9.1 %collective-permute-start.13 = (f32[4,8832]{1,0:T(4,128)S(1)}, f32[4,8832]{1,0:T(4,128)S(1)}, u32[]{:S(2)}, u32[]{:S(2)}) collective-permute-start(f32[4,8832]{1,0:T(4,128)S(1)} %add.512), channel_id=1, source_target_pairs={{0,1},{1,0},{2,3},{3,2},{4,5},{5,4},{6,7},{7,6},{8,9},{9,8},{10,11... | collective-permute-start | bytes 423944 | tf_op jit(solution)/shard_map/ppermute | solution.py:74

commit v4 on v3

--- a/solution.py
+++ b/solution.py
@@ -3,7 +3,11 @@
 import jax
 import jax.numpy as jnp
 from jax import lax
+from jax.experimental import pallas as pl
+from jax.experimental.pallas import tpu as pltpu
 from jax.sharding import Mesh, PartitionSpec as P
+
+MESH_ID = pl.DeviceIdType.MESH
 
 root_half = 0.7071067811865476
 density_norm = 0.3989422804014327
@@ -56,6 +60,89 @@
                 2 - i : 2 - i + height, 2 - j : 2 - j + breadth
             ].astype(jnp.float32)
     return acc
+
+
+def torus_coords(b):
+    y_size, z_size = lax.axis_size("y"), lax.axis_size("z")
+    return (b // (y_size * z_size), lax.rem(b // y_size, z_size), lax.rem(b, y_size))
+
+
+def exchange_kernel(held_ref, edges_ref, body_out, lo_out, hi_out, body, lo, hi, send_sem, recv_sem):
+    core = lax.axis_index("pipe")
+    count = blk_count()
+    here = (lax.axis_index("x") * lax.axis_size("z") + lax.axis_index("z")) * lax.axis_size("y") + lax.axis_index("y")
+    right = torus_coords(lax.rem(here + 1, count))
+    left = torus_coords(lax.rem(here + count - 1, count))
+    mine = torus_coords(here)
+    partner = mine + (1 - core,)
+    targets = [partner] + [right + (m,) for m in range(2)] + [left + (m,) for m in range(2)]
+
+    barrier = pltpu.get_barrier_semaphore()
+    for target in targets:
+        pl.semaphore_signal(barrier, inc=1, device_id=target, device_id_type=MESH_ID)
+    pl.semaphore_wait(barrier, len(targets))
+
+    copies = [
+        pltpu.make_async_remote_copy(
+            src_ref=held_ref.at[1 - core], dst_ref=body,
+            send_sem=send_sem.at[0], recv_sem=recv_sem.at[0],
+            device_id=partner, device_id_type=MESH_ID,
+        )
+    ]
+    for m in range(2):
+        copies.append(pltpu.make_async_remote_copy(
+            src_ref=edges_ref.at[1, m], dst_ref=lo.at[core],
+            send_sem=send_sem.at[1 + m], recv_sem=recv_sem.at[1 + core],
+            device_id=right + (m,), device_id_type=MESH_ID,
+        ))
+        copies.append(pltpu.make_async_remote_copy(
+            src_ref=edges_ref.at[0, m], dst_ref=hi.at[core],
+            send_sem=send_sem.at[3 + m], recv_sem=recv_sem.at[3 + core],
+            device_id=left + (m,), device_id_type=MESH_ID,
+        ))
+    for copy in copies:
+        copy.start()
+    copies[0].wait_recv()
+    for k in range(2):
+        pltpu.make_async_remote_copy(
+            src_ref=edges_ref.at[1, k], dst_ref=lo.at[k],
+            send_sem=send_sem.at[1 + k], recv_sem=recv_sem.at[1 + k],
+            device_id=right + (k,), device_id_type=MESH_ID,
+        ).wait_recv()
+        pltpu.make_async_remote_copy(
+            src_ref=edges_ref.at[0, k], dst_ref=hi.at[k],
+            send_sem=send_sem.at[3 + k], recv_sem=recv_sem.at[3 + k],
+            device_id=left + (k,), device_id_type=MESH_ID,
+        ).wait_recv()
+    for copy in copies:
+        copy.wait_send()
+    body_out[...] = body[...]
+    lo_out[...] = lo[...]
+    hi_out[...] = hi[...]
+
+
+def exchange(held, edges):
+    grid_shape = held.shape[1:]
+    strip_shape = edges.shape[2:]
+    vmem = pl.BlockSpec(memory_space=pltpu.VMEM)
+    return pl.pallas_call(
+        exchange_kernel,
+        out_shape=(
+            jax.ShapeDtypeStruct(grid_shape, held.dtype),
+            jax.ShapeDtypeStruct((2,) + strip_shape, held.dtype),
+            jax.ShapeDtypeStruct((2,) + strip_shape, held.dtype),
+        ),
+        in_specs=[vmem, vmem],
+        out_specs=(vmem, vmem, vmem),
+        scratch_shapes=[
+            pltpu.VMEM(grid_shape, held.dtype),
+            pltpu.VMEM((2,) + strip_shape, held.dtype),
+            pltpu.VMEM((2,) + strip_shape, held.dtype),
+            pltpu.SemaphoreType.DMA((5,)),
+            pltpu.SemaphoreType.DMA((5,)),
+        ],
+        compiler_params=pltpu.CompilerParams(collective_id=0, has_side_effects=True),
+    )(held, edges)
 
 
 def all_reduce(flat, core):
@@ -85,24 +172,13 @@
     layers = layer_order.shape[0]
     core = lax.axis_index("pipe")
 
-    swap = [(0, 1), (1, 0)]
-    sent = select_row(held, 1 - core)
-    received = lax.ppermute(sent, "pipe", swap)
+    edges = jnp.stack([held[:, :, :X_HALO], held[:, :, breadth - X_HALO :]])
+    body, lo, hi = exchange(held, edges)
     mine = select_row(held, core)
-    x_in = jnp.where(core == 0, mine, received)
-    g_in = jnp.where(core == 0, received, mine)
-
-    edge_x_hi = x_in[:, breadth - X_HALO :]
-    edge_x_lo = x_in[:, :X_HALO]
-    edge_g_hi = g_in[:, breadth - G_HALO :]
-    edge_g_lo = g_in[:, :G_HALO]
-    size = blk_count()
-    up = [(i, (i + 1) % size) for i in range(size)]
-    down = [(j, i) for i, j in up]
-    from_left = lax.ppermute(jnp.concatenate([edge_x_hi, edge_g_hi], axis=1), BLK_AXES, up)
-    from_right = lax.ppermute(jnp.concatenate([edge_x_lo, edge_g_lo], axis=1), BLK_AXES, down)
-    x_wide = jnp.concatenate([from_left[:, :X_HALO], x_in, from_right[:, :X_HALO]], axis=1)
-    g_wide = jnp.concatenate([from_left[:, X_HALO:], g_in, from_right[:, X_HALO:]], axis=1)
+    x_in = jnp.where(core == 0, mine, body)
+    g_in = jnp.where(core == 0, body, mine)
+    x_wide = jnp.concatenate([lo[0], x_in, hi[0]], axis=1)
+    g_wide = jnp.concatenate([lo[1][:, X_HALO - G_HALO :], g_in, hi[1][:, :G_HALO]], axis=1)
 
     live = (jnp.arange(height)[:, None, None] < select_row(row_counts, core)).astype(jnp.float32)
 

time: 110 us -> 102 us (0.927)
  Pallas kernels: 0 us -> 16.2 us
  starting transfers between devices: 34.6 us -> 21.3 us
  waiting for transfers between devices: 35.7 us -> 25.4 us
    pallas_call x0 -> x1, Pallas kernels: none -> 16.2 us  [exchange(): pl.pallas_call(exchange_kernel, out_shape=(jax.ShapeDtypeStruct(grid_shap...]
    ppermute x3 -> x0, starting transfers between devices: 12 us -> none  [the longest x1 8.56 us: shards(): lax.ppermute(jnp.concatenate([edge_x_lo, edge_g_lo], axis=1), BLK_AXES, d...]
    ppermute x3 -> x0, waiting for transfers between devices: 7.08 us -> none  [the longest x1 6.67 us: shards(): lax.ppermute(jnp.concatenate([edge_x_hi, edge_g_hi], axis=1), BLK_AXES, up)]
    ppermute x7, starting transfers between devices: 0.87 us -> 6.74 us  [all_reduce(): acc = acc + lax.ppermute(acc, axis, pairs)]
    ppermute x1, starting transfers between devices: 10.8 us -> 6.44 us  [shards(): got_grad = lax.ppermute(input_grad, 'pipe', [(1, 0)])]
    ppermute x7, waiting for transfers between devices: 27.6 us -> 24.4 us  [all_reduce(): acc = acc + lax.ppermute(acc, axis, pairs)]
    ppermute x1, starting transfers between devices: 8.14 us -> 6.32 us  [all_reduce(): theirs = lax.ppermute(acc, 'pipe', swap)]
    unnamed x22 -> x20, local copies, waits for them, and re-layouts: 2.81 us -> 2.11 us
  transfers between devices with their start and end apart: 14 -> 11, of which waited for: 9 -> 8; matrix products, arithmetic and copies ran while one was open for 5% -> 3% of each run, Pallas kernels for 0% -> 0%
where the time goes in v4:
time: 102 us
  waiting for transfers between devices  25.4 us (25%)
  starting transfers between devices  21.3 us (21%)
  other arithmetic  16.6 us (16%)
  Pallas kernels  16.2 us (16%)
  between operations  8.88 us (9%)
  local copies, waits for them, and re-layouts  7.59 us (7%)
  matrix products  5.96 us (6%)
    ppermute x7, waiting for transfers between devices, all_reduce(): acc = acc + lax.ppermute(acc, axis, pairs)  24.4 us
    pallas_call x1, Pallas kernels, exchange(): pl.pallas_call(exchange_kernel, out_shape=(jax.ShapeDtypeStruct(grid_shap...  16.2 us
    ppermute x7, starting transfers between devices, all_reduce(): acc = acc + lax.ppermute(acc, axis, pairs)  6.74 us
    ppermute x1, starting transfers between devices, shards(): got_grad = lax.ppermute(input_grad, 'pipe', [(1, 0)])  6.44 us
    ppermute x1, starting transfers between devices, all_reduce(): theirs = lax.ppermute(acc, 'pipe', swap)  6.32 us
    convert_element_type x3, other arithmetic, shards(): gated = (masked * gelu_pair(preact)[1]).astype(jnp.bfloat16)  4.75 us
    reduce_sum x4, other arithmetic, shards(): jnp.sum(back_in * padded[i:i + height, start:start + breadth].astype(jnp....  3.28 us
    dot_general x4, matrix products, shards(): jnp.dot(mixed.reshape(rows * span, channels), point, preferred_element_ty...  3.08 us
  transfers between devices with their start and end apart: 11, of which 8 were waited for; matrix products, arithmetic and copies ran while one was open for 3% of the time, Pallas kernels for 0%

profile of v4, /device:TPU:1, one launch (start us, length us, event | category | flops | bytes accessed | tf_op | source)
XLA Modules:
  0.0 101.8 jit_solution(14675831587555270325)
XLA Ops:
  0.7 0.7 copy-done.5
  1.3 0.6 fusion.143
  7.1 0.6 copy-done.7
  7.7 0.6 dynamic_slice.54
  8.3 0.6 compare_convert_fusion
  8.9 0.8 slice_bitcast_fusion.2
  9.8 0.7 pad_maximum_fusion.1.edges_ref
  10.4 16.2 %shard_map.93 = (bf16[12,128,128]{2,1,0:T(8,128)(2,1)}, bf16[2,12,8,128]{3,2,1,0:T(8,128)(2,1)}, bf16[2,12,8,128]{3,2,1,0:T(8,128)(2,1)}) custom-call(bf16[2,12,128,128]{3,2,1,0:T(8,128)(2,1)} %bitcast.238, bf16[2,2,12,8,128]{4,3,2,1,0:T(8,128)(2,1)} %pad_maximum_fusion.1.edges_ref), custom_call_target="tpu_custom_call" | custom-call | tf_op jit(solution)/shard_map/pallas_call | solution.py:128
  29.4 0.8 slice_bitcast_fusion.5
  30.3 0.2 multiply_convert_fusion
  30.5 0.7 fusion.5
  31.2 0.5 fusion.7
  31.7 0.7 fusion.13
  32.4 0.5 fusion.15
  33.0 0.7 fusion.21
  33.7 0.5 fusion.23
  34.2 0.7 add_convert_fusion
  34.9 1.6 %fusion.29 = (bf16[12,136,128]{2,1,0:T(8,128)(2,1)S(1)}, f32[12,136,128]{2,1,0:T(8,128)S(1)}, f32[12,136,128]{2,1,0:T(8,128)S(1)}, f32[12,136,128]{2,1,0:T(8,128)}) fusion(f32[12]{0:T(128)S(1)} %compare_convert_fusion, bf16[12,4,128]{2,1,0:T(4,128)(2,1)S(1)} %slice.794, bf16[12,128,128]{2,1,0:T(8,128)(2,1)S(1)} %get-tuple-element.60, ...), kind=kOutput, calls=%fused_computation.87 | convolution fusion | flops 57237504 | bytes 3793924 | tf_op jit(solution)/shard_map/dot_general | solution.py:199
  36.4 0.4 convolution_convert_fusion.3
  36.8 0.2 convert_reduce_fusion
  37.0 1.7 %fusion.35 = (bf16[12,134,128]{2,1,0:T(8,128)(2,1)S(1)}, f32[12,134,128]{2,1,0:T(8,128)S(1)}) fusion(f32[12,138,128]{2,1,0:T(8,128)S(1)} %get-tuple-element.124, f32[12]{0:T(128)S(1)} %compare_convert_fusion, f32[128]{0:T(128)S(1)} %get-tuple-element.76, f32[128]{0:T(128)S(1)} %get-tuple-element.77, f32[128]{0:T(128)S(1)} %get-tuple-element.78, ...), kind=kLoop, calls=%fused_computation.93 | loop fusion | flops 8438784 | bytes 4582400 | tf_op jit(solution)/shard_map/convert_element_type | solution.py:220
  38.7 0.4 convolution_convert_fusion.2
  39.1 0.2 convert_reduce_fusion.1
  39.3 1.5 %fusion.41 = (bf16[12,132,128]{2,1,0:T(8,128)(2,1)S(1)}, f32[12,132,128]{2,1,0:T(8,128)S(1)}) fusion(f32[12,140,128]{2,1,0:T(8,128)S(1)} %get-tuple-element.122, f32[12]{0:T(128)S(1)} %compare_convert_fusion, f32[128]{0:T(128)S(1)} %get-tuple-element.85, f32[128]{0:T(128)S(1)} %get-tuple-element.86, f32[128]{0:T(128)S(1)} %get-tuple-element.87, ...), kind=kLoop, calls=%fused_computation.99 | loop fusion | flops 8312832 | bytes 4563968 | tf_op jit(solution)/shard_map/convert_element_type | solution.py:220
  40.9 0.4 convolution_convert_fusion.1
  41.3 0.2 convert_reduce_fusion.2
  41.5 1.5 %fusion.47 = (bf16[12,130,128]{2,1,0:T(8,128)(2,1)S(1)}, f32[12,130,128]{2,1,0:T(8,128)S(1)}) fusion(f32[12,142,128]{2,1,0:T(8,128)S(1)} %get-tuple-element.120, f32[12]{0:T(128)S(1)} %compare_convert_fusion, f32[128]{0:T(128)S(1)} %get-tuple-element.94, f32[128]{0:T(128)S(1)} %get-tuple-element.95, f32[128]{0:T(128)S(1)} %get-tuple-element.96, ...), kind=kLoop, calls=%fused_computation.105 | loop fusion | flops 8186880 | bytes 4545536 | tf_op jit(solution)/shard_map/convert_element_type | solution.py:220
  43.0 0.4 convolution_convert_fusion
  43.4 0.2 convert_reduce_fusion.3
  43.6 0.3 fusion.100
  44.0 0.3 fusion.102
  44.3 0.3 fusion.104
  44.7 0.3 fusion.106
  45.0 0.9 fusion.72
  45.9 0.9 fusion.63
  46.7 0.7 fusion.54
  47.7 0.8 fusion.89
  48.6 0.3 maximum_maximum_fusion
  48.9 0.5 collective-permute-start.2
  49.4 1.0 collective-permute-done.2
  50.5 1.1 %collective-permute-start.3 = (f32[4,8832]{1,0:T(4,128)S(1)}, f32[4,8832]{1,0:T(4,128)S(1)}, u32[]{:S(2)}, u32[]{:S(2)}) collective-permute-start(f32[4,8832]{1,0:T(4,128)S(1)} %dynamic-slice_add_fusion), channel_id=1, source_target_pairs={{0,2},{2,0},{4,6},{6,4},{1,3},{3,1},{5,7},{7,5},{8,10},{10,8},{12,... | collective-permute-start | bytes 423944 | tf_op jit(solution)/shard_map/ppermute | solution.py:159
  51.6 3.8 %collective-permute-done.3 = f32[4,8832]{1,0:T(4,128)S(1)} collective-permute-done((f32[4,8832]{1,0:T(4,128)S(1)}, f32[4,8832]{1,0:T(4,128)S(1)}, u32[]{:S(2)}, u32[]{:S(2)}) %collective-permute-start.3) | collective-permute-done | bytes 141344 | tf_op jit(solution)/shard_map/ppermute | solution.py:159
  55.6 0.3 fusion.99
  55.9 1.3 %collective-permute-start = (bf16[12,128,128]{2,1,0:T(8,128)(2,1)S(1)}, bf16[12,128,128]{2,1,0:T(8,128)(2,1)S(1)}, u32[]{:S(2)}, u32[]{:S(2)}) collective-permute-start(bf16[12,128,128]{2,1,0:T(8,128)(2,1)S(1)} %fusion.99), channel_id=1, source_target_pairs={{0,1},{2,3},{4,5},{6,7},{8,9},{10,11},{12,13},{14,15},{16,17},{18,... | collective-permute-start | bytes 1179656 | tf_op jit(solution)/shard_map/ppermute | solution.py:255
  57.2 3.8 %collective-permute-done.4 = f32[4,8832]{1,0:T(4,128)S(1)} collective-permute-done((f32[4,8832]{1,0:T(4,128)S(1)}, f32[4,8832]{1,0:T(4,128)S(1)}, u32[]{:S(2)}, u32[]{:S(2)}) %collective-permute-start.4) | collective-permute-done | bytes 141344 | tf_op jit(solution)/shard_map/ppermute | solution.py:159
  61.2 3.9 %collective-permute-done.5 = f32[4,8832]{1,0:T(4,128)S(1)} collective-permute-done((f32[4,8832]{1,0:T(4,128)S(1)}, f32[4,8832]{1,0:T(4,128)S(1)}, u32[]{:S(2)}, u32[]{:S(2)}) %collective-permute-start.5) | collective-permute-done | bytes 141344 | tf_op jit(solution)/shard_map/ppermute | solution.py:159
  65.1 0.3 collective-permute-start.6
  65.5 0.6 scatter_custom_fusion
  66.1 5.4 %collective-permute-done.6 = f32[4,8832]{1,0:T(4,128)S(1)} collective-permute-done((f32[4,8832]{1,0:T(4,128)S(1)}, f32[4,8832]{1,0:T(4,128)S(1)}, u32[]{:S(2)}, u32[]{:S(2)}) %collective-permute-start.6) | collective-permute-done | bytes 141344 | tf_op jit(solution)/shard_map/ppermute | solution.py:159
  71.5 1.4 %collective-permute-start.7 = (f32[4,8832]{1,0:T(4,128)S(1)}, f32[4,8832]{1,0:T(4,128)S(1)}, u32[]{:S(2)}, u32[]{:S(2)}) collective-permute-start(f32[4,8832]{1,0:T(4,128)S(1)} %add.504), channel_id=1, source_target_pairs={{0,32},{8,40},{16,48},{24,56},{32,0},{40,8},{48,16},{56,24},{1,33}... | collective-permute-start | bytes 423944 | tf_op jit(solution)/shard_map/ppermute | solution.py:159
  72.9 0.9 select_bitcast_fusion.1
  73.9 6.4 %collective-permute-start.1 = (bf16[12,128,128]{2,1,0:T(8,128)(2,1)S(1)}, bf16[12,128,128]{2,1,0:T(8,128)(2,1)S(1)}, u32[]{:S(2)}, u32[]{:S(2)}) collective-permute-start(bf16[12,128,128]{2,1,0:T(8,128)(2,1)S(1)} %get-tuple-element.51), channel_id=1, source_target_pairs={{1,0},{3,2},{5,4},{7,6},{9,8},{11,10},{13,12},{15,14},{17,16},{19,... | collective-permute-start | bytes 1179656 | tf_op jit(solution)/shard_map/ppermute | solution.py:256
  80.3 0.1 collective-permute-done.7
  80.5 1.3 %collective-permute-start.8 = (f32[4,8832]{1,0:T(4,128)S(1)}, f32[4,8832]{1,0:T(4,128)S(1)}, u32[]{:S(2)}, u32[]{:S(2)}) collective-permute-start(f32[4,8832]{1,0:T(4,128)S(1)} %add.505), channel_id=1, source_target_pairs={{0,64},{64,0},{128,192},{192,128},{1,65},{65,1},{129,193},{193,129... | collective-permute-start | bytes 423944 | tf_op jit(solution)/shard_map/ppermute | solution.py:159
  81.8 3.0 %collective-permute-done.8 = f32[4,8832]{1,0:T(4,128)S(1)} collective-permute-done((f32[4,8832]{1,0:T(4,128)S(1)}, f32[4,8832]{1,0:T(4,128)S(1)}, u32[]{:S(2)}, u32[]{:S(2)}) %collective-permute-start.8) | collective-permute-done | bytes 141344 | tf_op jit(solution)/shard_map/ppermute | solution.py:159
  84.8 2.5 %collective-permute-start.9 = (f32[4,8832]{1,0:T(4,128)S(1)}, f32[4,8832]{1,0:T(4,128)S(1)}, u32[]{:S(2)}, u32[]{:S(2)}) collective-permute-start(f32[4,8832]{1,0:T(4,128)S(1)} %add.506), channel_id=1, source_target_pairs={{0,128},{64,192},{128,0},{192,64},{1,129},{65,193},{129,1},{193,65... | collective-permute-start | bytes 423944 | tf_op jit(solution)/shard_map/ppermute | solution.py:159
  87.4 4.2 %collective-permute-done.9 = f32[4,8832]{1,0:T(4,128)S(1)} collective-permute-done((f32[4,8832]{1,0:T(4,128)S(1)}, f32[4,8832]{1,0:T(4,128)S(1)}, u32[]{:S(2)}, u32[]{:S(2)}) %collective-permute-start.9) | collective-permute-done | bytes 141344 | tf_op jit(solution)/shard_map/ppermute | solution.py:159
  91.6 6.3 %collective-permute-start.10 = (f32[4,8832]{1,0:T(4,128)S(1)}, f32[4,8832]{1,0:T(4,128)S(1)}, u32[]{:S(2)}, u32[]{:S(2)}) collective-permute-start(f32[4,8832]{1,0:T(4,128)S(1)} %add.507), channel_id=1, source_target_pairs={{0,1},{1,0},{2,3},{3,2},{4,5},{5,4},{6,7},{7,6},{8,9},{9,8},{10,11... | collective-permute-start | bytes 423944 | tf_op jit(solution)/shard_map/ppermute | solution.py:161
  98.0 0.9 maximum_bitcast_fusion
  99.0 0.7 gather_fusion
  99.7 0.2 select_multiply_fusion
  99.9 0.6 slice.888
  100.5 0.6 slice.890
  101.1 0.7 copy.33
  (69 shorter events, 1.2 us)
Async XLA Ops:
  0.6 30.6 %copy-start = (bf16[4,128,128]{2,1,0:T(8,128)(2,1)S(1)}, bf16[4,128,128]{2,1,0:T(8,128)(2,1)}, u32[]{:S(2)}) copy-start(bf16[4,128,128]{2,1,0:T(8,128)(2,1)} %param.10) | copy-start | bytes 393220
  0.7 0.7 copy-start.5
  7.0 0.7 copy-start.7
  9.8 20.5 %copy-start.2 = (bf16[1,2,12,128,128]{4,3,2,1,0:T(8,128)(2,1)S(1)}, bf16[1,2,12,128,128]{4,3,2,1,0:T(8,128)(2,1)}, u32[]{:S(2)}) copy-start(bf16[1,2,12,128,128]{4,3,2,1,0:T(8,128)(2,1)} %param.6) | copy-start | bytes 2359300
  10.4 18.8 %copy-start.6 = (f32[4,128]{1,0:T(4,128)S(1)}, f32[4,128]{1,0:T(4,128)}, u32[]{:S(2)}) copy-start(f32[4,128]{1,0:T(4,128)} %param.11) | copy-start | bytes 6148
  10.4 18.8 %copy-start.4 = (f32[4,3,3,128]{3,0,2,1:T(4,128)S(1)}, f32[4,3,3,128]{3,0,2,1:T(4,128)}, u32[]{:S(2)}) copy-start(f32[4,3,3,128]{3,0,2,1:T(4,128)} %param.9) | copy-start | bytes 55300
  26.6 3.6 %copy-start.3 = (bf16[12,128,128]{2,1,0:T(8,128)(2,1)S(1)}, bf16[12,128,128]{2,1,0:T(8,128)(2,1)}, u32[]{:S(2)}) copy-start(bf16[12,128,128]{2,1,0:T(8,128)(2,1)} %get-tuple-element.8) | copy-start | bytes 1179652
  48.9 1.5 %collective-permute-start.2 = (f32[4,8832]{1,0:T(4,128)S(1)}, f32[4,8832]{1,0:T(4,128)S(1)}, u32[]{:S(2)}, u32[]{:S(2)}) collective-permute-start(f32[4,8832]{1,0:T(4,128)S(1)} %constant_dynamic-slice_fusion), channel_id=1, source_target_pairs={{0,1},{1,0},{2,3},{3,2},{4,5},{5,4},{6,7},{7,6},{8,9},{9,8},{10,11... | collective-permute-start | bytes 423944 | tf_op jit(solution)/shard_map/ppermute | solution.py:153
  50.4 5.2 %copy-start.1 = (f32[12,136,128]{2,1,0:T(8,128)S(1)}, f32[12,136,128]{2,1,0:T(8,128)}, u32[]{:S(2)}) copy-start(f32[12,136,128]{2,1,0:T(8,128)} %get-tuple-element.125) | copy-start | bytes 2506756
  50.5 5.0 %collective-permute-start.3 = (f32[4,8832]{1,0:T(4,128)S(1)}, f32[4,8832]{1,0:T(4,128)S(1)}, u32[]{:S(2)}, u32[]{:S(2)}) collective-permute-start(f32[4,8832]{1,0:T(4,128)S(1)} %dynamic-slice_add_fusion), channel_id=1, source_target_pairs={{0,2},{2,0},{4,6},{6,4},{1,3},{3,1},{5,7},{7,5},{8,10},{10,8},{12,... | collective-permute-start | bytes 423944 | tf_op jit(solution)/shard_map/ppermute | solution.py:159
  55.5 5.5 %collective-permute-start.4 = (f32[4,8832]{1,0:T(4,128)S(1)}, f32[4,8832]{1,0:T(4,128)S(1)}, u32[]{:S(2)}, u32[]{:S(2)}) collective-permute-start(f32[4,8832]{1,0:T(4,128)S(1)} %add.501), channel_id=1, source_target_pairs={{0,4},{2,6},{4,0},{6,2},{1,5},{3,7},{5,1},{7,3},{8,12},{10,14},{12... | collective-permute-start | bytes 423944 | tf_op jit(solution)/shard_map/ppermute | solution.py:159
  55.9 17.0 %collective-permute-start = (bf16[12,128,128]{2,1,0:T(8,128)(2,1)S(1)}, bf16[12,128,128]{2,1,0:T(8,128)(2,1)S(1)}, u32[]{:S(2)}, u32[]{:S(2)}) collective-permute-start(bf16[12,128,128]{2,1,0:T(8,128)(2,1)S(1)} %fusion.99), channel_id=1, source_target_pairs={{0,1},{2,3},{4,5},{6,7},{8,9},{10,11},{12,13},{14,15},{16,17},{18,... | collective-permute-start | bytes 1179656 | tf_op jit(solution)/shard_map/ppermute | solution.py:255
  61.1 4.0 %collective-permute-start.5 = (f32[4,8832]{1,0:T(4,128)S(1)}, f32[4,8832]{1,0:T(4,128)S(1)}, u32[]{:S(2)}, u32[]{:S(2)}) collective-permute-start(f32[4,8832]{1,0:T(4,128)S(1)} %add.502), channel_id=1, source_target_pairs={{0,8},{8,0},{16,24},{24,16},{32,40},{40,32},{48,56},{56,48},{1,9},... | collective-permute-start | bytes 423944 | tf_op jit(solution)/shard_map/ppermute | solution.py:159
  65.1 6.4 %collective-permute-start.6 = (f32[4,8832]{1,0:T(4,128)S(1)}, f32[4,8832]{1,0:T(4,128)S(1)}, u32[]{:S(2)}, u32[]{:S(2)}) collective-permute-start(f32[4,8832]{1,0:T(4,128)S(1)} %add.503), channel_id=1, source_target_pairs={{0,16},{8,24},{16,0},{24,8},{32,48},{40,56},{48,32},{56,40},{1,17}... | collective-permute-start | bytes 423944 | tf_op jit(solution)/shard_map/ppermute | solution.py:159
  71.5 8.9 %collective-permute-start.7 = (f32[4,8832]{1,0:T(4,128)S(1)}, f32[4,8832]{1,0:T(4,128)S(1)}, u32[]{:S(2)}, u32[]{:S(2)}) collective-permute-start(f32[4,8832]{1,0:T(4,128)S(1)} %add.504), channel_id=1, source_target_pairs={{0,32},{8,40},{16,48},{24,56},{32,0},{40,8},{48,16},{56,24},{1,33}... | collective-permute-start | bytes 423944 | tf_op jit(solution)/shard_map/ppermute | solution.py:159
  73.9 24.0 %collective-permute-start.1 = (bf16[12,128,128]{2,1,0:T(8,128)(2,1)S(1)}, bf16[12,128,128]{2,1,0:T(8,128)(2,1)S(1)}, u32[]{:S(2)}, u32[]{:S(2)}) collective-permute-start(bf16[12,128,128]{2,1,0:T(8,128)(2,1)S(1)} %get-tuple-element.51), channel_id=1, source_target_pairs={{1,0},{3,2},{5,4},{7,6},{9,8},{11,10},{13,12},{15,14},{17,16},{19,... | collective-permute-start | bytes 1179656 | tf_op jit(solution)/shard_map/ppermute | solution.py:256
  80.5 4.3 %collective-permute-start.8 = (f32[4,8832]{1,0:T(4,128)S(1)}, f32[4,8832]{1,0:T(4,128)S(1)}, u32[]{:S(2)}, u32[]{:S(2)}) collective-permute-start(f32[4,8832]{1,0:T(4,128)S(1)} %add.505), channel_id=1, source_target_pairs={{0,64},{64,0},{128,192},{192,128},{1,65},{65,1},{129,193},{193,129... | collective-permute-start | bytes 423944 | tf_op jit(solution)/shard_map/ppermute | solution.py:159
  84.8 6.7 %collective-permute-start.9 = (f32[4,8832]{1,0:T(4,128)S(1)}, f32[4,8832]{1,0:T(4,128)S(1)}, u32[]{:S(2)}, u32[]{:S(2)}) collective-permute-start(f32[4,8832]{1,0:T(4,128)S(1)} %add.506), channel_id=1, source_target_pairs={{0,128},{64,192},{128,0},{192,64},{1,129},{65,193},{129,1},{193,65... | collective-permute-start | bytes 423944 | tf_op jit(solution)/shard_map/ppermute | solution.py:159
  91.6 7.3 %collective-permute-start.10 = (f32[4,8832]{1,0:T(4,128)S(1)}, f32[4,8832]{1,0:T(4,128)S(1)}, u32[]{:S(2)}, u32[]{:S(2)}) collective-permute-start(f32[4,8832]{1,0:T(4,128)S(1)} %add.507), channel_id=1, source_target_pairs={{0,1},{1,0},{2,3},{3,2},{4,5},{5,4},{6,7},{7,6},{8,9},{9,8},{10,11... | collective-permute-start | bytes 423944 | tf_op jit(solution)/shard_map/ppermute | solution.py:161

commit v5 on v4

--- a/solution.py
+++ b/solution.py
@@ -145,23 +145,90 @@
     )(held, edges)
 
 
-def all_reduce(flat, core):
-    half = flat.shape[1] // 2
-    swap = [(0, 1), (1, 0)]
-    mine = lax.dynamic_slice_in_dim(flat, core * half, half, axis=1)
-    other = lax.dynamic_slice_in_dim(flat, (1 - core) * half, half, axis=1)
-    acc = mine + lax.ppermute(other, "pipe", swap)
-    for axis in ("y", "z", "x"):
-        size = lax.axis_size(axis)
+def flip(index, bit):
+    return index + bit - 2 * bit * lax.rem(index // bit, 2)
+
+
+def reduce_kernel(flat_ref, out_ref, acc, recv, send_sem, recv_sem):
+    core = lax.axis_index("pipe")
+    half = flat_ref.shape[1] // 2
+    coords = {axis: lax.axis_index(axis) for axis in BLK_AXES}
+    order_a, order_b = [], []
+    for axis in ("z", "y", "x"):
         bit = 1
-        while bit < size:
-            pairs = [(i, i ^ bit) for i in range(size)]
-            acc = acc + lax.ppermute(acc, axis, pairs)
+        while bit < lax.axis_size(axis):
+            order_a.append((axis, bit))
             bit *= 2
-    theirs = lax.ppermute(acc, "pipe", swap)
-    low = jnp.where(core == 0, acc, theirs)
-    high = jnp.where(core == 0, theirs, acc)
-    return jnp.concatenate([low, high], axis=1)
+    for axis in ("y", "x", "z"):
+        bit = 1
+        while bit < lax.axis_size(axis):
+            order_b.append((axis, bit))
+            bit *= 2
+    partner = tuple(coords[axis] for axis in BLK_AXES) + (1 - core,)
+    peers = []
+    for (axis_a, bit_a), (axis_b, bit_b) in zip(order_a, order_b):
+        peer = []
+        for axis in BLK_AXES:
+            flip_a = flip(coords[axis], bit_a) if axis == axis_a else coords[axis]
+            flip_b = flip(coords[axis], bit_b) if axis == axis_b else coords[axis]
+            peer.append(flip_a * (1 - core) + flip_b * core)
+        peers.append(tuple(peer) + (core,))
+
+    barrier = pltpu.get_barrier_semaphore()
+    for target in [partner] + peers:
+        pl.semaphore_signal(barrier, inc=1, device_id=target, device_id_type=MESH_ID)
+    pl.semaphore_wait(barrier, 1 + len(peers))
+
+    own = pl.ds(pl.multiple_of(core * half, 128), half)
+    other = pl.ds(pl.multiple_of((1 - core) * half, 128), half)
+    first = pltpu.make_async_remote_copy(
+        src_ref=flat_ref.at[:, other], dst_ref=recv.at[0],
+        send_sem=send_sem.at[0], recv_sem=recv_sem.at[0],
+        device_id=partner, device_id_type=MESH_ID,
+    )
+    first.start()
+    first.wait()
+    acc[0] = flat_ref[:, own] + recv[0]
+    for step, peer in enumerate(peers):
+        copy = pltpu.make_async_remote_copy(
+            src_ref=acc.at[step], dst_ref=recv.at[step + 1],
+            send_sem=send_sem.at[step + 1], recv_sem=recv_sem.at[step + 1],
+            device_id=peer, device_id_type=MESH_ID,
+        )
+        copy.start()
+        copy.wait()
+        acc[step + 1] = acc[step] + recv[step + 1]
+    last = len(peers)
+    final = pltpu.make_async_remote_copy(
+        src_ref=acc.at[last], dst_ref=recv.at[last + 1],
+        send_sem=send_sem.at[last + 1], recv_sem=recv_sem.at[last + 1],
+        device_id=partner, device_id_type=MESH_ID,
+    )
+    final.start()
+    final.wait()
+    out_ref[:, own] = acc[last]
+    out_ref[:, other] = recv[last + 1]
+
+
+def all_reduce(flat):
+    rows, width = flat.shape
+    steps = 0
+    for axis in BLK_AXES:
+        steps += max(lax.axis_size(axis) - 1, 0).bit_length()
+    vmem = pl.BlockSpec(memory_space=pltpu.VMEM)
+    return pl.pallas_call(
+        reduce_kernel,
+        out_shape=jax.ShapeDtypeStruct(flat.shape, flat.dtype),
+        in_specs=[vmem],
+        out_specs=vmem,
+        scratch_shapes=[
+            pltpu.VMEM((steps + 1, rows, width // 2), flat.dtype),
+            pltpu.VMEM((steps + 2, rows, width // 2), flat.dtype),
+            pltpu.SemaphoreType.DMA((steps + 2,)),
+            pltpu.SemaphoreType.DMA((steps + 2,)),
+        ],
+        compiler_params=pltpu.CompilerParams(collective_id=1, has_side_effects=True),
+    )(flat)
 
 
 def shards(endpoints, row_counts, layer_order, depth_weight, point_weight, point_bias):
@@ -260,7 +327,7 @@
 
     pieces = (jnp.stack(depth_terms), jnp.stack(point_terms), jnp.stack(bias_terms))
     flat = jnp.concatenate([piece.reshape(layers, -1) for piece in pieces], axis=1)
-    flat = all_reduce(flat, core)
+    flat = all_reduce(flat)
     inverse = jnp.zeros((layers,), jnp.int32).at[layer_order].set(jnp.arange(layers, dtype=jnp.int32))
     factor = 1.0 / math.sqrt(held.shape[0] * height * breadth * blk_count())
     flat = jnp.take(flat, inverse, axis=0) * factor

time: 102 us -> 108 us (1.059)
  Pallas kernels: 16.2 us -> 60.6 us
  waiting for transfers between devices: 25.4 us -> 0.01 us
  starting transfers between devices: 21.3 us -> 3.55 us
  local copies, waits for them, and re-layouts: 7.59 us -> 11.5 us
  other arithmetic: 16.6 us -> 17.7 us
    pallas_call x0 -> x1, Pallas kernels: none -> 44.4 us  [all_reduce(): pl.pallas_call(reduce_kernel, out_shape=jax.ShapeDtypeStruct(flat.shape,...]
    ppermute x9 -> x0, waiting for transfers between devices: 25.4 us -> none  [the longest x7 24.4 us: all_reduce(): acc = acc + lax.ppermute(acc, axis, pairs)]
    ppermute x9 -> x0, starting transfers between devices: 13.5 us -> none  [the longest x7 6.74 us: all_reduce(): acc = acc + lax.ppermute(acc, axis, pairs)]
    ppermute x1, starting transfers between devices: 6.44 us -> 2.08 us  [shards(): got_grad = lax.ppermute(input_grad, 'pipe', [(1, 0)])]
    gather x1, local copies, waits for them, and re-layouts: 0.69 us -> 4.65 us  [shards(): flat = jnp.take(flat, inverse, axis=0) * factor]
  transfers between devices with their start and end apart: 11 -> 2, of which waited for: 8 -> 0; matrix products, arithmetic and copies ran while one was open for 3% -> 19% of each run, Pallas kernels for 0% -> 41%
where the time goes in v5:
time: 108 us; the launch traced here: 107 us
  Pallas kernels  60.6 us (56%)
  other arithmetic  17.7 us (16%)
  local copies, waits for them, and re-layouts  11.5 us (11%)
  between operations  8.78 us (8%)
  matrix products  5.24 us (5%)
  starting transfers between devices  3.55 us (3%)
    pallas_call x1, Pallas kernels, all_reduce(): pl.pallas_call(reduce_kernel, out_shape=jax.ShapeDtypeStruct(flat.shape,...  44.4 us
    pallas_call x1, Pallas kernels, exchange(): pl.pallas_call(exchange_kernel, out_shape=(jax.ShapeDtypeStruct(grid_shap...  16.2 us
    gather x1, local copies, waits for them, and re-layouts, shards(): flat = jnp.take(flat, inverse, axis=0) * factor  4.65 us
    convert_element_type x3, other arithmetic, shards(): gated = (masked * gelu_pair(preact)[1]).astype(jnp.bfloat16)  4.57 us
    reduce_sum x4, other arithmetic, shards(): jnp.sum(back_in * padded[i:i + height, start:start + breadth].astype(jnp....  3.28 us
    unnamed x20, local copies, waits for them, and re-layouts  2.83 us
    convert_element_type x4, other arithmetic, shards(): mixed = conv_forward(pad_rows(activation), depth).astype(jnp.bfloat16)  2.83 us
    dot_general x4, matrix products, shards(): jnp.dot(mixed.reshape(rows * span, channels), point, preferred_element_ty...  2.36 us
  transfers between devices with their start and end apart: 2, of which 0 were waited for; matrix products, arithmetic and copies ran while one was open for 19% of the time, Pallas kernels for 41%

profile of v5, /device:TPU:1, one launch (start us, length us, event | category | flops | bytes accessed | tf_op | source)
XLA Modules:
  0.0 107.4 jit_solution(6109939980040144908)
XLA Ops:
  0.6 0.0 copy-start
  0.7 0.0 copy-start.5
  0.7 0.7 copy-done.5
  1.3 0.6 fusion.143
  7.0 0.0 copy-start.7
  7.1 0.6 copy-done.7
  7.7 0.6 dynamic_slice.48
  8.3 0.6 compare_convert_fusion
  8.9 0.0 copy-start.1
  9.0 0.9 slice_bitcast_fusion.2
  9.9 0.7 pad_maximum_fusion.edges_ref
  10.5 16.2 %shard_map.93 = (bf16[12,128,128]{2,1,0:T(8,128)(2,1)}, bf16[2,12,8,128]{3,2,1,0:T(8,128)(2,1)}, bf16[2,12,8,128]{3,2,1,0:T(8,128)(2,1)}) custom-call(bf16[2,12,128,128]{3,2,1,0:T(8,128)(2,1)} %bitcast.238, bf16[2,2,12,8,128]{4,3,2,1,0:T(8,128)(2,1)} %pad_maximum_fusion.edges_ref), custom_call_target="tpu_custom_call" | custom-call | tf_op jit(solution)/shard_map/pallas_call | solution.py:128
  28.0 0.0 copy-start.6
  29.3 0.0 copy-done.6
  29.3 0.0 copy-done.4
  29.4 0.0 copy-start.2
  29.4 0.7 copy-done.3
  30.1 0.0 copy-done.2
  30.2 1.1 bitcast_select_fusion.1
  31.2 0.2 multiply_convert_fusion
  31.4 0.7 fusion.5
  32.1 0.5 fusion.7
  32.6 0.7 fusion.13
  33.3 0.5 fusion.15
  33.9 0.7 fusion.21
  34.6 0.5 fusion.23
  35.1 0.1 slice_convert_fusion
  35.2 0.7 add_convert_fusion
  35.9 0.9 fusion.29
  36.8 0.3 fusion.99
  37.0 1.5 %collective-permute-start = (bf16[12,128,128]{2,1,0:T(8,128)(2,1)S(1)}, bf16[12,128,128]{2,1,0:T(8,128)(2,1)S(1)}, u32[]{:S(2)}, u32[]{:S(2)}) collective-permute-start(bf16[12,128,128]{2,1,0:T(8,128)(2,1)S(1)} %fusion.99), channel_id=1, source_target_pairs={{0,1},{2,3},{4,5},{6,7},{8,9},{10,11},{12,13},{14,15},{16,17},{18,... | collective-permute-start | bytes 1179656 | tf_op jit(solution)/shard_map/ppermute | solution.py:322
  38.5 0.4 convolution_convert_fusion.3
  38.9 0.2 convert_reduce_fusion
  39.1 1.5 %fusion.35 = (bf16[12,134,128]{2,1,0:T(8,128)(2,1)S(1)}, f32[12,134,128]{2,1,0:T(8,128)S(1)}) fusion(f32[12,138,128]{2,1,0:T(8,128)S(1)} %get-tuple-element.122, f32[12]{0:T(128)S(1)} %compare_convert_fusion, f32[128]{0:T(128)S(1)} %get-tuple-element.74, f32[128]{0:T(128)S(1)} %get-tuple-element.75, f32[128]{0:T(128)S(1)} %get-tuple-element.76, ...), kind=kLoop, calls=%fused_computation.93 | loop fusion | flops 8438784 | bytes 4582400 | tf_op jit(solution)/shard_map/convert_element_type | solution.py:287
  40.7 0.4 convolution_convert_fusion.2
  41.0 0.2 convert_reduce_fusion.1
  41.3 1.5 %fusion.41 = (bf16[12,132,128]{2,1,0:T(8,128)(2,1)S(1)}, f32[12,132,128]{2,1,0:T(8,128)S(1)}) fusion(f32[12,140,128]{2,1,0:T(8,128)S(1)} %get-tuple-element.120, f32[12]{0:T(128)S(1)} %compare_convert_fusion, f32[128]{0:T(128)S(1)} %get-tuple-element.83, f32[128]{0:T(128)S(1)} %get-tuple-element.84, f32[128]{0:T(128)S(1)} %get-tuple-element.85, ...), kind=kLoop, calls=%fused_computation.99 | loop fusion | flops 8312832 | bytes 4563968 | tf_op jit(solution)/shard_map/convert_element_type | solution.py:287
  42.8 0.4 convolution_convert_fusion.1
  43.2 0.2 convert_reduce_fusion.2
  43.4 1.5 %fusion.47 = (bf16[12,130,128]{2,1,0:T(8,128)(2,1)S(1)}, f32[12,130,128]{2,1,0:T(8,128)S(1)}) fusion(f32[12,142,128]{2,1,0:T(8,128)S(1)} %get-tuple-element.118, f32[12]{0:T(128)S(1)} %compare_convert_fusion, f32[128]{0:T(128)S(1)} %get-tuple-element.92, f32[128]{0:T(128)S(1)} %get-tuple-element.93, f32[128]{0:T(128)S(1)} %get-tuple-element.94, ...), kind=kLoop, calls=%fused_computation.105 | loop fusion | flops 8186880 | bytes 4545536 | tf_op jit(solution)/shard_map/convert_element_type | solution.py:287
  44.9 0.4 convolution_convert_fusion
  45.3 0.2 convert_reduce_fusion.3
  45.5 0.3 fusion.100
  45.9 0.3 fusion.102
  46.2 0.3 fusion.104
  46.6 0.3 fusion.106
  46.9 0.9 fusion.72
  47.8 0.9 fusion.63
  48.6 0.7 fusion.54
  49.6 0.8 fusion.89
  50.6 0.6 scatter_custom_fusion
  51.1 1.0 maximum_maximum_fusion.flat_ref
  52.1 44.4 %shard_map.94 = f32[4,17664]{1,0:T(4,128)} custom-call(f32[4,17664]{1,0:T(4,128)} %maximum_maximum_fusion.flat_ref), custom_call_target="tpu_custom_call" | custom-call | tf_op jit(solution)/shard_map/pallas_call | solution.py:219
  96.6 4.6 %gather_fusion = f32[4,17664]{1,0:T(4,128)S(1)} fusion(f32[4,17664]{1,0:T(4,128)} %shard_map.94, s32[1024]{0:T(1024)S(1)} %pad_clamp_fusion), kind=kCustom, calls=%fused_computation | custom fusion | bytes 565264 | tf_op jit(solution)/shard_map/jit(_take)/gather | solution.py:333
  101.3 0.0 collective-permute-done
  101.3 1.0 select_bitcast_fusion.1
  102.2 2.1 %collective-permute-start.1 = (bf16[12,128,128]{2,1,0:T(8,128)(2,1)S(1)}, bf16[12,128,128]{2,1,0:T(8,128)(2,1)S(1)}, u32[]{:S(2)}, u32[]{:S(2)}) collective-permute-start(bf16[12,128,128]{2,1,0:T(8,128)(2,1)S(1)} %get-tuple-element.51), channel_id=1, source_target_pairs={{1,0},{3,2},{5,4},{7,6},{9,8},{11,10},{13,12},{15,14},{17,16},{19,... | collective-permute-start | bytes 1179656 | tf_op jit(solution)/shard_map/ppermute | solution.py:323
  104.3 0.2 select_multiply_fusion
  104.5 0.6 slice.888
  105.1 0.6 slice.890
  105.7 0.7 copy.33
  106.4 0.0 collective-permute-done.1
  106.4 0.1 select_bitcast_fusion
  106.5 0.9 maximum_bitcast_fusion
  (41 shorter events, 0.4 us)
Async XLA Ops:
  0.6 31.5 %copy-start = (bf16[4,128,128]{2,1,0:T(8,128)(2,1)S(1)}, bf16[4,128,128]{2,1,0:T(8,128)(2,1)}, u32[]{:S(2)}) copy-start(bf16[4,128,128]{2,1,0:T(8,128)(2,1)} %param.10) | copy-start | bytes 393220
  0.7 0.7 copy-start.5
  7.0 0.7 copy-start.7
  8.9 21.2 %copy-start.1 = (bf16[1,2,12,128,128]{4,3,2,1,0:T(8,128)(2,1)S(1)}, bf16[1,2,12,128,128]{4,3,2,1,0:T(8,128)(2,1)}, u32[]{:S(2)}) copy-start(bf16[1,2,12,128,128]{4,3,2,1,0:T(8,128)(2,1)} %param.6) | copy-start | bytes 2359300
  10.5 18.8 %copy-start.4 = (f32[4,3,3,128]{3,0,2,1:T(4,128)S(1)}, f32[4,3,3,128]{3,0,2,1:T(4,128)}, u32[]{:S(2)}) copy-start(f32[4,3,3,128]{3,0,2,1:T(4,128)} %param.9) | copy-start | bytes 55300
  28.0 1.3 %copy-start.6 = (f32[4,128]{1,0:T(4,128)S(1)}, f32[4,128]{1,0:T(4,128)}, u32[]{:S(2)}) copy-start(f32[4,128]{1,0:T(4,128)} %param.11) | copy-start | bytes 6148
  29.3 0.8 copy-start.3
  29.4 0.8 copy-start.2
  37.0 64.2 %collective-permute-start = (bf16[12,128,128]{2,1,0:T(8,128)(2,1)S(1)}, bf16[12,128,128]{2,1,0:T(8,128)(2,1)S(1)}, u32[]{:S(2)}, u32[]{:S(2)}) collective-permute-start(bf16[12,128,128]{2,1,0:T(8,128)(2,1)S(1)} %fusion.99), channel_id=1, source_target_pairs={{0,1},{2,3},{4,5},{6,7},{8,9},{10,11},{12,13},{14,15},{16,17},{18,... | collective-permute-start | bytes 1179656 | tf_op jit(solution)/shard_map/ppermute | solution.py:322
  102.2 4.2 %collective-permute-start.1 = (bf16[12,128,128]{2,1,0:T(8,128)(2,1)S(1)}, bf16[12,128,128]{2,1,0:T(8,128)(2,1)S(1)}, u32[]{:S(2)}, u32[]{:S(2)}) collective-permute-start(bf16[12,128,128]{2,1,0:T(8,128)(2,1)S(1)} %get-tuple-element.51), channel_id=1, source_target_pairs={{1,0},{3,2},{5,4},{7,6},{9,8},{11,10},{13,12},{15,14},{17,16},{19,... | collective-permute-start | bytes 1179656 | tf_op jit(solution)/shard_map/ppermute | solution.py:323

commit v6 on v5

--- a/solution.py
+++ b/solution.py
@@ -151,7 +151,7 @@
 
 def reduce_kernel(flat_ref, out_ref, acc, recv, send_sem, recv_sem):
     core = lax.axis_index("pipe")
-    half = flat_ref.shape[1] // 2
+    half = flat_ref.shape[0] // 2
     coords = {axis: lax.axis_index(axis) for axis in BLK_AXES}
     order_a, order_b = [], []
     for axis in ("z", "y", "x"):
@@ -179,16 +179,16 @@
         pl.semaphore_signal(barrier, inc=1, device_id=target, device_id_type=MESH_ID)
     pl.semaphore_wait(barrier, 1 + len(peers))
 
-    own = pl.ds(pl.multiple_of(core * half, 128), half)
-    other = pl.ds(pl.multiple_of((1 - core) * half, 128), half)
+    own = pl.ds(pl.multiple_of(core * half, 8), half)
+    other = pl.ds(pl.multiple_of((1 - core) * half, 8), half)
     first = pltpu.make_async_remote_copy(
-        src_ref=flat_ref.at[:, other], dst_ref=recv.at[0],
+        src_ref=flat_ref.at[other], dst_ref=recv.at[0],
         send_sem=send_sem.at[0], recv_sem=recv_sem.at[0],
         device_id=partner, device_id_type=MESH_ID,
     )
     first.start()
     first.wait()
-    acc[0] = flat_ref[:, own] + recv[0]
+    acc[0] = flat_ref[own] + recv[0]
     for step, peer in enumerate(peers):
         copy = pltpu.make_async_remote_copy(
             src_ref=acc.at[step], dst_ref=recv.at[step + 1],
@@ -206,8 +206,8 @@
     )
     final.start()
     final.wait()
-    out_ref[:, own] = acc[last]
-    out_ref[:, other] = recv[last + 1]
+    out_ref[own] = acc[last]
+    out_ref[other] = recv[last + 1]
 
 
 def all_reduce(flat):
@@ -222,8 +222,8 @@
         in_specs=[vmem],
         out_specs=vmem,
         scratch_shapes=[
-            pltpu.VMEM((steps + 1, rows, width // 2), flat.dtype),
-            pltpu.VMEM((steps + 2, rows, width // 2), flat.dtype),
+            pltpu.VMEM((steps + 1, rows // 2, width), flat.dtype),
+            pltpu.VMEM((steps + 2, rows // 2, width), flat.dtype),
             pltpu.SemaphoreType.DMA((steps + 2,)),
             pltpu.SemaphoreType.DMA((steps + 2,)),
         ],
@@ -325,17 +325,26 @@
     second = jnp.where(core == 0, got_grad, outcome)
     result = jnp.stack([first, second])[None]
 
-    pieces = (jnp.stack(depth_terms), jnp.stack(point_terms), jnp.stack(bias_terms))
-    flat = jnp.concatenate([piece.reshape(layers, -1) for piece in pieces], axis=1)
-    flat = all_reduce(flat)
-    inverse = jnp.zeros((layers,), jnp.int32).at[layer_order].set(jnp.arange(layers, dtype=jnp.int32))
+    pieces = []
+    for terms in (depth_terms, point_terms, bias_terms):
+        by_layer = []
+        for w in range(layers):
+            picked = jnp.zeros_like(terms[0])
+            for p in range(layers):
+                picked = picked + jnp.where(layer_order[p] == w, terms[p], 0.0)
+            by_layer.append(picked)
+        pieces.append(jnp.stack(by_layer))
+    flat = jnp.concatenate([piece.reshape(-1) for piece in pieces])
+    lanes = 128
+    rows = -(-flat.shape[0] // lanes)
+    rows = -(-rows // 16) * 16
+    flat = jnp.pad(flat, (0, rows * lanes - flat.shape[0])).reshape(rows, lanes)
     factor = 1.0 / math.sqrt(held.shape[0] * height * breadth * blk_count())
-    flat = jnp.take(flat, inverse, axis=0) * factor
+    flat = (all_reduce(flat) * factor).reshape(-1)
     ordered, at = [], 0
     for piece in pieces:
-        width = piece[0].size
-        ordered.append(flat[:, at : at + width].reshape(piece.shape))
-        at += width
+        ordered.append(flat[at : at + piece.size].reshape(piece.shape))
+        at += piece.size
     return (result, ordered[0], ordered[1], ordered[2])
 
 

time: 108 us -> 133 us (1.23)
  between operations: 8.78 us -> 18.8 us
  other arithmetic: 17.7 us -> 27.1 us
  matrix products: 5.24 us -> 9.96 us
    unnamed x20 -> x175, local copies, waits for them, and re-layouts: 2.83 us -> 8.97 us
    convert_element_type x3, other arithmetic: 4.57 us -> 10.1 us  [shards(): gated = (masked * gelu_pair(preact)[1]).astype(jnp.bfloat16)]
    gather x1 -> x0, local copies, waits for them, and re-layouts: 4.65 us -> none  [shards(): flat = jnp.take(flat, inverse, axis=0) * factor]
    dot_general x4, matrix products: 2.36 us -> 5.11 us  [shards(): jnp.dot(mixed.reshape(rows * span, channels), point, preferred_element_ty...]
    reduce_sum x4, other arithmetic: 0.88 us -> 3.03 us  [shards(): bias_terms[p] = jnp.sum(gate_in.astype(jnp.float32), axis=0)]
  transfers between devices with their start and end apart: 2 -> 2, of which waited for: 0 -> 0; matrix products, arithmetic and copies ran while one was open for 19% -> 19% of each run, Pallas kernels for 41% -> 33%
where the time goes in v6:
time: 133 us; the launch traced here: 132 us
  Pallas kernels  59.8 us (45%)
  other arithmetic  27.1 us (20%)
  between operations  18.8 us (14%)
  local copies, waits for them, and re-layouts  12.5 us (9%)
  matrix products  9.96 us (7%)
  starting transfers between devices  4.11 us (3%)
    pallas_call x1, Pallas kernels, all_reduce(): pl.pallas_call(reduce_kernel, out_shape=jax.ShapeDtypeStruct(flat.shape,...  43.6 us
    pallas_call x1, Pallas kernels, exchange(): pl.pallas_call(exchange_kernel, out_shape=(jax.ShapeDtypeStruct(grid_shap...  16.2 us
    convert_element_type x3, other arithmetic, shards(): gated = (masked * gelu_pair(preact)[1]).astype(jnp.bfloat16)  10.1 us
    unnamed x175, local copies, waits for them, and re-layouts  8.97 us
    dot_general x4, matrix products, shards(): jnp.dot(mixed.reshape(rows * span, channels), point, preferred_element_ty...  5.11 us
    reduce_sum x4, other arithmetic, shards(): jnp.sum(back_in * padded[i:i + height, start:start + breadth].astype(jnp....  3.29 us
    reduce_sum x4, other arithmetic, shards(): bias_terms[p] = jnp.sum(gate_in.astype(jnp.float32), axis=0)  3.03 us
    convert_element_type x4, other arithmetic, shards(): mixed = conv_forward(pad_rows(activation), depth).astype(jnp.bfloat16)  2.82 us
  transfers between devices with their start and end apart: 2, of which 0 were waited for; matrix products, arithmetic and copies ran while one was open for 19% of the time, Pallas kernels for 33%

profile of v6, /device:TPU:1, one launch (start us, length us, event | category | flops | bytes accessed | tf_op | source)
XLA Modules:
  0.0 132.3 jit_solution(3583297108300226696)
XLA Ops:
  0.7 0.7 copy-done.21
  1.3 0.6 fusion.154
  6.8 0.6 copy-done.85
  7.4 0.6 dynamic_slice.48
  8.0 0.6 compare_convert_fusion
  8.7 0.9 slice_bitcast_fusion.1
  9.6 0.7 pad_maximum_fusion.1.edges_ref
  10.2 16.2 %shard_map.93 = (bf16[12,128,128]{2,1,0:T(8,128)(2,1)}, bf16[2,12,8,128]{3,2,1,0:T(8,128)(2,1)}, bf16[2,12,8,128]{3,2,1,0:T(8,128)(2,1)}) custom-call(bf16[2,12,128,128]{3,2,1,0:T(8,128)(2,1)} %bitcast.246, bf16[2,2,12,8,128]{4,3,2,1,0:T(8,128)(2,1)} %pad_maximum_fusion.1.edges_ref), custom_call_target="tpu_custom_call" | custom-call | tf_op jit(solution)/shard_map/pallas_call | solution.py:128
  29.3 0.4 copy-done.19
  29.7 1.1 bitcast_select_fusion.1
  30.8 0.2 multiply_convert_fusion
  31.0 0.7 fusion.5
  31.8 1.4 %fusion.7 = (bf16[12,142,128]{2,1,0:T(8,128)(2,1)S(1)}, f32[12,142,128]{2,1,0:T(8,128)}) fusion(f32[12]{0:T(128)S(1)} %compare_convert_fusion, bf16[12,144,128]{2,1,0:T(8,128)(2,1)S(1)} %multiply_convert_fusion, f32[128]{0:T(128)S(1)} %get-tuple-element.121, bf16[12,142,128]{2,1,0:T(8,128)(2,1)S(1)} %fusion.5, bf16[4,128,128]{2,1,0:T(8,128)(2,1)S(1)} %copy-done, ...), kind=kOutput, calls=%fused_computation.66 | convolution fusion | flops 57799680 | bytes 2227204 | tf_op jit(solution)/shard_map/dot_general | solution.py:266
  33.3 0.7 fusion.13
  34.0 1.4 %fusion.15 = (bf16[12,140,128]{2,1,0:T(8,128)(2,1)S(1)}, f32[12,140,128]{2,1,0:T(8,128)}) fusion(f32[12]{0:T(128)S(1)} %compare_convert_fusion, bf16[12,142,128]{2,1,0:T(8,128)(2,1)S(1)} %get-tuple-element.127, f32[128]{0:T(128)S(1)} %get-tuple-element.120, bf16[12,140,128]{2,1,0:T(8,128)(2,1)S(1)} %fusion.13, bf16[4,128,128]{2,1,0:T(8,128)(2,1)S(1)} %copy-done, ...), kind=kOutput, calls=%fused_computation.74 | convolution fusion | flops 56985600 | bytes 2208772 | tf_op jit(solution)/shard_map/dot_general | solution.py:266
  35.5 0.7 fusion.21
  36.3 1.4 %fusion.23 = (bf16[12,138,128]{2,1,0:T(8,128)(2,1)S(1)}, f32[12,138,128]{2,1,0:T(8,128)}) fusion(f32[12]{0:T(128)S(1)} %compare_convert_fusion, bf16[12,140,128]{2,1,0:T(8,128)(2,1)S(1)} %get-tuple-element.129, f32[128]{0:T(128)S(1)} %get-tuple-element.122, bf16[12,138,128]{2,1,0:T(8,128)(2,1)S(1)} %fusion.21, bf16[4,128,128]{2,1,0:T(8,128)(2,1)S(1)} %copy-done, ...), kind=kOutput, calls=%fused_computation.82 | convolution fusion | flops 56171520 | bytes 2190340 | tf_op jit(solution)/shard_map/dot_general | solution.py:266
  37.7 0.1 slice_convert_fusion
  37.9 0.4 copy-done.68
  38.5 0.7 add_convert_fusion
  39.2 0.8 fusion.29
  40.0 0.3 fusion.99
  40.3 1.5 %collective-permute-start = (bf16[12,128,128]{2,1,0:T(8,128)(2,1)S(1)}, bf16[12,128,128]{2,1,0:T(8,128)(2,1)}, u32[]{:S(2)}, u32[]{:S(2)}) collective-permute-start(bf16[12,128,128]{2,1,0:T(8,128)(2,1)S(1)} %fusion.99), channel_id=1, source_target_pairs={{0,1},{2,3},{4,5},{6,7},{8,9},{10,11},{12,13},{14,15},{16,17},{18,... | collective-permute-start | bytes 1179656 | tf_op jit(solution)/shard_map/ppermute | solution.py:322
  41.8 0.4 convolution_convert_fusion.3
  42.2 0.8 convert_reduce_fusion
  43.6 0.6 copy-done.69
  44.2 3.3 %fusion.35 = (bf16[12,134,128]{2,1,0:T(8,128)(2,1)S(1)}, f32[12,134,128]{2,1,0:T(8,128)}) fusion(f32[12,138,128]{2,1,0:T(8,128)} %get-tuple-element.132, f32[12]{0:T(128)S(1)} %compare_convert_fusion, f32[128]{0:T(128)S(1)} %copy-done.71, f32[128]{0:T(128)S(1)} %copy-done.73, f32[128]{0:T(128)} %copy-done.74, ...), kind=kLoop, calls=%fused_computation.95 | loop fusion | flops 8438784 | bytes 4570112 | tf_op jit(solution)/shard_map/convert_element_type | solution.py:287
  47.5 0.4 convolution_convert_fusion.2
  47.9 0.4 copy-done.3
  48.3 0.8 convert_reduce_fusion.1
  49.7 0.6 copy-done.51
  50.3 3.4 %fusion.41 = (bf16[12,132,128]{2,1,0:T(8,128)(2,1)S(1)}, f32[12,132,128]{2,1,0:T(8,128)}) fusion(f32[12,140,128]{2,1,0:T(8,128)} %get-tuple-element.130, f32[12]{0:T(128)S(1)} %compare_convert_fusion, f32[128]{0:T(128)S(1)} %copy-done.53, f32[128]{0:T(128)S(1)} %copy-done.55, f32[128]{0:T(128)S(1)} %copy-done.57, ...), kind=kLoop, calls=%fused_computation.101 | loop fusion | flops 8312832 | bytes 4514816 | tf_op jit(solution)/shard_map/convert_element_type | solution.py:287
  53.7 0.4 convolution_convert_fusion.1
  54.1 0.4 copy-done.5
  54.5 0.8 convert_reduce_fusion.2
  55.9 0.6 copy-done.39
  56.6 3.4 %fusion.47 = (bf16[12,130,128]{2,1,0:T(8,128)(2,1)S(1)}, f32[12,130,128]{2,1,0:T(8,128)}) fusion(f32[12,142,128]{2,1,0:T(8,128)} %get-tuple-element.128, f32[12]{0:T(128)S(1)} %compare_convert_fusion, f32[128]{0:T(128)S(1)} %copy-done.41, f32[128]{0:T(128)S(1)} %copy-done.43, f32[128]{0:T(128)} %copy-done.44, ...), kind=kLoop, calls=%fused_computation.107 | loop fusion | flops 8186880 | bytes 4471808 | tf_op jit(solution)/shard_map/convert_element_type | solution.py:287
  60.0 1.2 convolution_convert_fusion
  61.2 0.7 convert_reduce_fusion.3
  69.7 1.6 %convolution_bitcast_fusion = f32[128,128]{1,0:T(8,128)S(1)} fusion(bf16[12,136,128]{2,1,0:T(8,128)(2,1)} %copy-done.11, bf16[12,136,128]{2,1,0:T(8,128)(2,1)} %copy-done.2), kind=kOutput, calls=%fused_computation.49 | convolution fusion | flops 50331648 | bytes 851968 | tf_op jit(solution)/shard_map/dot_general | solution.py:297
  71.3 0.3 convolution_bitcast_fusion.1
  71.6 0.6 copy-done.6
  72.3 0.1 copy-done.15
  72.4 0.3 convolution_bitcast_fusion.2
  72.8 0.6 copy-done.8
  73.4 0.1 copy-done.13
  73.5 0.3 convolution_bitcast_fusion.3
  73.9 0.9 fusion.72
  74.8 0.9 fusion.63
  75.6 0.7 fusion.54
  76.3 0.3 copy-done.1
  76.6 0.8 fusion.89
  77.9 0.6 copy-done.80
  78.7 0.5 copy-done.29
  79.2 0.1 copy-done.31
  79.3 1.9 %select_bitcast_fusion.1 = (bf16[1,12,128,128]{3,2,1,0:T(8,128)(2,1)S(1)}, bf16[12,128,128]{2,1,0:T(8,128)(2,1)S(1)}) fusion(bf16[12,128,128]{2,1,0:T(8,128)(2,1)} %collective-permute-done, pred[]{:T(512)S(6)} %eq.34, f32[12]{0:T(128)S(1)} %compare_convert_fusion, f32[128]{0:T(128)S(1)} %copy-done.23, f32[128]{0:T(128)S(1)} %copy-done.25, ...), kind=kLoop, calls=%fused_computation.193 | loop fusion | flops 5898240 | bytes 3568641 | tf_op jit(solution)/shard_map/stack | solution.py:326
  81.3 2.6 %collective-permute-start.1 = (bf16[12,128,128]{2,1,0:T(8,128)(2,1)S(1)}, bf16[12,128,128]{2,1,0:T(8,128)(2,1)S(1)}, u32[]{:S(2)}, u32[]{:S(2)}) collective-permute-start(bf16[12,128,128]{2,1,0:T(8,128)(2,1)S(1)} %get-tuple-element.55), channel_id=1, source_target_pairs={{1,0},{3,2},{5,4},{7,6},{9,8},{11,10},{13,12},{15,14},{17,16},{19,... | collective-permute-start | bytes 1179656 | tf_op jit(solution)/shard_map/ppermute | solution.py:323
  84.0 0.7 fusion.108.flat_ref
  84.7 43.6 %shard_map.94 = f32[560,128]{1,0:T(8,128)} custom-call(f32[560,128]{1,0:T(8,128)} %fusion.108.flat_ref), custom_call_target="tpu_custom_call" | custom-call | tf_op jit(solution)/shard_map/pallas_call | solution.py:219
  128.3 1.0 broadcast_multiply_fusion
  129.3 0.7 slice.938
  130.1 0.6 slice.939
  130.7 0.6 copy.19
  131.3 0.9 maximum_bitcast_fusion
  (195 shorter events, 1.2 us)
Async XLA Ops:
  0.6 31.1 %copy-start = (bf16[4,128,128]{2,1,0:T(8,128)(2,1)S(1)}, bf16[4,128,128]{2,1,0:T(8,128)(2,1)}, u32[]{:S(2)}) copy-start(bf16[4,128,128]{2,1,0:T(8,128)(2,1)} %param.10) | copy-start | bytes 393220
  0.7 0.7 copy-start.21
  8.6 21.1 %copy-start.10 = (bf16[1,2,12,128,128]{4,3,2,1,0:T(8,128)(2,1)S(1)}, bf16[1,2,12,128,128]{4,3,2,1,0:T(8,128)(2,1)}, u32[]{:S(2)}) copy-start(bf16[1,2,12,128,128]{4,3,2,1,0:T(8,128)(2,1)} %param.6) | copy-start | bytes 2359300
  10.2 18.7 %copy-start.20 = (f32[4,3,3,128]{3,0,2,1:T(4,128)S(1)}, f32[4,3,3,128]{3,0,2,1:T(4,128)}, u32[]{:S(2)}) copy-start(f32[4,3,3,128]{3,0,2,1:T(4,128)} %param.9) | copy-start | bytes 55300
  27.7 1.2 copy-start.84
  28.9 0.8 copy-start.19
  28.9 0.8 copy-start.18
  29.0 2.0 %copy-start.22 = (f32[128]{0:T(128)}, f32[128]{0:T(128)S(1)}, u32[]{:S(2)}) copy-start(f32[128]{0:T(128)S(1)} %get-tuple-element.108) | copy-start | bytes 1540
  29.0 2.0 %copy-start.24 = (f32[128]{0:T(128)}, f32[128]{0:T(128)S(1)}, u32[]{:S(2)}) copy-start(f32[128]{0:T(128)S(1)} %get-tuple-element.109) | copy-start | bytes 1540
  29.0 2.0 %copy-start.26 = (f32[128]{0:T(128)}, f32[128]{0:T(128)S(1)}, u32[]{:S(2)}) copy-start(f32[128]{0:T(128)S(1)} %get-tuple-element.110) | copy-start | bytes 1540
  29.0 2.0 %copy-start.28 = (f32[128]{0:T(128)}, f32[128]{0:T(128)S(1)}, u32[]{:S(2)}) copy-start(f32[128]{0:T(128)S(1)} %get-tuple-element.111) | copy-start | bytes 1540
  29.0 2.0 %copy-start.30 = (f32[128]{0:T(128)}, f32[128]{0:T(128)S(1)}, u32[]{:S(2)}) copy-start(f32[128]{0:T(128)S(1)} %get-tuple-element.112) | copy-start | bytes 1540
  29.0 2.0 %copy-start.32 = (f32[128]{0:T(128)}, f32[128]{0:T(128)S(1)}, u32[]{:S(2)}) copy-start(f32[128]{0:T(128)S(1)} %get-tuple-element.113) | copy-start | bytes 1540
  29.0 2.0 %copy-start.34 = (f32[128]{0:T(128)}, f32[128]{0:T(128)S(1)}, u32[]{:S(2)}) copy-start(f32[128]{0:T(128)S(1)} %get-tuple-element.114) | copy-start | bytes 1540
  29.0 2.0 %copy-start.36 = (f32[128]{0:T(128)}, f32[128]{0:T(128)S(1)}, u32[]{:S(2)}) copy-start(f32[128]{0:T(128)S(1)} %get-tuple-element.115) | copy-start | bytes 1540
  29.1 4.1 %copy-start.38 = (f32[128]{0:T(128)}, f32[128]{0:T(128)S(1)}, u32[]{:S(2)}) copy-start(f32[128]{0:T(128)S(1)} %get-tuple-element.98) | copy-start | bytes 1540
  29.1 4.1 %copy-start.40 = (f32[128]{0:T(128)}, f32[128]{0:T(128)S(1)}, u32[]{:S(2)}) copy-start(f32[128]{0:T(128)S(1)} %get-tuple-element.99) | copy-start | bytes 1540
  29.1 4.1 %copy-start.42 = (f32[128]{0:T(128)}, f32[128]{0:T(128)S(1)}, u32[]{:S(2)}) copy-start(f32[128]{0:T(128)S(1)} %get-tuple-element.100) | copy-start | bytes 1540
  29.1 4.1 %copy-start.44 = (f32[128]{0:T(128)}, f32[128]{0:T(128)S(1)}, u32[]{:S(2)}) copy-start(f32[128]{0:T(128)S(1)} %get-tuple-element.101) | copy-start | bytes 1540
  29.1 4.1 %copy-start.45 = (f32[128]{0:T(128)}, f32[128]{0:T(128)S(1)}, u32[]{:S(2)}) copy-start(f32[128]{0:T(128)S(1)} %get-tuple-element.102) | copy-start | bytes 1540
  29.1 4.1 %copy-start.46 = (f32[128]{0:T(128)}, f32[128]{0:T(128)S(1)}, u32[]{:S(2)}) copy-start(f32[128]{0:T(128)S(1)} %get-tuple-element.103) | copy-start | bytes 1540
  29.1 4.1 %copy-start.47 = (f32[128]{0:T(128)}, f32[128]{0:T(128)S(1)}, u32[]{:S(2)}) copy-start(f32[128]{0:T(128)S(1)} %get-tuple-element.104) | copy-start | bytes 1540
  29.1 4.1 %copy-start.48 = (f32[128]{0:T(128)}, f32[128]{0:T(128)S(1)}, u32[]{:S(2)}) copy-start(f32[128]{0:T(128)S(1)} %get-tuple-element.105) | copy-start | bytes 1540
  29.2 4.1 %copy-start.49 = (f32[128]{0:T(128)}, f32[128]{0:T(128)S(1)}, u32[]{:S(2)}) copy-start(f32[128]{0:T(128)S(1)} %get-tuple-element.106) | copy-start | bytes 1540
  29.2 6.3 %copy-start.50 = (f32[128]{0:T(128)}, f32[128]{0:T(128)S(1)}, u32[]{:S(2)}) copy-start(f32[128]{0:T(128)S(1)} %get-tuple-element.89) | copy-start | bytes 1540
  29.2 6.3 %copy-start.52 = (f32[128]{0:T(128)}, f32[128]{0:T(128)S(1)}, u32[]{:S(2)}) copy-start(f32[128]{0:T(128)S(1)} %get-tuple-element.90) | copy-start | bytes 1540
  29.2 6.3 %copy-start.54 = (f32[128]{0:T(128)}, f32[128]{0:T(128)S(1)}, u32[]{:S(2)}) copy-start(f32[128]{0:T(128)S(1)} %get-tuple-element.91) | copy-start | bytes 1540
  29.2 6.3 %copy-start.56 = (f32[128]{0:T(128)}, f32[128]{0:T(128)S(1)}, u32[]{:S(2)}) copy-start(f32[128]{0:T(128)S(1)} %get-tuple-element.92) | copy-start | bytes 1540
  29.2 6.3 %copy-start.58 = (f32[128]{0:T(128)}, f32[128]{0:T(128)S(1)}, u32[]{:S(2)}) copy-start(f32[128]{0:T(128)S(1)} %get-tuple-element.93) | copy-start | bytes 1540
  29.2 6.3 %copy-start.60 = (f32[128]{0:T(128)}, f32[128]{0:T(128)S(1)}, u32[]{:S(2)}) copy-start(f32[128]{0:T(128)S(1)} %get-tuple-element.94) | copy-start | bytes 1540
  29.2 6.3 %copy-start.62 = (f32[128]{0:T(128)}, f32[128]{0:T(128)S(1)}, u32[]{:S(2)}) copy-start(f32[128]{0:T(128)S(1)} %get-tuple-element.95) | copy-start | bytes 1540
  29.2 6.3 %copy-start.64 = (f32[128]{0:T(128)}, f32[128]{0:T(128)S(1)}, u32[]{:S(2)}) copy-start(f32[128]{0:T(128)S(1)} %get-tuple-element.96) | copy-start | bytes 1540
  29.3 6.3 %copy-start.66 = (f32[128]{0:T(128)}, f32[128]{0:T(128)S(1)}, u32[]{:S(2)}) copy-start(f32[128]{0:T(128)S(1)} %get-tuple-element.97) | copy-start | bytes 1540
  31.8 1.4 %copy-start.12 = (bf16[12,142,128]{2,1,0:T(8,128)(2,1)}, bf16[12,142,128]{2,1,0:T(8,128)(2,1)S(1)}, u32[]{:S(2)}) copy-start(bf16[12,142,128]{2,1,0:T(8,128)(2,1)S(1)} %fusion.5) | copy-start | bytes 1308676
  34.0 1.4 %copy-start.14 = (bf16[12,140,128]{2,1,0:T(8,128)(2,1)}, bf16[12,140,128]{2,1,0:T(8,128)(2,1)S(1)}, u32[]{:S(2)}) copy-start(bf16[12,140,128]{2,1,0:T(8,128)(2,1)S(1)} %fusion.13) | copy-start | bytes 1290244
  36.2 1.4 %copy-start.16 = (bf16[12,138,128]{2,1,0:T(8,128)(2,1)}, bf16[12,138,128]{2,1,0:T(8,128)(2,1)S(1)}, u32[]{:S(2)}) copy-start(bf16[12,138,128]{2,1,0:T(8,128)(2,1)S(1)} %fusion.21) | copy-start | bytes 1271812
  39.1 0.9 copy-start.11
  40.0 2.2 %copy-start.2 = (bf16[12,136,128]{2,1,0:T(8,128)(2,1)}, bf16[12,136,128]{2,1,0:T(8,128)(2,1)S(1)}, u32[]{:S(2)}) copy-start(bf16[12,136,128]{2,1,0:T(8,128)(2,1)S(1)} %get-tuple-element.62) | copy-start | bytes 1253380
  40.3 38.4 %collective-permute-start = (bf16[12,128,128]{2,1,0:T(8,128)(2,1)S(1)}, bf16[12,128,128]{2,1,0:T(8,128)(2,1)}, u32[]{:S(2)}, u32[]{:S(2)}) collective-permute-start(bf16[12,128,128]{2,1,0:T(8,128)(2,1)S(1)} %fusion.99), channel_id=1, source_target_pairs={{0,1},{2,3},{4,5},{6,7},{8,9},{10,11},{12,13},{14,15},{16,17},{18,... | collective-permute-start | bytes 1179656 | tf_op jit(solution)/shard_map/ppermute | solution.py:322
  47.5 0.8 copy-start.3
  48.3 1.4 %copy-start.57 = (f32[128]{0:T(128)S(1)}, f32[128]{0:T(128)}, u32[]{:S(2)}) copy-start(f32[128]{0:T(128)} %copy-done.56) | copy-start | bytes 1540
  48.3 1.4 %copy-start.59 = (f32[128]{0:T(128)S(1)}, f32[128]{0:T(128)}, u32[]{:S(2)}) copy-start(f32[128]{0:T(128)} %copy-done.58) | copy-start | bytes 1540
  48.3 1.4 %copy-start.61 = (f32[128]{0:T(128)S(1)}, f32[128]{0:T(128)}, u32[]{:S(2)}) copy-start(f32[128]{0:T(128)} %copy-done.60) | copy-start | bytes 1540
  48.3 1.4 %copy-start.63 = (f32[128]{0:T(128)S(1)}, f32[128]{0:T(128)}, u32[]{:S(2)}) copy-start(f32[128]{0:T(128)} %copy-done.62) | copy-start | bytes 1540
  48.3 1.4 %copy-start.65 = (f32[128]{0:T(128)S(1)}, f32[128]{0:T(128)}, u32[]{:S(2)}) copy-start(f32[128]{0:T(128)} %copy-done.64) | copy-start | bytes 1540
  48.3 1.4 %copy-start.67 = (f32[128]{0:T(128)S(1)}, f32[128]{0:T(128)}, u32[]{:S(2)}) copy-start(f32[128]{0:T(128)} %copy-done.66) | copy-start | bytes 1540
  49.7 0.7 copy-start.55
  53.7 0.8 copy-start.5
  55.9 0.7 copy-start.39
  60.0 1.2 copy-start.7
  69.7 1.6 %copy-start.4 = (bf16[12,134,128]{2,1,0:T(8,128)(2,1)S(1)}, bf16[12,134,128]{2,1,0:T(8,128)(2,1)}, u32[]{:S(2)}) copy-start(bf16[12,134,128]{2,1,0:T(8,128)(2,1)} %copy-done.3) | copy-start | bytes 1234948
  69.7 1.6 %copy-start.17 = (bf16[12,138,128]{2,1,0:T(8,128)(2,1)S(1)}, bf16[12,138,128]{2,1,0:T(8,128)(2,1)}, u32[]{:S(2)}) copy-start(bf16[12,138,128]{2,1,0:T(8,128)(2,1)} %copy-done.16) | copy-start | bytes 1271812
  71.3 1.0 copy-start.6
  71.3 1.1 copy-start.15
  72.4 1.0 copy-start.8
  72.4 1.1 copy-start.13
  75.6 1.0 copy-start.1
  77.5 1.2 copy-start.9
  77.8 0.7 copy-start.82
  78.6 0.7 copy-start.31
  78.6 0.7 copy-start.33
  78.6 0.7 copy-start.35
  78.6 0.7 copy-start.37
  81.3 50.0 %collective-permute-start.1 = (bf16[12,128,128]{2,1,0:T(8,128)(2,1)S(1)}, bf16[12,128,128]{2,1,0:T(8,128)(2,1)S(1)}, u32[]{:S(2)}, u32[]{:S(2)}) collective-permute-start(bf16[12,128,128]{2,1,0:T(8,128)(2,1)S(1)} %get-tuple-element.55), channel_id=1, source_target_pairs={{1,0},{3,2},{5,4},{7,6},{9,8},{11,10},{13,12},{15,14},{17,16},{19,... | collective-permute-start | bytes 1179656 | tf_op jit(solution)/shard_map/ppermute | solution.py:323
  (24 other events, 14.6 us)

commit v7 on v4

--- a/solution.py
+++ b/solution.py
@@ -145,6 +145,20 @@
     )(held, edges)
 
 
+def gather_sum(acc, axis):
+    size = lax.axis_size(axis)
+    index = lax.axis_index(axis)
+    shifted = [acc] + [
+        lax.ppermute(acc, axis, [(j, (j + k) % size) for j in range(size)])
+        for k in range(1, size)
+    ]
+    stacked = jnp.stack(shifted)
+    values = [select_row(stacked, lax.rem(index - j + size, size)) for j in range(size)]
+    while len(values) > 1:
+        values = [values[k] + values[k + 1] for k in range(0, len(values), 2)]
+    return values[0]
+
+
 def all_reduce(flat, core):
     half = flat.shape[1] // 2
     swap = [(0, 1), (1, 0)]
@@ -153,6 +167,9 @@
     acc = mine + lax.ppermute(other, "pipe", swap)
     for axis in ("y", "z", "x"):
         size = lax.axis_size(axis)
+        if size == 4:
+            acc = gather_sum(acc, axis)
+            continue
         bit = 1
         while bit < size:
             pairs = [(i, i ^ bit) for i in range(size)]
@@ -261,9 +278,14 @@
     pieces = (jnp.stack(depth_terms), jnp.stack(point_terms), jnp.stack(bias_terms))
     flat = jnp.concatenate([piece.reshape(layers, -1) for piece in pieces], axis=1)
     flat = all_reduce(flat, core)
-    inverse = jnp.zeros((layers,), jnp.int32).at[layer_order].set(jnp.arange(layers, dtype=jnp.int32))
     factor = 1.0 / math.sqrt(held.shape[0] * height * breadth * blk_count())
-    flat = jnp.take(flat, inverse, axis=0) * factor
+    by_layer = []
+    for w in range(layers):
+        picked = jnp.zeros_like(flat[0])
+        for p in range(layers):
+            picked = picked + jnp.where(layer_order[p] == w, flat[p], 0.0)
+        by_layer.append(picked)
+    flat = jnp.stack(by_layer) * factor
     ordered, at = [], 0
     for piece in pieces:
         width = piece[0].size

time: 102 us -> 107 us (1.049)
  between operations: 8.88 us -> 19.1 us
  waiting for transfers between devices: 25.4 us -> 20.6 us
  starting transfers between devices: 21.3 us -> 19.4 us
  other arithmetic: 16.6 us -> 17.8 us
    ppermute x7 -> x3, waiting for transfers between devices: 24.4 us -> 9.66 us  [all_reduce(): acc = acc + lax.ppermute(acc, axis, pairs)]
    ppermute x0 -> x6, waiting for transfers between devices: none -> 9.96 us  [gather_sum(): lax.ppermute(acc, axis, [(j, (j + k) % size) for j in range(size)])]
    ppermute x0 -> x6, starting transfers between devices: none -> 7.31 us  [gather_sum(): lax.ppermute(acc, axis, [(j, (j + k) % size) for j in range(size)])]
    ppermute x1, starting transfers between devices: 6.32 us -> 1.47 us  [all_reduce(): theirs = lax.ppermute(acc, 'pipe', swap)]
    ppermute x1, starting transfers between devices: 6.44 us -> 4.19 us  [shards(): got_grad = lax.ppermute(input_grad, 'pipe', [(1, 0)])]
    ppermute x7 -> x3, starting transfers between devices: 6.74 us -> 4.66 us  [all_reduce(): acc = acc + lax.ppermute(acc, axis, pairs)]
  transfers between devices with their start and end apart: 11 -> 13, of which waited for: 8 -> 7; matrix products, arithmetic and copies ran while one was open for 3% -> 3% of each run, Pallas kernels for 0% -> 0%
where the time goes in v7:
time: 107 us; the launch traced here: 106 us
  waiting for transfers between devices  20.6 us (19%)
  starting transfers between devices  19.4 us (18%)
  between operations  19.1 us (18%)
  other arithmetic  17.8 us (17%)
  Pallas kernels  16.2 us (15%)
  local copies, waits for them, and re-layouts  6.94 us (6%)
  matrix products  5.94 us (6%)
    pallas_call x1, Pallas kernels, exchange(): pl.pallas_call(exchange_kernel, out_shape=(jax.ShapeDtypeStruct(grid_shap...  16.2 us
    ppermute x6, waiting for transfers between devices, gather_sum(): lax.ppermute(acc, axis, [(j, (j + k) % size) for j in range(size)])  9.96 us
    ppermute x3, waiting for transfers between devices, all_reduce(): acc = acc + lax.ppermute(acc, axis, pairs)  9.66 us
    ppermute x6, starting transfers between devices, gather_sum(): lax.ppermute(acc, axis, [(j, (j + k) % size) for j in range(size)])  7.31 us
    convert_element_type x3, other arithmetic, shards(): gated = (masked * gelu_pair(preact)[1]).astype(jnp.bfloat16)  4.75 us
    ppermute x3, starting transfers between devices, all_reduce(): acc = acc + lax.ppermute(acc, axis, pairs)  4.66 us
    ppermute x1, starting transfers between devices, shards(): got_grad = lax.ppermute(input_grad, 'pipe', [(1, 0)])  4.19 us
    reduce_sum x4, other arithmetic, shards(): jnp.sum(back_in * padded[i:i + height, start:start + breadth].astype(jnp....  3.28 us
  transfers between devices with their start and end apart: 13, of which 7 were waited for; matrix products, arithmetic and copies ran while one was open for 3% of the time, Pallas kernels for 0%

profile of v7, /device:TPU:1, one launch (start us, length us, event | category | flops | bytes accessed | tf_op | source)
XLA Modules:
  0.0 106.1 jit_solution(10825045268801549076)
XLA Ops:
  0.7 0.7 copy-done.5
  1.3 0.7 fusion.156
  7.1 0.6 copy-done.7
  7.8 0.6 dynamic_slice.79
  8.3 0.6 compare_convert_fusion
  9.0 0.8 slice_bitcast_fusion.2
  9.8 0.7 pad_maximum_fusion.2.edges_ref
  10.5 16.2 %shard_map.93 = (bf16[12,128,128]{2,1,0:T(8,128)(2,1)}, bf16[2,12,8,128]{3,2,1,0:T(8,128)(2,1)}, bf16[2,12,8,128]{3,2,1,0:T(8,128)(2,1)}) custom-call(bf16[2,12,128,128]{3,2,1,0:T(8,128)(2,1)} %bitcast.254, bf16[2,2,12,8,128]{4,3,2,1,0:T(8,128)(2,1)} %pad_maximum_fusion.2.edges_ref), custom_call_target="tpu_custom_call" | custom-call | tf_op jit(solution)/shard_map/pallas_call | solution.py:128
  29.5 0.8 slice_bitcast_fusion.5
  30.6 0.7 fusion.5
  31.3 0.5 fusion.7
  31.8 0.7 fusion.13
  32.5 0.5 fusion.15
  33.0 0.7 fusion.21
  33.8 0.5 fusion.23
  34.3 0.7 add_convert_fusion
  34.9 1.6 %fusion.29 = (bf16[12,136,128]{2,1,0:T(8,128)(2,1)S(1)}, f32[12,136,128]{2,1,0:T(8,128)S(1)}, f32[12,136,128]{2,1,0:T(8,128)S(1)}, f32[12,136,128]{2,1,0:T(8,128)}) fusion(f32[12]{0:T(128)S(1)} %compare_convert_fusion, bf16[12,4,128]{2,1,0:T(4,128)(2,1)S(1)} %slice.836, bf16[12,128,128]{2,1,0:T(8,128)(2,1)S(1)} %get-tuple-element.58, ...), kind=kOutput, calls=%fused_computation.85 | convolution fusion | flops 57237504 | bytes 3793924 | tf_op jit(solution)/shard_map/dot_general | solution.py:216
  36.5 0.4 convolution_convert_fusion.3
  36.9 0.2 convert_reduce_fusion
  37.1 1.7 %fusion.35 = (bf16[12,134,128]{2,1,0:T(8,128)(2,1)S(1)}, f32[12,134,128]{2,1,0:T(8,128)S(1)}) fusion(f32[12,138,128]{2,1,0:T(8,128)S(1)} %get-tuple-element.125, f32[12]{0:T(128)S(1)} %compare_convert_fusion, f32[128]{0:T(128)S(1)} %get-tuple-element.77, f32[128]{0:T(128)S(1)} %get-tuple-element.78, f32[128]{0:T(128)S(1)} %get-tuple-element.79, ...), kind=kLoop, calls=%fused_computation.91 | loop fusion | flops 8438784 | bytes 4582400 | tf_op jit(solution)/shard_map/convert_element_type | solution.py:237
  38.8 0.4 convolution_convert_fusion.2
  39.2 0.2 convert_reduce_fusion.1
  39.4 1.5 %fusion.41 = (bf16[12,132,128]{2,1,0:T(8,128)(2,1)S(1)}, f32[12,132,128]{2,1,0:T(8,128)S(1)}) fusion(f32[12,140,128]{2,1,0:T(8,128)S(1)} %get-tuple-element.123, f32[12]{0:T(128)S(1)} %compare_convert_fusion, f32[128]{0:T(128)S(1)} %get-tuple-element.86, f32[128]{0:T(128)S(1)} %get-tuple-element.87, f32[128]{0:T(128)S(1)} %get-tuple-element.88, ...), kind=kLoop, calls=%fused_computation.97 | loop fusion | flops 8312832 | bytes 4563968 | tf_op jit(solution)/shard_map/convert_element_type | solution.py:237
  40.9 0.4 convolution_convert_fusion.1
  41.3 0.2 convert_reduce_fusion.2
  41.5 1.5 %fusion.47 = (bf16[12,130,128]{2,1,0:T(8,128)(2,1)S(1)}, f32[12,130,128]{2,1,0:T(8,128)S(1)}) fusion(f32[12,142,128]{2,1,0:T(8,128)S(1)} %get-tuple-element.121, f32[12]{0:T(128)S(1)} %compare_convert_fusion, f32[128]{0:T(128)S(1)} %get-tuple-element.95, f32[128]{0:T(128)S(1)} %get-tuple-element.96, f32[128]{0:T(128)S(1)} %get-tuple-element.97, ...), kind=kLoop, calls=%fused_computation.103 | loop fusion | flops 8186880 | bytes 4545536 | tf_op jit(solution)/shard_map/convert_element_type | solution.py:237
  43.1 0.4 convolution_convert_fusion
  43.5 0.2 convert_reduce_fusion.3
  43.7 0.3 fusion.100
  44.0 0.3 fusion.102
  44.4 0.3 fusion.104
  44.7 0.3 fusion.106
  45.1 0.9 fusion.72
  45.9 0.9 fusion.63
  46.8 0.7 fusion.54
  47.8 0.8 fusion.89
  48.7 0.3 maximum_maximum_fusion
  49.0 0.5 collective-permute-start.2
  49.5 1.0 collective-permute-done.2
  50.6 2.8 %collective-permute-start.4 = (f32[4,8832]{1,0:T(4,128)S(1)}, f32[4,8832]{1,0:T(4,128)S(1)}, u32[]{:S(2)}, u32[]{:S(2)}) collective-permute-start(f32[4,8832]{1,0:T(4,128)S(1)} %dynamic-slice_add_fusion), channel_id=1, source_target_pairs={{0,4},{2,6},{4,0},{6,2},{1,5},{3,7},{5,1},{7,3},{8,12},{10,14},{12... | collective-permute-start | bytes 423944 | tf_op jit(solution)/shard_map/ppermute | solution.py:152
  53.5 2.1 %collective-permute-done.5 = f32[4,8832]{1,0:T(4,128)S(1)} collective-permute-done((f32[4,8832]{1,0:T(4,128)S(1)}, f32[4,8832]{1,0:T(4,128)S(1)}, u32[]{:S(2)}, u32[]{:S(2)}) %collective-permute-start.5) | collective-permute-done | bytes 141344 | tf_op jit(solution)/shard_map/ppermute | solution.py:152
  55.5 1.6 %collective-permute-done.4 = f32[4,8832]{1,0:T(4,128)S(1)} collective-permute-done((f32[4,8832]{1,0:T(4,128)S(1)}, f32[4,8832]{1,0:T(4,128)S(1)}, u32[]{:S(2)}, u32[]{:S(2)}) %collective-permute-start.4) | collective-permute-done | bytes 141344 | tf_op jit(solution)/shard_map/ppermute | solution.py:152
  57.2 3.2 %collective-permute-done.3 = f32[4,8832]{1,0:T(4,128)S(1)} collective-permute-done((f32[4,8832]{1,0:T(4,128)S(1)}, f32[4,8832]{1,0:T(4,128)S(1)}, u32[]{:S(2)}, u32[]{:S(2)}) %collective-permute-start.3) | collective-permute-done | bytes 141344 | tf_op jit(solution)/shard_map/ppermute | solution.py:152
  60.5 0.3 collective-permute-start.6
  60.9 0.6 copy-done.1
  61.5 0.3 fusion.99
  61.7 1.3 %collective-permute-start = (bf16[12,128,128]{2,1,0:T(8,128)(2,1)S(1)}, bf16[12,128,128]{2,1,0:T(8,128)(2,1)S(1)}, u32[]{:S(2)}, u32[]{:S(2)}) collective-permute-start(bf16[12,128,128]{2,1,0:T(8,128)(2,1)S(1)} %fusion.99), channel_id=1, source_target_pairs={{0,1},{2,3},{4,5},{6,7},{8,9},{10,11},{12,13},{14,15},{16,17},{18,... | collective-permute-start | bytes 1179656 | tf_op jit(solution)/shard_map/ppermute | solution.py:272
  63.0 1.7 %collective-permute-done.6 = f32[4,8832]{1,0:T(4,128)S(1)} collective-permute-done((f32[4,8832]{1,0:T(4,128)S(1)}, f32[4,8832]{1,0:T(4,128)S(1)}, u32[]{:S(2)}, u32[]{:S(2)}) %collective-permute-start.6) | collective-permute-done | bytes 141344 | tf_op jit(solution)/shard_map/ppermute | solution.py:176
  64.9 0.8 collective-permute-start.7
  65.7 7.9 %collective-permute-done.7 = f32[4,8832]{1,0:T(4,128)S(1)} collective-permute-done((f32[4,8832]{1,0:T(4,128)S(1)}, f32[4,8832]{1,0:T(4,128)S(1)}, u32[]{:S(2)}, u32[]{:S(2)}) %collective-permute-start.7) | collective-permute-done | bytes 141344 | tf_op jit(solution)/shard_map/ppermute | solution.py:176
  73.6 3.5 %collective-permute-start.8 = (f32[4,8832]{1,0:T(4,128)S(1)}, f32[4,8832]{1,0:T(4,128)S(1)}, u32[]{:S(2)}, u32[]{:S(2)}) collective-permute-start(f32[4,8832]{1,0:T(4,128)S(1)} %add.636), channel_id=1, source_target_pairs={{0,32},{8,40},{16,48},{24,56},{32,0},{40,8},{48,16},{56,24},{1,33}... | collective-permute-start | bytes 423944 | tf_op jit(solution)/shard_map/ppermute | solution.py:176
  87.5 3.8 %collective-permute-start.11 = (f32[4,8832]{1,0:T(4,128)S(1)}, f32[4,8832]{1,0:T(4,128)S(1)}, u32[]{:S(2)}, u32[]{:S(2)}) collective-permute-start(f32[4,8832]{1,0:T(4,128)S(1)} %add.637), channel_id=1, source_target_pairs={{0,192},{64,0},{128,64},{192,128},{1,193},{65,1},{129,65},{193,129... | collective-permute-start | bytes 423944 | tf_op jit(solution)/shard_map/ppermute | solution.py:152
  91.3 0.7 collective-permute-start.9
  91.9 0.9 select_bitcast_fusion.1
  92.9 4.2 %collective-permute-start.1 = (bf16[12,128,128]{2,1,0:T(8,128)(2,1)S(1)}, bf16[12,128,128]{2,1,0:T(8,128)(2,1)S(1)}, u32[]{:S(2)}, u32[]{:S(2)}) collective-permute-start(bf16[12,128,128]{2,1,0:T(8,128)(2,1)S(1)} %get-tuple-element.49), channel_id=1, source_target_pairs={{1,0},{3,2},{5,4},{7,6},{9,8},{11,10},{13,12},{15,14},{17,16},{19,... | collective-permute-start | bytes 1179656 | tf_op jit(solution)/shard_map/ppermute | solution.py:273
  97.1 3.1 %collective-permute-done.9 = f32[4,8832]{1,0:T(4,128)S(1)} collective-permute-done((f32[4,8832]{1,0:T(4,128)S(1)}, f32[4,8832]{1,0:T(4,128)S(1)}, u32[]{:S(2)}, u32[]{:S(2)}) %collective-permute-start.9) | collective-permute-done | bytes 141344 | tf_op jit(solution)/shard_map/ppermute | solution.py:152
  100.5 1.5 %collective-permute-start.12 = (f32[4,8832]{1,0:T(4,128)S(1)}, f32[4,8832]{1,0:T(4,128)S(1)}, u32[]{:S(2)}, u32[]{:S(2)}) collective-permute-start(f32[4,8832]{1,0:T(4,128)S(1)} %add_bitcast_fusion), channel_id=1, source_target_pairs={{0,1},{1,0},{2,3},{3,2},{4,5},{5,4},{6,7},{7,6},{8,9},{9,8},{10,11... | collective-permute-start | bytes 423944 | tf_op jit(solution)/shard_map/ppermute | solution.py:178
  102.0 0.9 maximum_bitcast_fusion
  103.0 0.3 fusion.114
  103.3 0.5 fusion.117
  103.8 0.3 maximum_multiply_fusion
  104.1 0.6 slice.936
  104.8 0.6 slice.938
  105.3 0.7 copy.32
  (67 shorter events, 1.6 us)
Async XLA Ops:
  0.6 30.7 %copy-start = (bf16[4,128,128]{2,1,0:T(8,128)(2,1)S(1)}, bf16[4,128,128]{2,1,0:T(8,128)(2,1)}, u32[]{:S(2)}) copy-start(bf16[4,128,128]{2,1,0:T(8,128)(2,1)} %param.10) | copy-start | bytes 393220
  0.7 0.7 copy-start.5
  7.1 0.7 copy-start.7
  9.8 20.5 %copy-start.2 = (bf16[1,2,12,128,128]{4,3,2,1,0:T(8,128)(2,1)S(1)}, bf16[1,2,12,128,128]{4,3,2,1,0:T(8,128)(2,1)}, u32[]{:S(2)}) copy-start(bf16[1,2,12,128,128]{4,3,2,1,0:T(8,128)(2,1)} %param.6) | copy-start | bytes 2359300
  10.5 18.8 %copy-start.6 = (f32[4,128]{1,0:T(4,128)S(1)}, f32[4,128]{1,0:T(4,128)}, u32[]{:S(2)}) copy-start(f32[4,128]{1,0:T(4,128)} %param.11) | copy-start | bytes 6148
  10.5 18.9 %copy-start.4 = (f32[4,3,3,128]{3,0,2,1:T(4,128)S(1)}, f32[4,3,3,128]{3,0,2,1:T(4,128)}, u32[]{:S(2)}) copy-start(f32[4,3,3,128]{3,0,2,1:T(4,128)} %param.9) | copy-start | bytes 55300
  26.7 3.6 %copy-start.3 = (bf16[12,128,128]{2,1,0:T(8,128)(2,1)S(1)}, bf16[12,128,128]{2,1,0:T(8,128)(2,1)}, u32[]{:S(2)}) copy-start(bf16[12,128,128]{2,1,0:T(8,128)(2,1)} %get-tuple-element.8) | copy-start | bytes 1179652
  49.0 1.5 %collective-permute-start.2 = (f32[4,8832]{1,0:T(4,128)S(1)}, f32[4,8832]{1,0:T(4,128)S(1)}, u32[]{:S(2)}, u32[]{:S(2)}) collective-permute-start(f32[4,8832]{1,0:T(4,128)S(1)} %constant_dynamic-slice_fusion), channel_id=1, source_target_pairs={{0,1},{1,0},{2,3},{3,2},{4,5},{5,4},{6,7},{7,6},{8,9},{9,8},{10,11... | collective-permute-start | bytes 423944 | tf_op jit(solution)/shard_map/ppermute | solution.py:167
  50.5 5.0 %collective-permute-start.5 = (f32[4,8832]{1,0:T(4,128)S(1)}, f32[4,8832]{1,0:T(4,128)S(1)}, u32[]{:S(2)}, u32[]{:S(2)}) collective-permute-start(f32[4,8832]{1,0:T(4,128)S(1)} %dynamic-slice_add_fusion), channel_id=1, source_target_pairs={{0,6},{2,0},{4,2},{6,4},{1,7},{3,1},{5,3},{7,5},{8,14},{10,8},{12,... | collective-permute-start | bytes 423944 | tf_op jit(solution)/shard_map/ppermute | solution.py:152
  50.6 6.5 %collective-permute-start.4 = (f32[4,8832]{1,0:T(4,128)S(1)}, f32[4,8832]{1,0:T(4,128)S(1)}, u32[]{:S(2)}, u32[]{:S(2)}) collective-permute-start(f32[4,8832]{1,0:T(4,128)S(1)} %dynamic-slice_add_fusion), channel_id=1, source_target_pairs={{0,4},{2,6},{4,0},{6,2},{1,5},{3,7},{5,1},{7,3},{8,12},{10,14},{12... | collective-permute-start | bytes 423944 | tf_op jit(solution)/shard_map/ppermute | solution.py:152
  53.4 6.9 %collective-permute-start.3 = (f32[4,8832]{1,0:T(4,128)S(1)}, f32[4,8832]{1,0:T(4,128)S(1)}, u32[]{:S(2)}, u32[]{:S(2)}) collective-permute-start(f32[4,8832]{1,0:T(4,128)S(1)} %dynamic-slice_add_fusion), channel_id=1, source_target_pairs={{0,2},{2,4},{4,6},{6,0},{1,3},{3,5},{5,7},{7,1},{8,10},{10,12},{12... | collective-permute-start | bytes 423944 | tf_op jit(solution)/shard_map/ppermute | solution.py:152
  60.3 1.2 %copy-start.1 = (f32[12,136,128]{2,1,0:T(8,128)S(1)}, f32[12,136,128]{2,1,0:T(8,128)}, u32[]{:S(2)}) copy-start(f32[12,136,128]{2,1,0:T(8,128)} %get-tuple-element.126) | copy-start | bytes 2506756
  60.5 4.2 %collective-permute-start.6 = (f32[4,8832]{1,0:T(4,128)S(1)}, f32[4,8832]{1,0:T(4,128)S(1)}, u32[]{:S(2)}, u32[]{:S(2)}) collective-permute-start(f32[4,8832]{1,0:T(4,128)S(1)} %add_bitcast_fusion.1), channel_id=1, source_target_pairs={{0,8},{8,0},{16,24},{24,16},{32,40},{40,32},{48,56},{56,48},{1,9},... | collective-permute-start | bytes 423944 | tf_op jit(solution)/shard_map/ppermute | solution.py:176
  61.7 30.2 %collective-permute-start = (bf16[12,128,128]{2,1,0:T(8,128)(2,1)S(1)}, bf16[12,128,128]{2,1,0:T(8,128)(2,1)S(1)}, u32[]{:S(2)}, u32[]{:S(2)}) collective-permute-start(bf16[12,128,128]{2,1,0:T(8,128)(2,1)S(1)} %fusion.99), channel_id=1, source_target_pairs={{0,1},{2,3},{4,5},{6,7},{8,9},{10,11},{12,13},{14,15},{16,17},{18,... | collective-permute-start | bytes 1179656 | tf_op jit(solution)/shard_map/ppermute | solution.py:272
  64.9 8.7 %collective-permute-start.7 = (f32[4,8832]{1,0:T(4,128)S(1)}, f32[4,8832]{1,0:T(4,128)S(1)}, u32[]{:S(2)}, u32[]{:S(2)}) collective-permute-start(f32[4,8832]{1,0:T(4,128)S(1)} %fusion.165), channel_id=1, source_target_pairs={{0,16},{8,24},{16,0},{24,8},{32,48},{40,56},{48,32},{56,40},{1,17}... | collective-permute-start | bytes 423944 | tf_op jit(solution)/shard_map/ppermute | solution.py:176
  73.6 13.8 %collective-permute-start.8 = (f32[4,8832]{1,0:T(4,128)S(1)}, f32[4,8832]{1,0:T(4,128)S(1)}, u32[]{:S(2)}, u32[]{:S(2)}) collective-permute-start(f32[4,8832]{1,0:T(4,128)S(1)} %add.636), channel_id=1, source_target_pairs={{0,32},{8,40},{16,48},{24,56},{32,0},{40,8},{48,16},{56,24},{1,33}... | collective-permute-start | bytes 423944 | tf_op jit(solution)/shard_map/ppermute | solution.py:176
  87.5 9.6 %collective-permute-start.11 = (f32[4,8832]{1,0:T(4,128)S(1)}, f32[4,8832]{1,0:T(4,128)S(1)}, u32[]{:S(2)}, u32[]{:S(2)}) collective-permute-start(f32[4,8832]{1,0:T(4,128)S(1)} %add.637), channel_id=1, source_target_pairs={{0,192},{64,0},{128,64},{192,128},{1,193},{65,1},{129,65},{193,129... | collective-permute-start | bytes 423944 | tf_op jit(solution)/shard_map/ppermute | solution.py:152
  91.3 5.8 %collective-permute-start.10 = (f32[4,8832]{1,0:T(4,128)S(1)}, f32[4,8832]{1,0:T(4,128)S(1)}, u32[]{:S(2)}, u32[]{:S(2)}) collective-permute-start(f32[4,8832]{1,0:T(4,128)S(1)} %add.637), channel_id=1, source_target_pairs={{0,128},{64,192},{128,0},{192,64},{1,129},{65,193},{129,1},{193,65... | collective-permute-start | bytes 423944 | tf_op jit(solution)/shard_map/ppermute | solution.py:152
  91.3 9.0 %collective-permute-start.9 = (f32[4,8832]{1,0:T(4,128)S(1)}, f32[4,8832]{1,0:T(4,128)S(1)}, u32[]{:S(2)}, u32[]{:S(2)}) collective-permute-start(f32[4,8832]{1,0:T(4,128)S(1)} %add.637), channel_id=1, source_target_pairs={{0,64},{64,128},{128,192},{192,0},{1,65},{65,129},{129,193},{193,1... | collective-permute-start | bytes 423944 | tf_op jit(solution)/shard_map/ppermute | solution.py:152
  92.9 9.1 %collective-permute-start.1 = (bf16[12,128,128]{2,1,0:T(8,128)(2,1)S(1)}, bf16[12,128,128]{2,1,0:T(8,128)(2,1)S(1)}, u32[]{:S(2)}, u32[]{:S(2)}) collective-permute-start(bf16[12,128,128]{2,1,0:T(8,128)(2,1)S(1)} %get-tuple-element.49), channel_id=1, source_target_pairs={{1,0},{3,2},{5,4},{7,6},{9,8},{11,10},{13,12},{15,14},{17,16},{19,... | collective-permute-start | bytes 1179656 | tf_op jit(solution)/shard_map/ppermute | solution.py:273
  100.5 2.5 %collective-permute-start.12 = (f32[4,8832]{1,0:T(4,128)S(1)}, f32[4,8832]{1,0:T(4,128)S(1)}, u32[]{:S(2)}, u32[]{:S(2)}) collective-permute-start(f32[4,8832]{1,0:T(4,128)S(1)} %add_bitcast_fusion), channel_id=1, source_target_pairs={{0,1},{1,0},{2,3},{3,2},{4,5},{5,4},{6,7},{7,6},{8,9},{9,8},{10,11... | collective-permute-start | bytes 423944 | tf_op jit(solution)/shard_map/ppermute | solution.py:178

commit v8 on v4

--- a/solution.py
+++ b/solution.py
@@ -145,19 +145,40 @@
     )(held, edges)
 
 
+def xor_pairs(size, bit):
+    return [(i, i ^ bit) for i in range(size)]
+
+
 def all_reduce(flat, core):
     half = flat.shape[1] // 2
     swap = [(0, 1), (1, 0)]
     mine = lax.dynamic_slice_in_dim(flat, core * half, half, axis=1)
     other = lax.dynamic_slice_in_dim(flat, (1 - core) * half, half, axis=1)
-    acc = mine + lax.ppermute(other, "pipe", swap)
+    acc = (mine + lax.ppermute(other, "pipe", swap)).reshape(-1)
+    block = 128 * 8 * 8
+    padded = -(-acc.shape[0] // block) * block
+    acc = jnp.pad(acc, (0, padded - acc.shape[0])).reshape(padded // 128, 128)
+
+    halving, doubling = [], []
     for axis in ("y", "z", "x"):
-        size = lax.axis_size(axis)
         bit = 1
-        while bit < size:
-            pairs = [(i, i ^ bit) for i in range(size)]
-            acc = acc + lax.ppermute(acc, axis, pairs)
+        while bit < lax.axis_size(axis):
+            (halving if bit == 1 else doubling).append((axis, bit))
             bit *= 2
+    for axis, bit in halving:
+        side = lax.rem(lax.axis_index(axis) // bit, 2)
+        rows = acc.shape[0] // 2
+        kept = lax.dynamic_slice_in_dim(acc, side * rows, rows, axis=0)
+        sent = lax.dynamic_slice_in_dim(acc, (1 - side) * rows, rows, axis=0)
+        acc = kept + lax.ppermute(sent, axis, xor_pairs(lax.axis_size(axis), bit))
+    for axis, bit in doubling:
+        acc = acc + lax.ppermute(acc, axis, xor_pairs(lax.axis_size(axis), bit))
+    for axis, bit in reversed(halving):
+        side = lax.rem(lax.axis_index(axis) // bit, 2)
+        got = lax.ppermute(acc, axis, xor_pairs(lax.axis_size(axis), bit))
+        acc = jnp.concatenate([jnp.where(side == 0, acc, got), jnp.where(side == 0, got, acc)], axis=0)
+    acc = acc.reshape(-1)[: half * flat.shape[0]].reshape(flat.shape[0], half)
+
     theirs = lax.ppermute(acc, "pipe", swap)
     low = jnp.where(core == 0, acc, theirs)
     high = jnp.where(core == 0, theirs, acc)
@@ -261,9 +282,14 @@
     pieces = (jnp.stack(depth_terms), jnp.stack(point_terms), jnp.stack(bias_terms))
     flat = jnp.concatenate([piece.reshape(layers, -1) for piece in pieces], axis=1)
     flat = all_reduce(flat, core)
-    inverse = jnp.zeros((layers,), jnp.int32).at[layer_order].set(jnp.arange(layers, dtype=jnp.int32))
     factor = 1.0 / math.sqrt(held.shape[0] * height * breadth * blk_count())
-    flat = jnp.take(flat, inverse, axis=0) * factor
+    by_layer = []
+    for w in range(layers):
+        picked = jnp.zeros_like(flat[0])
+        for p in range(layers):
+            picked = picked + jnp.where(layer_order[p] == w, flat[p], 0.0)
+        by_layer.append(picked)
+    flat = jnp.stack(by_layer) * factor
     ordered, at = [], 0
     for piece in pieces:
         width = piece[0].size

time: 102 us -> 117 us (1.15)
  between operations: 8.88 us -> 19.2 us
  waiting for transfers between devices: 25.4 us -> 30.4 us
  other arithmetic: 16.6 us -> 19.6 us
  starting transfers between devices: 21.3 us -> 18.4 us
    ppermute x8 -> x11, waiting for transfers between devices: 25.4 us -> 30.4 us  [the longest x4 16.9 us: all_reduce(): acc = acc + lax.ppermute(acc, axis, xor_pairs(lax.axis_size(axis), bit))]
    ppermute x1, starting transfers between devices: 6.44 us -> 1.95 us  [shards(): got_grad = lax.ppermute(input_grad, 'pipe', [(1, 0)])]
    ppermute x1, starting transfers between devices: 6.32 us -> 10.8 us  [all_reduce(): theirs = lax.ppermute(acc, 'pipe', swap)]
    ppermute x8 -> x11, starting transfers between devices: 7.21 us -> 4.42 us  [the longest x4 1.77 us: all_reduce(): acc = acc + lax.ppermute(acc, axis, xor_pairs(lax.axis_size(axis), bit))]
    convert_element_type x1, other arithmetic: 0.27 us -> 1.71 us  [shards(): activation = ((activation[:, 1:-1].astype(jnp.float32) + gelu_pair(preact...]
  transfers between devices with their start and end apart: 11 -> 14, of which waited for: 8 -> 10; matrix products, arithmetic and copies ran while one was open for 3% -> 6% of each run, Pallas kernels for 0% -> 0%
where the time goes in v8:
time: 117 us; the launch traced here: 116 us
  waiting for transfers between devices  30.4 us (26%)
  other arithmetic  19.6 us (17%)
  between operations  19.2 us (16%)
  starting transfers between devices  18.4 us (16%)
  Pallas kernels  16.2 us (14%)
  local copies, waits for them, and re-layouts  6.49 us (6%)
  matrix products  5.93 us (5%)
    ppermute x4, waiting for transfers between devices, all_reduce(): acc = acc + lax.ppermute(acc, axis, xor_pairs(lax.axis_size(axis), bit))  16.9 us
    pallas_call x1, Pallas kernels, exchange(): pl.pallas_call(exchange_kernel, out_shape=(jax.ShapeDtypeStruct(grid_shap...  16.2 us
    ppermute x1, starting transfers between devices, all_reduce(): theirs = lax.ppermute(acc, 'pipe', swap)  10.8 us
    ppermute x3, waiting for transfers between devices, all_reduce(): acc = kept + lax.ppermute(sent, axis, xor_pairs(lax.axis_size(axis), bit))  8.1 us
    convert_element_type x3, other arithmetic, shards(): gated = (masked * gelu_pair(preact)[1]).astype(jnp.bfloat16)  4.75 us
    ppermute x3, waiting for transfers between devices, all_reduce(): got = lax.ppermute(acc, axis, xor_pairs(lax.axis_size(axis), bit))  4.47 us
    reduce_sum x4, other arithmetic, shards(): jnp.sum(back_in * padded[i:i + height, start:start + breadth].astype(jnp....  3.29 us
    dot_general x4, matrix products, shards(): jnp.dot(mixed.reshape(rows * span, channels), point, preferred_element_ty...  3.07 us
  transfers between devices with their start and end apart: 14, of which 10 were waited for; matrix products, arithmetic and copies ran while one was open for 6% of the time, Pallas kernels for 0%

profile of v8, /device:TPU:1, one launch (start us, length us, event | category | flops | bytes accessed | tf_op | source)
XLA Modules:
  0.0 116.2 jit_solution(11289846361211179811)
XLA Ops:
  0.7 0.7 copy-done.4
  1.3 0.6 fusion.156
  7.1 0.6 copy-done.6
  7.7 0.6 dynamic_slice.72
  8.3 0.6 compare_convert_fusion
  9.0 0.8 slice_bitcast_fusion.2
  9.8 0.7 pad_maximum_fusion.1.edges_ref
  10.5 16.2 %shard_map.93 = (bf16[12,128,128]{2,1,0:T(8,128)(2,1)}, bf16[2,12,8,128]{3,2,1,0:T(8,128)(2,1)}, bf16[2,12,8,128]{3,2,1,0:T(8,128)(2,1)}) custom-call(bf16[2,12,128,128]{3,2,1,0:T(8,128)(2,1)} %bitcast.240, bf16[2,2,12,8,128]{4,3,2,1,0:T(8,128)(2,1)} %pad_maximum_fusion.1.edges_ref), custom_call_target="tpu_custom_call" | custom-call | tf_op jit(solution)/shard_map/pallas_call | solution.py:128
  29.4 0.8 slice_bitcast_fusion.5
  30.5 0.7 fusion.5
  31.3 0.5 fusion.7
  31.8 0.7 fusion.13
  32.5 0.5 fusion.15
  33.0 0.7 fusion.21
  33.7 0.5 fusion.23
  34.2 0.7 add_convert_fusion
  34.9 1.6 %fusion.29 = (bf16[12,136,128]{2,1,0:T(8,128)(2,1)S(1)}, f32[12,136,128]{2,1,0:T(8,128)S(1)}, f32[12,136,128]{2,1,0:T(8,128)S(1)}, f32[12,136,128]{2,1,0:T(8,128)}) fusion(f32[12]{0:T(128)S(1)} %compare_convert_fusion, bf16[12,4,128]{2,1,0:T(4,128)(2,1)S(1)} %slice.841, bf16[12,128,128]{2,1,0:T(8,128)(2,1)S(1)} %get-tuple-element.58, ...), kind=kOutput, calls=%fused_computation.85 | convolution fusion | flops 57237504 | bytes 3793924 | tf_op jit(solution)/shard_map/dot_general | solution.py:220
  36.5 0.4 convolution_convert_fusion.3
  36.9 0.2 convert_reduce_fusion
  37.1 1.7 %fusion.35 = (bf16[12,134,128]{2,1,0:T(8,128)(2,1)S(1)}, f32[12,134,128]{2,1,0:T(8,128)S(1)}) fusion(f32[12,138,128]{2,1,0:T(8,128)S(1)} %get-tuple-element.131, f32[12]{0:T(128)S(1)} %compare_convert_fusion, f32[128]{0:T(128)S(1)} %get-tuple-element.83, f32[128]{0:T(128)S(1)} %get-tuple-element.84, f32[128]{0:T(128)S(1)} %get-tuple-element.85, ...), kind=kLoop, calls=%fused_computation.91 | loop fusion | flops 8438784 | bytes 4582400 | tf_op jit(solution)/shard_map/convert_element_type | solution.py:241
  38.8 0.4 convolution_convert_fusion.2
  39.2 0.2 convert_reduce_fusion.1
  39.4 1.5 %fusion.41 = (bf16[12,132,128]{2,1,0:T(8,128)(2,1)S(1)}, f32[12,132,128]{2,1,0:T(8,128)S(1)}) fusion(f32[12,140,128]{2,1,0:T(8,128)S(1)} %get-tuple-element.129, f32[12]{0:T(128)S(1)} %compare_convert_fusion, f32[128]{0:T(128)S(1)} %get-tuple-element.92, f32[128]{0:T(128)S(1)} %get-tuple-element.93, f32[128]{0:T(128)S(1)} %get-tuple-element.94, ...), kind=kLoop, calls=%fused_computation.97 | loop fusion | flops 8312832 | bytes 4563968 | tf_op jit(solution)/shard_map/convert_element_type | solution.py:241
  40.9 0.4 convolution_convert_fusion.1
  41.3 0.2 convert_reduce_fusion.2
  41.5 1.5 %fusion.47 = (bf16[12,130,128]{2,1,0:T(8,128)(2,1)S(1)}, f32[12,130,128]{2,1,0:T(8,128)S(1)}) fusion(f32[12,142,128]{2,1,0:T(8,128)S(1)} %get-tuple-element.127, f32[12]{0:T(128)S(1)} %compare_convert_fusion, f32[128]{0:T(128)S(1)} %get-tuple-element.101, f32[128]{0:T(128)S(1)} %get-tuple-element.102, f32[128]{0:T(128)S(1)} %get-tuple-element.103, ...), kind=kLoop, calls=%fused_computation.103 | loop fusion | flops 8186880 | bytes 4545536 | tf_op jit(solution)/shard_map/convert_element_type | solution.py:241
  43.0 0.4 convolution_convert_fusion
  43.6 0.3 fusion.100
  44.0 0.3 fusion.102
  44.3 0.3 fusion.104
  44.7 0.3 fusion.106
  45.0 0.9 fusion.72
  45.9 0.9 fusion.63
  46.8 0.7 fusion.54
  47.7 0.9 fusion.89
  48.6 0.3 maximum_maximum_fusion
  49.0 0.5 collective-permute-start.2
  49.4 1.0 collective-permute-done.2
  50.6 1.1 collective-permute-start.3
  51.7 2.7 %collective-permute-done.3 = f32[160,128]{1,0:T(8,128)S(1)} collective-permute-done((f32[160,128]{1,0:T(8,128)S(1)}, f32[160,128]{1,0:T(8,128)S(1)}, u32[]{:S(2)}, u32[]{:S(2)}) %collective-permute-start.3) | collective-permute-done | bytes 81952 | tf_op jit(solution)/shard_map/ppermute | solution.py:173
  54.5 2.8 %collective-permute-done.4 = f32[80,128]{1,0:T(8,128)S(1)} collective-permute-done((f32[80,128]{1,0:T(8,128)S(1)}, f32[80,128]{1,0:T(8,128)S(1)}, u32[]{:S(2)}, u32[]{:S(2)}) %collective-permute-start.4) | collective-permute-done | bytes 40992 | tf_op jit(solution)/shard_map/ppermute | solution.py:173
  57.5 2.6 %collective-permute-done.5 = f32[40,128]{1,0:T(8,128)S(1)} collective-permute-done((f32[40,128]{1,0:T(8,128)S(1)}, f32[40,128]{1,0:T(8,128)S(1)}, u32[]{:S(2)}, u32[]{:S(2)}) %collective-permute-start.5) | collective-permute-done | bytes 20512 | tf_op jit(solution)/shard_map/ppermute | solution.py:173
  60.1 4.1 %collective-permute-done.6 = f32[40,128]{1,0:T(8,128)S(1)} collective-permute-done((f32[40,128]{1,0:T(8,128)S(1)}, f32[40,128]{1,0:T(8,128)S(1)}, u32[]{:S(2)}, u32[]{:S(2)}) %collective-permute-start.6) | collective-permute-done | bytes 20512 | tf_op jit(solution)/shard_map/ppermute | solution.py:175
  64.2 3.8 %collective-permute-done.7 = f32[40,128]{1,0:T(8,128)S(1)} collective-permute-done((f32[40,128]{1,0:T(8,128)S(1)}, f32[40,128]{1,0:T(8,128)S(1)}, u32[]{:S(2)}, u32[]{:S(2)}) %collective-permute-start.7) | collective-permute-done | bytes 20512 | tf_op jit(solution)/shard_map/ppermute | solution.py:175
  68.0 1.2 %collective-permute-start.8 = (f32[40,128]{1,0:T(8,128)S(1)}, f32[40,128]{1,0:T(8,128)S(1)}, u32[]{:S(2)}, u32[]{:S(2)}) collective-permute-start(f32[40,128]{1,0:T(8,128)S(1)} %add.573), channel_id=1, source_target_pairs={{0,32},{8,40},{16,48},{24,56},{32,0},{40,8},{48,16},{56,24},{1,33}... | collective-permute-start | bytes 61448 | tf_op jit(solution)/shard_map/ppermute | solution.py:175
  69.3 5.3 %collective-permute-done.8 = f32[40,128]{1,0:T(8,128)S(1)} collective-permute-done((f32[40,128]{1,0:T(8,128)S(1)}, f32[40,128]{1,0:T(8,128)S(1)}, u32[]{:S(2)}, u32[]{:S(2)}) %collective-permute-start.8) | collective-permute-done | bytes 20512 | tf_op jit(solution)/shard_map/ppermute | solution.py:175
  74.6 0.5 collective-permute-start.9
  75.1 3.6 %collective-permute-done.9 = f32[40,128]{1,0:T(8,128)S(1)} collective-permute-done((f32[40,128]{1,0:T(8,128)S(1)}, f32[40,128]{1,0:T(8,128)S(1)}, u32[]{:S(2)}, u32[]{:S(2)}) %collective-permute-start.9) | collective-permute-done | bytes 20512 | tf_op jit(solution)/shard_map/ppermute | solution.py:175
  78.7 2.6 %collective-permute-done.10 = f32[40,128]{1,0:T(8,128)S(1)} collective-permute-done((f32[40,128]{1,0:T(8,128)S(1)}, f32[40,128]{1,0:T(8,128)S(1)}, u32[]{:S(2)}, u32[]{:S(2)}) %collective-permute-start.10) | collective-permute-done | bytes 20512 | tf_op jit(solution)/shard_map/ppermute | solution.py:178
  81.5 1.0 slice_convert_fusion
  82.5 1.8 %collective-permute-done.11 = f32[80,128]{1,0:T(8,128)S(1)} collective-permute-done((f32[80,128]{1,0:T(8,128)S(1)}, f32[80,128]{1,0:T(8,128)S(1)}, u32[]{:S(2)}, u32[]{:S(2)}) %collective-permute-start.11) | collective-permute-done | bytes 40992 | tf_op jit(solution)/shard_map/ppermute | solution.py:178
  84.4 0.8 collective-permute-start.12
  85.1 1.7 %fusion.99 = bf16[12,128,128]{2,1,0:T(8,128)(2,1)S(1)} fusion(f32[12,136,128]{2,1,0:T(8,128)} %slice_convert_fusion, f32[12,136,128]{2,1,0:T(8,128)S(1)} %get-tuple-element.57, f32[12,136,128]{2,1,0:T(8,128)} %get-tuple-element.132, f32[12]{0:T(128)S(1)} %compare_convert_fusion), kind=kLoop, calls=%fused_computation.165 | loop fusion | flops 786432 | bytes 2752560 | tf_op jit(solution)/shard_map/convert_element_type | solution.py:227
  86.9 1.3 %collective-permute-start = (bf16[12,128,128]{2,1,0:T(8,128)(2,1)S(1)}, bf16[12,128,128]{2,1,0:T(8,128)(2,1)S(1)}, u32[]{:S(2)}, u32[]{:S(2)}) collective-permute-start(bf16[12,128,128]{2,1,0:T(8,128)(2,1)S(1)} %fusion.99), channel_id=1, source_target_pairs={{0,1},{2,3},{4,5},{6,7},{8,9},{10,11},{12,13},{14,15},{16,17},{18,... | collective-permute-start | bytes 1179656 | tf_op jit(solution)/shard_map/ppermute | solution.py:276
  98.5 10.8 %collective-permute-start.13 = (f32[4,8832]{1,0:T(4,128)S(1)}, f32[4,8832]{1,0:T(4,128)S(1)}, u32[]{:S(2)}, u32[]{:S(2)}) collective-permute-start(f32[4,8832]{1,0:T(4,128)S(1)} %reshape.103), channel_id=1, source_target_pairs={{0,1},{1,0},{2,3},{3,2},{4,5},{5,4},{6,7},{7,6},{8,9},{9,8},{10,11... | collective-permute-start | bytes 423944 | tf_op jit(solution)/shard_map/ppermute | solution.py:182
  109.2 0.9 select_bitcast_fusion.1
  110.2 2.0 %collective-permute-start.1 = (bf16[12,128,128]{2,1,0:T(8,128)(2,1)S(1)}, bf16[12,128,128]{2,1,0:T(8,128)(2,1)S(1)}, u32[]{:S(2)}, u32[]{:S(2)}) collective-permute-start(bf16[12,128,128]{2,1,0:T(8,128)(2,1)S(1)} %get-tuple-element.49), channel_id=1, source_target_pairs={{1,0},{3,2},{5,4},{7,6},{9,8},{11,10},{13,12},{15,14},{17,16},{19,... | collective-permute-start | bytes 1179656 | tf_op jit(solution)/shard_map/ppermute | solution.py:277
  112.2 0.3 fusion.114
  112.5 0.5 fusion.117
  113.0 0.3 maximum_multiply_fusion
  113.3 0.6 slice.941
  113.9 0.6 slice.943
  114.5 0.7 copy.32
  115.3 0.9 maximum_bitcast_fusion
  (79 shorter events, 1.5 us)
Async XLA Ops:
  0.6 30.6 %copy-start = (bf16[4,128,128]{2,1,0:T(8,128)(2,1)S(1)}, bf16[4,128,128]{2,1,0:T(8,128)(2,1)}, u32[]{:S(2)}) copy-start(bf16[4,128,128]{2,1,0:T(8,128)(2,1)} %param.10) | copy-start | bytes 393220
  0.7 0.7 copy-start.4
  7.1 0.7 copy-start.6
  9.8 20.5 %copy-start.1 = (bf16[1,2,12,128,128]{4,3,2,1,0:T(8,128)(2,1)S(1)}, bf16[1,2,12,128,128]{4,3,2,1,0:T(8,128)(2,1)}, u32[]{:S(2)}) copy-start(bf16[1,2,12,128,128]{4,3,2,1,0:T(8,128)(2,1)} %param.6) | copy-start | bytes 2359300
  10.5 18.8 %copy-start.5 = (f32[4,128]{1,0:T(4,128)S(1)}, f32[4,128]{1,0:T(4,128)}, u32[]{:S(2)}) copy-start(f32[4,128]{1,0:T(4,128)} %param.11) | copy-start | bytes 6148
  10.5 18.9 %copy-start.3 = (f32[4,3,3,128]{3,0,2,1:T(4,128)S(1)}, f32[4,3,3,128]{3,0,2,1:T(4,128)}, u32[]{:S(2)}) copy-start(f32[4,3,3,128]{3,0,2,1:T(4,128)} %param.9) | copy-start | bytes 55300
  26.7 3.6 %copy-start.2 = (bf16[12,128,128]{2,1,0:T(8,128)(2,1)S(1)}, bf16[12,128,128]{2,1,0:T(8,128)(2,1)}, u32[]{:S(2)}) copy-start(bf16[12,128,128]{2,1,0:T(8,128)(2,1)} %get-tuple-element.8) | copy-start | bytes 1179652
  49.0 1.5 %collective-permute-start.2 = (f32[4,8832]{1,0:T(4,128)S(1)}, f32[4,8832]{1,0:T(4,128)S(1)}, u32[]{:S(2)}, u32[]{:S(2)}) collective-permute-start(f32[4,8832]{1,0:T(4,128)S(1)} %constant_dynamic-slice_fusion.3), channel_id=1, source_target_pairs={{0,1},{1,0},{2,3},{3,2},{4,5},{5,4},{6,7},{7,6},{8,9},{9,8},{10,11... | collective-permute-start | bytes 423944 | tf_op jit(solution)/shard_map/ppermute | solution.py:157
  50.6 3.8 %collective-permute-start.3 = (f32[160,128]{1,0:T(8,128)S(1)}, f32[160,128]{1,0:T(8,128)S(1)}, u32[]{:S(2)}, u32[]{:S(2)}) collective-permute-start(f32[160,128]{1,0:T(8,128)S(1)} %constant_dynamic-slice_fusion.2), channel_id=1, source_target_pairs={{0,2},{2,0},{4,6},{6,4},{1,3},{3,1},{5,7},{7,5},{8,10},{10,8},{12,... | collective-permute-start | bytes 245768 | tf_op jit(solution)/shard_map/ppermute | solution.py:173
  54.4 2.9 %collective-permute-start.4 = (f32[80,128]{1,0:T(8,128)S(1)}, f32[80,128]{1,0:T(8,128)S(1)}, u32[]{:S(2)}, u32[]{:S(2)}) collective-permute-start(f32[80,128]{1,0:T(8,128)S(1)} %constant_dynamic-slice_fusion.1), channel_id=1, source_target_pairs={{0,8},{8,0},{16,24},{24,16},{32,40},{40,32},{48,56},{56,48},{1,9},... | collective-permute-start | bytes 122888 | tf_op jit(solution)/shard_map/ppermute | solution.py:173
  57.3 2.7 %collective-permute-start.5 = (f32[40,128]{1,0:T(8,128)S(1)}, f32[40,128]{1,0:T(8,128)S(1)}, u32[]{:S(2)}, u32[]{:S(2)}) collective-permute-start(f32[40,128]{1,0:T(8,128)S(1)} %constant_dynamic-slice_fusion), channel_id=1, source_target_pairs={{0,64},{64,0},{128,192},{192,128},{1,65},{65,1},{129,193},{193,129... | collective-permute-start | bytes 61448 | tf_op jit(solution)/shard_map/ppermute | solution.py:173
  60.1 4.1 %collective-permute-start.6 = (f32[40,128]{1,0:T(8,128)S(1)}, f32[40,128]{1,0:T(8,128)S(1)}, u32[]{:S(2)}, u32[]{:S(2)}) collective-permute-start(f32[40,128]{1,0:T(8,128)S(1)} %dynamic-slice_add_fusion.3), channel_id=1, source_target_pairs={{0,4},{2,6},{4,0},{6,2},{1,5},{3,7},{5,1},{7,3},{8,12},{10,14},{12... | collective-permute-start | bytes 61448 | tf_op jit(solution)/shard_map/ppermute | solution.py:175
  64.2 3.8 %collective-permute-start.7 = (f32[40,128]{1,0:T(8,128)S(1)}, f32[40,128]{1,0:T(8,128)S(1)}, u32[]{:S(2)}, u32[]{:S(2)}) collective-permute-start(f32[40,128]{1,0:T(8,128)S(1)} %add.572), channel_id=1, source_target_pairs={{0,16},{8,24},{16,0},{24,8},{32,48},{40,56},{48,32},{56,40},{1,17}... | collective-permute-start | bytes 61448 | tf_op jit(solution)/shard_map/ppermute | solution.py:175
  68.0 6.5 %collective-permute-start.8 = (f32[40,128]{1,0:T(8,128)S(1)}, f32[40,128]{1,0:T(8,128)S(1)}, u32[]{:S(2)}, u32[]{:S(2)}) collective-permute-start(f32[40,128]{1,0:T(8,128)S(1)} %add.573), channel_id=1, source_target_pairs={{0,32},{8,40},{16,48},{24,56},{32,0},{40,8},{48,16},{56,24},{1,33}... | collective-permute-start | bytes 61448 | tf_op jit(solution)/shard_map/ppermute | solution.py:175
  74.6 4.1 %collective-permute-start.9 = (f32[40,128]{1,0:T(8,128)S(1)}, f32[40,128]{1,0:T(8,128)S(1)}, u32[]{:S(2)}, u32[]{:S(2)}) collective-permute-start(f32[40,128]{1,0:T(8,128)S(1)} %add.574), channel_id=1, source_target_pairs={{0,128},{64,192},{128,0},{192,64},{1,129},{65,193},{129,1},{193,65... | collective-permute-start | bytes 61448 | tf_op jit(solution)/shard_map/ppermute | solution.py:175
  78.7 2.6 %collective-permute-start.10 = (f32[40,128]{1,0:T(8,128)S(1)}, f32[40,128]{1,0:T(8,128)S(1)}, u32[]{:S(2)}, u32[]{:S(2)}) collective-permute-start(f32[40,128]{1,0:T(8,128)S(1)} %add.575), channel_id=1, source_target_pairs={{0,64},{64,0},{128,192},{192,128},{1,65},{65,1},{129,193},{193,129... | collective-permute-start | bytes 61448 | tf_op jit(solution)/shard_map/ppermute | solution.py:178
  81.4 2.9 %collective-permute-start.11 = (f32[80,128]{1,0:T(8,128)S(1)}, f32[80,128]{1,0:T(8,128)S(1)}, u32[]{:S(2)}, u32[]{:S(2)}) collective-permute-start(f32[80,128]{1,0:T(8,128)S(1)} %pad_maximum_fusion.4), channel_id=1, source_target_pairs={{0,8},{8,0},{16,24},{24,16},{32,40},{40,32},{48,56},{56,48},{1,9},... | collective-permute-start | bytes 122888 | tf_op jit(solution)/shard_map/ppermute | solution.py:178
  84.4 14.0 %collective-permute-start.12 = (f32[160,128]{1,0:T(8,128)S(1)}, f32[160,128]{1,0:T(8,128)S(1)}, u32[]{:S(2)}, u32[]{:S(2)}) collective-permute-start(f32[160,128]{1,0:T(8,128)S(1)} %pad_maximum_fusion.2), channel_id=1, source_target_pairs={{0,2},{2,0},{4,6},{6,4},{1,3},{3,1},{5,7},{7,5},{8,10},{10,8},{12,... | collective-permute-start | bytes 245768 | tf_op jit(solution)/shard_map/ppermute | solution.py:178
  86.9 22.4 %collective-permute-start = (bf16[12,128,128]{2,1,0:T(8,128)(2,1)S(1)}, bf16[12,128,128]{2,1,0:T(8,128)(2,1)S(1)}, u32[]{:S(2)}, u32[]{:S(2)}) collective-permute-start(bf16[12,128,128]{2,1,0:T(8,128)(2,1)S(1)} %fusion.99), channel_id=1, source_target_pairs={{0,1},{2,3},{4,5},{6,7},{8,9},{10,11},{12,13},{14,15},{16,17},{18,... | collective-permute-start | bytes 1179656 | tf_op jit(solution)/shard_map/ppermute | solution.py:276
  98.5 13.7 %collective-permute-start.13 = (f32[4,8832]{1,0:T(4,128)S(1)}, f32[4,8832]{1,0:T(4,128)S(1)}, u32[]{:S(2)}, u32[]{:S(2)}) collective-permute-start(f32[4,8832]{1,0:T(4,128)S(1)} %reshape.103), channel_id=1, source_target_pairs={{0,1},{1,0},{2,3},{3,2},{4,5},{5,4},{6,7},{7,6},{8,9},{9,8},{10,11... | collective-permute-start | bytes 423944 | tf_op jit(solution)/shard_map/ppermute | solution.py:182
  110.2 5.0 %collective-permute-start.1 = (bf16[12,128,128]{2,1,0:T(8,128)(2,1)S(1)}, bf16[12,128,128]{2,1,0:T(8,128)(2,1)S(1)}, u32[]{:S(2)}, u32[]{:S(2)}) collective-permute-start(bf16[12,128,128]{2,1,0:T(8,128)(2,1)S(1)} %get-tuple-element.49), channel_id=1, source_target_pairs={{1,0},{3,2},{5,4},{7,6},{9,8},{11,10},{13,12},{15,14},{17,16},{19,... | collective-permute-start | bytes 1179656 | tf_op jit(solution)/shard_map/ppermute | solution.py:277

commit v9 on v7

--- a/solution.py
+++ b/solution.py
@@ -145,40 +145,123 @@
     )(held, edges)
 
 
-def gather_sum(acc, axis):
-    size = lax.axis_size(axis)
-    index = lax.axis_index(axis)
-    shifted = [acc] + [
-        lax.ppermute(acc, axis, [(j, (j + k) % size) for j in range(size)])
-        for k in range(1, size)
-    ]
-    stacked = jnp.stack(shifted)
-    values = [select_row(stacked, lax.rem(index - j + size, size)) for j in range(size)]
+def group_members(axis):
+    here = [lax.axis_index(name) for name in BLK_AXES] + [lax.axis_index("pipe")]
+    slot = BLK_AXES.index(axis)
+    return [tuple(here[:slot]) + (j,) + tuple(here[slot + 1 :]) for j in range(lax.axis_size(axis))]
+
+
+def tree_sum(values):
     while len(values) > 1:
         values = [values[k] + values[k + 1] for k in range(0, len(values), 2)]
     return values[0]
 
 
-def all_reduce(flat, core):
-    half = flat.shape[1] // 2
-    swap = [(0, 1), (1, 0)]
-    mine = lax.dynamic_slice_in_dim(flat, core * half, half, axis=1)
-    other = lax.dynamic_slice_in_dim(flat, (1 - core) * half, half, axis=1)
-    acc = mine + lax.ppermute(other, "pipe", swap)
-    for axis in ("y", "z", "x"):
-        size = lax.axis_size(axis)
-        if size == 4:
-            acc = gather_sum(acc, axis)
-            continue
-        bit = 1
-        while bit < size:
-            pairs = [(i, i ^ bit) for i in range(size)]
-            acc = acc + lax.ppermute(acc, axis, pairs)
-            bit *= 2
-    theirs = lax.ppermute(acc, "pipe", swap)
-    low = jnp.where(core == 0, acc, theirs)
-    high = jnp.where(core == 0, theirs, acc)
-    return jnp.concatenate([low, high], axis=1)
+def reduce_kernel(flat_ref, out_ref, own, part, whole, got_pipe, got_y, got_z, got_x, got_back, got_end,
+                  send_sem, recv_pipe, recv_y, recv_z, recv_x, recv_back, recv_end):
+    core = lax.axis_index("pipe")
+    here = tuple(lax.axis_index(name) for name in BLK_AXES)
+    partner = here + (1 - core,)
+    my_y, my_z, my_x = (lax.axis_index(name) for name in ("y", "z", "x"))
+    groups = {axis: group_members(axis) for axis in ("y", "z", "x")}
+
+    barrier = pltpu.get_barrier_semaphore()
+    pl.semaphore_signal(barrier, inc=1, device_id=partner, device_id_type=MESH_ID)
+    count = 1
+    for axis, mine in (("y", my_y), ("z", my_z), ("x", my_x)):
+        for j, member in enumerate(groups[axis]):
+            @pl.when(j != mine)
+            def _():
+                pl.semaphore_signal(barrier, inc=1, device_id=member, device_id_type=MESH_ID)
+        count += len(groups[axis]) - 1
+    pl.semaphore_wait(barrier, count)
+
+    sends = iter(range(send_sem.shape[0]))
+
+    def one(src, dst, sem, target):
+        copy = pltpu.make_async_remote_copy(
+            src_ref=src, dst_ref=dst, send_sem=send_sem.at[next(sends)], recv_sem=sem,
+            device_id=target, device_id_type=MESH_ID,
+        )
+        copy.start()
+        copy.wait()
+
+    def spread(axis, mine, src_of, dst, sems):
+        copies = []
+        for j, member in enumerate(groups[axis]):
+            copy = pltpu.make_async_remote_copy(
+                src_ref=src_of(j), dst_ref=dst.at[mine], send_sem=send_sem.at[next(sends)],
+                recv_sem=sems.at[mine], device_id=member, device_id_type=MESH_ID,
+            )
+            copies.append((j, copy))
+
+            @pl.when(j != mine)
+            def _():
+                copy.start()
+        for j, copy in copies:
+            @pl.when(j != mine)
+            def _():
+                copy.wait_send()
+                pltpu.make_async_remote_copy(
+                    src_ref=src_of(j), dst_ref=dst.at[j], send_sem=send_sem.at[0],
+                    recv_sem=sems.at[j], device_id=groups[axis][j], device_id_type=MESH_ID,
+                ).wait_recv()
+
+    one(flat_ref.at[1 - core], got_pipe, recv_pipe.at[0], partner)
+    own[...] = flat_ref[core] + got_pipe[...]
+
+    ny = len(groups["y"])
+    got_y[my_y] = own[my_y]
+    spread("y", my_y, lambda j: own.at[j], got_y, recv_y)
+    part[...] = tree_sum([got_y[k] for k in range(ny)])
+
+    got_z[my_z] = part[...]
+    spread("z", my_z, lambda j: part, got_z, recv_z)
+    part[...] = tree_sum([got_z[k] for k in range(len(groups["z"]))])
+
+    got_x[my_x] = part[...]
+    spread("x", my_x, lambda j: part, got_x, recv_x)
+    part[...] = tree_sum([got_x[k] for k in range(len(groups["x"]))])
+
+    got_back[my_y] = part[...]
+    spread("y", my_y, lambda j: part, got_back, recv_back)
+
+    one(got_back, got_end, recv_end.at[0], partner)
+    out_ref[core] = got_back[...]
+    out_ref[1 - core] = got_end[...]
+
+
+def all_reduce(flat):
+    halves, ny, rows, lanes = flat.shape
+    nz, nx = lax.axis_size("z"), lax.axis_size("x")
+    chunk = (rows, lanes)
+    sends = 1 + ny + nz + nx + ny + 1
+    vmem = pl.BlockSpec(memory_space=pltpu.VMEM)
+    return pl.pallas_call(
+        reduce_kernel,
+        out_shape=jax.ShapeDtypeStruct(flat.shape, flat.dtype),
+        in_specs=[vmem],
+        out_specs=vmem,
+        scratch_shapes=[
+            pltpu.VMEM((ny,) + chunk, flat.dtype),
+            pltpu.VMEM(chunk, flat.dtype),
+            pltpu.VMEM((ny,) + chunk, flat.dtype),
+            pltpu.VMEM((ny,) + chunk, flat.dtype),
+            pltpu.VMEM((ny,) + chunk, flat.dtype),
+            pltpu.VMEM((nz,) + chunk, flat.dtype),
+            pltpu.VMEM((nx,) + chunk, flat.dtype),
+            pltpu.VMEM((ny,) + chunk, flat.dtype),
+            pltpu.VMEM((ny,) + chunk, flat.dtype),
+            pltpu.SemaphoreType.DMA((sends,)),
+            pltpu.SemaphoreType.DMA((1,)),
+            pltpu.SemaphoreType.DMA((ny,)),
+            pltpu.SemaphoreType.DMA((nz,)),
+            pltpu.SemaphoreType.DMA((nx,)),
+            pltpu.SemaphoreType.DMA((ny,)),
+            pltpu.SemaphoreType.DMA((1,)),
+        ],
+        compiler_params=pltpu.CompilerParams(collective_id=1, has_side_effects=True),
+    )(flat)
 
 
 def shards(endpoints, row_counts, layer_order, depth_weight, point_weight, point_bias):
@@ -277,7 +360,12 @@
 
     pieces = (jnp.stack(depth_terms), jnp.stack(point_terms), jnp.stack(bias_terms))
     flat = jnp.concatenate([piece.reshape(layers, -1) for piece in pieces], axis=1)
-    flat = all_reduce(flat, core)
+    ny = lax.axis_size("y")
+    size = flat.size
+    rows = -(-size // (2 * ny * 128))
+    rows = -(-rows // 8) * 8
+    packed = jnp.pad(flat.reshape(-1), (0, 2 * ny * rows * 128 - size)).reshape(2, ny, rows, 128)
+    flat = all_reduce(packed).reshape(-1)[:size].reshape(flat.shape)
     factor = 1.0 / math.sqrt(held.shape[0] * height * breadth * blk_count())
     by_layer = []
     for w in range(layers):

time: 107 us -> 98.7 us (0.922)
  Pallas kernels: 16.2 us -> 44.7 us
  waiting for transfers between devices: 20.6 us -> 0.01 us
  starting transfers between devices: 19.4 us -> 3.55 us
    pallas_call x0 -> x1, Pallas kernels: none -> 28.5 us  [all_reduce(): pl.pallas_call(reduce_kernel, out_shape=jax.ShapeDtypeStruct(flat.shape,...]
    ppermute x11 -> x0, waiting for transfers between devices: 20.6 us -> none  [the longest x6 9.96 us: gather_sum(): lax.ppermute(acc, axis, [(j, (j + k) % size) for j in range(size)])]
    ppermute x11 -> x0, starting transfers between devices: 13.9 us -> none  [the longest x6 7.31 us: gather_sum(): lax.ppermute(acc, axis, [(j, (j + k) % size) for j in range(size)])]
    ppermute x1, starting transfers between devices: 4.19 us -> 2.08 us  [shards(): got_grad = lax.ppermute(input_grad, 'pipe', [(1, 0)])]
    unnamed x20 -> x22, local copies, waits for them, and re-layouts: 2.7 us -> 2.84 us
  transfers between devices with their start and end apart: 13 -> 2, of which waited for: 7 -> 0; matrix products, arithmetic and copies ran while one was open for 3% -> 17% of each run, Pallas kernels for 0% -> 29%
where the time goes in v9:
time: 98.7 us; the launch traced here: 98.1 us
  Pallas kernels  44.7 us (45%)
  between operations  19 us (19%)
  other arithmetic  18.2 us (18%)
  local copies, waits for them, and re-layouts  7.34 us (7%)
  matrix products  5.23 us (5%)
  starting transfers between devices  3.55 us (4%)
    pallas_call x1, Pallas kernels, all_reduce(): pl.pallas_call(reduce_kernel, out_shape=jax.ShapeDtypeStruct(flat.shape,...  28.5 us
    pallas_call x1, Pallas kernels, exchange(): pl.pallas_call(exchange_kernel, out_shape=(jax.ShapeDtypeStruct(grid_shap...  16.2 us
    convert_element_type x3, other arithmetic, shards(): gated = (masked * gelu_pair(preact)[1]).astype(jnp.bfloat16)  4.57 us
    reduce_sum x4, other arithmetic, shards(): jnp.sum(back_in * padded[i:i + height, start:start + breadth].astype(jnp....  3.28 us
    unnamed x22, local copies, waits for them, and re-layouts  2.84 us
    convert_element_type x4, other arithmetic, shards(): mixed = conv_forward(pad_rows(activation), depth).astype(jnp.bfloat16)  2.83 us
    dot_general x4, matrix products, shards(): jnp.dot(mixed.reshape(rows * span, channels), point, preferred_element_ty...  2.36 us
    ppermute x1, starting transfers between devices, shards(): got_grad = lax.ppermute(input_grad, 'pipe', [(1, 0)])  2.08 us
  transfers between devices with their start and end apart: 2, of which 0 were waited for; matrix products, arithmetic and copies ran while one was open for 17% of the time, Pallas kernels for 29%

profile of v9, /device:TPU:1, one launch (start us, length us, event | category | flops | bytes accessed | tf_op | source)
XLA Modules:
  0.0 98.1 jit_solution(2407306297310589894)
XLA Ops:
  0.6 0.0 copy-start
  0.7 0.7 copy-done.6
  1.3 0.6 fusion.141
  7.0 0.0 copy-start.8
  7.1 0.6 copy-done.8
  7.7 0.6 dynamic_slice.48
  8.3 0.6 compare_convert_fusion
  8.9 0.0 copy-start.2
  8.9 0.9 slice_bitcast_fusion.2
  9.9 0.7 pad_maximum_fusion.edges_ref
  10.5 16.2 %shard_map.93 = (bf16[12,128,128]{2,1,0:T(8,128)(2,1)}, bf16[2,12,8,128]{3,2,1,0:T(8,128)(2,1)}, bf16[2,12,8,128]{3,2,1,0:T(8,128)(2,1)}) custom-call(bf16[2,12,128,128]{3,2,1,0:T(8,128)(2,1)} %bitcast.242, bf16[2,2,12,8,128]{4,3,2,1,0:T(8,128)(2,1)} %pad_maximum_fusion.edges_ref), custom_call_target="tpu_custom_call" | custom-call | tf_op jit(solution)/shard_map/pallas_call | solution.py:128
  28.0 0.0 copy-start.7
  29.4 0.7 copy-done.4
  30.1 0.0 copy-done.3
  30.2 1.1 %bitcast_select_fusion.1 = (bf16[12,128,128]{2,1,0:T(8,128)(2,1)S(1)}, bf16[12,128,128]{2,1,0:T(8,128)(2,1)S(1)}) fusion(bf16[12,128,128]{2,1,0:T(8,128)(2,1)} %get-tuple-element.8, pred[]{:T(512)S(6)} %eq.54, bf16[1,2,12,128,128]{4,3,2,1,0:T(8,128)(2,1)S(1)} %copy-done.2, s32[]{:T(128)S(6)} %select_n.148), kind=kLoop, calls=%fused_computation.191 | loop fusion | flops 393216 | bytes 1572869 | tf_op jit(solution)/shard_map/jit(_where)/select_n | solution.py:279
  31.2 0.2 multiply_convert_fusion
  31.4 0.7 fusion.5
  32.1 0.5 fusion.7
  32.6 0.7 fusion.13
  33.3 0.5 fusion.15
  33.8 0.7 fusion.21
  34.6 0.5 fusion.23
  35.1 0.1 slice_convert_fusion
  35.2 0.7 add_convert_fusion
  35.9 0.8 fusion.29
  36.8 0.3 fusion.99
  37.0 1.5 %collective-permute-start = (bf16[12,128,128]{2,1,0:T(8,128)(2,1)S(1)}, bf16[12,128,128]{2,1,0:T(8,128)(2,1)S(1)}, u32[]{:S(2)}, u32[]{:S(2)}) collective-permute-start(bf16[12,128,128]{2,1,0:T(8,128)(2,1)S(1)} %fusion.99), channel_id=1, source_target_pairs={{0,1},{2,3},{4,5},{6,7},{8,9},{10,11},{12,13},{14,15},{16,17},{18,... | collective-permute-start | bytes 1179656 | tf_op jit(solution)/shard_map/ppermute | solution.py:355
  38.5 0.4 convolution_convert_fusion.3
  38.9 0.2 convert_reduce_fusion
  39.1 1.5 %fusion.35 = (bf16[12,134,128]{2,1,0:T(8,128)(2,1)S(1)}, f32[12,134,128]{2,1,0:T(8,128)S(1)}) fusion(f32[12,138,128]{2,1,0:T(8,128)S(1)} %get-tuple-element.122, f32[12]{0:T(128)S(1)} %compare_convert_fusion, f32[128]{0:T(128)S(1)} %get-tuple-element.74, f32[128]{0:T(128)S(1)} %get-tuple-element.75, f32[128]{0:T(128)S(1)} %get-tuple-element.76, ...), kind=kLoop, calls=%fused_computation.91 | loop fusion | flops 8438784 | bytes 4582400 | tf_op jit(solution)/shard_map/convert_element_type | solution.py:320
  40.6 0.4 convolution_convert_fusion.2
  41.0 0.2 convert_reduce_fusion.1
  41.2 1.5 %fusion.41 = (bf16[12,132,128]{2,1,0:T(8,128)(2,1)S(1)}, f32[12,132,128]{2,1,0:T(8,128)S(1)}) fusion(f32[12,140,128]{2,1,0:T(8,128)S(1)} %get-tuple-element.120, f32[12]{0:T(128)S(1)} %compare_convert_fusion, f32[128]{0:T(128)S(1)} %get-tuple-element.83, f32[128]{0:T(128)S(1)} %get-tuple-element.84, f32[128]{0:T(128)S(1)} %get-tuple-element.85, ...), kind=kLoop, calls=%fused_computation.97 | loop fusion | flops 8312832 | bytes 4563968 | tf_op jit(solution)/shard_map/convert_element_type | solution.py:320
  42.8 0.4 convolution_convert_fusion.1
  43.2 0.2 convert_reduce_fusion.2
  43.4 1.5 %fusion.47 = (bf16[12,130,128]{2,1,0:T(8,128)(2,1)S(1)}, f32[12,130,128]{2,1,0:T(8,128)S(1)}) fusion(f32[12,142,128]{2,1,0:T(8,128)S(1)} %get-tuple-element.118, f32[12]{0:T(128)S(1)} %compare_convert_fusion, f32[128]{0:T(128)S(1)} %get-tuple-element.92, f32[128]{0:T(128)S(1)} %get-tuple-element.93, f32[128]{0:T(128)S(1)} %get-tuple-element.94, ...), kind=kLoop, calls=%fused_computation.103 | loop fusion | flops 8186880 | bytes 4545536 | tf_op jit(solution)/shard_map/convert_element_type | solution.py:320
  44.9 0.4 convolution_convert_fusion
  45.3 0.2 convert_reduce_fusion.3
  45.5 0.3 fusion.100
  45.9 0.3 fusion.102
  46.2 0.3 fusion.104
  46.6 0.3 fusion.106
  46.9 0.9 fusion.72
  47.8 0.9 fusion.63
  48.6 0.7 fusion.54
  59.8 0.8 fusion.89
  60.7 0.3 maximum_maximum_fusion
  61.0 0.1 reshape.107
  61.1 0.7 pad.48
  61.8 28.5 %shard_map.94 = f32[2,4,72,128]{3,2,1,0:T(8,128)} custom-call(f32[2,4,72,128]{3,2,1,0:T(8,128)} %bitcast.243), custom_call_target="tpu_custom_call" | custom-call | tf_op jit(solution)/shard_map/pallas_call | solution.py:240
  90.4 1.1 %select_add_fusion.1 = (f32[17664]{0:T(1024)S(1)}, f32[17664]{0:T(1024)S(1)}) fusion(f32[73728]{0:T(1024)} %bitcast.239, pred[]{:T(512)S(6)} %eq.66, pred[]{:T(512)S(6)} %eq.65, pred[]{:T(512)S(6)} %eq.64, pred[]{:T(512)S(6)} %eq.63, pred[]{:T(512)S(6)} %eq.70, pred[]{:T(512)S(6)} %eq.69, pred[]{:T(512)S(6)} %eq.68, pred[]{:T(512)S(6)} %eq.67), kind=kLoop, calls=%fused_computation.208 | loop fusion | flops 247296 | bytes 423944 | tf_op jit(solution)/shard_map/add | solution.py:374
  91.5 0.1 stack.358
  91.5 0.1 stack.357
  91.6 0.1 select_add_fusion.3
  91.7 0.1 stack.356
  91.7 0.1 stack.355
  91.8 1.0 select_bitcast_fusion.1
  92.8 2.1 %collective-permute-start.1 = (bf16[12,128,128]{2,1,0:T(8,128)(2,1)S(1)}, bf16[12,128,128]{2,1,0:T(8,128)(2,1)S(1)}, u32[]{:S(2)}, u32[]{:S(2)}) collective-permute-start(bf16[12,128,128]{2,1,0:T(8,128)(2,1)S(1)} %get-tuple-element.47), channel_id=1, source_target_pairs={{1,0},{3,2},{5,4},{7,6},{9,8},{11,10},{13,12},{15,14},{17,16},{19,... | collective-permute-start | bytes 1179656 | tf_op jit(solution)/shard_map/ppermute | solution.py:356
  94.8 0.3 maximum_multiply_fusion
  95.1 0.6 slice.943
  95.8 0.6 slice.945
  96.4 0.7 copy.32
  97.1 0.1 select_bitcast_fusion
  97.1 0.9 maximum_bitcast_fusion
  (44 shorter events, 0.4 us)
Async XLA Ops:
  0.6 31.5 %copy-start = (bf16[4,128,128]{2,1,0:T(8,128)(2,1)S(1)}, bf16[4,128,128]{2,1,0:T(8,128)(2,1)}, u32[]{:S(2)}) copy-start(bf16[4,128,128]{2,1,0:T(8,128)(2,1)} %param.10) | copy-start | bytes 393220
  0.7 0.7 copy-start.6
  7.0 0.7 copy-start.8
  8.9 21.2 %copy-start.2 = (bf16[1,2,12,128,128]{4,3,2,1,0:T(8,128)(2,1)S(1)}, bf16[1,2,12,128,128]{4,3,2,1,0:T(8,128)(2,1)}, u32[]{:S(2)}) copy-start(bf16[1,2,12,128,128]{4,3,2,1,0:T(8,128)(2,1)} %param.6) | copy-start | bytes 2359300
  10.5 18.8 %copy-start.5 = (f32[4,3,3,128]{3,0,2,1:T(4,128)S(1)}, f32[4,3,3,128]{3,0,2,1:T(4,128)}, u32[]{:S(2)}) copy-start(f32[4,3,3,128]{3,0,2,1:T(4,128)} %param.9) | copy-start | bytes 55300
  28.0 1.3 %copy-start.7 = (f32[4,128]{1,0:T(4,128)S(1)}, f32[4,128]{1,0:T(4,128)}, u32[]{:S(2)}) copy-start(f32[4,128]{1,0:T(4,128)} %param.11) | copy-start | bytes 6148
  29.3 0.8 copy-start.4
  29.3 0.8 copy-start.3
  37.0 54.8 %collective-permute-start = (bf16[12,128,128]{2,1,0:T(8,128)(2,1)S(1)}, bf16[12,128,128]{2,1,0:T(8,128)(2,1)S(1)}, u32[]{:S(2)}, u32[]{:S(2)}) collective-permute-start(bf16[12,128,128]{2,1,0:T(8,128)(2,1)S(1)} %fusion.99), channel_id=1, source_target_pairs={{0,1},{2,3},{4,5},{6,7},{8,9},{10,11},{12,13},{14,15},{16,17},{18,... | collective-permute-start | bytes 1179656 | tf_op jit(solution)/shard_map/ppermute | solution.py:355
  90.4 1.2 %copy-start.1 = (f32[2,4,72,128]{3,2,1,0:T(8,128)S(1)}, f32[2,4,72,128]{3,2,1,0:T(8,128)}, u32[]{:S(2)}) copy-start(f32[2,4,72,128]{3,2,1,0:T(8,128)} %shard_map.94) | copy-start | bytes 884740
  92.8 4.3 %collective-permute-start.1 = (bf16[12,128,128]{2,1,0:T(8,128)(2,1)S(1)}, bf16[12,128,128]{2,1,0:T(8,128)(2,1)S(1)}, u32[]{:S(2)}, u32[]{:S(2)}) collective-permute-start(bf16[12,128,128]{2,1,0:T(8,128)(2,1)S(1)} %get-tuple-element.47), channel_id=1, source_target_pairs={{1,0},{3,2},{5,4},{7,6},{9,8},{11,10},{13,12},{15,14},{17,16},{19,... | collective-permute-start | bytes 1179656 | tf_op jit(solution)/shard_map/ppermute | solution.py:356

commit v10 on v9

--- a/solution.py
+++ b/solution.py
@@ -367,13 +367,8 @@
     packed = jnp.pad(flat.reshape(-1), (0, 2 * ny * rows * 128 - size)).reshape(2, ny, rows, 128)
     flat = all_reduce(packed).reshape(-1)[:size].reshape(flat.shape)
     factor = 1.0 / math.sqrt(held.shape[0] * height * breadth * blk_count())
-    by_layer = []
-    for w in range(layers):
-        picked = jnp.zeros_like(flat[0])
-        for p in range(layers):
-            picked = picked + jnp.where(layer_order[p] == w, flat[p], 0.0)
-        by_layer.append(picked)
-    flat = jnp.stack(by_layer) * factor
+    chosen = layer_order[None, :] == jnp.arange(layers, dtype=layer_order.dtype)[:, None]
+    flat = jnp.sum(jnp.where(chosen[:, :, None], flat[None, :, :], 0.0), axis=1) * factor
     ordered, at = [], 0
     for piece in pieces:
         width = piece[0].size

time: 98.7 us -> 88.8 us (0.90)
  between operations: 19 us -> 8.75 us
  local copies, waits for them, and re-layouts: 7.34 us -> 8.37 us
    unnamed x22 -> x14, local copies, waits for them, and re-layouts: 2.84 us -> 0.78 us
    add x2 -> x0, other arithmetic: 1.15 us -> none  [shards(): picked = picked + jnp.where(layer_order[p] == w, flat[p], 0.0)]
  transfers between devices with their start and end apart: 2 -> 2, of which waited for: 0 -> 0; matrix products, arithmetic and copies ran while one was open for 17% -> 19% of each run, Pallas kernels for 29% -> 32%
where the time goes in v10:
time: 88.8 us; the launch traced here: 88.3 us
  Pallas kernels  44.7 us (50%)
  other arithmetic  17.7 us (20%)
  between operations  8.75 us (10%)
  local copies, waits for them, and re-layouts  8.37 us (9%)
  matrix products  5.24 us (6%)
  starting transfers between devices  3.55 us (4%)
    pallas_call x1, Pallas kernels, all_reduce(): pl.pallas_call(reduce_kernel, out_shape=jax.ShapeDtypeStruct(flat.shape,...  28.5 us
    pallas_call x1, Pallas kernels, exchange(): pl.pallas_call(exchange_kernel, out_shape=(jax.ShapeDtypeStruct(grid_shap...  16.2 us
    convert_element_type x3, other arithmetic, shards(): gated = (masked * gelu_pair(preact)[1]).astype(jnp.bfloat16)  4.57 us
    reduce_sum x4, other arithmetic, shards(): jnp.sum(back_in * padded[i:i + height, start:start + breadth].astype(jnp....  3.28 us
    convert_element_type x4, other arithmetic, shards(): mixed = conv_forward(pad_rows(activation), depth).astype(jnp.bfloat16)  2.83 us
    dot_general x4, matrix products, shards(): jnp.dot(mixed.reshape(rows * span, channels), point, preferred_element_ty...  2.36 us
    ppermute x1, starting transfers between devices, shards(): got_grad = lax.ppermute(input_grad, 'pipe', [(1, 0)])  2.08 us
  transfers between devices with their start and end apart: 2, of which 0 were waited for; matrix products, arithmetic and copies ran while one was open for 19% of the time, Pallas kernels for 32%

profile of v10, /device:TPU:1, one launch (start us, length us, event | category | flops | bytes accessed | tf_op | source)
XLA Modules:
  0.0 88.3 jit_solution(4457883935203140586)
XLA Ops:
  0.6 0.0 copy-start
  0.6 0.0 copy-start.1
  0.7 0.0 copy-start.4
  0.7 0.0 copy-start.2
  0.7 1.4 %fusion.141 = (s32[1]{0:T(128)}, s32[1]{0:T(128)}, s32[1]{0:T(128)}, s32[1]{0:T(128)}) fusion(s32[4]{0:T(128)} %param.8), kind=kLoop, calls=%fused_computation.308 | loop fusion | bytes 32 | tf_op jit(solution)/shard_map/slice | solution.py:287
  7.2 1.2 %dynamic_slice.48 = s32[1]{0:T(128)} dynamic-slice(s32[2]{0:T(128)} %param.7, s32[]{:T(128)S(6)} %select_n.54), dynamic_slice_sizes={1} | dynamic-slice | bytes 12 | tf_op jit(solution)/shard_map/jit(dynamic_index_in_dim)/dynamic_slice | solution.py:36
  8.4 0.6 compare_convert_fusion
  9.1 0.8 slice_bitcast_fusion.2
  9.9 0.7 pad_maximum_fusion.edges_ref
  10.6 16.2 %shard_map.93 = (bf16[12,128,128]{2,1,0:T(8,128)(2,1)}, bf16[2,12,8,128]{3,2,1,0:T(8,128)(2,1)}, bf16[2,12,8,128]{3,2,1,0:T(8,128)(2,1)}) custom-call(bf16[2,12,128,128]{3,2,1,0:T(8,128)(2,1)} %bitcast.240, bf16[2,2,12,8,128]{4,3,2,1,0:T(8,128)(2,1)} %pad_maximum_fusion.edges_ref), custom_call_target="tpu_custom_call" | custom-call | tf_op jit(solution)/shard_map/pallas_call | solution.py:128
  29.3 0.0 copy-done.4
  29.3 0.0 copy-done.2
  29.4 0.8 slice_bitcast_fusion.5
  30.2 0.0 copy-done.1
  30.2 1.1 %bitcast_select_fusion.1 = (bf16[12,128,128]{2,1,0:T(8,128)(2,1)S(1)}, bf16[12,128,128]{2,1,0:T(8,128)(2,1)S(1)}) fusion(bf16[12,128,128]{2,1,0:T(8,128)(2,1)} %get-tuple-element.8, pred[]{:T(512)S(6)} %eq.23, bf16[1,2,12,128,128]{4,3,2,1,0:T(8,128)(2,1)S(1)} %copy-done.1, s32[]{:T(128)S(6)} %select_n.54), kind=kLoop, calls=%fused_computation.192 | loop fusion | flops 393216 | bytes 1572869 | tf_op jit(solution)/shard_map/jit(_where)/select_n | solution.py:279
  31.3 0.2 multiply_convert_fusion
  31.5 0.7 fusion.5
  32.2 0.0 copy-done
  32.2 0.5 fusion.7
  32.7 0.7 fusion.13
  33.4 0.5 fusion.15
  33.9 0.7 fusion.21
  34.7 0.5 fusion.23
  35.2 0.1 slice_convert_fusion
  35.3 0.7 add_convert_fusion
  36.0 0.8 fusion.29
  36.9 0.3 fusion.99
  37.1 1.5 %collective-permute-start = (bf16[12,128,128]{2,1,0:T(8,128)(2,1)S(1)}, bf16[12,128,128]{2,1,0:T(8,128)(2,1)S(1)}, u32[]{:S(2)}, u32[]{:S(2)}) collective-permute-start(bf16[12,128,128]{2,1,0:T(8,128)(2,1)S(1)} %fusion.99), channel_id=1, source_target_pairs={{0,1},{2,3},{4,5},{6,7},{8,9},{10,11},{12,13},{14,15},{16,17},{18,... | collective-permute-start | bytes 1179656 | tf_op jit(solution)/shard_map/ppermute | solution.py:355
  38.6 0.4 convolution_convert_fusion.3
  39.0 0.2 convert_reduce_fusion
  39.2 1.5 %fusion.35 = (bf16[12,134,128]{2,1,0:T(8,128)(2,1)S(1)}, f32[12,134,128]{2,1,0:T(8,128)S(1)}) fusion(f32[12,138,128]{2,1,0:T(8,128)S(1)} %get-tuple-element.122, f32[12]{0:T(128)S(1)} %compare_convert_fusion, f32[128]{0:T(128)S(1)} %get-tuple-element.74, f32[128]{0:T(128)S(1)} %get-tuple-element.75, f32[128]{0:T(128)S(1)} %get-tuple-element.76, ...), kind=kLoop, calls=%fused_computation.92 | loop fusion | flops 8438784 | bytes 4582400 | tf_op jit(solution)/shard_map/convert_element_type | solution.py:320
  40.7 0.4 convolution_convert_fusion.2
  41.1 0.2 convert_reduce_fusion.1
  41.3 1.5 %fusion.41 = (bf16[12,132,128]{2,1,0:T(8,128)(2,1)S(1)}, f32[12,132,128]{2,1,0:T(8,128)S(1)}) fusion(f32[12,140,128]{2,1,0:T(8,128)S(1)} %get-tuple-element.120, f32[12]{0:T(128)S(1)} %compare_convert_fusion, f32[128]{0:T(128)S(1)} %get-tuple-element.83, f32[128]{0:T(128)S(1)} %get-tuple-element.84, f32[128]{0:T(128)S(1)} %get-tuple-element.85, ...), kind=kLoop, calls=%fused_computation.98 | loop fusion | flops 8312832 | bytes 4563968 | tf_op jit(solution)/shard_map/convert_element_type | solution.py:320
  42.9 0.4 convolution_convert_fusion.1
  43.2 0.2 convert_reduce_fusion.2
  43.5 1.5 %fusion.47 = (bf16[12,130,128]{2,1,0:T(8,128)(2,1)S(1)}, f32[12,130,128]{2,1,0:T(8,128)S(1)}) fusion(f32[12,142,128]{2,1,0:T(8,128)S(1)} %get-tuple-element.118, f32[12]{0:T(128)S(1)} %compare_convert_fusion, f32[128]{0:T(128)S(1)} %get-tuple-element.92, f32[128]{0:T(128)S(1)} %get-tuple-element.93, f32[128]{0:T(128)S(1)} %get-tuple-element.94, ...), kind=kLoop, calls=%fused_computation.104 | loop fusion | flops 8186880 | bytes 4545536 | tf_op jit(solution)/shard_map/convert_element_type | solution.py:320
  45.0 0.4 convolution_convert_fusion
  45.4 0.2 convert_reduce_fusion.3
  45.6 0.3 fusion.100
  45.9 0.3 fusion.102
  46.3 0.3 fusion.104
  46.6 0.3 fusion.106
  47.0 0.9 fusion.72
  47.9 0.9 fusion.63
  48.7 0.7 fusion.54
  49.7 0.8 fusion.89
  50.6 0.3 maximum_maximum_fusion
  50.9 0.1 reshape.117
  51.0 0.7 pad.48
  51.7 28.5 %shard_map.94 = f32[2,4,72,128]{3,2,1,0:T(8,128)} custom-call(f32[2,4,72,128]{3,2,1,0:T(8,128)} %bitcast.241), custom_call_target="tpu_custom_call" | custom-call | tf_op jit(solution)/shard_map/pallas_call | solution.py:240
  80.3 1.0 %slice.890 = f32[70656]{0:T(1024)S(1)} slice(f32[73728]{0:T(1024)} %bitcast.242), slice={[0:70656]} | slice | bytes 565248 | tf_op jit(solution)/shard_map/slice | solution.py:368
  81.3 0.1 broadcast_in_dim.35
  81.4 0.8 select_reduce_fusion
  82.2 0.0 collective-permute-done
  82.3 1.0 %select_bitcast_fusion.1 = (bf16[1,12,128,128]{3,2,1,0:T(8,128)(2,1)S(1)}, bf16[12,128,128]{2,1,0:T(8,128)(2,1)S(1)}) fusion(bf16[12,128,128]{2,1,0:T(8,128)(2,1)S(1)} %collective-permute-done, pred[]{:T(512)S(6)} %eq.23, f32[12]{0:T(128)S(1)} %compare_convert_fusion, f32[128]{0:T(128)S(1)} %get-tuple-element.101, f32[128]{0:T(128)S(1)} %get-tuple-element.102, ...), kind=kLoop, calls=%fused_computation.194 | loop fusion | flops 5898240 | bytes 3568641 | tf_op jit(solution)/shard_map/stack | solution.py:359
  83.2 2.1 %collective-permute-start.1 = (bf16[12,128,128]{2,1,0:T(8,128)(2,1)S(1)}, bf16[12,128,128]{2,1,0:T(8,128)(2,1)S(1)}, u32[]{:S(2)}, u32[]{:S(2)}) collective-permute-start(bf16[12,128,128]{2,1,0:T(8,128)(2,1)S(1)} %get-tuple-element.51), channel_id=1, source_target_pairs={{1,0},{3,2},{5,4},{7,6},{9,8},{11,10},{13,12},{15,14},{17,16},{19,... | collective-permute-start | bytes 1179656 | tf_op jit(solution)/shard_map/ppermute | solution.py:356
  85.3 0.1 broadcast_multiply_fusion
  85.4 0.6 slice.891
  86.0 0.6 slice.893
  86.6 0.7 copy.41
  87.3 0.0 collective-permute-done.1
  87.3 0.1 select_bitcast_fusion
  87.4 0.9 %maximum_bitcast_fusion = bf16[1,2,12,128,128]{4,3,2,1,0:T(8,128)(2,1)} fusion(bf16[1,12,128,128]{3,2,1,0:T(8,128)(2,1)S(1)} %select_bitcast_fusion, bf16[1,12,128,128]{3,2,1,0:T(8,128)(2,1)S(1)} %get-tuple-element.50), kind=kLoop, calls=%fused_computation.168 | loop fusion | flops 393216 | bytes 1572864 | tf_op jit(solution)/shard_map/broadcast_in_dim | solution.py:359
  (34 shorter events, 0.3 us)
Async XLA Ops:
  0.6 31.6 %copy-start = (bf16[4,128,128]{2,1,0:T(8,128)(2,1)S(1)}, bf16[4,128,128]{2,1,0:T(8,128)(2,1)}, u32[]{:S(2)}) copy-start(bf16[4,128,128]{2,1,0:T(8,128)(2,1)} %param.10) | copy-start | bytes 393220
  0.6 29.6 %copy-start.1 = (bf16[1,2,12,128,128]{4,3,2,1,0:T(8,128)(2,1)S(1)}, bf16[1,2,12,128,128]{4,3,2,1,0:T(8,128)(2,1)}, u32[]{:S(2)}) copy-start(bf16[1,2,12,128,128]{4,3,2,1,0:T(8,128)(2,1)} %param.6) | copy-start | bytes 2359300
  0.7 28.6 %copy-start.4 = (f32[4,128]{1,0:T(4,128)S(1)}, f32[4,128]{1,0:T(4,128)}, u32[]{:S(2)}) copy-start(f32[4,128]{1,0:T(4,128)} %param.11) | copy-start | bytes 6148
  0.7 28.7 %copy-start.2 = (f32[4,3,3,128]{3,0,2,1:T(4,128)S(1)}, f32[4,3,3,128]{3,0,2,1:T(4,128)}, u32[]{:S(2)}) copy-start(f32[4,3,3,128]{3,0,2,1:T(4,128)} %param.9) | copy-start | bytes 55300
  37.1 45.1 %collective-permute-start = (bf16[12,128,128]{2,1,0:T(8,128)(2,1)S(1)}, bf16[12,128,128]{2,1,0:T(8,128)(2,1)S(1)}, u32[]{:S(2)}, u32[]{:S(2)}) collective-permute-start(bf16[12,128,128]{2,1,0:T(8,128)(2,1)S(1)} %fusion.99), channel_id=1, source_target_pairs={{0,1},{2,3},{4,5},{6,7},{8,9},{10,11},{12,13},{14,15},{16,17},{18,... | collective-permute-start | bytes 1179656 | tf_op jit(solution)/shard_map/ppermute | solution.py:355
  51.7 29.7 %copy-start.3 = (s32[4]{0:T(128)S(1)}, s32[4]{0:T(128)}, u32[]{:S(2)}) copy-start(s32[4]{0:T(128)} %param.8) | copy-start | bytes 52
  83.2 4.1 %collective-permute-start.1 = (bf16[12,128,128]{2,1,0:T(8,128)(2,1)S(1)}, bf16[12,128,128]{2,1,0:T(8,128)(2,1)S(1)}, u32[]{:S(2)}, u32[]{:S(2)}) collective-permute-start(bf16[12,128,128]{2,1,0:T(8,128)(2,1)S(1)} %get-tuple-element.51), channel_id=1, source_target_pairs={{1,0},{3,2},{5,4},{7,6},{9,8},{11,10},{13,12},{15,14},{17,16},{19,... | collective-permute-start | bytes 1179656 | tf_op jit(solution)/shard_map/ppermute | solution.py:356

commit v11 on v10

--- a/solution.py
+++ b/solution.py
@@ -280,14 +280,17 @@
     x_wide = jnp.concatenate([lo[0], x_in, hi[0]], axis=1)
     g_wide = jnp.concatenate([lo[1][:, X_HALO - G_HALO :], g_in, hi[1][:, :G_HALO]], axis=1)
 
-    live = (jnp.arange(height)[:, None, None] < select_row(row_counts, core)).astype(jnp.float32)
-
-    weights = []
-    for p in range(layers):
-        w = layer_order[p]
-        weights.append(
-            (select_row(depth_weight, w), select_row(point_weight, w), select_row(point_bias, w))
-        )
+    counts = jnp.where(core == 0, row_counts[0:1], row_counts[1:2])
+    live = (jnp.arange(height)[:, None, None] < counts[None, None, :]).astype(jnp.float32)
+
+    placed = layer_order[:, None] == jnp.arange(layers, dtype=layer_order.dtype)[None, :]
+
+    def pick(table):
+        mask = placed.reshape(placed.shape + (1,) * (table.ndim - 1))
+        return jnp.sum(jnp.where(mask, table[None], jnp.zeros((), table.dtype)), axis=1, dtype=table.dtype)
+
+    by_position = [pick(table) for table in (depth_weight, point_weight, point_bias)]
+    weights = [tuple(table[p] for table in by_position) for p in range(layers)]
 
     activation = (x_wide.astype(jnp.float32) * live).astype(jnp.bfloat16)
     acts, mixes, preacts = [], [], []

time: 88.8 us -> 83.6 us (0.941)
  between operations: 8.75 us -> 2.33 us
  other arithmetic: 17.7 us -> 20.6 us
  local copies, waits for them, and re-layouts: 8.37 us -> 7.02 us
    reduce_sum x0 -> x3, other arithmetic: none -> 2.67 us  [pick(): jnp.sum(jnp.where(mask, table[None], jnp.zeros((), table.dtype)), axis=1,...]
    dynamic_slice x2 -> x0, local copies, waits for them, and re-layouts: 1.27 us -> none  [select_row(): return lax.dynamic_index_in_dim(table, chosen, 0, keepdims=False)]
  transfers between devices with their start and end apart: 2 -> 2, of which waited for: 0 -> 0; matrix products, arithmetic and copies ran while one was open for 19% -> 20% of each run, Pallas kernels for 32% -> 34%
where the time goes in v11:
time: 83.6 us; the launch traced here: 83.2 us
  Pallas kernels  44.7 us (53%)
  other arithmetic  20.6 us (25%)
  local copies, waits for them, and re-layouts  7.02 us (8%)
  matrix products  5 us (6%)
  starting transfers between devices  3.55 us (4%)
  between operations  2.33 us (3%)
    pallas_call x1, Pallas kernels, all_reduce(): pl.pallas_call(reduce_kernel, out_shape=jax.ShapeDtypeStruct(flat.shape,...  28.5 us
    pallas_call x1, Pallas kernels, exchange(): pl.pallas_call(exchange_kernel, out_shape=(jax.ShapeDtypeStruct(grid_shap...  16.2 us
    convert_element_type x3, other arithmetic, shards(): gated = (masked * gelu_pair(preact)[1]).astype(jnp.bfloat16)  4.58 us
    reduce_sum x4, other arithmetic, shards(): jnp.sum(back_in * padded[i:i + height, start:start + breadth].astype(jnp....  3.3 us
    convert_element_type x4, other arithmetic, shards(): mixed = conv_forward(pad_rows(activation), depth).astype(jnp.bfloat16)  2.83 us
    reduce_sum x3, other arithmetic, pick(): jnp.sum(jnp.where(mask, table[None], jnp.zeros((), table.dtype)), axis=1,...  2.67 us
    dot_general x4, matrix products, shards(): jnp.dot(mixed.reshape(rows * span, channels), point, preferred_element_ty...  2.15 us
    ppermute x1, starting transfers between devices, shards(): got_grad = lax.ppermute(input_grad, 'pipe', [(1, 0)])  2.08 us
  transfers between devices with their start and end apart: 2, of which 0 were waited for; matrix products, arithmetic and copies ran while one was open for 20% of the time, Pallas kernels for 34%

profile of v11, /device:TPU:1, one launch (start us, length us, event | category | flops | bytes accessed | tf_op | source)
XLA Modules:
  0.0 83.2 jit_solution(5216476346473047518)
XLA Ops:
  0.6 1.3 %fusion.113 = (s32[1]{0:T(128)}, s32[1]{0:T(128)}) fusion(s32[2]{0:T(128)} %param.7), kind=kLoop, calls=%fused_computation.284 | loop fusion | bytes 16 | tf_op jit(solution)/shard_map/slice | solution.py:283
  3.3 0.8 iota_compare_fusion
  4.1 0.8 select_reduce_fusion.3
  4.8 0.9 %select_reduce_fusion.2 = f32[4,3,3,128]{3,2,1,0:T(4,128)S(1)} fusion(f32[4,3,3,128]{3,0,2,1:T(4,128)} %param.9, pred[4,4]{1,0:T(4,128)(4,1)S(1)} %get-tuple-element.114), kind=kLoop, calls=%fused_computation.209 | loop fusion | flops 32256 | bytes 36880 | tf_op jit(solution)/shard_map/reduce_sum | solution.py:290
  5.7 0.0 copy-start
  5.7 0.9 %slice_bitcast_fusion.2 = (bf16[1,2,12,8,128]{4,3,2,1,0:T(8,128)(2,1)S(1)}, bf16[1,2,12,8,128]{4,3,2,1,0:T(8,128)(2,1)S(1)}) fusion(bf16[2,12,128,128]{3,2,1,0:T(8,128)(2,1)} %bitcast.232), kind=kLoop, calls=%fused_computation.211 | loop fusion | bytes 196608 | tf_op jit(solution)/shard_map/stack | solution.py:275
  6.6 1.0 %select_reduce_fusion.1 = bf16[4,128,128]{2,1,0:T(8,128)(2,1)S(1)} fusion(pred[4,4]{1,0:T(4,128)(4,1)S(1)} %get-tuple-element.114, bf16[4,128,128]{2,1,0:T(8,128)(2,1)} %param.10), kind=kLoop, calls=%fused_computation.173 | loop fusion | flops 458752 | bytes 262160 | tf_op jit(solution)/shard_map/reduce_sum | solution.py:290
  7.7 0.7 pad_maximum_fusion.edges_ref
  8.3 16.2 %shard_map.93 = (bf16[12,128,128]{2,1,0:T(8,128)(2,1)}, bf16[2,12,8,128]{3,2,1,0:T(8,128)(2,1)}, bf16[2,12,8,128]{3,2,1,0:T(8,128)(2,1)}) custom-call(bf16[2,12,128,128]{3,2,1,0:T(8,128)(2,1)} %bitcast.233, bf16[2,2,12,8,128]{4,3,2,1,0:T(8,128)(2,1)} %pad_maximum_fusion.edges_ref), custom_call_target="tpu_custom_call" | custom-call | tf_op jit(solution)/shard_map/pallas_call | solution.py:128
  24.5 0.8 slice_bitcast_fusion.17
  25.4 0.0 copy-done
  25.4 1.1 %bitcast_select_fusion.1 = (bf16[12,128,128]{2,1,0:T(8,128)(2,1)S(1)}, bf16[12,128,128]{2,1,0:T(8,128)(2,1)S(1)}) fusion(bf16[12,128,128]{2,1,0:T(8,128)(2,1)} %get-tuple-element.8, pred[]{:T(512)} %eq.49, bf16[1,2,12,128,128]{4,3,2,1,0:T(8,128)(2,1)S(1)} %copy-done, s32[]{:T(128)S(6)} %select_n.49), kind=kLoop, calls=%fused_computation.193 | loop fusion | flops 393216 | bytes 1572869 | tf_op jit(solution)/shard_map/jit(_where)/select_n | solution.py:279
  26.5 0.2 multiply_convert_fusion
  26.6 0.7 fusion.5
  27.3 0.5 fusion.7
  27.8 0.7 fusion.13
  28.6 0.5 fusion.15
  29.1 0.7 fusion.21
  29.8 0.5 fusion.23
  30.3 0.1 slice_convert_fusion
  30.4 0.7 add_convert_fusion
  31.1 0.7 fusion.29
  31.7 0.3 fusion.99
  32.0 1.5 %collective-permute-start = (bf16[12,128,128]{2,1,0:T(8,128)(2,1)S(1)}, bf16[12,128,128]{2,1,0:T(8,128)(2,1)S(1)}, u32[]{:S(2)}, u32[]{:S(2)}) collective-permute-start(bf16[12,128,128]{2,1,0:T(8,128)(2,1)S(1)} %fusion.99), channel_id=1, source_target_pairs={{0,1},{2,3},{4,5},{6,7},{8,9},{10,11},{12,13},{14,15},{16,17},{18,... | collective-permute-start | bytes 1179656 | tf_op jit(solution)/shard_map/ppermute | solution.py:358
  33.5 0.3 fusion.100
  33.9 0.2 convert_reduce_fusion
  34.1 0.4 convolution_convert_fusion.3
  34.4 0.9 %fusion.72 = (f32[128]{0:T(128)S(1)}, f32[128]{0:T(128)S(1)}, f32[128]{0:T(128)S(1)}, f32[128]{0:T(128)S(1)}, f32[128]{0:T(128)S(1)}, /*index=5*/f32[128]{0:T(12...) fusion(bf16[12,138,128]{2,1,0:T(8,128)(2,1)S(1)} %get-tuple-element.121, ...), kind=kLoop, calls=%fused_computation.138 | loop fusion | flops 5503872 | bytes 2019840 | tf_op jit(solution)/shard_map/reduce_sum | solution.py:346
  35.3 1.5 %fusion.35 = (bf16[12,134,128]{2,1,0:T(8,128)(2,1)S(1)}, f32[12,134,128]{2,1,0:T(8,128)S(1)}) fusion(f32[12,138,128]{2,1,0:T(8,128)S(1)} %get-tuple-element.122, f32[12]{0:T(128)S(1)} %compare_convert_fusion, f32[128]{0:T(128)S(1)} %get-tuple-element.142, f32[128]{0:T(128)S(1)} %get-tuple-element.141, f32[128]{0:T(128)S(1)} %get-tuple-element.140, ...), kind=kLoop, calls=%fused_computation.92 | loop fusion | flops 8438784 | bytes 4582400 | tf_op jit(solution)/shard_map/convert_element_type | solution.py:323
  36.8 0.3 fusion.102
  37.2 0.2 convert_reduce_fusion.1
  37.4 0.4 convolution_convert_fusion.2
  37.8 0.9 %fusion.63 = (f32[128]{0:T(128)S(1)}, f32[128]{0:T(128)S(1)}, f32[128]{0:T(128)S(1)}, f32[128]{0:T(128)S(1)}, f32[128]{0:T(128)S(1)}, /*index=5*/f32[128]{0:T(12...) fusion(bf16[12,140,128]{2,1,0:T(8,128)(2,1)S(1)} %get-tuple-element.119, ...), kind=kLoop, calls=%fused_computation.129 | loop fusion | flops 5503872 | bytes 2019840 | tf_op jit(solution)/shard_map/reduce_sum | solution.py:346
  38.6 1.5 %fusion.41 = (bf16[12,132,128]{2,1,0:T(8,128)(2,1)S(1)}, f32[12,132,128]{2,1,0:T(8,128)S(1)}) fusion(f32[12,140,128]{2,1,0:T(8,128)S(1)} %get-tuple-element.120, f32[12]{0:T(128)S(1)} %compare_convert_fusion, f32[128]{0:T(128)S(1)} %get-tuple-element.83, f32[128]{0:T(128)S(1)} %get-tuple-element.84, f32[128]{0:T(128)S(1)} %get-tuple-element.85, ...), kind=kLoop, calls=%fused_computation.98 | loop fusion | flops 8312832 | bytes 4563968 | tf_op jit(solution)/shard_map/convert_element_type | solution.py:323
  40.2 0.3 fusion.104
  40.5 0.2 convert_reduce_fusion.2
  40.8 0.4 convolution_convert_fusion.1
  41.1 0.7 fusion.54
  41.9 1.5 %fusion.47 = (bf16[12,130,128]{2,1,0:T(8,128)(2,1)S(1)}, f32[12,130,128]{2,1,0:T(8,128)S(1)}) fusion(f32[12,142,128]{2,1,0:T(8,128)S(1)} %get-tuple-element.118, f32[12]{0:T(128)S(1)} %compare_convert_fusion, f32[128]{0:T(128)S(1)} %get-tuple-element.133, f32[128]{0:T(128)S(1)} %get-tuple-element.132, f32[128]{0:T(128)S(1)} %get-tuple-element.131, ...), kind=kLoop, calls=%fused_computation.104 | loop fusion | flops 8186880 | bytes 4545536 | tf_op jit(solution)/shard_map/convert_element_type | solution.py:323
  43.4 0.3 fusion.106
  43.7 0.2 convert_reduce_fusion.3
  44.0 0.4 convolution_convert_fusion
  44.3 0.9 %fusion.89 = (f32[128]{0:T(128)S(1)}, f32[128]{0:T(128)S(1)}, f32[128]{0:T(128)S(1)}, f32[128]{0:T(128)S(1)}, f32[128]{0:T(128)S(1)}, /*index=5*/f32[128]{0:T(12...) fusion(bf16[12,144,128]{2,1,0:T(8,128)(2,1)S(1)} %multiply_convert_fusion, ...), kind=kLoop, calls=%fused_computation.155 | loop fusion | flops 5503872 | bytes 2019840 | tf_op jit(solution)/shard_map/reduce_sum | solution.py:346
  45.5 0.3 maximum_maximum_fusion
  45.8 0.1 reshape.182
  45.9 0.7 pad.48
  46.6 28.5 %shard_map.94 = f32[2,4,72,128]{3,2,1,0:T(8,128)} custom-call(f32[2,4,72,128]{3,2,1,0:T(8,128)} %bitcast.234), custom_call_target="tpu_custom_call" | custom-call | tf_op jit(solution)/shard_map/pallas_call | solution.py:240
  75.2 1.0 %slice.938 = f32[70656]{0:T(1024)S(1)} slice(f32[73728]{0:T(1024)} %bitcast.235), slice={[0:70656]} | slice | bytes 565248 | tf_op jit(solution)/shard_map/slice | solution.py:371
  76.2 0.1 broadcast_in_dim.106
  76.3 0.8 select_reduce_fusion
  77.1 0.0 collective-permute-done
  77.1 0.9 %select_bitcast_fusion.1 = (bf16[1,12,128,128]{3,2,1,0:T(8,128)(2,1)S(1)}, bf16[12,128,128]{2,1,0:T(8,128)(2,1)S(1)}) fusion(bf16[12,128,128]{2,1,0:T(8,128)(2,1)S(1)} %collective-permute-done, pred[]{:T(512)} %eq.49, f32[12]{0:T(128)S(1)} %compare_convert_fusion, f32[128]{0:T(128)S(1)} %get-tuple-element.101, f32[128]{0:T(128)S(1)} %get-tuple-element.102, ...), kind=kLoop, calls=%fused_computation.195 | loop fusion | flops 5898240 | bytes 3568641 | tf_op jit(solution)/shard_map/stack | solution.py:362
  78.1 2.1 %collective-permute-start.1 = (bf16[12,128,128]{2,1,0:T(8,128)(2,1)S(1)}, bf16[12,128,128]{2,1,0:T(8,128)(2,1)S(1)}, u32[]{:S(2)}, u32[]{:S(2)}) collective-permute-start(bf16[12,128,128]{2,1,0:T(8,128)(2,1)S(1)} %get-tuple-element.51), channel_id=1, source_target_pairs={{1,0},{3,2},{5,4},{7,6},{9,8},{11,10},{13,12},{15,14},{17,16},{19,... | collective-permute-start | bytes 1179656 | tf_op jit(solution)/shard_map/ppermute | solution.py:359
  80.2 0.1 broadcast_multiply_fusion
  80.2 0.6 slice.941
  80.8 0.6 slice.939
  81.5 0.7 copy.30
  82.2 0.0 collective-permute-done.1
  82.2 0.9 %maximum_bitcast_fusion = bf16[1,2,12,128,128]{4,3,2,1,0:T(8,128)(2,1)} fusion(bf16[1,12,128,128]{3,2,1,0:T(8,128)(2,1)S(1)} %select_bitcast_fusion, bf16[1,12,128,128]{3,2,1,0:T(8,128)(2,1)S(1)} %get-tuple-element.50), kind=kLoop, calls=%fused_computation.168 | loop fusion | flops 393216 | bytes 1572864 | tf_op jit(solution)/shard_map/broadcast_in_dim | solution.py:362
  (29 shorter events, 0.3 us)
Async XLA Ops:
  5.7 19.7 %copy-start = (bf16[1,2,12,128,128]{4,3,2,1,0:T(8,128)(2,1)S(1)}, bf16[1,2,12,128,128]{4,3,2,1,0:T(8,128)(2,1)}, u32[]{:S(2)}) copy-start(bf16[1,2,12,128,128]{4,3,2,1,0:T(8,128)(2,1)} %param.6) | copy-start | bytes 2359300
  32.0 45.1 %collective-permute-start = (bf16[12,128,128]{2,1,0:T(8,128)(2,1)S(1)}, bf16[12,128,128]{2,1,0:T(8,128)(2,1)S(1)}, u32[]{:S(2)}, u32[]{:S(2)}) collective-permute-start(bf16[12,128,128]{2,1,0:T(8,128)(2,1)S(1)} %fusion.99), channel_id=1, source_target_pairs={{0,1},{2,3},{4,5},{6,7},{8,9},{10,11},{12,13},{14,15},{16,17},{18,... | collective-permute-start | bytes 1179656 | tf_op jit(solution)/shard_map/ppermute | solution.py:358
  78.1 4.1 %collective-permute-start.1 = (bf16[12,128,128]{2,1,0:T(8,128)(2,1)S(1)}, bf16[12,128,128]{2,1,0:T(8,128)(2,1)S(1)}, u32[]{:S(2)}, u32[]{:S(2)}) collective-permute-start(bf16[12,128,128]{2,1,0:T(8,128)(2,1)S(1)} %get-tuple-element.51), channel_id=1, source_target_pairs={{1,0},{3,2},{5,4},{7,6},{9,8},{11,10},{13,12},{15,14},{17,16},{19,... | collective-permute-start | bytes 1179656 | tf_op jit(solution)/shard_map/ppermute | solution.py:359

commit v12 on v11

--- a/solution.py
+++ b/solution.py
@@ -368,6 +368,7 @@
     rows = -(-size // (2 * ny * 128))
     rows = -(-rows // 8) * 8
     packed = jnp.pad(flat.reshape(-1), (0, 2 * ny * rows * 128 - size)).reshape(2, ny, rows, 128)
+    result, packed = lax.optimization_barrier((result, packed))
     flat = all_reduce(packed).reshape(-1)[:size].reshape(flat.shape)
     factor = 1.0 / math.sqrt(held.shape[0] * height * breadth * blk_count())
     chosen = layer_order[None, :] == jnp.arange(layers, dtype=layer_order.dtype)[:, None]

time: 83.6 us -> 87.9 us (1.051)
  other arithmetic: 20.6 us -> 22.6 us
  matrix products: 5 us -> 6.25 us
  starting transfers between devices: 3.55 us -> 4.55 us
    reduce_sum x4, other arithmetic: 0.88 us -> 2.51 us  [shards(): bias_terms[p] = jnp.sum(gate_in.astype(jnp.float32), axis=0)]
    dot_general x4, matrix products: 1.38 us -> 2.65 us  [shards(): lax.dot_general(mix_in, gate_in, (((0,), (0,)), ((), ())), preferred_elem...]
    ppermute x1, starting transfers between devices: 2.08 us -> 3.07 us  [shards(): got_grad = lax.ppermute(input_grad, 'pipe', [(1, 0)])]
  transfers between devices with their start and end apart: 2 -> 2, of which waited for: 0 -> 1; matrix products, arithmetic and copies ran while one was open for 20% -> 18% of each run, Pallas kernels for 34% -> 0%
where the time goes in v12:
time: 87.9 us; the launch traced here: 87.5 us
  Pallas kernels  43.9 us (50%)
  other arithmetic  22.6 us (26%)
  local copies, waits for them, and re-layouts  7.38 us (8%)
  matrix products  6.25 us (7%)
  starting transfers between devices  4.55 us (5%)
  between operations  2.59 us (3%)
    pallas_call x1, Pallas kernels, all_reduce(): pl.pallas_call(reduce_kernel, out_shape=jax.ShapeDtypeStruct(flat.shape,...  27.8 us
    pallas_call x1, Pallas kernels, exchange(): pl.pallas_call(exchange_kernel, out_shape=(jax.ShapeDtypeStruct(grid_shap...  16.2 us
    convert_element_type x3, other arithmetic, shards(): gated = (masked * gelu_pair(preact)[1]).astype(jnp.bfloat16)  4.58 us
    reduce_sum x4, other arithmetic, shards(): jnp.sum(back_in * padded[i:i + height, start:start + breadth].astype(jnp....  3.3 us
    ppermute x1, starting transfers between devices, shards(): got_grad = lax.ppermute(input_grad, 'pipe', [(1, 0)])  3.07 us
    convert_element_type x4, other arithmetic, shards(): mixed = conv_forward(pad_rows(activation), depth).astype(jnp.bfloat16)  2.83 us
    reduce_sum x3, other arithmetic, pick(): jnp.sum(jnp.where(mask, table[None], jnp.zeros((), table.dtype)), axis=1,...  2.67 us
    dot_general x4, matrix products, shards(): lax.dot_general(mix_in, gate_in, (((0,), (0,)), ((), ())), preferred_elem...  2.65 us
  transfers between devices with their start and end apart: 2, of which 1 were waited for; matrix products, arithmetic and copies ran while one was open for 18% of the time, Pallas kernels for 0%

profile of v12, /device:TPU:1, one launch (start us, length us, event | category | flops | bytes accessed | tf_op | source)
XLA Modules:
  0.0 87.5 jit_solution(14177836609455105358)
XLA Ops:
  0.6 1.3 %fusion.113 = (s32[1]{0:T(128)}, s32[1]{0:T(128)}) fusion(s32[2]{0:T(128)} %param.7), kind=kLoop, calls=%fused_computation.284 | loop fusion | bytes 16 | tf_op jit(solution)/shard_map/slice | solution.py:283
  3.3 1.2 %iota_compare_fusion = (pred[4,4]{1,0:T(4,128)(4,1)}, pred[4,4]{1,0:T(4,128)(4,1)S(1)}) fusion(s32[4]{0:T(128)} %param.8), kind=kLoop, calls=%fused_computation.241 | loop fusion | flops 32 | bytes 48 | tf_op jit(solution)/shard_map/eq | solution.py:374
  4.5 0.8 select_reduce_fusion.3
  5.3 0.9 select_reduce_fusion.2
  6.2 0.0 copy-start
  6.2 0.9 %slice_bitcast_fusion.2 = (bf16[1,2,12,8,128]{4,3,2,1,0:T(8,128)(2,1)S(1)}, bf16[1,2,12,8,128]{4,3,2,1,0:T(8,128)(2,1)S(1)}) fusion(bf16[2,12,128,128]{3,2,1,0:T(8,128)(2,1)} %bitcast.232), kind=kLoop, calls=%fused_computation.211 | loop fusion | bytes 196608 | tf_op jit(solution)/shard_map/stack | solution.py:275
  7.1 1.1 %select_reduce_fusion.1 = bf16[4,128,128]{2,1,0:T(8,128)(2,1)S(1)} fusion(pred[4,4]{1,0:T(4,128)(4,1)S(1)} %get-tuple-element.118, bf16[4,128,128]{2,1,0:T(8,128)(2,1)} %param.10), kind=kLoop, calls=%fused_computation.173 | loop fusion | flops 458752 | bytes 262160 | tf_op jit(solution)/shard_map/reduce_sum | solution.py:290
  8.1 0.7 pad_maximum_fusion.edges_ref
  8.8 16.2 %shard_map.93 = (bf16[12,128,128]{2,1,0:T(8,128)(2,1)}, bf16[2,12,8,128]{3,2,1,0:T(8,128)(2,1)}, bf16[2,12,8,128]{3,2,1,0:T(8,128)(2,1)}) custom-call(bf16[2,12,128,128]{3,2,1,0:T(8,128)(2,1)} %bitcast.233, bf16[2,2,12,8,128]{4,3,2,1,0:T(8,128)(2,1)} %pad_maximum_fusion.edges_ref), custom_call_target="tpu_custom_call" | custom-call | tf_op jit(solution)/shard_map/pallas_call | solution.py:128
  25.0 0.8 slice_bitcast_fusion.17
  25.9 1.1 %bitcast_select_fusion.1 = (bf16[12,128,128]{2,1,0:T(8,128)(2,1)S(1)}, bf16[12,128,128]{2,1,0:T(8,128)(2,1)S(1)}) fusion(bf16[12,128,128]{2,1,0:T(8,128)(2,1)} %get-tuple-element.10, pred[]{:T(512)} %eq.49, bf16[1,2,12,128,128]{4,3,2,1,0:T(8,128)(2,1)S(1)} %copy-done, s32[]{:T(128)S(6)} %select_n.49), kind=kLoop, calls=%fused_computation.193 | loop fusion | flops 393216 | bytes 1572869 | tf_op jit(solution)/shard_map/jit(_where)/select_n | solution.py:279
  27.0 0.2 multiply_convert_fusion
  27.2 0.7 fusion.5
  27.9 0.5 fusion.7
  28.4 0.7 fusion.13
  29.2 0.5 fusion.15
  29.7 0.7 fusion.21
  30.4 0.5 fusion.23
  30.9 0.1 slice_convert_fusion
  31.0 0.7 add_convert_fusion
  31.7 0.7 fusion.29
  32.3 0.3 fusion.99
  32.6 1.5 %collective-permute-start = (bf16[12,128,128]{2,1,0:T(8,128)(2,1)S(1)}, bf16[12,128,128]{2,1,0:T(8,128)(2,1)S(1)}, u32[]{:S(2)}, u32[]{:S(2)}) collective-permute-start(bf16[12,128,128]{2,1,0:T(8,128)(2,1)S(1)} %fusion.99), channel_id=1, source_target_pairs={{0,1},{2,3},{4,5},{6,7},{8,9},{10,11},{12,13},{14,15},{16,17},{18,... | collective-permute-start | bytes 1179656 | tf_op jit(solution)/shard_map/ppermute | solution.py:358
  34.1 0.3 fusion.100
  34.4 0.8 convert_reduce_fusion
  35.3 0.4 convolution_convert_fusion.3
  35.6 0.9 fusion.72
  36.5 1.5 %fusion.35 = (bf16[12,134,128]{2,1,0:T(8,128)(2,1)S(1)}, f32[12,134,128]{2,1,0:T(8,128)S(1)}) fusion(f32[12,138,128]{2,1,0:T(8,128)S(1)} %get-tuple-element.126, f32[12]{0:T(128)S(1)} %compare_convert_fusion, f32[128]{0:T(128)S(1)} %get-tuple-element.146, f32[128]{0:T(128)S(1)} %get-tuple-element.145, f32[128]{0:T(128)S(1)} %get-tuple-element.144, ...), kind=kLoop, calls=%fused_computation.92 | loop fusion | flops 8438784 | bytes 4582400 | tf_op jit(solution)/shard_map/convert_element_type | solution.py:323
  38.0 1.0 %fusion.102 = f32[128,128,1]{1,0,2:T(8,128)} fusion(bf16[12,138,128]{2,1,0:T(8,128)(2,1)S(1)} %fusion.21, bf16[12,134,128]{2,1,0:T(8,128)(2,1)S(1)} %get-tuple-element.60), kind=kOutput, calls=%fused_computation.186 | convolution fusion | flops 50331648 | bytes 851968 | tf_op jit(solution)/shard_map/dot_general | solution.py:333
  39.0 0.7 convert_reduce_fusion.1
  39.7 0.4 convolution_convert_fusion.2
  40.1 0.9 fusion.63
  41.0 1.5 %fusion.41 = (bf16[12,132,128]{2,1,0:T(8,128)(2,1)S(1)}, f32[12,132,128]{2,1,0:T(8,128)S(1)}) fusion(f32[12,140,128]{2,1,0:T(8,128)S(1)} %get-tuple-element.124, f32[12]{0:T(128)S(1)} %compare_convert_fusion, f32[128]{0:T(128)S(1)} %get-tuple-element.87, f32[128]{0:T(128)S(1)} %get-tuple-element.88, f32[128]{0:T(128)S(1)} %get-tuple-element.89, ...), kind=kLoop, calls=%fused_computation.98 | loop fusion | flops 8312832 | bytes 4563968 | tf_op jit(solution)/shard_map/convert_element_type | solution.py:323
  42.5 1.0 %fusion.104 = f32[128,128,1]{1,0,2:T(8,128)} fusion(bf16[12,140,128]{2,1,0:T(8,128)(2,1)S(1)} %fusion.13, bf16[12,132,128]{2,1,0:T(8,128)(2,1)S(1)} %get-tuple-element.58), kind=kOutput, calls=%fused_computation.188 | convolution fusion | flops 50331648 | bytes 851968 | tf_op jit(solution)/shard_map/dot_general | solution.py:333
  43.5 0.4 convolution_convert_fusion.1
  43.8 0.7 fusion.54
  44.6 1.5 %fusion.47 = (bf16[12,130,128]{2,1,0:T(8,128)(2,1)S(1)}, f32[12,130,128]{2,1,0:T(8,128)S(1)}) fusion(f32[12,142,128]{2,1,0:T(8,128)S(1)} %get-tuple-element.122, f32[12]{0:T(128)S(1)} %compare_convert_fusion, f32[128]{0:T(128)S(1)} %get-tuple-element.137, f32[128]{0:T(128)S(1)} %get-tuple-element.136, f32[128]{0:T(128)S(1)} %get-tuple-element.135, ...), kind=kLoop, calls=%fused_computation.104 | loop fusion | flops 8186880 | bytes 4545536 | tf_op jit(solution)/shard_map/convert_element_type | solution.py:323
  46.1 0.8 convert_reduce_fusion.3
  46.9 0.4 convolution_convert_fusion
  47.2 0.9 fusion.89
  48.4 0.2 convert_reduce_fusion.2
  48.6 0.0 copy-start.8
  48.6 0.0 copy-start.10
  48.7 0.3 fusion.106
  49.0 0.0 collective-permute-done
  49.1 0.2 copy-done.4
  49.3 0.0 copy-done.8
  49.3 0.0 copy-done.14
  49.3 0.0 copy-start.2
  49.4 1.0 %select_bitcast_fusion.1 = (bf16[1,12,128,128]{3,2,1,0:T(8,128)(2,1)S(1)}, bf16[12,128,128]{2,1,0:T(8,128)(2,1)S(1)}) fusion(bf16[12,128,128]{2,1,0:T(8,128)(2,1)S(1)} %collective-permute-done, pred[]{:T(512)} %eq.49, f32[12]{0:T(128)S(1)} %compare_convert_fusion, f32[128]{0:T(128)S(1)} %copy-done.4, f32[128]{0:T(128)S(1)} %copy-done.6, ...), kind=kLoop, calls=%fused_computation.195 | loop fusion | flops 5898240 | bytes 3568641 | tf_op jit(solution)/shard_map/stack | solution.py:362
  50.3 3.1 %collective-permute-start.1 = (bf16[12,128,128]{2,1,0:T(8,128)(2,1)S(1)}, bf16[12,128,128]{2,1,0:T(8,128)(2,1)S(1)}, u32[]{:S(2)}, u32[]{:S(2)}) collective-permute-start(bf16[12,128,128]{2,1,0:T(8,128)(2,1)S(1)} %get-tuple-element.55), channel_id=1, source_target_pairs={{1,0},{3,2},{5,4},{7,6},{9,8},{11,10},{13,12},{15,14},{17,16},{19,... | collective-permute-start | bytes 1179656 | tf_op jit(solution)/shard_map/ppermute | solution.py:359
  53.5 0.3 maximum_maximum_fusion
  53.8 0.1 reshape.182
  53.9 0.7 pad.48
  54.6 0.1 collective-permute-done.1
  54.8 0.9 %maximum_bitcast_fusion = bf16[1,2,12,128,128]{4,3,2,1,0:T(8,128)(2,1)} fusion(bf16[1,12,128,128]{3,2,1,0:T(8,128)(2,1)S(1)} %select_bitcast_fusion, bf16[1,12,128,128]{3,2,1,0:T(8,128)(2,1)S(1)} %get-tuple-element.54), kind=kLoop, calls=%fused_computation.168 | loop fusion | flops 393216 | bytes 1572864 | tf_op jit(solution)/shard_map/broadcast_in_dim | solution.py:362
  55.7 27.8 %shard_map.94 = f32[2,4,72,128]{3,2,1,0:T(8,128)} custom-call(f32[2,4,72,128]{3,2,1,0:T(8,128)} %bitcast.234), custom_call_target="tpu_custom_call" | custom-call | tf_op jit(solution)/shard_map/pallas_call | solution.py:240
  83.5 1.0 %slice.938 = f32[70656]{0:T(1024)S(1)} slice(f32[73728]{0:T(1024)} %bitcast.235), slice={[0:70656]} | slice | bytes 565248 | tf_op jit(solution)/shard_map/slice | solution.py:372
  84.5 0.1 broadcast_in_dim.106
  84.6 0.8 select_reduce_fusion
  85.5 0.1 broadcast_multiply_fusion
  85.5 0.6 slice.941
  86.1 0.6 slice.939
  86.7 0.7 copy.30
  (68 shorter events, 0.4 us)
Async XLA Ops:
  6.2 19.8 %copy-start = (bf16[1,2,12,128,128]{4,3,2,1,0:T(8,128)(2,1)S(1)}, bf16[1,2,12,128,128]{4,3,2,1,0:T(8,128)(2,1)}, u32[]{:S(2)}) copy-start(bf16[1,2,12,128,128]{4,3,2,1,0:T(8,128)(2,1)} %param.6) | copy-start | bytes 2359300
  25.8 1.3 %copy-start.3 = (f32[128]{0:T(128)}, f32[128]{0:T(128)S(1)}, u32[]{:S(2)}) copy-start(f32[128]{0:T(128)S(1)} %get-tuple-element.105) | copy-start | bytes 1540
  25.8 1.3 %copy-start.5 = (f32[128]{0:T(128)}, f32[128]{0:T(128)S(1)}, u32[]{:S(2)}) copy-start(f32[128]{0:T(128)S(1)} %get-tuple-element.106) | copy-start | bytes 1540
  25.8 1.3 %copy-start.7 = (f32[128]{0:T(128)}, f32[128]{0:T(128)S(1)}, u32[]{:S(2)}) copy-start(f32[128]{0:T(128)S(1)} %get-tuple-element.107) | copy-start | bytes 1540
  25.8 1.3 %copy-start.9 = (f32[128]{0:T(128)}, f32[128]{0:T(128)S(1)}, u32[]{:S(2)}) copy-start(f32[128]{0:T(128)S(1)} %get-tuple-element.108) | copy-start | bytes 1540
  25.9 1.3 %copy-start.11 = (f32[128]{0:T(128)}, f32[128]{0:T(128)S(1)}, u32[]{:S(2)}) copy-start(f32[128]{0:T(128)S(1)} %get-tuple-element.109) | copy-start | bytes 1540
  25.9 1.3 %copy-start.13 = (f32[128]{0:T(128)}, f32[128]{0:T(128)S(1)}, u32[]{:S(2)}) copy-start(f32[128]{0:T(128)S(1)} %get-tuple-element.110) | copy-start | bytes 1540
  25.9 1.3 %copy-start.15 = (f32[128]{0:T(128)}, f32[128]{0:T(128)S(1)}, u32[]{:S(2)}) copy-start(f32[128]{0:T(128)S(1)} %get-tuple-element.111) | copy-start | bytes 1540
  25.9 1.3 %copy-start.17 = (f32[128]{0:T(128)}, f32[128]{0:T(128)S(1)}, u32[]{:S(2)}) copy-start(f32[128]{0:T(128)S(1)} %get-tuple-element.112) | copy-start | bytes 1540
  32.6 16.4 %collective-permute-start = (bf16[12,128,128]{2,1,0:T(8,128)(2,1)S(1)}, bf16[12,128,128]{2,1,0:T(8,128)(2,1)S(1)}, u32[]{:S(2)}, u32[]{:S(2)}) collective-permute-start(bf16[12,128,128]{2,1,0:T(8,128)(2,1)S(1)} %fusion.99), channel_id=1, source_target_pairs={{0,1},{2,3},{4,5},{6,7},{8,9},{10,11},{12,13},{14,15},{16,17},{18,... | collective-permute-start | bytes 1179656 | tf_op jit(solution)/shard_map/ppermute | solution.py:358
  48.6 0.7 copy-start.4
  48.6 0.7 copy-start.6
  48.6 0.7 copy-start.8
  48.6 0.7 copy-start.10
  48.6 0.7 copy-start.12
  48.7 0.7 copy-start.14
  48.7 0.7 copy-start.16
  48.7 0.7 copy-start.18
  49.3 4.1 %copy-start.1 = (f32[128,128,1]{1,0,2:T(8,128)S(1)}, f32[128,128,1]{1,0,2:T(8,128)}, u32[]{:S(2)}) copy-start(f32[128,128,1]{1,0,2:T(8,128)} %fusion.102) | copy-start | bytes 196612
  49.3 4.1 %copy-start.2 = (f32[128,128,1]{1,0,2:T(8,128)S(1)}, f32[128,128,1]{1,0,2:T(8,128)}, u32[]{:S(2)}) copy-start(f32[128,128,1]{1,0,2:T(8,128)} %fusion.104) | copy-start | bytes 196612
  49.4 4.1 %copy-start.20 = (f32[128]{0:T(128)S(1)}, f32[128]{0:T(128)}, u32[]{:S(2)}) copy-start(f32[128]{0:T(128)} %convert_reduce_fusion) | copy-start | bytes 1540
  49.4 4.1 %copy-start.21 = (f32[128]{0:T(128)S(1)}, f32[128]{0:T(128)}, u32[]{:S(2)}) copy-start(f32[128]{0:T(128)} %convert_reduce_fusion.1) | copy-start | bytes 1540
  49.4 4.1 %copy-start.22 = (f32[128]{0:T(128)S(1)}, f32[128]{0:T(128)}, u32[]{:S(2)}) copy-start(f32[128]{0:T(128)} %convert_reduce_fusion.3) | copy-start | bytes 1540
  50.3 4.4 %collective-permute-start.1 = (bf16[12,128,128]{2,1,0:T(8,128)(2,1)S(1)}, bf16[12,128,128]{2,1,0:T(8,128)(2,1)S(1)}, u32[]{:S(2)}, u32[]{:S(2)}) collective-permute-start(bf16[12,128,128]{2,1,0:T(8,128)(2,1)S(1)} %get-tuple-element.55), channel_id=1, source_target_pairs={{1,0},{3,2},{5,4},{7,6},{9,8},{11,10},{13,12},{15,14},{17,16},{19,... | collective-permute-start | bytes 1179656 | tf_op jit(solution)/shard_map/ppermute | solution.py:359
  55.7 28.9 %copy-start.19 = (pred[4,4]{1,0:T(4,128)(4,1)S(1)}, pred[4,4]{1,0:T(4,128)(4,1)}, u32[]{:S(2)}) copy-start(pred[4,4]{1,0:T(4,128)(4,1)} %get-tuple-element.117) | copy-start | bytes 52

commit v13 on v11

--- a/solution.py
+++ b/solution.py
@@ -157,20 +157,24 @@
     return values[0]
 
 
-def reduce_kernel(flat_ref, out_ref, own, part, whole, got_pipe, got_y, got_z, got_x, got_back, got_end,
-                  send_sem, recv_pipe, recv_y, recv_z, recv_x, recv_back, recv_end):
+def reduce_kernel(flat_ref, out_ref, part, got_a, got_z, got_x, got_b,
+                  send_sem, recv_a, recv_z, recv_x, recv_b):
     core = lax.axis_index("pipe")
-    here = tuple(lax.axis_index(name) for name in BLK_AXES)
-    partner = here + (1 - core,)
     my_y, my_z, my_x = (lax.axis_index(name) for name in ("y", "z", "x"))
-    groups = {axis: group_members(axis) for axis in ("y", "z", "x")}
+    ny = lax.axis_size("y")
+    row = [lax.axis_index(name) for name in BLK_AXES]
+    groups = {
+        "py": [(row[0], row[1], j, h) for h in range(2) for j in range(ny)],
+        "z": group_members("z"),
+        "x": group_members("x"),
+    }
+    places = {"py": core * ny + my_y, "z": my_z, "x": my_x}
 
     barrier = pltpu.get_barrier_semaphore()
-    pl.semaphore_signal(barrier, inc=1, device_id=partner, device_id_type=MESH_ID)
-    count = 1
-    for axis, mine in (("y", my_y), ("z", my_z), ("x", my_x)):
+    count = 0
+    for axis in ("py", "z", "x"):
         for j, member in enumerate(groups[axis]):
-            @pl.when(j != mine)
+            @pl.when(j != places[axis])
             def _():
                 pl.semaphore_signal(barrier, inc=1, device_id=member, device_id_type=MESH_ID)
         count += len(groups[axis]) - 1
@@ -178,15 +182,8 @@
 
     sends = iter(range(send_sem.shape[0]))
 
-    def one(src, dst, sem, target):
-        copy = pltpu.make_async_remote_copy(
-            src_ref=src, dst_ref=dst, send_sem=send_sem.at[next(sends)], recv_sem=sem,
-            device_id=target, device_id_type=MESH_ID,
-        )
-        copy.start()
-        copy.wait()
-
-    def spread(axis, mine, src_of, dst, sems):
+    def spread(axis, src_of, dst, sems):
+        mine = places[axis]
         copies = []
         for j, member in enumerate(groups[axis]):
             copy = pltpu.make_async_remote_copy(
@@ -207,35 +204,28 @@
                     recv_sem=sems.at[j], device_id=groups[axis][j], device_id_type=MESH_ID,
                 ).wait_recv()
 
-    one(flat_ref.at[1 - core], got_pipe, recv_pipe.at[0], partner)
-    own[...] = flat_ref[core] + got_pipe[...]
-
-    ny = len(groups["y"])
-    got_y[my_y] = own[my_y]
-    spread("y", my_y, lambda j: own.at[j], got_y, recv_y)
-    part[...] = tree_sum([got_y[k] for k in range(ny)])
+    got_a[places["py"]] = flat_ref[places["py"]]
+    spread("py", lambda j: flat_ref.at[j], got_a, recv_a)
+    part[...] = tree_sum([got_a[k] for k in range(len(groups["py"]))])
 
     got_z[my_z] = part[...]
-    spread("z", my_z, lambda j: part, got_z, recv_z)
+    spread("z", lambda j: part, got_z, recv_z)
     part[...] = tree_sum([got_z[k] for k in range(len(groups["z"]))])
 
     got_x[my_x] = part[...]
-    spread("x", my_x, lambda j: part, got_x, recv_x)
+    spread("x", lambda j: part, got_x, recv_x)
     part[...] = tree_sum([got_x[k] for k in range(len(groups["x"]))])
 
-    got_back[my_y] = part[...]
-    spread("y", my_y, lambda j: part, got_back, recv_back)
-
-    one(got_back, got_end, recv_end.at[0], partner)
-    out_ref[core] = got_back[...]
-    out_ref[1 - core] = got_end[...]
+    got_b[places["py"]] = part[...]
+    spread("py", lambda j: part, got_b, recv_b)
+    out_ref[...] = got_b[...]
 
 
 def all_reduce(flat):
-    halves, ny, rows, lanes = flat.shape
+    chunks, rows, lanes = flat.shape
     nz, nx = lax.axis_size("z"), lax.axis_size("x")
     chunk = (rows, lanes)
-    sends = 1 + ny + nz + nx + ny + 1
+    sends = chunks + nz + nx + chunks
     vmem = pl.BlockSpec(memory_space=pltpu.VMEM)
     return pl.pallas_call(
         reduce_kernel,
@@ -243,22 +233,16 @@
         in_specs=[vmem],
         out_specs=vmem,
         scratch_shapes=[
-            pltpu.VMEM((ny,) + chunk, flat.dtype),
             pltpu.VMEM(chunk, flat.dtype),
-            pltpu.VMEM((ny,) + chunk, flat.dtype),
-            pltpu.VMEM((ny,) + chunk, flat.dtype),
-            pltpu.VMEM((ny,) + chunk, flat.dtype),
+            pltpu.VMEM((chunks,) + chunk, flat.dtype),
             pltpu.VMEM((nz,) + chunk, flat.dtype),
             pltpu.VMEM((nx,) + chunk, flat.dtype),
-            pltpu.VMEM((ny,) + chunk, flat.dtype),
-            pltpu.VMEM((ny,) + chunk, flat.dtype),
+            pltpu.VMEM((chunks,) + chunk, flat.dtype),
             pltpu.SemaphoreType.DMA((sends,)),
-            pltpu.SemaphoreType.DMA((1,)),
-            pltpu.SemaphoreType.DMA((ny,)),
+            pltpu.SemaphoreType.DMA((chunks,)),
             pltpu.SemaphoreType.DMA((nz,)),
             pltpu.SemaphoreType.DMA((nx,)),
-            pltpu.SemaphoreType.DMA((ny,)),
-            pltpu.SemaphoreType.DMA((1,)),
+            pltpu.SemaphoreType.DMA((chunks,)),
         ],
         compiler_params=pltpu.CompilerParams(collective_id=1, has_side_effects=True),
     )(flat)
@@ -367,7 +351,7 @@
     size = flat.size
     rows = -(-size // (2 * ny * 128))
     rows = -(-rows // 8) * 8
-    packed = jnp.pad(flat.reshape(-1), (0, 2 * ny * rows * 128 - size)).reshape(2, ny, rows, 128)
+    packed = jnp.pad(flat.reshape(-1), (0, 2 * ny * rows * 128 - size)).reshape(2 * ny, rows, 128)
     flat = all_reduce(packed).reshape(-1)[:size].reshape(flat.shape)
     factor = 1.0 / math.sqrt(held.shape[0] * height * breadth * blk_count())
     chosen = layer_order[None, :] == jnp.arange(layers, dtype=layer_order.dtype)[:, None]

time: 83.6 us -> 82 us (0.981)
  Pallas kernels: 44.7 us -> 43.1 us
    pallas_call x1, Pallas kernels: 28.5 us -> 27 us  [all_reduce(): pl.pallas_call(reduce_kernel, out_shape=jax.ShapeDtypeStruct(flat.shape,...]
  transfers between devices with their start and end apart: 2 -> 2, of which waited for: 0 -> 0; matrix products, arithmetic and copies ran while one was open for 20% -> 21% of each run, Pallas kernels for 34% -> 33%
where the time goes in v13:
time: 82 us; the launch traced here: 81.4 us
  Pallas kernels  43.1 us (53%)
  other arithmetic  20.6 us (25%)
  local copies, waits for them, and re-layouts  7.02 us (9%)
  matrix products  5 us (6%)
  starting transfers between devices  3.32 us (4%)
  between operations  2.33 us (3%)
    pallas_call x1, Pallas kernels, all_reduce(): pl.pallas_call(reduce_kernel, out_shape=jax.ShapeDtypeStruct(flat.shape,...  27 us
    pallas_call x1, Pallas kernels, exchange(): pl.pallas_call(exchange_kernel, out_shape=(jax.ShapeDtypeStruct(grid_shap...  16.2 us
    convert_element_type x3, other arithmetic, shards(): gated = (masked * gelu_pair(preact)[1]).astype(jnp.bfloat16)  4.58 us
    reduce_sum x4, other arithmetic, shards(): jnp.sum(back_in * padded[i:i + height, start:start + breadth].astype(jnp....  3.3 us
    convert_element_type x4, other arithmetic, shards(): mixed = conv_forward(pad_rows(activation), depth).astype(jnp.bfloat16)  2.83 us
    reduce_sum x3, other arithmetic, pick(): jnp.sum(jnp.where(mask, table[None], jnp.zeros((), table.dtype)), axis=1,...  2.67 us
    dot_general x4, matrix products, shards(): jnp.dot(mixed.reshape(rows * span, channels), point, preferred_element_ty...  2.15 us
    ppermute x1, starting transfers between devices, shards(): got_grad = lax.ppermute(input_grad, 'pipe', [(1, 0)])  1.84 us
  transfers between devices with their start and end apart: 2, of which 0 were waited for; matrix products, arithmetic and copies ran while one was open for 21% of the time, Pallas kernels for 33%

profile of v13, /device:TPU:1, one launch (start us, length us, event | category | flops | bytes accessed | tf_op | source)
XLA Modules:
  0.0 81.4 jit_solution(762658916517135034)
XLA Ops:
  0.6 1.3 %fusion.113 = (s32[1]{0:T(128)}, s32[1]{0:T(128)}) fusion(s32[2]{0:T(128)} %param.7), kind=kLoop, calls=%fused_computation.284 | loop fusion | bytes 16 | tf_op jit(solution)/shard_map/slice | solution.py:267
  3.3 0.8 iota_compare_fusion
  4.1 0.8 select_reduce_fusion.3
  4.8 0.9 %select_reduce_fusion.2 = f32[4,3,3,128]{3,2,1,0:T(4,128)S(1)} fusion(f32[4,3,3,128]{3,0,2,1:T(4,128)} %param.9, pred[4,4]{1,0:T(4,128)(4,1)S(1)} %get-tuple-element.114), kind=kLoop, calls=%fused_computation.209 | loop fusion | flops 32256 | bytes 36880 | tf_op jit(solution)/shard_map/reduce_sum | solution.py:274
  5.7 0.0 copy-start
  5.7 0.9 %slice_bitcast_fusion.2 = (bf16[1,2,12,8,128]{4,3,2,1,0:T(8,128)(2,1)S(1)}, bf16[1,2,12,8,128]{4,3,2,1,0:T(8,128)(2,1)S(1)}) fusion(bf16[2,12,128,128]{3,2,1,0:T(8,128)(2,1)} %bitcast.232), kind=kLoop, calls=%fused_computation.211 | loop fusion | bytes 196608 | tf_op jit(solution)/shard_map/stack | solution.py:259
  6.6 1.0 %select_reduce_fusion.1 = bf16[4,128,128]{2,1,0:T(8,128)(2,1)S(1)} fusion(pred[4,4]{1,0:T(4,128)(4,1)S(1)} %get-tuple-element.114, bf16[4,128,128]{2,1,0:T(8,128)(2,1)} %param.10), kind=kLoop, calls=%fused_computation.173 | loop fusion | flops 458752 | bytes 262160 | tf_op jit(solution)/shard_map/reduce_sum | solution.py:274
  7.7 0.7 pad_maximum_fusion.edges_ref
  8.3 16.2 %shard_map.93 = (bf16[12,128,128]{2,1,0:T(8,128)(2,1)}, bf16[2,12,8,128]{3,2,1,0:T(8,128)(2,1)}, bf16[2,12,8,128]{3,2,1,0:T(8,128)(2,1)}) custom-call(bf16[2,12,128,128]{3,2,1,0:T(8,128)(2,1)} %bitcast.233, bf16[2,2,12,8,128]{4,3,2,1,0:T(8,128)(2,1)} %pad_maximum_fusion.edges_ref), custom_call_target="tpu_custom_call" | custom-call | tf_op jit(solution)/shard_map/pallas_call | solution.py:128
  24.5 0.8 slice_bitcast_fusion.17
  25.4 0.0 copy-done
  25.4 1.1 %bitcast_select_fusion.1 = (bf16[12,128,128]{2,1,0:T(8,128)(2,1)S(1)}, bf16[12,128,128]{2,1,0:T(8,128)(2,1)S(1)}) fusion(bf16[12,128,128]{2,1,0:T(8,128)(2,1)} %get-tuple-element.8, pred[]{:T(512)} %eq.49, bf16[1,2,12,128,128]{4,3,2,1,0:T(8,128)(2,1)S(1)} %copy-done, s32[]{:T(128)S(6)} %select_n.49), kind=kLoop, calls=%fused_computation.193 | loop fusion | flops 393216 | bytes 1572869 | tf_op jit(solution)/shard_map/jit(_where)/select_n | solution.py:263
  26.5 0.2 multiply_convert_fusion
  26.6 0.7 fusion.5
  27.3 0.5 fusion.7
  27.8 0.7 fusion.13
  28.6 0.5 fusion.15
  29.1 0.7 fusion.21
  29.8 0.5 fusion.23
  30.3 0.1 slice_convert_fusion
  30.4 0.7 add_convert_fusion
  31.1 0.7 fusion.29
  31.7 0.3 fusion.99
  32.0 1.5 %collective-permute-start = (bf16[12,128,128]{2,1,0:T(8,128)(2,1)S(1)}, bf16[12,128,128]{2,1,0:T(8,128)(2,1)S(1)}, u32[]{:S(2)}, u32[]{:S(2)}) collective-permute-start(bf16[12,128,128]{2,1,0:T(8,128)(2,1)S(1)} %fusion.99), channel_id=1, source_target_pairs={{0,1},{2,3},{4,5},{6,7},{8,9},{10,11},{12,13},{14,15},{16,17},{18,... | collective-permute-start | bytes 1179656 | tf_op jit(solution)/shard_map/ppermute | solution.py:342
  33.5 0.3 fusion.100
  33.9 0.2 convert_reduce_fusion
  34.1 0.4 convolution_convert_fusion.3
  34.4 0.9 %fusion.72 = (f32[128]{0:T(128)S(1)}, f32[128]{0:T(128)S(1)}, f32[128]{0:T(128)S(1)}, f32[128]{0:T(128)S(1)}, f32[128]{0:T(128)S(1)}, /*index=5*/f32[128]{0:T(12...) fusion(bf16[12,138,128]{2,1,0:T(8,128)(2,1)S(1)} %get-tuple-element.121, ...), kind=kLoop, calls=%fused_computation.138 | loop fusion | flops 5503872 | bytes 2019840 | tf_op jit(solution)/shard_map/reduce_sum | solution.py:330
  35.3 1.5 %fusion.35 = (bf16[12,134,128]{2,1,0:T(8,128)(2,1)S(1)}, f32[12,134,128]{2,1,0:T(8,128)S(1)}) fusion(f32[12,138,128]{2,1,0:T(8,128)S(1)} %get-tuple-element.122, f32[12]{0:T(128)S(1)} %compare_convert_fusion, f32[128]{0:T(128)S(1)} %get-tuple-element.142, f32[128]{0:T(128)S(1)} %get-tuple-element.141, f32[128]{0:T(128)S(1)} %get-tuple-element.140, ...), kind=kLoop, calls=%fused_computation.92 | loop fusion | flops 8438784 | bytes 4582400 | tf_op jit(solution)/shard_map/convert_element_type | solution.py:307
  36.8 0.3 fusion.102
  37.2 0.2 convert_reduce_fusion.1
  37.4 0.4 convolution_convert_fusion.2
  37.8 0.9 %fusion.63 = (f32[128]{0:T(128)S(1)}, f32[128]{0:T(128)S(1)}, f32[128]{0:T(128)S(1)}, f32[128]{0:T(128)S(1)}, f32[128]{0:T(128)S(1)}, /*index=5*/f32[128]{0:T(12...) fusion(bf16[12,140,128]{2,1,0:T(8,128)(2,1)S(1)} %get-tuple-element.119, ...), kind=kLoop, calls=%fused_computation.129 | loop fusion | flops 5503872 | bytes 2019840 | tf_op jit(solution)/shard_map/reduce_sum | solution.py:330
  38.6 1.5 %fusion.41 = (bf16[12,132,128]{2,1,0:T(8,128)(2,1)S(1)}, f32[12,132,128]{2,1,0:T(8,128)S(1)}) fusion(f32[12,140,128]{2,1,0:T(8,128)S(1)} %get-tuple-element.120, f32[12]{0:T(128)S(1)} %compare_convert_fusion, f32[128]{0:T(128)S(1)} %get-tuple-element.83, f32[128]{0:T(128)S(1)} %get-tuple-element.84, f32[128]{0:T(128)S(1)} %get-tuple-element.85, ...), kind=kLoop, calls=%fused_computation.98 | loop fusion | flops 8312832 | bytes 4563968 | tf_op jit(solution)/shard_map/convert_element_type | solution.py:307
  40.2 0.3 fusion.104
  40.5 0.2 convert_reduce_fusion.2
  40.8 0.4 convolution_convert_fusion.1
  41.1 0.7 fusion.54
  41.9 1.5 %fusion.47 = (bf16[12,130,128]{2,1,0:T(8,128)(2,1)S(1)}, f32[12,130,128]{2,1,0:T(8,128)S(1)}) fusion(f32[12,142,128]{2,1,0:T(8,128)S(1)} %get-tuple-element.118, f32[12]{0:T(128)S(1)} %compare_convert_fusion, f32[128]{0:T(128)S(1)} %get-tuple-element.133, f32[128]{0:T(128)S(1)} %get-tuple-element.132, f32[128]{0:T(128)S(1)} %get-tuple-element.131, ...), kind=kLoop, calls=%fused_computation.104 | loop fusion | flops 8186880 | bytes 4545536 | tf_op jit(solution)/shard_map/convert_element_type | solution.py:307
  43.4 0.3 fusion.106
  43.7 0.2 convert_reduce_fusion.3
  44.0 0.4 convolution_convert_fusion
  44.3 0.9 %fusion.89 = (f32[128]{0:T(128)S(1)}, f32[128]{0:T(128)S(1)}, f32[128]{0:T(128)S(1)}, f32[128]{0:T(128)S(1)}, f32[128]{0:T(128)S(1)}, /*index=5*/f32[128]{0:T(12...) fusion(bf16[12,144,128]{2,1,0:T(8,128)(2,1)S(1)} %multiply_convert_fusion, ...), kind=kLoop, calls=%fused_computation.155 | loop fusion | flops 5503872 | bytes 2019840 | tf_op jit(solution)/shard_map/reduce_sum | solution.py:330
  45.5 0.3 maximum_maximum_fusion
  45.8 0.1 reshape.182
  45.9 0.7 pad.48
  46.6 27.0 %shard_map.94 = f32[8,72,128]{2,1,0:T(8,128)} custom-call(f32[8,72,128]{2,1,0:T(8,128)} %bitcast.234), custom_call_target="tpu_custom_call" | custom-call | tf_op jit(solution)/shard_map/pallas_call | solution.py:230
  73.6 1.0 %slice.938 = f32[70656]{0:T(1024)S(1)} slice(f32[73728]{0:T(1024)} %bitcast.235), slice={[0:70656]} | slice | bytes 565248 | tf_op jit(solution)/shard_map/slice | solution.py:355
  74.6 0.1 broadcast_in_dim.106
  74.7 0.8 %select_reduce_fusion = f32[4,17664]{1,0:T(4,128)S(1)} fusion(f32[4,17664]{1,0:T(4,128)S(1)} %broadcast_in_dim.106, pred[4,4]{1,0:T(4,128)(4,1)S(1)} %get-tuple-element.113), kind=kLoop, calls=%fused_computation.49 | loop fusion | flops 494592 | bytes 565264 | tf_op jit(solution)/shard_map/reduce_sum | solution.py:358
  75.5 0.0 collective-permute-done
  75.5 0.9 %select_bitcast_fusion.1 = (bf16[1,12,128,128]{3,2,1,0:T(8,128)(2,1)S(1)}, bf16[12,128,128]{2,1,0:T(8,128)(2,1)S(1)}) fusion(bf16[12,128,128]{2,1,0:T(8,128)(2,1)S(1)} %collective-permute-done, pred[]{:T(512)} %eq.49, f32[12]{0:T(128)S(1)} %compare_convert_fusion, f32[128]{0:T(128)S(1)} %get-tuple-element.101, f32[128]{0:T(128)S(1)} %get-tuple-element.102, ...), kind=kLoop, calls=%fused_computation.195 | loop fusion | flops 5898240 | bytes 3568641 | tf_op jit(solution)/shard_map/stack | solution.py:346
  76.5 1.8 %collective-permute-start.1 = (bf16[12,128,128]{2,1,0:T(8,128)(2,1)S(1)}, bf16[12,128,128]{2,1,0:T(8,128)(2,1)S(1)}, u32[]{:S(2)}, u32[]{:S(2)}) collective-permute-start(bf16[12,128,128]{2,1,0:T(8,128)(2,1)S(1)} %get-tuple-element.51), channel_id=1, source_target_pairs={{1,0},{3,2},{5,4},{7,6},{9,8},{11,10},{13,12},{15,14},{17,16},{19,... | collective-permute-start | bytes 1179656 | tf_op jit(solution)/shard_map/ppermute | solution.py:343
  78.4 0.1 broadcast_multiply_fusion
  78.4 0.6 slice.941
  79.0 0.6 slice.939
  79.6 0.7 copy.30
  80.4 0.0 collective-permute-done.1
  80.4 0.9 %maximum_bitcast_fusion = bf16[1,2,12,128,128]{4,3,2,1,0:T(8,128)(2,1)} fusion(bf16[1,12,128,128]{3,2,1,0:T(8,128)(2,1)S(1)} %select_bitcast_fusion, bf16[1,12,128,128]{3,2,1,0:T(8,128)(2,1)S(1)} %get-tuple-element.50), kind=kLoop, calls=%fused_computation.168 | loop fusion | flops 393216 | bytes 1572864 | tf_op jit(solution)/shard_map/broadcast_in_dim | solution.py:346
  (29 shorter events, 0.3 us)
Async XLA Ops:
  5.7 19.7 %copy-start = (bf16[1,2,12,128,128]{4,3,2,1,0:T(8,128)(2,1)S(1)}, bf16[1,2,12,128,128]{4,3,2,1,0:T(8,128)(2,1)}, u32[]{:S(2)}) copy-start(bf16[1,2,12,128,128]{4,3,2,1,0:T(8,128)(2,1)} %param.6) | copy-start | bytes 2359300
  32.0 43.5 %collective-permute-start = (bf16[12,128,128]{2,1,0:T(8,128)(2,1)S(1)}, bf16[12,128,128]{2,1,0:T(8,128)(2,1)S(1)}, u32[]{:S(2)}, u32[]{:S(2)}) collective-permute-start(bf16[12,128,128]{2,1,0:T(8,128)(2,1)S(1)} %fusion.99), channel_id=1, source_target_pairs={{0,1},{2,3},{4,5},{6,7},{8,9},{10,11},{12,13},{14,15},{16,17},{18,... | collective-permute-start | bytes 1179656 | tf_op jit(solution)/shard_map/ppermute | solution.py:342
  76.5 3.9 %collective-permute-start.1 = (bf16[12,128,128]{2,1,0:T(8,128)(2,1)S(1)}, bf16[12,128,128]{2,1,0:T(8,128)(2,1)S(1)}, u32[]{:S(2)}, u32[]{:S(2)}) collective-permute-start(bf16[12,128,128]{2,1,0:T(8,128)(2,1)S(1)} %get-tuple-element.51), channel_id=1, source_target_pairs={{1,0},{3,2},{5,4},{7,6},{9,8},{11,10},{13,12},{15,14},{17,16},{19,... | collective-permute-start | bytes 1179656 | tf_op jit(solution)/shard_map/ppermute | solution.py:343

commit v14 on v13

--- a/solution.py
+++ b/solution.py
@@ -157,22 +157,21 @@
     return values[0]
 
 
-def reduce_kernel(flat_ref, out_ref, part, got_a, got_z, got_x, got_b,
-                  send_sem, recv_a, recv_z, recv_x, recv_b):
+def reduce_kernel(flat_ref, out_ref, part, got_a, got_z, got_b,
+                  send_sem, recv_a, recv_z, recv_b):
     core = lax.axis_index("pipe")
     my_y, my_z, my_x = (lax.axis_index(name) for name in ("y", "z", "x"))
-    ny = lax.axis_size("y")
+    ny, nx = lax.axis_size("y"), lax.axis_size("x")
     row = [lax.axis_index(name) for name in BLK_AXES]
     groups = {
-        "py": [(row[0], row[1], j, h) for h in range(2) for j in range(ny)],
+        "py": [(i, row[1], j, h) for h in range(2) for i in range(nx) for j in range(ny)],
         "z": group_members("z"),
-        "x": group_members("x"),
     }
-    places = {"py": core * ny + my_y, "z": my_z, "x": my_x}
+    places = {"py": (core * nx + my_x) * ny + my_y, "z": my_z}
 
     barrier = pltpu.get_barrier_semaphore()
     count = 0
-    for axis in ("py", "z", "x"):
+    for axis in ("py", "z"):
         for j, member in enumerate(groups[axis]):
             @pl.when(j != places[axis])
             def _():
@@ -212,10 +211,6 @@
     spread("z", lambda j: part, got_z, recv_z)
     part[...] = tree_sum([got_z[k] for k in range(len(groups["z"]))])
 
-    got_x[my_x] = part[...]
-    spread("x", lambda j: part, got_x, recv_x)
-    part[...] = tree_sum([got_x[k] for k in range(len(groups["x"]))])
-
     got_b[places["py"]] = part[...]
     spread("py", lambda j: part, got_b, recv_b)
     out_ref[...] = got_b[...]
@@ -223,9 +218,9 @@
 
 def all_reduce(flat):
     chunks, rows, lanes = flat.shape
-    nz, nx = lax.axis_size("z"), lax.axis_size("x")
+    nz = lax.axis_size("z")
     chunk = (rows, lanes)
-    sends = chunks + nz + nx + chunks
+    sends = chunks + nz + chunks
     vmem = pl.BlockSpec(memory_space=pltpu.VMEM)
     return pl.pallas_call(
         reduce_kernel,
@@ -236,12 +231,10 @@
             pltpu.VMEM(chunk, flat.dtype),
             pltpu.VMEM((chunks,) + chunk, flat.dtype),
             pltpu.VMEM((nz,) + chunk, flat.dtype),
-            pltpu.VMEM((nx,) + chunk, flat.dtype),
             pltpu.VMEM((chunks,) + chunk, flat.dtype),
             pltpu.SemaphoreType.DMA((sends,)),
             pltpu.SemaphoreType.DMA((chunks,)),
             pltpu.SemaphoreType.DMA((nz,)),
-            pltpu.SemaphoreType.DMA((nx,)),
             pltpu.SemaphoreType.DMA((chunks,)),
         ],
         compiler_params=pltpu.CompilerParams(collective_id=1, has_side_effects=True),
@@ -347,11 +340,11 @@
 
     pieces = (jnp.stack(depth_terms), jnp.stack(point_terms), jnp.stack(bias_terms))
     flat = jnp.concatenate([piece.reshape(layers, -1) for piece in pieces], axis=1)
-    ny = lax.axis_size("y")
+    chunks = 2 * lax.axis_size("y") * lax.axis_size("x")
     size = flat.size
-    rows = -(-size // (2 * ny * 128))
+    rows = -(-size // (chunks * 128))
     rows = -(-rows // 8) * 8
-    packed = jnp.pad(flat.reshape(-1), (0, 2 * ny * rows * 128 - size)).reshape(2 * ny, rows, 128)
+    packed = jnp.pad(flat.reshape(-1), (0, chunks * rows * 128 - size)).reshape(chunks, rows, 128)
     flat = all_reduce(packed).reshape(-1)[:size].reshape(flat.shape)
     factor = 1.0 / math.sqrt(held.shape[0] * height * breadth * blk_count())
     chosen = layer_order[None, :] == jnp.arange(layers, dtype=layer_order.dtype)[:, None]

time: 82 us -> 81.5 us (level)
  no operation moved by 1% of the time
where the time goes in v14:
time: 81.5 us; the launch traced here: 81 us
  Pallas kernels  43.3 us (53%)
  other arithmetic  20.6 us (25%)
  local copies, waits for them, and re-layouts  7.06 us (9%)
  matrix products  4.97 us (6%)
  starting transfers between devices  2.79 us (3%)
  between operations  2.33 us (3%)
    pallas_call x1, Pallas kernels, all_reduce(): pl.pallas_call(reduce_kernel, out_shape=jax.ShapeDtypeStruct(flat.shape,...  27.1 us
    pallas_call x1, Pallas kernels, exchange(): pl.pallas_call(exchange_kernel, out_shape=(jax.ShapeDtypeStruct(grid_shap...  16.2 us
    convert_element_type x3, other arithmetic, shards(): gated = (masked * gelu_pair(preact)[1]).astype(jnp.bfloat16)  4.58 us
    reduce_sum x4, other arithmetic, shards(): jnp.sum(back_in * padded[i:i + height, start:start + breadth].astype(jnp....  3.3 us
    convert_element_type x4, other arithmetic, shards(): mixed = conv_forward(pad_rows(activation), depth).astype(jnp.bfloat16)  2.83 us
    reduce_sum x3, other arithmetic, pick(): jnp.sum(jnp.where(mask, table[None], jnp.zeros((), table.dtype)), axis=1,...  2.67 us
    dot_general x4, matrix products, shards(): jnp.dot(mixed.reshape(rows * span, channels), point, preferred_element_ty...  2.13 us
  transfers between devices with their start and end apart: 2, of which 0 were waited for; matrix products, arithmetic and copies ran while one was open for 21% of the time, Pallas kernels for 33%

profile of v14, /device:TPU:1, one launch (start us, length us, event | category | flops | bytes accessed | tf_op | source)
XLA Modules:
  0.0 81.0 jit_solution(1087867911530735148)
XLA Ops:
  0.6 1.3 %fusion.113 = (s32[1]{0:T(128)}, s32[1]{0:T(128)}) fusion(s32[2]{0:T(128)} %param.7), kind=kLoop, calls=%fused_computation.284 | loop fusion | bytes 16 | tf_op jit(solution)/shard_map/slice | solution.py:260
  3.3 0.8 iota_compare_fusion
  4.1 0.8 select_reduce_fusion.3
  4.8 0.9 %select_reduce_fusion.2 = f32[4,3,3,128]{3,2,1,0:T(4,128)S(1)} fusion(f32[4,3,3,128]{3,0,2,1:T(4,128)} %param.9, pred[4,4]{1,0:T(4,128)(4,1)S(1)} %get-tuple-element.114), kind=kLoop, calls=%fused_computation.209 | loop fusion | flops 32256 | bytes 36880 | tf_op jit(solution)/shard_map/reduce_sum | solution.py:267
  5.7 0.0 copy-start
  5.7 0.9 %slice_bitcast_fusion.2 = (bf16[1,2,12,8,128]{4,3,2,1,0:T(8,128)(2,1)S(1)}, bf16[1,2,12,8,128]{4,3,2,1,0:T(8,128)(2,1)S(1)}) fusion(bf16[2,12,128,128]{3,2,1,0:T(8,128)(2,1)} %bitcast.231), kind=kLoop, calls=%fused_computation.211 | loop fusion | bytes 196608 | tf_op jit(solution)/shard_map/stack | solution.py:252
  6.6 1.1 %select_reduce_fusion.1 = bf16[4,128,128]{2,1,0:T(8,128)(2,1)S(1)} fusion(pred[4,4]{1,0:T(4,128)(4,1)S(1)} %get-tuple-element.114, bf16[4,128,128]{2,1,0:T(8,128)(2,1)} %param.10), kind=kLoop, calls=%fused_computation.173 | loop fusion | flops 458752 | bytes 262160 | tf_op jit(solution)/shard_map/reduce_sum | solution.py:267
  7.7 0.7 pad_maximum_fusion.edges_ref
  8.3 16.2 %shard_map.93 = (bf16[12,128,128]{2,1,0:T(8,128)(2,1)}, bf16[2,12,8,128]{3,2,1,0:T(8,128)(2,1)}, bf16[2,12,8,128]{3,2,1,0:T(8,128)(2,1)}) custom-call(bf16[2,12,128,128]{3,2,1,0:T(8,128)(2,1)} %bitcast.232, bf16[2,2,12,8,128]{4,3,2,1,0:T(8,128)(2,1)} %pad_maximum_fusion.edges_ref), custom_call_target="tpu_custom_call" | custom-call | tf_op jit(solution)/shard_map/pallas_call | solution.py:128
  24.5 0.8 slice_bitcast_fusion.17
  25.4 0.0 copy-done
  25.4 1.1 %bitcast_select_fusion.1 = (bf16[12,128,128]{2,1,0:T(8,128)(2,1)S(1)}, bf16[12,128,128]{2,1,0:T(8,128)(2,1)S(1)}) fusion(bf16[12,128,128]{2,1,0:T(8,128)(2,1)} %get-tuple-element.8, pred[]{:T(512)} %eq.49, bf16[1,2,12,128,128]{4,3,2,1,0:T(8,128)(2,1)S(1)} %copy-done, s32[]{:T(128)S(6)} %select_n.49), kind=kLoop, calls=%fused_computation.193 | loop fusion | flops 393216 | bytes 1572869 | tf_op jit(solution)/shard_map/jit(_where)/select_n | solution.py:256
  26.5 0.2 multiply_convert_fusion
  26.6 0.7 fusion.5
  27.3 0.5 fusion.7
  27.8 0.7 fusion.13
  28.6 0.5 fusion.15
  29.1 0.7 fusion.21
  29.8 0.5 fusion.23
  30.3 0.1 slice_convert_fusion
  30.4 0.7 add_convert_fusion
  31.1 0.7 fusion.29
  31.7 0.3 fusion.99
  32.0 1.5 %collective-permute-start = (bf16[12,128,128]{2,1,0:T(8,128)(2,1)S(1)}, bf16[12,128,128]{2,1,0:T(8,128)(2,1)S(1)}, u32[]{:S(2)}, u32[]{:S(2)}) collective-permute-start(bf16[12,128,128]{2,1,0:T(8,128)(2,1)S(1)} %fusion.99), channel_id=1, source_target_pairs={{0,1},{2,3},{4,5},{6,7},{8,9},{10,11},{12,13},{14,15},{16,17},{18,... | collective-permute-start | bytes 1179656 | tf_op jit(solution)/shard_map/ppermute | solution.py:335
  33.5 0.3 fusion.100
  33.9 0.2 convert_reduce_fusion
  34.1 0.4 convolution_convert_fusion.3
  34.5 0.9 %fusion.72 = (f32[128]{0:T(128)S(1)}, f32[128]{0:T(128)S(1)}, f32[128]{0:T(128)S(1)}, f32[128]{0:T(128)S(1)}, f32[128]{0:T(128)S(1)}, /*index=5*/f32[128]{0:T(12...) fusion(bf16[12,138,128]{2,1,0:T(8,128)(2,1)S(1)} %get-tuple-element.121, ...), kind=kLoop, calls=%fused_computation.138 | loop fusion | flops 5503872 | bytes 2019840 | tf_op jit(solution)/shard_map/reduce_sum | solution.py:323
  35.3 1.5 %fusion.35 = (bf16[12,134,128]{2,1,0:T(8,128)(2,1)S(1)}, f32[12,134,128]{2,1,0:T(8,128)S(1)}) fusion(f32[12,138,128]{2,1,0:T(8,128)S(1)} %get-tuple-element.122, f32[12]{0:T(128)S(1)} %compare_convert_fusion, f32[128]{0:T(128)S(1)} %get-tuple-element.142, f32[128]{0:T(128)S(1)} %get-tuple-element.141, f32[128]{0:T(128)S(1)} %get-tuple-element.140, ...), kind=kLoop, calls=%fused_computation.92 | loop fusion | flops 8438784 | bytes 4582400 | tf_op jit(solution)/shard_map/convert_element_type | solution.py:300
  36.8 0.3 fusion.102
  37.2 0.2 convert_reduce_fusion.1
  37.4 0.4 convolution_convert_fusion.2
  37.8 0.9 %fusion.63 = (f32[128]{0:T(128)S(1)}, f32[128]{0:T(128)S(1)}, f32[128]{0:T(128)S(1)}, f32[128]{0:T(128)S(1)}, f32[128]{0:T(128)S(1)}, /*index=5*/f32[128]{0:T(12...) fusion(bf16[12,140,128]{2,1,0:T(8,128)(2,1)S(1)} %get-tuple-element.119, ...), kind=kLoop, calls=%fused_computation.129 | loop fusion | flops 5503872 | bytes 2019840 | tf_op jit(solution)/shard_map/reduce_sum | solution.py:323
  38.6 1.5 %fusion.41 = (bf16[12,132,128]{2,1,0:T(8,128)(2,1)S(1)}, f32[12,132,128]{2,1,0:T(8,128)S(1)}) fusion(f32[12,140,128]{2,1,0:T(8,128)S(1)} %get-tuple-element.120, f32[12]{0:T(128)S(1)} %compare_convert_fusion, f32[128]{0:T(128)S(1)} %get-tuple-element.83, f32[128]{0:T(128)S(1)} %get-tuple-element.84, f32[128]{0:T(128)S(1)} %get-tuple-element.85, ...), kind=kLoop, calls=%fused_computation.98 | loop fusion | flops 8312832 | bytes 4563968 | tf_op jit(solution)/shard_map/convert_element_type | solution.py:300
  40.2 0.3 fusion.104
  40.5 0.2 convert_reduce_fusion.2
  40.8 0.4 convolution_convert_fusion.1
  41.1 0.7 fusion.54
  41.9 1.5 %fusion.47 = (bf16[12,130,128]{2,1,0:T(8,128)(2,1)S(1)}, f32[12,130,128]{2,1,0:T(8,128)S(1)}) fusion(f32[12,142,128]{2,1,0:T(8,128)S(1)} %get-tuple-element.118, f32[12]{0:T(128)S(1)} %compare_convert_fusion, f32[128]{0:T(128)S(1)} %get-tuple-element.133, f32[128]{0:T(128)S(1)} %get-tuple-element.132, f32[128]{0:T(128)S(1)} %get-tuple-element.131, ...), kind=kLoop, calls=%fused_computation.104 | loop fusion | flops 8186880 | bytes 4545536 | tf_op jit(solution)/shard_map/convert_element_type | solution.py:300
  43.4 0.3 fusion.106
  43.7 0.2 convert_reduce_fusion.3
  44.0 0.4 convolution_convert_fusion
  44.3 0.9 %fusion.89 = (f32[128]{0:T(128)S(1)}, f32[128]{0:T(128)S(1)}, f32[128]{0:T(128)S(1)}, f32[128]{0:T(128)S(1)}, f32[128]{0:T(128)S(1)}, /*index=5*/f32[128]{0:T(12...) fusion(bf16[12,144,128]{2,1,0:T(8,128)(2,1)S(1)} %multiply_convert_fusion, ...), kind=kLoop, calls=%fused_computation.155 | loop fusion | flops 5503872 | bytes 2019840 | tf_op jit(solution)/shard_map/reduce_sum | solution.py:323
  45.5 0.3 maximum_maximum_fusion
  45.8 0.1 reshape.182
  45.9 0.8 pad.48
  46.7 27.1 %shard_map.94 = f32[32,24,128]{2,1,0:T(8,128)} custom-call(f32[32,24,128]{2,1,0:T(8,128)} %bitcast.233), custom_call_target="tpu_custom_call" | custom-call | tf_op jit(solution)/shard_map/pallas_call | solution.py:225
  73.8 1.0 %slice.830 = f32[23,24,128]{2,1,0:T(8,128)S(1)} slice(f32[32,24,128]{2,1,0:T(8,128)} %shard_map.94), slice={[0:23], [0:24], [0:128]} | slice | bytes 565248 | tf_op jit(solution)/shard_map/slice | solution.py:348
  74.8 0.1 broadcast_in_dim.106
  74.9 0.8 %select_reduce_fusion = f32[4,17664]{1,0:T(4,128)S(1)} fusion(f32[4,17664]{1,0:T(4,128)S(1)} %broadcast_in_dim.106, pred[4,4]{1,0:T(4,128)(4,1)S(1)} %get-tuple-element.113), kind=kLoop, calls=%fused_computation.49 | loop fusion | flops 494592 | bytes 565264 | tf_op jit(solution)/shard_map/reduce_sum | solution.py:351
  75.7 0.0 collective-permute-done
  75.7 0.9 %select_bitcast_fusion.1 = (bf16[1,12,128,128]{3,2,1,0:T(8,128)(2,1)S(1)}, bf16[12,128,128]{2,1,0:T(8,128)(2,1)S(1)}) fusion(bf16[12,128,128]{2,1,0:T(8,128)(2,1)S(1)} %collective-permute-done, pred[]{:T(512)} %eq.49, f32[12]{0:T(128)S(1)} %compare_convert_fusion, f32[128]{0:T(128)S(1)} %get-tuple-element.101, f32[128]{0:T(128)S(1)} %get-tuple-element.102, ...), kind=kLoop, calls=%fused_computation.195 | loop fusion | flops 5898240 | bytes 3568641 | tf_op jit(solution)/shard_map/stack | solution.py:339
  76.7 1.3 %collective-permute-start.1 = (bf16[12,128,128]{2,1,0:T(8,128)(2,1)S(1)}, bf16[12,128,128]{2,1,0:T(8,128)(2,1)S(1)}, u32[]{:S(2)}, u32[]{:S(2)}) collective-permute-start(bf16[12,128,128]{2,1,0:T(8,128)(2,1)S(1)} %get-tuple-element.51), channel_id=1, source_target_pairs={{1,0},{3,2},{5,4},{7,6},{9,8},{11,10},{13,12},{15,14},{17,16},{19,... | collective-permute-start | bytes 1179656 | tf_op jit(solution)/shard_map/ppermute | solution.py:336
  78.0 0.1 broadcast_multiply_fusion
  78.1 0.6 slice.941
  78.7 0.6 slice.939
  79.3 0.7 copy.30
  80.0 0.0 collective-permute-done.1
  80.1 0.9 %maximum_bitcast_fusion = bf16[1,2,12,128,128]{4,3,2,1,0:T(8,128)(2,1)} fusion(bf16[1,12,128,128]{3,2,1,0:T(8,128)(2,1)S(1)} %select_bitcast_fusion, bf16[1,12,128,128]{3,2,1,0:T(8,128)(2,1)S(1)} %get-tuple-element.50), kind=kLoop, calls=%fused_computation.168 | loop fusion | flops 393216 | bytes 1572864 | tf_op jit(solution)/shard_map/broadcast_in_dim | solution.py:339
  (29 shorter events, 0.3 us)
Async XLA Ops:
  5.7 19.7 %copy-start = (bf16[1,2,12,128,128]{4,3,2,1,0:T(8,128)(2,1)S(1)}, bf16[1,2,12,128,128]{4,3,2,1,0:T(8,128)(2,1)}, u32[]{:S(2)}) copy-start(bf16[1,2,12,128,128]{4,3,2,1,0:T(8,128)(2,1)} %param.6) | copy-start | bytes 2359300
  32.0 43.7 %collective-permute-start = (bf16[12,128,128]{2,1,0:T(8,128)(2,1)S(1)}, bf16[12,128,128]{2,1,0:T(8,128)(2,1)S(1)}, u32[]{:S(2)}, u32[]{:S(2)}) collective-permute-start(bf16[12,128,128]{2,1,0:T(8,128)(2,1)S(1)} %fusion.99), channel_id=1, source_target_pairs={{0,1},{2,3},{4,5},{6,7},{8,9},{10,11},{12,13},{14,15},{16,17},{18,... | collective-permute-start | bytes 1179656 | tf_op jit(solution)/shard_map/ppermute | solution.py:335
  76.7 3.3 %collective-permute-start.1 = (bf16[12,128,128]{2,1,0:T(8,128)(2,1)S(1)}, bf16[12,128,128]{2,1,0:T(8,128)(2,1)S(1)}, u32[]{:S(2)}, u32[]{:S(2)}) collective-permute-start(bf16[12,128,128]{2,1,0:T(8,128)(2,1)S(1)} %get-tuple-element.51), channel_id=1, source_target_pairs={{1,0},{3,2},{5,4},{7,6},{9,8},{11,10},{13,12},{15,14},{17,16},{19,... | collective-permute-start | bytes 1179656 | tf_op jit(solution)/shard_map/ppermute | solution.py:336

commit v15 on v14

--- a/solution.py
+++ b/solution.py
@@ -157,8 +157,8 @@
     return values[0]
 
 
-def reduce_kernel(flat_ref, out_ref, part, got_a, got_z, got_b,
-                  send_sem, recv_a, recv_z, recv_b):
+def reduce_kernel(flat_ref, piece_ref, out_ref, other_ref, part, got_a, got_z, got_b, got_piece,
+                  send_sem, recv_a, recv_z, recv_b, piece_send, piece_recv):
     core = lax.axis_index("pipe")
     my_y, my_z, my_x = (lax.axis_index(name) for name in ("y", "z", "x"))
     ny, nx = lax.axis_size("y"), lax.axis_size("x")
@@ -180,6 +180,12 @@
     pl.semaphore_wait(barrier, count)
 
     sends = iter(range(send_sem.shape[0]))
+
+    handover = pltpu.make_async_remote_copy(
+        src_ref=piece_ref, dst_ref=got_piece, send_sem=piece_send.at[0], recv_sem=piece_recv.at[0],
+        device_id=tuple(row) + (1 - core,), device_id_type=MESH_ID,
+    )
+    handover.start()
 
     def spread(axis, src_of, dst, sems):
         mine = places[axis]
@@ -214,9 +220,11 @@
     got_b[places["py"]] = part[...]
     spread("py", lambda j: part, got_b, recv_b)
     out_ref[...] = got_b[...]
-
-
-def all_reduce(flat):
+    handover.wait()
+    other_ref[...] = got_piece[...]
+
+
+def all_reduce(flat, piece):
     chunks, rows, lanes = flat.shape
     nz = lax.axis_size("z")
     chunk = (rows, lanes)
@@ -224,21 +232,27 @@
     vmem = pl.BlockSpec(memory_space=pltpu.VMEM)
     return pl.pallas_call(
         reduce_kernel,
-        out_shape=jax.ShapeDtypeStruct(flat.shape, flat.dtype),
-        in_specs=[vmem],
-        out_specs=vmem,
+        out_shape=(
+            jax.ShapeDtypeStruct(flat.shape, flat.dtype),
+            jax.ShapeDtypeStruct(piece.shape, piece.dtype),
+        ),
+        in_specs=[vmem, vmem],
+        out_specs=(vmem, vmem),
         scratch_shapes=[
             pltpu.VMEM(chunk, flat.dtype),
             pltpu.VMEM((chunks,) + chunk, flat.dtype),
             pltpu.VMEM((nz,) + chunk, flat.dtype),
             pltpu.VMEM((chunks,) + chunk, flat.dtype),
+            pltpu.VMEM(piece.shape, piece.dtype),
             pltpu.SemaphoreType.DMA((sends,)),
             pltpu.SemaphoreType.DMA((chunks,)),
             pltpu.SemaphoreType.DMA((nz,)),
             pltpu.SemaphoreType.DMA((chunks,)),
+            pltpu.SemaphoreType.DMA((1,)),
+            pltpu.SemaphoreType.DMA((1,)),
         ],
         compiler_params=pltpu.CompilerParams(collective_id=1, has_side_effects=True),
-    )(flat)
+    )(flat, piece)
 
 
 def shards(endpoints, row_counts, layer_order, depth_weight, point_weight, point_bias):
@@ -332,11 +346,6 @@
         cotangent = ((masked[:, 1:-1] + earlier) * live).astype(jnp.bfloat16)
     input_grad = cotangent
 
-    got_outcome = lax.ppermute(outcome, "pipe", [(0, 1)])
-    got_grad = lax.ppermute(input_grad, "pipe", [(1, 0)])
-    first = jnp.where(core == 0, input_grad, got_outcome)
-    second = jnp.where(core == 0, got_grad, outcome)
-    result = jnp.stack([first, second])[None]
 
     pieces = (jnp.stack(depth_terms), jnp.stack(point_terms), jnp.stack(bias_terms))
     flat = jnp.concatenate([piece.reshape(layers, -1) for piece in pieces], axis=1)
@@ -345,7 +354,12 @@
     rows = -(-size // (chunks * 128))
     rows = -(-rows // 8) * 8
     packed = jnp.pad(flat.reshape(-1), (0, chunks * rows * 128 - size)).reshape(chunks, rows, 128)
-    flat = all_reduce(packed).reshape(-1)[:size].reshape(flat.shape)
+    piece = jnp.where(core == 0, outcome, input_grad)
+    reduced, other = all_reduce(packed, piece)
+    flat = reduced.reshape(-1)[:size].reshape(flat.shape)
+    first = jnp.where(core == 0, input_grad, other)
+    second = jnp.where(core == 0, other, outcome)
+    result = jnp.stack([first, second])[None]
     factor = 1.0 / math.sqrt(held.shape[0] * height * breadth * blk_count())
     chosen = layer_order[None, :] == jnp.arange(layers, dtype=layer_order.dtype)[:, None]
     flat = jnp.sum(jnp.where(chosen[:, :, None], flat[None, :, :], 0.0), axis=1) * factor

time: 81.5 us -> 82 us (level)
  local copies, waits for them, and re-layouts: 7.06 us -> 9.95 us
  starting transfers between devices: 2.79 us -> 0 us
  matrix products: 4.97 us -> 6.15 us
    unnamed x4 -> x52, local copies, waits for them, and re-layouts: 0.74 us -> 5.15 us
    select_n x0 -> x1, other arithmetic: none -> 3.1 us  [shards(): piece = jnp.where(core == 0, outcome, input_grad)]
    ppermute x2 -> x0, starting transfers between devices: 2.79 us -> none  [the longest x1 1.47 us: shards(): got_outcome = lax.ppermute(outcome, 'pipe', [(0, 1)])]
    reduce_sum x3, other arithmetic: 2.67 us -> 0.38 us  [pick(): jnp.sum(jnp.where(mask, table[None], jnp.zeros((), table.dtype)), axis=1,...]
    dot_general x4, matrix products: 2.13 us -> 3.31 us  [shards(): jnp.dot(mixed.reshape(rows * span, channels), point, preferred_element_ty...]
    another operation x2 -> x1, other arithmetic: 0.99 us -> 0.07 us  [shards(): result = jnp.stack([first, second])[None]]
  transfers between devices with their start and end apart: 2 -> 0, of which waited for: 0 -> 0; matrix products, arithmetic and copies ran while one was open for 21% -> 0% of each run, Pallas kernels for 33% -> 0%
where the time goes in v15:
time: 82 us; the launch traced here: 81.5 us
  Pallas kernels  42.8 us (52%)
  other arithmetic  20.2 us (25%)
  local copies, waits for them, and re-layouts  9.95 us (12%)
  matrix products  6.15 us (8%)
  between operations  2.46 us (3%)
    pallas_call x1, Pallas kernels, all_reduce(): pl.pallas_call(reduce_kernel, out_shape=(jax.ShapeDtypeStruct(flat.shape,...  26.6 us
    pallas_call x1, Pallas kernels, exchange(): pl.pallas_call(exchange_kernel, out_shape=(jax.ShapeDtypeStruct(grid_shap...  16.2 us
    convert_element_type x3, other arithmetic, shards(): gated = (masked * gelu_pair(preact)[1]).astype(jnp.bfloat16)  5.34 us
    unnamed x52, local copies, waits for them, and re-layouts  5.15 us
    dot_general x4, matrix products, shards(): jnp.dot(mixed.reshape(rows * span, channels), point, preferred_element_ty...  3.31 us
    reduce_sum x4, other arithmetic, shards(): jnp.sum(back_in * padded[i:i + height, start:start + breadth].astype(jnp....  3.3 us
    select_n x1, other arithmetic, shards(): piece = jnp.where(core == 0, outcome, input_grad)  3.1 us
    convert_element_type x4, other arithmetic, shards(): mixed = conv_forward(pad_rows(activation), depth).astype(jnp.bfloat16)  2.82 us

profile of v15, /device:TPU:1, one launch (start us, length us, event | category | flops | bytes accessed | tf_op | source)
XLA Modules:
  0.0 81.5 jit_solution(12768855514313294503)
XLA Ops:
  0.6 0.9 %slice_bitcast_fusion.2 = (bf16[1,2,12,8,128]{4,3,2,1,0:T(8,128)(2,1)S(1)}, bf16[1,2,12,8,128]{4,3,2,1,0:T(8,128)(2,1)S(1)}) fusion(bf16[2,12,128,128]{3,2,1,0:T(8,128)(2,1)} %bitcast.231), kind=kLoop, calls=%fused_computation.212 | loop fusion | bytes 196608 | tf_op jit(solution)/shard_map/stack | solution.py:266
  1.6 0.7 pad_maximum_fusion.edges_ref
  2.2 16.2 %shard_map.93 = (bf16[12,128,128]{2,1,0:T(8,128)(2,1)}, bf16[2,12,8,128]{3,2,1,0:T(8,128)(2,1)}, bf16[2,12,8,128]{3,2,1,0:T(8,128)(2,1)}) custom-call(bf16[2,12,128,128]{3,2,1,0:T(8,128)(2,1)} %bitcast.232, bf16[2,2,12,8,128]{4,3,2,1,0:T(8,128)(2,1)} %pad_maximum_fusion.edges_ref), custom_call_target="tpu_custom_call" | custom-call | tf_op jit(solution)/shard_map/pallas_call | solution.py:128
  18.4 1.1 %bitcast_select_fusion.1 = (bf16[12,128,128]{2,1,0:T(8,128)(2,1)S(1)}, bf16[12,128,128]{2,1,0:T(8,128)(2,1)S(1)}) fusion(bf16[12,128,128]{2,1,0:T(8,128)(2,1)} %get-tuple-element.10, pred[]{:T(512)} %eq.50, bf16[1,2,12,128,128]{4,3,2,1,0:T(8,128)(2,1)S(1)} %copy-done.8, s32[]{:T(128)S(6)} %select_n.53), kind=kLoop, calls=%fused_computation.193 | loop fusion | flops 393216 | bytes 1572869 | tf_op jit(solution)/shard_map/jit(_where)/select_n | solution.py:270
  19.6 0.6 fusion.114
  21.5 0.2 multiply_convert_fusion
  21.6 0.1 iota_compare_fusion
  21.7 0.1 select_reduce_fusion.2
  21.9 0.7 fusion.5
  22.6 0.2 copy-done.18
  22.8 0.1 select_reduce_fusion.1
  23.0 0.1 select_reduce_fusion.3
  23.1 0.5 fusion.7
  23.6 0.7 fusion.13
  24.3 0.5 fusion.15
  24.8 0.3 copy-done.13
  25.1 0.7 fusion.21
  25.8 0.5 fusion.23
  26.3 0.3 copy-done.15
  26.6 0.7 add_convert_fusion
  27.3 1.8 %fusion.29 = (bf16[12,136,128]{2,1,0:T(8,128)(2,1)S(1)}, f32[12,136,128]{2,1,0:T(8,128)}, f32[12,136,128]{2,1,0:T(8,128)S(1)}, f32[12,136,128]{2,1,0:T(8,128)}) fusion(f32[12]{0:T(128)S(1)} %compare_convert_fusion, bf16[12,4,128]{2,1,0:T(4,128)(2,1)S(1)} %slice.837, bf16[12,128,128]{2,1,0:T(8,128)(2,1)S(1)} %get-tuple-element.65, ...), kind=kOutput, calls=%fused_computation.86 | convolution fusion | flops 57237504 | bytes 3793920 | tf_op jit(solution)/shard_map/dot_general | solution.py:293
  29.1 0.4 convolution_convert_fusion.3
  29.5 0.4 copy-done.4
  29.9 1.5 %fusion.35 = (bf16[12,134,128]{2,1,0:T(8,128)(2,1)S(1)}, f32[12,134,128]{2,1,0:T(8,128)S(1)}) fusion(f32[12,138,128]{2,1,0:T(8,128)S(1)} %get-tuple-element.129, f32[12]{0:T(128)S(1)} %compare_convert_fusion, f32[128]{0:T(128)S(1)} %get-tuple-element.147, f32[128]{0:T(128)S(1)} %get-tuple-element.146, f32[128]{0:T(128)S(1)} %get-tuple-element.145, ...), kind=kLoop, calls=%fused_computation.92 | loop fusion | flops 8438784 | bytes 4582400 | tf_op jit(solution)/shard_map/convert_element_type | solution.py:314
  31.4 0.4 convolution_convert_fusion.2
  31.8 1.5 %fusion.41 = (bf16[12,132,128]{2,1,0:T(8,128)(2,1)S(1)}, f32[12,132,128]{2,1,0:T(8,128)S(1)}) fusion(f32[12,140,128]{2,1,0:T(8,128)S(1)} %get-tuple-element.127, f32[12]{0:T(128)S(1)} %compare_convert_fusion, f32[128]{0:T(128)S(1)} %get-tuple-element.90, f32[128]{0:T(128)S(1)} %get-tuple-element.91, f32[128]{0:T(128)S(1)} %get-tuple-element.92, ...), kind=kLoop, calls=%fused_computation.98 | loop fusion | flops 8312832 | bytes 4563968 | tf_op jit(solution)/shard_map/convert_element_type | solution.py:314
  33.3 0.4 convolution_convert_fusion.1
  33.7 2.3 %fusion.47 = (bf16[12,130,128]{2,1,0:T(8,128)(2,1)S(1)}, f32[12,130,128]{2,1,0:T(8,128)}) fusion(f32[12,142,128]{2,1,0:T(8,128)S(1)} %get-tuple-element.125, f32[12]{0:T(128)S(1)} %compare_convert_fusion, f32[128]{0:T(128)S(1)} %get-tuple-element.138, f32[128]{0:T(128)S(1)} %get-tuple-element.137, f32[128]{0:T(128)S(1)} %get-tuple-element.136, ...), kind=kLoop, calls=%fused_computation.104 | loop fusion | flops 8186880 | bytes 4545536 | tf_op jit(solution)/shard_map/convert_element_type | solution.py:314
  36.0 0.4 convolution_convert_fusion
  36.4 0.9 %fusion.89 = (f32[128]{0:T(128)S(1)}, f32[128]{0:T(128)S(1)}, f32[128]{0:T(128)S(1)}, f32[128]{0:T(128)S(1)}, f32[128]{0:T(128)S(1)}, /*index=5*/f32[128]{0:T(12...) fusion(bf16[12,144,128]{2,1,0:T(8,128)(2,1)S(1)} %multiply_convert_fusion, ...), kind=kLoop, calls=%fused_computation.155 | loop fusion | flops 5503872 | bytes 2019840 | tf_op jit(solution)/shard_map/reduce_sum | solution.py:337
  37.3 0.7 fusion.54
  38.1 0.9 %fusion.63 = (f32[128]{0:T(128)S(1)}, f32[128]{0:T(128)S(1)}, f32[128]{0:T(128)S(1)}, f32[128]{0:T(128)S(1)}, f32[128]{0:T(128)S(1)}, /*index=5*/f32[128]{0:T(12...) fusion(bf16[12,140,128]{2,1,0:T(8,128)(2,1)S(1)} %get-tuple-element.126, ...), kind=kLoop, calls=%fused_computation.129 | loop fusion | flops 5503872 | bytes 2019840 | tf_op jit(solution)/shard_map/reduce_sum | solution.py:337
  39.1 0.9 %fusion.72 = (f32[128]{0:T(128)S(1)}, f32[128]{0:T(128)S(1)}, f32[128]{0:T(128)S(1)}, f32[128]{0:T(128)S(1)}, f32[128]{0:T(128)S(1)}, /*index=5*/f32[128]{0:T(12...) fusion(bf16[12,138,128]{2,1,0:T(8,128)(2,1)S(1)} %get-tuple-element.128, ...), kind=kLoop, calls=%fused_computation.138 | loop fusion | flops 5503872 | bytes 2019840 | tf_op jit(solution)/shard_map/reduce_sum | solution.py:337
  40.1 0.1 copy-done.14
  40.2 0.3 fusion.104
  40.6 0.7 copy-done.3
  41.2 0.1 copy-done.12
  41.4 0.3 fusion.106
  41.7 0.7 copy-done.16
  42.4 0.3 fusion.102
  42.7 0.7 copy-done.5
  43.4 0.1 copy-done.10
  43.5 0.3 fusion.100
  43.9 0.2 convert_reduce_fusion.3
  44.1 0.2 convert_reduce_fusion.2
  44.3 0.2 convert_reduce_fusion.1
  44.5 0.2 convert_reduce_fusion
  44.7 0.3 maximum_maximum_fusion
  45.0 0.1 reshape.182
  45.2 0.8 pad.48
  45.9 0.1 slice_convert_fusion
  46.0 0.4 copy-done.6
  46.4 0.3 copy-done.7
  46.7 3.1 %broadcast_select_fusion = (bf16[12,128,128]{2,1,0:T(8,128)(2,1)}, bf16[12,128,128]{2,1,0:T(8,128)(2,1)S(1)}, bf16[12,128,128]{2,1,0:T(8,128)(2,1)S(1)}) fusion(pred[]{:T(512)} %eq.50, f32[12]{0:T(128)S(1)} %compare_convert_fusion, f32[128]{0:T(128)S(1)} %get-tuple-element.108, f32[128]{0:T(128)S(1)} %get-tuple-element.109, f32[128]{0:T(128)S(1)} %get-tuple-element.110, ...), kind=kLoop, calls=%fused_computation.200 | loop fusion | flops 6684672 | bytes 5927937 | tf_op jit(solution)/shard_map/jit(_where)/select_n | solution.py:357
  49.8 26.6 %shard_map.94 = (f32[32,24,128]{2,1,0:T(8,128)}, bf16[12,128,128]{2,1,0:T(8,128)(2,1)}) custom-call(f32[32,24,128]{2,1,0:T(8,128)} %bitcast.233, bf16[12,128,128]{2,1,0:T(8,128)(2,1)} %get-tuple-element.54.piece_ref), custom_call_target="tpu_custom_call" | custom-call | tf_op jit(solution)/shard_map/pallas_call | solution.py:233
  76.4 1.0 %slice.830 = f32[23,24,128]{2,1,0:T(8,128)S(1)} slice(f32[32,24,128]{2,1,0:T(8,128)} %get-tuple-element.13), slice={[0:23], [0:24], [0:128]} | slice | bytes 565248 | tf_op jit(solution)/shard_map/slice | solution.py:359
  77.4 0.1 broadcast_in_dim.106
  77.5 0.8 %select_reduce_fusion = f32[4,17664]{1,0:T(4,128)S(1)} fusion(f32[4,17664]{1,0:T(4,128)S(1)} %broadcast_in_dim.106, pred[4,4]{1,0:T(4,128)(4,1)S(1)} %get-tuple-element.120), kind=kLoop, calls=%fused_computation.49 | loop fusion | flops 494592 | bytes 565264 | tf_op jit(solution)/shard_map/reduce_sum | solution.py:365
  78.3 0.1 broadcast_multiply_fusion
  78.5 0.7 copy.30
  79.2 0.2 copy-done.17
  79.4 0.9 %maximum_bitcast_fusion = bf16[1,2,12,128,128]{4,3,2,1,0:T(8,128)(2,1)} fusion(bf16[1,12,128,128]{3,2,1,0:T(8,128)(2,1)S(1)} %get-tuple-element.71, bf16[1,12,128,128]{3,2,1,0:T(8,128)(2,1)S(1)} %get-tuple-element.70), kind=kLoop, calls=%fused_computation.168 | loop fusion | flops 393216 | bytes 1572864 | tf_op jit(solution)/shard_map/broadcast_in_dim | solution.py:362
  80.4 0.6 slice.939
  81.0 0.6 slice.941
  (67 shorter events, 0.5 us)
Async XLA Ops:
  0.6 17.8 %copy-start.8 = (bf16[1,2,12,128,128]{4,3,2,1,0:T(8,128)(2,1)S(1)}, bf16[1,2,12,128,128]{4,3,2,1,0:T(8,128)(2,1)}, u32[]{:S(2)}) copy-start(bf16[1,2,12,128,128]{4,3,2,1,0:T(8,128)(2,1)} %param.6) | copy-start | bytes 2359300
  18.4 1.1 %copy-start.19 = (bf16[2,12,8,128]{3,2,1,0:T(8,128)(2,1)S(1)}, bf16[2,12,8,128]{3,2,1,0:T(8,128)(2,1)}, u32[]{:S(2)}) copy-start(bf16[2,12,8,128]{3,2,1,0:T(8,128)(2,1)} %get-tuple-element.9) | copy-start | bytes 147460
  18.4 1.1 %copy-start.20 = (bf16[2,12,8,128]{3,2,1,0:T(8,128)(2,1)S(1)}, bf16[2,12,8,128]{3,2,1,0:T(8,128)(2,1)}, u32[]{:S(2)}) copy-start(bf16[2,12,8,128]{3,2,1,0:T(8,128)(2,1)} %get-tuple-element.11) | copy-start | bytes 147460
  18.4 1.1 %copy-start.23 = (s32[2]{0:T(128)S(1)}, s32[2]{0:T(128)}, u32[]{:S(2)}) copy-start(s32[2]{0:T(128)} %param.7) | copy-start | bytes 28
  19.5 2.1 %copy-start.24 = (s32[4]{0:T(128)S(1)}, s32[4]{0:T(128)}, u32[]{:S(2)}) copy-start(s32[4]{0:T(128)} %param.8) | copy-start | bytes 52
  19.5 2.2 %copy-start.21 = (f32[4,3,3,128]{3,0,2,1:T(4,128)S(1)}, f32[4,3,3,128]{3,0,2,1:T(4,128)}, u32[]{:S(2)}) copy-start(f32[4,3,3,128]{3,0,2,1:T(4,128)} %param.9) | copy-start | bytes 55300
  21.9 0.9 %copy-start.18 = (bf16[4,128,128]{2,1,0:T(8,128)(2,1)S(1)}, bf16[4,128,128]{2,1,0:T(8,128)(2,1)}, u32[]{:S(2)}) copy-start(bf16[4,128,128]{2,1,0:T(8,128)(2,1)} %param.10) | copy-start | bytes 393220
  21.9 1.1 %copy-start.22 = (f32[4,128]{1,0:T(4,128)S(1)}, f32[4,128]{1,0:T(4,128)}, u32[]{:S(2)}) copy-start(f32[4,128]{1,0:T(4,128)} %param.11) | copy-start | bytes 6148
  22.8 0.8 copy-start.11
  24.3 0.8 copy-start.13
  25.8 0.8 copy-start.15
  27.2 1.9 %copy-start.9 = (bf16[12,136,128]{2,1,0:T(8,128)(2,1)}, bf16[12,136,128]{2,1,0:T(8,128)(2,1)S(1)}, u32[]{:S(2)}) copy-start(bf16[12,136,128]{2,1,0:T(8,128)(2,1)S(1)} %add_convert_fusion) | copy-start | bytes 1253380
  29.1 0.8 copy-start.4
  33.3 2.7 %copy-start = (bf16[12,132,128]{2,1,0:T(8,128)(2,1)}, bf16[12,132,128]{2,1,0:T(8,128)(2,1)S(1)}, u32[]{:S(2)}) copy-start(bf16[12,132,128]{2,1,0:T(8,128)(2,1)S(1)} %get-tuple-element.59) | copy-start | bytes 1216516
  36.0 1.2 %copy-start.2 = (bf16[12,130,128]{2,1,0:T(8,128)(2,1)}, bf16[12,130,128]{2,1,0:T(8,128)(2,1)S(1)}, u32[]{:S(2)}) copy-start(bf16[12,130,128]{2,1,0:T(8,128)(2,1)S(1)} %get-tuple-element.57) | copy-start | bytes 1198084
  39.1 1.0 %copy-start.1 = (bf16[12,132,128]{2,1,0:T(8,128)(2,1)S(1)}, bf16[12,132,128]{2,1,0:T(8,128)(2,1)}, u32[]{:S(2)}) copy-start(bf16[12,132,128]{2,1,0:T(8,128)(2,1)} %copy-done) | copy-start | bytes 1216516
  39.1 1.1 %copy-start.14 = (bf16[12,140,128]{2,1,0:T(8,128)(2,1)S(1)}, bf16[12,140,128]{2,1,0:T(8,128)(2,1)}, u32[]{:S(2)}) copy-start(bf16[12,140,128]{2,1,0:T(8,128)(2,1)} %copy-done.13) | copy-start | bytes 1290244
  40.2 1.0 %copy-start.3 = (bf16[12,130,128]{2,1,0:T(8,128)(2,1)S(1)}, bf16[12,130,128]{2,1,0:T(8,128)(2,1)}, u32[]{:S(2)}) copy-start(bf16[12,130,128]{2,1,0:T(8,128)(2,1)} %copy-done.2) | copy-start | bytes 1198084
  40.2 1.1 %copy-start.12 = (bf16[12,142,128]{2,1,0:T(8,128)(2,1)S(1)}, bf16[12,142,128]{2,1,0:T(8,128)(2,1)}, u32[]{:S(2)}) copy-start(bf16[12,142,128]{2,1,0:T(8,128)(2,1)} %copy-done.11) | copy-start | bytes 1308676
  41.4 1.0 %copy-start.16 = (bf16[12,138,128]{2,1,0:T(8,128)(2,1)S(1)}, bf16[12,138,128]{2,1,0:T(8,128)(2,1)}, u32[]{:S(2)}) copy-start(bf16[12,138,128]{2,1,0:T(8,128)(2,1)} %copy-done.15) | copy-start | bytes 1271812
  42.4 1.0 %copy-start.5 = (bf16[12,136,128]{2,1,0:T(8,128)(2,1)S(1)}, bf16[12,136,128]{2,1,0:T(8,128)(2,1)}, u32[]{:S(2)}) copy-start(bf16[12,136,128]{2,1,0:T(8,128)(2,1)} %copy-done.4) | copy-start | bytes 1253380
  42.4 1.1 %copy-start.10 = (bf16[12,136,128]{2,1,0:T(8,128)(2,1)S(1)}, bf16[12,136,128]{2,1,0:T(8,128)(2,1)}, u32[]{:S(2)}) copy-start(bf16[12,136,128]{2,1,0:T(8,128)(2,1)} %copy-done.9) | copy-start | bytes 1253380
  45.1 1.3 %copy-start.6 = (f32[12,136,128]{2,1,0:T(8,128)S(1)}, f32[12,136,128]{2,1,0:T(8,128)}, u32[]{:S(2)}) copy-start(f32[12,136,128]{2,1,0:T(8,128)} %get-tuple-element.64) | copy-start | bytes 2506756
  45.1 1.5 %copy-start.7 = (f32[12,136,128]{2,1,0:T(8,128)S(1)}, f32[12,136,128]{2,1,0:T(8,128)}, u32[]{:S(2)}) copy-start(f32[12,136,128]{2,1,0:T(8,128)} %get-tuple-element.130) | copy-start | bytes 2506756
  78.3 1.0 %copy-start.17 = (bf16[12,128,128]{2,1,0:T(8,128)(2,1)S(1)}, bf16[12,128,128]{2,1,0:T(8,128)(2,1)}, u32[]{:S(2)}) copy-start(bf16[12,128,128]{2,1,0:T(8,128)(2,1)} %get-tuple-element.12) | copy-start | bytes 1179652

commit v16 on v14

--- a/solution.py
+++ b/solution.py
@@ -257,8 +257,8 @@
     x_wide = jnp.concatenate([lo[0], x_in, hi[0]], axis=1)
     g_wide = jnp.concatenate([lo[1][:, X_HALO - G_HALO :], g_in, hi[1][:, :G_HALO]], axis=1)
 
-    counts = jnp.where(core == 0, row_counts[0:1], row_counts[1:2])
-    live = (jnp.arange(height)[:, None, None] < counts[None, None, :]).astype(jnp.float32)
+    both = (jnp.arange(height, dtype=row_counts.dtype)[:, None] < row_counts[None, :]).astype(jnp.float32)
+    live = jnp.where(core == 0, both[:, 0], both[:, 1])[:, None, None]
 
     placed = layer_order[:, None] == jnp.arange(layers, dtype=layer_order.dtype)[None, :]
 

time: 81.5 us -> 79.5 us (0.975)
  local copies, waits for them, and re-layouts: 7.06 us -> 5.75 us
  between operations: 2.33 us -> 1.03 us
    slice x1 -> x0, local copies, waits for them, and re-layouts: 1.31 us -> none  [shards(): counts = jnp.where(core == 0, row_counts[0:1], row_counts[1:2])]
  transfers between devices with their start and end apart: 2 -> 2, of which waited for: 0 -> 0; matrix products, arithmetic and copies ran while one was open for 21% -> 21% of each run, Pallas kernels for 33% -> 34%
where the time goes in v16:
time: 79.5 us; the launch traced here: 79.1 us
  Pallas kernels  43.2 us (54%)
  other arithmetic  21.3 us (27%)
  local copies, waits for them, and re-layouts  5.75 us (7%)
  matrix products  4.98 us (6%)
  starting transfers between devices  2.79 us (4%)
  between operations  1.03 us (1%)
    pallas_call x1, Pallas kernels, all_reduce(): pl.pallas_call(reduce_kernel, out_shape=jax.ShapeDtypeStruct(flat.shape,...  27.1 us
    pallas_call x1, Pallas kernels, exchange(): pl.pallas_call(exchange_kernel, out_shape=(jax.ShapeDtypeStruct(grid_shap...  16.2 us
    convert_element_type x3, other arithmetic, shards(): gated = (masked * gelu_pair(preact)[1]).astype(jnp.bfloat16)  4.58 us
    reduce_sum x4, other arithmetic, shards(): jnp.sum(back_in * padded[i:i + height, start:start + breadth].astype(jnp....  3.3 us
    convert_element_type x4, other arithmetic, shards(): mixed = conv_forward(pad_rows(activation), depth).astype(jnp.bfloat16)  2.83 us
    reduce_sum x3, other arithmetic, pick(): jnp.sum(jnp.where(mask, table[None], jnp.zeros((), table.dtype)), axis=1,...  2.67 us
    dot_general x4, matrix products, shards(): jnp.dot(mixed.reshape(rows * span, channels), point, preferred_element_ty...  2.14 us
  transfers between devices with their start and end apart: 2, of which 0 were waited for; matrix products, arithmetic and copies ran while one was open for 21% of the time, Pallas kernels for 34%

profile of v16, /device:TPU:1, one launch (start us, length us, event | category | flops | bytes accessed | tf_op | source)
XLA Modules:
  0.0 79.1 jit_solution(721755219125184236)
XLA Ops:
  0.6 0.7 compare_convert_fusion
  1.4 0.8 %iota_compare_fusion = (pred[4,4]{1,0:T(4,128)(4,1)S(1)}, pred[4,4]{1,0:T(4,128)(4,1)S(1)}) fusion(s32[4]{0:T(128)} %param.8), kind=kLoop, calls=%fused_computation.241 | loop fusion | flops 32 | bytes 48 | tf_op jit(solution)/shard_map/eq | solution.py:350
  2.2 0.8 select_reduce_fusion.3
  2.9 0.9 %select_reduce_fusion.2 = f32[4,3,3,128]{3,2,1,0:T(4,128)S(1)} fusion(f32[4,3,3,128]{3,0,2,1:T(4,128)} %param.9, pred[4,4]{1,0:T(4,128)(4,1)S(1)} %get-tuple-element.114), kind=kLoop, calls=%fused_computation.209 | loop fusion | flops 32256 | bytes 36880 | tf_op jit(solution)/shard_map/reduce_sum | solution.py:267
  3.8 0.0 copy-start
  3.8 0.9 %slice_bitcast_fusion.2 = (bf16[1,2,12,8,128]{4,3,2,1,0:T(8,128)(2,1)S(1)}, bf16[1,2,12,8,128]{4,3,2,1,0:T(8,128)(2,1)S(1)}) fusion(bf16[2,12,128,128]{3,2,1,0:T(8,128)(2,1)} %bitcast.231), kind=kLoop, calls=%fused_computation.211 | loop fusion | bytes 196608 | tf_op jit(solution)/shard_map/stack | solution.py:252
  4.7 1.0 %select_reduce_fusion.1 = bf16[4,128,128]{2,1,0:T(8,128)(2,1)S(1)} fusion(pred[4,4]{1,0:T(4,128)(4,1)S(1)} %get-tuple-element.114, bf16[4,128,128]{2,1,0:T(8,128)(2,1)} %param.10), kind=kLoop, calls=%fused_computation.173 | loop fusion | flops 458752 | bytes 262160 | tf_op jit(solution)/shard_map/reduce_sum | solution.py:267
  5.8 0.7 pad_maximum_fusion.edges_ref
  6.4 16.2 %shard_map.93 = (bf16[12,128,128]{2,1,0:T(8,128)(2,1)}, bf16[2,12,8,128]{3,2,1,0:T(8,128)(2,1)}, bf16[2,12,8,128]{3,2,1,0:T(8,128)(2,1)}) custom-call(bf16[2,12,128,128]{3,2,1,0:T(8,128)(2,1)} %bitcast.232, bf16[2,2,12,8,128]{4,3,2,1,0:T(8,128)(2,1)} %pad_maximum_fusion.edges_ref), custom_call_target="tpu_custom_call" | custom-call | tf_op jit(solution)/shard_map/pallas_call | solution.py:128
  22.6 0.8 %slice_bitcast_fusion.17 = (bf16[12,8,128]{2,1,0:T(8,128)(2,1)S(1)}, bf16[12,8,128]{2,1,0:T(8,128)(2,1)S(1)}, bf16[12,8,128]{2,1,0:T(8,128)(2,1)S(1)}, bf16[12,8,128]{2,1,0:T(8,128)(2,1)S(1)}) fusion(bf16[2,12,8,128]{3,2,1,0:T(8,128)(2,1)} %get-tuple-element.9, bf16[2,12,8,128]{3,2,1,0:T(8,128)(2,1)} %get-tuple-element.7), kind=kLoop, calls=%fused_computation.218 | loop fusion | bytes 196608 | tf_op jit(solution)/shard_map/squeeze | solution.py:258
  23.5 0.0 copy-done
  23.5 1.1 %bitcast_select_fusion.1 = (bf16[12,128,128]{2,1,0:T(8,128)(2,1)S(1)}, bf16[12,128,128]{2,1,0:T(8,128)(2,1)S(1)}) fusion(bf16[12,128,128]{2,1,0:T(8,128)(2,1)} %get-tuple-element.8, pred[]{:T(512)S(6)} %eq.49, bf16[1,2,12,128,128]{4,3,2,1,0:T(8,128)(2,1)S(1)} %copy-done, s32[]{:T(128)S(6)} %select_n.56), kind=kLoop, calls=%fused_computation.193 | loop fusion | flops 393216 | bytes 1572869 | tf_op jit(solution)/shard_map/jit(_where)/select_n | solution.py:256
  24.6 0.2 multiply_convert_fusion
  24.7 0.7 fusion.5
  25.4 0.5 fusion.7
  25.9 0.7 fusion.13
  26.7 0.5 fusion.15
  27.2 0.7 fusion.21
  27.9 0.5 fusion.23
  28.4 0.1 slice_convert_fusion
  28.5 0.7 add_convert_fusion
  29.2 0.7 fusion.29
  29.8 0.3 fusion.99
  30.1 1.5 %collective-permute-start = (bf16[12,128,128]{2,1,0:T(8,128)(2,1)S(1)}, bf16[12,128,128]{2,1,0:T(8,128)(2,1)S(1)}, u32[]{:S(2)}, u32[]{:S(2)}) collective-permute-start(bf16[12,128,128]{2,1,0:T(8,128)(2,1)S(1)} %fusion.99), channel_id=1, source_target_pairs={{0,1},{2,3},{4,5},{6,7},{8,9},{10,11},{12,13},{14,15},{16,17},{18,... | collective-permute-start | bytes 1179656 | tf_op jit(solution)/shard_map/ppermute | solution.py:335
  31.6 0.3 fusion.100
  32.0 0.2 convert_reduce_fusion
  32.2 0.4 convolution_convert_fusion.3
  32.5 0.9 %fusion.72 = (f32[128]{0:T(128)S(1)}, f32[128]{0:T(128)S(1)}, f32[128]{0:T(128)S(1)}, f32[128]{0:T(128)S(1)}, f32[128]{0:T(128)S(1)}, /*index=5*/f32[128]{0:T(12...) fusion(bf16[12,138,128]{2,1,0:T(8,128)(2,1)S(1)} %get-tuple-element.119, ...), kind=kLoop, calls=%fused_computation.138 | loop fusion | flops 5503872 | bytes 2019840 | tf_op jit(solution)/shard_map/reduce_sum | solution.py:323
  33.4 1.5 %fusion.35 = (bf16[12,134,128]{2,1,0:T(8,128)(2,1)S(1)}, f32[12,134,128]{2,1,0:T(8,128)S(1)}) fusion(f32[12,138,128]{2,1,0:T(8,128)S(1)} %get-tuple-element.120, f32[12]{0:T(128)S(1)} %fusion.112, f32[128]{0:T(128)S(1)} %get-tuple-element.140, f32[128]{0:T(128)S(1)} %get-tuple-element.139, f32[128]{0:T(128)S(1)} %get-tuple-element.138, ...), kind=kLoop, calls=%fused_computation.92 | loop fusion | flops 8438784 | bytes 4582400 | tf_op jit(solution)/shard_map/convert_element_type | solution.py:300
  34.9 0.3 fusion.102
  35.3 0.2 convert_reduce_fusion.1
  35.5 0.4 convolution_convert_fusion.2
  35.9 0.9 %fusion.63 = (f32[128]{0:T(128)S(1)}, f32[128]{0:T(128)S(1)}, f32[128]{0:T(128)S(1)}, f32[128]{0:T(128)S(1)}, f32[128]{0:T(128)S(1)}, /*index=5*/f32[128]{0:T(12...) fusion(bf16[12,140,128]{2,1,0:T(8,128)(2,1)S(1)} %get-tuple-element.117, ...), kind=kLoop, calls=%fused_computation.129 | loop fusion | flops 5503872 | bytes 2019840 | tf_op jit(solution)/shard_map/reduce_sum | solution.py:323
  36.7 1.5 %fusion.41 = (bf16[12,132,128]{2,1,0:T(8,128)(2,1)S(1)}, f32[12,132,128]{2,1,0:T(8,128)S(1)}) fusion(f32[12,140,128]{2,1,0:T(8,128)S(1)} %get-tuple-element.118, f32[12]{0:T(128)S(1)} %fusion.112, f32[128]{0:T(128)S(1)} %get-tuple-element.83, f32[128]{0:T(128)S(1)} %get-tuple-element.84, f32[128]{0:T(128)S(1)} %get-tuple-element.85, ...), kind=kLoop, calls=%fused_computation.98 | loop fusion | flops 8312832 | bytes 4563968 | tf_op jit(solution)/shard_map/convert_element_type | solution.py:300
  38.3 0.3 fusion.104
  38.6 0.2 convert_reduce_fusion.2
  38.8 0.4 convolution_convert_fusion.1
  39.2 0.7 fusion.54
  40.0 1.5 %fusion.47 = (bf16[12,130,128]{2,1,0:T(8,128)(2,1)S(1)}, f32[12,130,128]{2,1,0:T(8,128)S(1)}) fusion(f32[12,142,128]{2,1,0:T(8,128)S(1)} %get-tuple-element.116, f32[12]{0:T(128)S(1)} %fusion.112, f32[128]{0:T(128)S(1)} %get-tuple-element.131, f32[128]{0:T(128)S(1)} %get-tuple-element.130, f32[128]{0:T(128)S(1)} %get-tuple-element.129, ...), kind=kLoop, calls=%fused_computation.104 | loop fusion | flops 8186880 | bytes 4545536 | tf_op jit(solution)/shard_map/convert_element_type | solution.py:300
  41.5 0.3 fusion.106
  41.8 0.2 convert_reduce_fusion.3
  42.1 0.4 convolution_convert_fusion
  42.4 0.9 %fusion.89 = (f32[128]{0:T(128)S(1)}, f32[128]{0:T(128)S(1)}, f32[128]{0:T(128)S(1)}, f32[128]{0:T(128)S(1)}, f32[128]{0:T(128)S(1)}, /*index=5*/f32[128]{0:T(12...) fusion(bf16[12,144,128]{2,1,0:T(8,128)(2,1)S(1)} %multiply_convert_fusion, ...), kind=kLoop, calls=%fused_computation.155 | loop fusion | flops 5503872 | bytes 2019840 | tf_op jit(solution)/shard_map/reduce_sum | solution.py:323
  43.6 0.3 maximum_maximum_fusion
  43.9 0.1 reshape.183
  44.0 0.8 pad.48
  44.8 27.1 %shard_map.94 = f32[32,24,128]{2,1,0:T(8,128)} custom-call(f32[32,24,128]{2,1,0:T(8,128)} %bitcast.233), custom_call_target="tpu_custom_call" | custom-call | tf_op jit(solution)/shard_map/pallas_call | solution.py:225
  71.8 1.0 %slice.830 = f32[23,24,128]{2,1,0:T(8,128)S(1)} slice(f32[32,24,128]{2,1,0:T(8,128)} %shard_map.94), slice={[0:23], [0:24], [0:128]} | slice | bytes 565248 | tf_op jit(solution)/shard_map/slice | solution.py:348
  72.8 0.1 broadcast_in_dim.107
  73.0 0.8 %select_reduce_fusion = f32[4,17664]{1,0:T(4,128)S(1)} fusion(f32[4,17664]{1,0:T(4,128)S(1)} %broadcast_in_dim.107, pred[4,4]{1,0:T(4,128)(4,1)S(1)} %get-tuple-element.113), kind=kLoop, calls=%fused_computation.49 | loop fusion | flops 494592 | bytes 565264 | tf_op jit(solution)/shard_map/reduce_sum | solution.py:351
  73.8 0.0 collective-permute-done
  73.8 0.9 %select_bitcast_fusion.1 = (bf16[1,12,128,128]{3,2,1,0:T(8,128)(2,1)S(1)}, bf16[12,128,128]{2,1,0:T(8,128)(2,1)S(1)}) fusion(bf16[12,128,128]{2,1,0:T(8,128)(2,1)S(1)} %collective-permute-done, pred[]{:T(512)S(6)} %eq.49, f32[12]{0:T(128)S(1)} %fusion.112, f32[128]{0:T(128)S(1)} %get-tuple-element.101, f32[128]{0:T(128)S(1)} %get-tuple-element.102, ...), kind=kLoop, calls=%fused_computation.195 | loop fusion | flops 5898240 | bytes 3568641 | tf_op jit(solution)/shard_map/stack | solution.py:339
  74.7 1.3 %collective-permute-start.1 = (bf16[12,128,128]{2,1,0:T(8,128)(2,1)S(1)}, bf16[12,128,128]{2,1,0:T(8,128)(2,1)S(1)}, u32[]{:S(2)}, u32[]{:S(2)}) collective-permute-start(bf16[12,128,128]{2,1,0:T(8,128)(2,1)S(1)} %get-tuple-element.51), channel_id=1, source_target_pairs={{1,0},{3,2},{5,4},{7,6},{9,8},{11,10},{13,12},{15,14},{17,16},{19,... | collective-permute-start | bytes 1179656 | tf_op jit(solution)/shard_map/ppermute | solution.py:336
  76.1 0.1 broadcast_multiply_fusion
  76.1 0.6 slice.941
  76.7 0.6 slice.939
  77.4 0.7 copy.30
  78.1 0.0 collective-permute-done.1
  78.1 0.1 select_bitcast_fusion
  78.1 0.9 %maximum_bitcast_fusion = bf16[1,2,12,128,128]{4,3,2,1,0:T(8,128)(2,1)} fusion(bf16[1,12,128,128]{3,2,1,0:T(8,128)(2,1)S(1)} %select_bitcast_fusion, bf16[1,12,128,128]{3,2,1,0:T(8,128)(2,1)S(1)} %get-tuple-element.50), kind=kLoop, calls=%fused_computation.168 | loop fusion | flops 393216 | bytes 1572864 | tf_op jit(solution)/shard_map/broadcast_in_dim | solution.py:339
  (28 shorter events, 0.3 us)
Async XLA Ops:
  3.8 19.7 %copy-start = (bf16[1,2,12,128,128]{4,3,2,1,0:T(8,128)(2,1)S(1)}, bf16[1,2,12,128,128]{4,3,2,1,0:T(8,128)(2,1)}, u32[]{:S(2)}) copy-start(bf16[1,2,12,128,128]{4,3,2,1,0:T(8,128)(2,1)} %param.6) | copy-start | bytes 2359300
  30.1 43.7 %collective-permute-start = (bf16[12,128,128]{2,1,0:T(8,128)(2,1)S(1)}, bf16[12,128,128]{2,1,0:T(8,128)(2,1)S(1)}, u32[]{:S(2)}, u32[]{:S(2)}) collective-permute-start(bf16[12,128,128]{2,1,0:T(8,128)(2,1)S(1)} %fusion.99), channel_id=1, source_target_pairs={{0,1},{2,3},{4,5},{6,7},{8,9},{10,11},{12,13},{14,15},{16,17},{18,... | collective-permute-start | bytes 1179656 | tf_op jit(solution)/shard_map/ppermute | solution.py:335
  74.7 3.3 %collective-permute-start.1 = (bf16[12,128,128]{2,1,0:T(8,128)(2,1)S(1)}, bf16[12,128,128]{2,1,0:T(8,128)(2,1)S(1)}, u32[]{:S(2)}, u32[]{:S(2)}) collective-permute-start(bf16[12,128,128]{2,1,0:T(8,128)(2,1)S(1)} %get-tuple-element.51), channel_id=1, source_target_pairs={{1,0},{3,2},{5,4},{7,6},{9,8},{11,10},{13,12},{15,14},{17,16},{19,... | collective-permute-start | bytes 1179656 | tf_op jit(solution)/shard_map/ppermute | solution.py:336

commit v17 on v16

--- a/solution.py
+++ b/solution.py
@@ -251,9 +251,8 @@
 
     edges = jnp.stack([held[:, :, :X_HALO], held[:, :, breadth - X_HALO :]])
     body, lo, hi = exchange(held, edges)
-    mine = select_row(held, core)
-    x_in = jnp.where(core == 0, mine, body)
-    g_in = jnp.where(core == 0, body, mine)
+    x_in = jnp.where(core == 0, held[0], body)
+    g_in = jnp.where(core == 0, body, held[1])
     x_wide = jnp.concatenate([lo[0], x_in, hi[0]], axis=1)
     g_wide = jnp.concatenate([lo[1][:, X_HALO - G_HALO :], g_in, hi[1][:, :G_HALO]], axis=1)
 

time: 79.5 us -> 79.6 us (level)
  no operation moved by 1% of the time
where the time goes in v17:
time: 79.6 us; the launch traced here: 79.1 us
  Pallas kernels  43.2 us (54%)
  other arithmetic  21.3 us (27%)
  local copies, waits for them, and re-layouts  5.75 us (7%)
  matrix products  5.01 us (6%)
  starting transfers between devices  2.79 us (4%)
  between operations  1.04 us (1%)
    pallas_call x1, Pallas kernels, all_reduce(): pl.pallas_call(reduce_kernel, out_shape=jax.ShapeDtypeStruct(flat.shape,...  27.1 us
    pallas_call x1, Pallas kernels, exchange(): pl.pallas_call(exchange_kernel, out_shape=(jax.ShapeDtypeStruct(grid_shap...  16.2 us
    convert_element_type x3, other arithmetic, shards(): gated = (masked * gelu_pair(preact)[1]).astype(jnp.bfloat16)  4.58 us
    reduce_sum x4, other arithmetic, shards(): jnp.sum(back_in * padded[i:i + height, start:start + breadth].astype(jnp....  3.3 us
    convert_element_type x4, other arithmetic, shards(): mixed = conv_forward(pad_rows(activation), depth).astype(jnp.bfloat16)  2.83 us
    reduce_sum x3, other arithmetic, pick(): jnp.sum(jnp.where(mask, table[None], jnp.zeros((), table.dtype)), axis=1,...  2.67 us
    dot_general x4, matrix products, shards(): jnp.dot(mixed.reshape(rows * span, channels), point, preferred_element_ty...  2.17 us
  transfers between devices with their start and end apart: 2, of which 0 were waited for; matrix products, arithmetic and copies ran while one was open for 21% of the time, Pallas kernels for 34%

profile of v17, /device:TPU:1, one launch (start us, length us, event | category | flops | bytes accessed | tf_op | source)
XLA Modules:
  0.0 79.1 jit_solution(16894217566472308275)
XLA Ops:
  0.6 0.7 compare_convert_fusion
  1.4 0.8 %iota_compare_fusion = (pred[4,4]{1,0:T(4,128)(4,1)S(1)}, pred[4,4]{1,0:T(4,128)(4,1)S(1)}) fusion(s32[4]{0:T(128)} %param.8), kind=kLoop, calls=%fused_computation.241 | loop fusion | flops 32 | bytes 48 | tf_op jit(solution)/shard_map/eq | solution.py:349
  2.2 0.8 select_reduce_fusion.3
  2.9 0.9 %select_reduce_fusion.2 = f32[4,3,3,128]{3,2,1,0:T(4,128)S(1)} fusion(f32[4,3,3,128]{3,0,2,1:T(4,128)} %param.9, pred[4,4]{1,0:T(4,128)(4,1)S(1)} %get-tuple-element.114), kind=kLoop, calls=%fused_computation.209 | loop fusion | flops 32256 | bytes 36880 | tf_op jit(solution)/shard_map/reduce_sum | solution.py:266
  3.8 0.0 copy-start
  3.8 0.9 %slice_bitcast_fusion.2 = (bf16[1,2,12,8,128]{4,3,2,1,0:T(8,128)(2,1)S(1)}, bf16[1,2,12,8,128]{4,3,2,1,0:T(8,128)(2,1)S(1)}) fusion(bf16[2,12,128,128]{3,2,1,0:T(8,128)(2,1)} %bitcast.232), kind=kLoop, calls=%fused_computation.211 | loop fusion | bytes 196608 | tf_op jit(solution)/shard_map/stack | solution.py:252
  4.7 1.0 %select_reduce_fusion.1 = bf16[4,128,128]{2,1,0:T(8,128)(2,1)S(1)} fusion(pred[4,4]{1,0:T(4,128)(4,1)S(1)} %get-tuple-element.114, bf16[4,128,128]{2,1,0:T(8,128)(2,1)} %param.10), kind=kLoop, calls=%fused_computation.173 | loop fusion | flops 458752 | bytes 262160 | tf_op jit(solution)/shard_map/reduce_sum | solution.py:266
  5.8 0.7 pad_maximum_fusion.edges_ref
  6.4 16.2 %shard_map.93 = (bf16[12,128,128]{2,1,0:T(8,128)(2,1)}, bf16[2,12,8,128]{3,2,1,0:T(8,128)(2,1)}, bf16[2,12,8,128]{3,2,1,0:T(8,128)(2,1)}) custom-call(bf16[2,12,128,128]{3,2,1,0:T(8,128)(2,1)} %bitcast.233, bf16[2,2,12,8,128]{4,3,2,1,0:T(8,128)(2,1)} %pad_maximum_fusion.edges_ref), custom_call_target="tpu_custom_call" | custom-call | tf_op jit(solution)/shard_map/pallas_call | solution.py:128
  22.6 0.8 %slice_bitcast_fusion.17 = (bf16[12,8,128]{2,1,0:T(8,128)(2,1)S(1)}, bf16[12,8,128]{2,1,0:T(8,128)(2,1)S(1)}, bf16[12,8,128]{2,1,0:T(8,128)(2,1)S(1)}, bf16[12,8,128]{2,1,0:T(8,128)(2,1)S(1)}) fusion(bf16[2,12,8,128]{3,2,1,0:T(8,128)(2,1)} %get-tuple-element.9, bf16[2,12,8,128]{3,2,1,0:T(8,128)(2,1)} %get-tuple-element.7), kind=kLoop, calls=%fused_computation.218 | loop fusion | bytes 196608 | tf_op jit(solution)/shard_map/squeeze | solution.py:257
  23.5 0.0 copy-done
  23.5 1.1 %bitcast_select_fusion.1 = (bf16[12,128,128]{2,1,0:T(8,128)(2,1)S(1)}, bf16[12,128,128]{2,1,0:T(8,128)(2,1)S(1)}) fusion(bf16[12,128,128]{2,1,0:T(8,128)(2,1)} %get-tuple-element.8, bf16[1,2,12,128,128]{4,3,2,1,0:T(8,128)(2,1)S(1)} %copy-done, pred[]{:T(512)S(6)} %eq.49), kind=kLoop, calls=%fused_computation.193 | loop fusion | flops 393216 | bytes 1966081 | tf_op jit(solution)/shard_map/jit(_where)/select_n | solution.py:255
  24.6 0.2 multiply_convert_fusion
  24.7 0.7 fusion.5
  25.5 0.5 fusion.7
  26.0 0.7 fusion.13
  26.7 0.5 fusion.15
  27.2 0.7 fusion.21
  27.9 0.5 fusion.23
  28.4 0.1 slice_convert_fusion
  28.5 0.7 add_convert_fusion
  29.2 0.7 fusion.29
  29.9 0.3 fusion.99
  30.2 1.5 %collective-permute-start = (bf16[12,128,128]{2,1,0:T(8,128)(2,1)S(1)}, bf16[12,128,128]{2,1,0:T(8,128)(2,1)S(1)}, u32[]{:S(2)}, u32[]{:S(2)}) collective-permute-start(bf16[12,128,128]{2,1,0:T(8,128)(2,1)S(1)} %fusion.99), channel_id=1, source_target_pairs={{0,1},{2,3},{4,5},{6,7},{8,9},{10,11},{12,13},{14,15},{16,17},{18,... | collective-permute-start | bytes 1179656 | tf_op jit(solution)/shard_map/ppermute | solution.py:334
  31.6 0.3 fusion.100
  32.0 0.2 convert_reduce_fusion
  32.2 0.4 convolution_convert_fusion.3
  32.6 0.9 %fusion.72 = (f32[128]{0:T(128)S(1)}, f32[128]{0:T(128)S(1)}, f32[128]{0:T(128)S(1)}, f32[128]{0:T(128)S(1)}, f32[128]{0:T(128)S(1)}, /*index=5*/f32[128]{0:T(12...) fusion(bf16[12,138,128]{2,1,0:T(8,128)(2,1)S(1)} %get-tuple-element.119, ...), kind=kLoop, calls=%fused_computation.138 | loop fusion | flops 5503872 | bytes 2019840 | tf_op jit(solution)/shard_map/reduce_sum | solution.py:322
  33.4 1.5 %fusion.35 = (bf16[12,134,128]{2,1,0:T(8,128)(2,1)S(1)}, f32[12,134,128]{2,1,0:T(8,128)S(1)}) fusion(f32[12,138,128]{2,1,0:T(8,128)S(1)} %get-tuple-element.120, f32[12]{0:T(128)S(1)} %fusion.112, f32[128]{0:T(128)S(1)} %get-tuple-element.140, f32[128]{0:T(128)S(1)} %get-tuple-element.139, f32[128]{0:T(128)S(1)} %get-tuple-element.138, ...), kind=kLoop, calls=%fused_computation.92 | loop fusion | flops 8438784 | bytes 4582400 | tf_op jit(solution)/shard_map/convert_element_type | solution.py:299
  35.0 0.3 fusion.102
  35.3 0.2 convert_reduce_fusion.1
  35.5 0.4 convolution_convert_fusion.2
  35.9 0.9 %fusion.63 = (f32[128]{0:T(128)S(1)}, f32[128]{0:T(128)S(1)}, f32[128]{0:T(128)S(1)}, f32[128]{0:T(128)S(1)}, f32[128]{0:T(128)S(1)}, /*index=5*/f32[128]{0:T(12...) fusion(bf16[12,140,128]{2,1,0:T(8,128)(2,1)S(1)} %get-tuple-element.117, ...), kind=kLoop, calls=%fused_computation.129 | loop fusion | flops 5503872 | bytes 2019840 | tf_op jit(solution)/shard_map/reduce_sum | solution.py:322
  36.8 1.5 %fusion.41 = (bf16[12,132,128]{2,1,0:T(8,128)(2,1)S(1)}, f32[12,132,128]{2,1,0:T(8,128)S(1)}) fusion(f32[12,140,128]{2,1,0:T(8,128)S(1)} %get-tuple-element.118, f32[12]{0:T(128)S(1)} %fusion.112, f32[128]{0:T(128)S(1)} %get-tuple-element.83, f32[128]{0:T(128)S(1)} %get-tuple-element.84, f32[128]{0:T(128)S(1)} %get-tuple-element.85, ...), kind=kLoop, calls=%fused_computation.98 | loop fusion | flops 8312832 | bytes 4563968 | tf_op jit(solution)/shard_map/convert_element_type | solution.py:299
  38.3 0.3 fusion.104
  38.7 0.2 convert_reduce_fusion.2
  38.9 0.4 convolution_convert_fusion.1
  39.3 0.7 fusion.54
  40.0 1.5 %fusion.47 = (bf16[12,130,128]{2,1,0:T(8,128)(2,1)S(1)}, f32[12,130,128]{2,1,0:T(8,128)S(1)}) fusion(f32[12,142,128]{2,1,0:T(8,128)S(1)} %get-tuple-element.116, f32[12]{0:T(128)S(1)} %fusion.112, f32[128]{0:T(128)S(1)} %get-tuple-element.131, f32[128]{0:T(128)S(1)} %get-tuple-element.130, f32[128]{0:T(128)S(1)} %get-tuple-element.129, ...), kind=kLoop, calls=%fused_computation.104 | loop fusion | flops 8186880 | bytes 4545536 | tf_op jit(solution)/shard_map/convert_element_type | solution.py:299
  41.5 0.3 fusion.106
  41.9 0.2 convert_reduce_fusion.3
  42.1 0.4 convolution_convert_fusion
  42.5 0.9 %fusion.89 = (f32[128]{0:T(128)S(1)}, f32[128]{0:T(128)S(1)}, f32[128]{0:T(128)S(1)}, f32[128]{0:T(128)S(1)}, f32[128]{0:T(128)S(1)}, /*index=5*/f32[128]{0:T(12...) fusion(bf16[12,144,128]{2,1,0:T(8,128)(2,1)S(1)} %multiply_convert_fusion, ...), kind=kLoop, calls=%fused_computation.155 | loop fusion | flops 5503872 | bytes 2019840 | tf_op jit(solution)/shard_map/reduce_sum | solution.py:322
  43.6 0.3 maximum_maximum_fusion
  43.9 0.1 reshape.185
  44.0 0.8 pad.48
  44.8 27.1 %shard_map.94 = f32[32,24,128]{2,1,0:T(8,128)} custom-call(f32[32,24,128]{2,1,0:T(8,128)} %bitcast.234), custom_call_target="tpu_custom_call" | custom-call | tf_op jit(solution)/shard_map/pallas_call | solution.py:225
  71.9 1.0 %slice.840 = f32[23,24,128]{2,1,0:T(8,128)S(1)} slice(f32[32,24,128]{2,1,0:T(8,128)} %shard_map.94), slice={[0:23], [0:24], [0:128]} | slice | bytes 565248 | tf_op jit(solution)/shard_map/slice | solution.py:347
  72.9 0.1 broadcast_in_dim.107
  73.0 0.8 %select_reduce_fusion = f32[4,17664]{1,0:T(4,128)S(1)} fusion(f32[4,17664]{1,0:T(4,128)S(1)} %broadcast_in_dim.107, pred[4,4]{1,0:T(4,128)(4,1)S(1)} %get-tuple-element.113), kind=kLoop, calls=%fused_computation.49 | loop fusion | flops 494592 | bytes 565264 | tf_op jit(solution)/shard_map/reduce_sum | solution.py:350
  73.8 0.0 collective-permute-done
  73.8 0.9 %select_bitcast_fusion.1 = (bf16[1,12,128,128]{3,2,1,0:T(8,128)(2,1)S(1)}, bf16[12,128,128]{2,1,0:T(8,128)(2,1)S(1)}) fusion(bf16[12,128,128]{2,1,0:T(8,128)(2,1)S(1)} %collective-permute-done, pred[]{:T(512)S(6)} %eq.49, f32[12]{0:T(128)S(1)} %fusion.112, f32[128]{0:T(128)S(1)} %get-tuple-element.101, f32[128]{0:T(128)S(1)} %get-tuple-element.102, ...), kind=kLoop, calls=%fused_computation.195 | loop fusion | flops 5898240 | bytes 3568641 | tf_op jit(solution)/shard_map/stack | solution.py:338
  74.8 1.3 %collective-permute-start.1 = (bf16[12,128,128]{2,1,0:T(8,128)(2,1)S(1)}, bf16[12,128,128]{2,1,0:T(8,128)(2,1)S(1)}, u32[]{:S(2)}, u32[]{:S(2)}) collective-permute-start(bf16[12,128,128]{2,1,0:T(8,128)(2,1)S(1)} %get-tuple-element.51), channel_id=1, source_target_pairs={{1,0},{3,2},{5,4},{7,6},{9,8},{11,10},{13,12},{15,14},{17,16},{19,... | collective-permute-start | bytes 1179656 | tf_op jit(solution)/shard_map/ppermute | solution.py:335
  76.1 0.1 broadcast_multiply_fusion
  76.2 0.6 slice.951
  76.8 0.6 slice.949
  77.4 0.7 copy.30
  78.1 0.0 collective-permute-done.1
  78.1 0.1 select_bitcast_fusion
  78.2 0.9 %maximum_bitcast_fusion = bf16[1,2,12,128,128]{4,3,2,1,0:T(8,128)(2,1)} fusion(bf16[1,12,128,128]{3,2,1,0:T(8,128)(2,1)S(1)} %select_bitcast_fusion, bf16[1,12,128,128]{3,2,1,0:T(8,128)(2,1)S(1)} %get-tuple-element.50), kind=kLoop, calls=%fused_computation.168 | loop fusion | flops 393216 | bytes 1572864 | tf_op jit(solution)/shard_map/broadcast_in_dim | solution.py:338
  (28 shorter events, 0.3 us)
Async XLA Ops:
  3.8 19.7 %copy-start = (bf16[1,2,12,128,128]{4,3,2,1,0:T(8,128)(2,1)S(1)}, bf16[1,2,12,128,128]{4,3,2,1,0:T(8,128)(2,1)}, u32[]{:S(2)}) copy-start(bf16[1,2,12,128,128]{4,3,2,1,0:T(8,128)(2,1)} %param.6) | copy-start | bytes 2359300
  30.2 43.6 %collective-permute-start = (bf16[12,128,128]{2,1,0:T(8,128)(2,1)S(1)}, bf16[12,128,128]{2,1,0:T(8,128)(2,1)S(1)}, u32[]{:S(2)}, u32[]{:S(2)}) collective-permute-start(bf16[12,128,128]{2,1,0:T(8,128)(2,1)S(1)} %fusion.99), channel_id=1, source_target_pairs={{0,1},{2,3},{4,5},{6,7},{8,9},{10,11},{12,13},{14,15},{16,17},{18,... | collective-permute-start | bytes 1179656 | tf_op jit(solution)/shard_map/ppermute | solution.py:334
  74.8 3.3 %collective-permute-start.1 = (bf16[12,128,128]{2,1,0:T(8,128)(2,1)S(1)}, bf16[12,128,128]{2,1,0:T(8,128)(2,1)S(1)}, u32[]{:S(2)}, u32[]{:S(2)}) collective-permute-start(bf16[12,128,128]{2,1,0:T(8,128)(2,1)S(1)} %get-tuple-element.51), channel_id=1, source_target_pairs={{1,0},{3,2},{5,4},{7,6},{9,8},{11,10},{13,12},{15,14},{17,16},{19,... | collective-permute-start | bytes 1179656 | tf_op jit(solution)/shard_map/ppermute | solution.py:335

commit v18 on v17

--- a/solution.py
+++ b/solution.py
@@ -333,9 +333,9 @@
 
     got_outcome = lax.ppermute(outcome, "pipe", [(0, 1)])
     got_grad = lax.ppermute(input_grad, "pipe", [(1, 0)])
-    first = jnp.where(core == 0, input_grad, got_outcome)
-    second = jnp.where(core == 0, got_grad, outcome)
-    result = jnp.stack([first, second])[None]
+    result = jnp.where(
+        core == 0, jnp.stack([input_grad, got_grad]), jnp.stack([got_outcome, outcome])
+    )[None]
 
     pieces = (jnp.stack(depth_terms), jnp.stack(point_terms), jnp.stack(bias_terms))
     flat = jnp.concatenate([piece.reshape(layers, -1) for piece in pieces], axis=1)

time: 79.6 us -> 76 us (0.955)
  other arithmetic: 21.3 us -> 17.6 us
  starting transfers between devices: 2.79 us -> 3.81 us
    reduce_sum x3, other arithmetic: 2.67 us -> 0.38 us  [pick(): jnp.sum(jnp.where(mask, table[None], jnp.zeros((), table.dtype)), axis=1,...]
    select_n x0 -> x1, other arithmetic: none -> 1.02 us  [shards(): jnp.where(core == 0, jnp.stack([input_grad, got_grad]), jnp.stack([got_ou...]
    ppermute x1, starting transfers between devices: 1.31 us -> 2.33 us  [shards(): got_grad = lax.ppermute(input_grad, 'pipe', [(1, 0)])]
    another operation x2 -> x0, other arithmetic: 1 us -> none  [shards(): result = jnp.stack([first, second])[None]]
    broadcast_in_dim x1 -> x0, other arithmetic: 0.95 us -> none  [shards(): result = jnp.stack([first, second])[None]]
    convert_element_type x1, other arithmetic: 0.29 us -> 1.14 us  [shards(): activation = ((activation[:, 1:-1].astype(jnp.float32) + gelu_pair(preact...]
  transfers between devices with their start and end apart: 2 -> 2, of which waited for: 0 -> 0; matrix products, arithmetic and copies ran while one was open for 21% -> 14% of each run, Pallas kernels for 34% -> 36%
where the time goes in v18:
time: 76 us; the launch traced here: 75.8 us
  Pallas kernels  43.2 us (57%)
  other arithmetic  17.6 us (23%)
  matrix products  5 us (7%)
  local copies, waits for them, and re-layouts  4.98 us (7%)
  starting transfers between devices  3.81 us (5%)
  between operations  1.1 us (1%)
    pallas_call x1, Pallas kernels, all_reduce(): pl.pallas_call(reduce_kernel, out_shape=jax.ShapeDtypeStruct(flat.shape,...  27.1 us
    pallas_call x1, Pallas kernels, exchange(): pl.pallas_call(exchange_kernel, out_shape=(jax.ShapeDtypeStruct(grid_shap...  16.2 us
    convert_element_type x3, other arithmetic, shards(): gated = (masked * gelu_pair(preact)[1]).astype(jnp.bfloat16)  4.6 us
    reduce_sum x4, other arithmetic, shards(): jnp.sum(back_in * padded[i:i + height, start:start + breadth].astype(jnp....  3.28 us
    convert_element_type x4, other arithmetic, shards(): mixed = conv_forward(pad_rows(activation), depth).astype(jnp.bfloat16)  2.83 us
    ppermute x1, starting transfers between devices, shards(): got_grad = lax.ppermute(input_grad, 'pipe', [(1, 0)])  2.33 us
    dot_general x4, matrix products, shards(): jnp.dot(mixed.reshape(rows * span, channels), point, preferred_element_ty...  2.15 us
  transfers between devices with their start and end apart: 2, of which 0 were waited for; matrix products, arithmetic and copies ran while one was open for 14% of the time, Pallas kernels for 36%

profile of v18, /device:TPU:1, one launch (start us, length us, event | category | flops | bytes accessed | tf_op | source)
XLA Modules:
  0.0 75.8 jit_solution(6402709454229632771)
XLA Ops:
  0.6 0.0 copy-start
  0.6 0.0 copy-start.7
  0.7 0.9 %slice_bitcast_fusion.2 = (bf16[1,2,12,8,128]{4,3,2,1,0:T(8,128)(2,1)S(1)}, bf16[1,2,12,8,128]{4,3,2,1,0:T(8,128)(2,1)S(1)}) fusion(bf16[2,12,128,128]{3,2,1,0:T(8,128)(2,1)} %bitcast.230), kind=kLoop, calls=%fused_computation.209 | loop fusion | bytes 196608 | tf_op jit(solution)/shard_map/stack | solution.py:252
  1.6 0.7 pad_maximum_fusion.edges_ref
  2.2 16.2 %shard_map.93 = (bf16[12,128,128]{2,1,0:T(8,128)(2,1)}, bf16[2,12,8,128]{3,2,1,0:T(8,128)(2,1)}, bf16[2,12,8,128]{3,2,1,0:T(8,128)(2,1)}) custom-call(bf16[2,12,128,128]{3,2,1,0:T(8,128)(2,1)} %bitcast.231, bf16[2,2,12,8,128]{4,3,2,1,0:T(8,128)(2,1)} %pad_maximum_fusion.edges_ref), custom_call_target="tpu_custom_call" | custom-call | tf_op jit(solution)/shard_map/pallas_call | solution.py:128
  18.4 0.0 copy-done.7
  18.4 0.1 compare_convert_fusion
  18.5 0.0 copy-done
  18.5 0.0 copy-start.5
  18.5 0.0 copy-start.2
  18.5 0.0 copy-start.3
  18.5 1.2 %bitcast_select_fusion.1 = (bf16[12,128,128]{2,1,0:T(8,128)(2,1)S(1)}, bf16[12,128,128]{2,1,0:T(8,128)(2,1)S(1)}) fusion(bf16[12,128,128]{2,1,0:T(8,128)(2,1)} %get-tuple-element.8, bf16[1,2,12,128,128]{4,3,2,1,0:T(8,128)(2,1)S(1)} %copy-done, pred[]{:T(512)S(6)} %eq.48), kind=kLoop, calls=%fused_computation.193 | loop fusion | flops 393216 | bytes 1966081 | tf_op jit(solution)/shard_map/jit(_where)/select_n | solution.py:255
  19.7 0.1 iota_compare_fusion
  19.8 0.1 select_reduce_fusion.2
  19.9 0.0 copy-done.1
  19.9 0.1 select_reduce_fusion.1
  20.1 0.0 copy-done.5
  20.1 0.1 select_reduce_fusion.3
  20.3 0.2 multiply_convert_fusion
  20.5 0.7 fusion.5
  21.2 0.5 fusion.7
  21.7 0.7 fusion.13
  22.4 0.5 fusion.15
  22.9 0.7 fusion.21
  23.6 0.5 fusion.23
  24.2 0.1 slice_convert_fusion
  24.2 0.7 add_convert_fusion
  24.9 0.7 fusion.29
  25.6 0.4 convolution_convert_fusion.3
  26.0 1.5 %fusion.35 = (bf16[12,134,128]{2,1,0:T(8,128)(2,1)S(1)}, f32[12,134,128]{2,1,0:T(8,128)S(1)}) fusion(f32[12,138,128]{2,1,0:T(8,128)S(1)} %get-tuple-element.120, f32[12]{0:T(128)S(1)} %fusion.112, f32[128]{0:T(128)S(1)} %get-tuple-element.140, f32[128]{0:T(128)S(1)} %get-tuple-element.139, f32[128]{0:T(128)S(1)} %get-tuple-element.138, ...), kind=kLoop, calls=%fused_computation.92 | loop fusion | flops 8438784 | bytes 4582400 | tf_op jit(solution)/shard_map/convert_element_type | solution.py:299
  27.5 0.4 convolution_convert_fusion.2
  27.9 1.5 %fusion.41 = (bf16[12,132,128]{2,1,0:T(8,128)(2,1)S(1)}, f32[12,132,128]{2,1,0:T(8,128)S(1)}) fusion(f32[12,140,128]{2,1,0:T(8,128)S(1)} %get-tuple-element.118, f32[12]{0:T(128)S(1)} %fusion.112, f32[128]{0:T(128)S(1)} %get-tuple-element.81, f32[128]{0:T(128)S(1)} %get-tuple-element.82, f32[128]{0:T(128)S(1)} %get-tuple-element.83, ...), kind=kLoop, calls=%fused_computation.98 | loop fusion | flops 8312832 | bytes 4563968 | tf_op jit(solution)/shard_map/convert_element_type | solution.py:299
  29.4 0.4 convolution_convert_fusion.1
  29.8 1.5 %fusion.47 = (bf16[12,130,128]{2,1,0:T(8,128)(2,1)S(1)}, f32[12,130,128]{2,1,0:T(8,128)S(1)}) fusion(f32[12,142,128]{2,1,0:T(8,128)S(1)} %get-tuple-element.116, f32[12]{0:T(128)S(1)} %fusion.112, f32[128]{0:T(128)S(1)} %get-tuple-element.131, f32[128]{0:T(128)S(1)} %get-tuple-element.130, f32[128]{0:T(128)S(1)} %get-tuple-element.129, ...), kind=kLoop, calls=%fused_computation.104 | loop fusion | flops 8186880 | bytes 4545536 | tf_op jit(solution)/shard_map/convert_element_type | solution.py:299
  31.3 0.4 convolution_convert_fusion
  31.7 1.1 %fusion.99 = (bf16[12,128,128]{2,1,0:T(8,128)(2,1)S(1)}, bf16[12,128,128]{2,1,0:T(8,128)(2,1)S(1)}) fusion(f32[12,136,128]{2,1,0:T(8,128)S(1)} %slice_convert_fusion, f32[12,136,128]{2,1,0:T(8,128)S(1)} %get-tuple-element.57, f32[12,136,128]{2,1,0:T(8,128)S(1)} %get-tuple-element.121, f32[12]{0:T(128)S(1)} %fusion.112, f32[128]{0:T(128)S(1)} %get-tuple-element.99, ...), kind=kLoop, calls=%fused_computation.166 | loop fusion | flops 6488064 | bytes 5534720 | tf_op jit(solution)/shard_map/convert_element_type | solution.py:285
  32.9 2.3 %collective-permute-start = (bf16[12,128,128]{2,1,0:T(8,128)(2,1)S(1)}, bf16[12,128,128]{2,1,0:T(8,128)(2,1)S(1)}, u32[]{:S(2)}, u32[]{:S(2)}) collective-permute-start(bf16[12,128,128]{2,1,0:T(8,128)(2,1)S(1)} %get-tuple-element.114), channel_id=1, source_target_pairs={{1,0},{3,2},{5,4},{7,6},{9,8},{11,10},{13,12},{15,14},{17,16},{19,... | collective-permute-start | bytes 1179656 | tf_op jit(solution)/shard_map/ppermute | solution.py:335
  35.2 1.5 %collective-permute-start.1 = (bf16[12,128,128]{2,1,0:T(8,128)(2,1)S(1)}, bf16[12,128,128]{2,1,0:T(8,128)(2,1)S(1)}, u32[]{:S(2)}, u32[]{:S(2)}) collective-permute-start(bf16[12,128,128]{2,1,0:T(8,128)(2,1)S(1)} %get-tuple-element.113), channel_id=1, source_target_pairs={{0,1},{2,3},{4,5},{6,7},{8,9},{10,11},{12,13},{14,15},{16,17},{18,... | collective-permute-start | bytes 1179656 | tf_op jit(solution)/shard_map/ppermute | solution.py:334
  36.7 0.8 %fusion.89 = (f32[128]{0:T(128)S(1)}, f32[128]{0:T(128)S(1)}, f32[128]{0:T(128)S(1)}, f32[128]{0:T(128)S(1)}, f32[128]{0:T(128)S(1)}, /*index=5*/f32[128]{0:T(12...) fusion(bf16[12,144,128]{2,1,0:T(8,128)(2,1)S(1)} %multiply_convert_fusion, ...), kind=kLoop, calls=%fused_computation.155 | loop fusion | flops 5503872 | bytes 2019840 | tf_op jit(solution)/shard_map/reduce_sum | solution.py:322
  37.5 0.7 fusion.54
  38.2 0.9 %fusion.63 = (f32[128]{0:T(128)S(1)}, f32[128]{0:T(128)S(1)}, f32[128]{0:T(128)S(1)}, f32[128]{0:T(128)S(1)}, f32[128]{0:T(128)S(1)}, /*index=5*/f32[128]{0:T(12...) fusion(bf16[12,140,128]{2,1,0:T(8,128)(2,1)S(1)} %get-tuple-element.117, ...), kind=kLoop, calls=%fused_computation.129 | loop fusion | flops 5503872 | bytes 2019840 | tf_op jit(solution)/shard_map/reduce_sum | solution.py:322
  39.1 0.9 %fusion.72 = (f32[128]{0:T(128)S(1)}, f32[128]{0:T(128)S(1)}, f32[128]{0:T(128)S(1)}, f32[128]{0:T(128)S(1)}, f32[128]{0:T(128)S(1)}, /*index=5*/f32[128]{0:T(12...) fusion(bf16[12,138,128]{2,1,0:T(8,128)(2,1)S(1)} %get-tuple-element.119, ...), kind=kLoop, calls=%fused_computation.138 | loop fusion | flops 5503872 | bytes 2019840 | tf_op jit(solution)/shard_map/reduce_sum | solution.py:322
  40.0 0.3 fusion.102
  40.3 0.3 fusion.100
  40.7 0.3 fusion.104
  41.0 0.3 fusion.106
  41.4 0.2 convert_reduce_fusion.3
  41.6 0.2 convert_reduce_fusion.2
  41.8 0.2 convert_reduce_fusion.1
  42.0 0.2 convert_reduce_fusion
  42.6 0.3 maximum_maximum_fusion
  42.8 0.1 reshape.244
  43.0 0.8 %pad.48 = f32[98304]{0:T(1024)} pad(f32[70656]{0:T(1024)S(1)} %reshape.244, f32[]{:T(128)} %constant.12.clone.1), padding=0_27648 | pad | bytes 675844 | tf_op jit(solution)/shard_map/jit(_pad)/pad | solution.py:346
  43.7 27.1 %shard_map.94 = f32[32,24,128]{2,1,0:T(8,128)} custom-call(f32[32,24,128]{2,1,0:T(8,128)} %bitcast.232), custom_call_target="tpu_custom_call" | custom-call | tf_op jit(solution)/shard_map/pallas_call | solution.py:225
  70.8 1.0 %slice.840 = f32[23,24,128]{2,1,0:T(8,128)S(1)} slice(f32[32,24,128]{2,1,0:T(8,128)} %shard_map.94), slice={[0:23], [0:24], [0:128]} | slice | bytes 565248 | tf_op jit(solution)/shard_map/slice | solution.py:347
  71.8 0.1 broadcast_in_dim.104
  71.9 0.8 %select_reduce_fusion = f32[4,17664]{1,0:T(4,128)S(1)} fusion(f32[4,17664]{1,0:T(4,128)S(1)} %broadcast_in_dim.104, pred[4,4]{1,0:T(4,128)(4,1)S(1)} %get-tuple-element.111), kind=kLoop, calls=%fused_computation.49 | loop fusion | flops 494592 | bytes 565264 | tf_op jit(solution)/shard_map/reduce_sum | solution.py:350
  72.7 0.1 broadcast_multiply_fusion
  72.8 0.6 slice.949
  73.4 0.6 slice.951
  74.0 0.7 copy.30
  74.8 0.0 collective-permute-done
  74.8 0.0 collective-permute-done.1
  74.8 1.0 %maximum_select_fusion = bf16[1,2,12,128,128]{4,3,2,1,0:T(8,128)(2,1)} fusion(bf16[1,1,12,128,128]{4,3,2,1,0:T(8,128)(2,1)S(1)} %bitcast.235, bf16[1,1,12,128,128]{4,3,2,1,0:T(8,128)(2,1)S(1)} %bitcast.234, bf16[1,1,12,128,128]{4,3,2,1,0:T(8,128)(2,1)S(1)} %bitcast.233, bf16[1,1,12,128,128]{4,3,2,1,0:T(8,128)(2,1)S(1)} %bitcast.236, pred[]{:T(512)S(6)} %eq.48), kind=kLoop, calls=%fused_computation.168 | loop fusion | flops 1179648 | bytes 2359297 | tf_op jit(solution)/shard_map/jit(_where)/select_n | solution.py:336
  (36 shorter events, 0.3 us)
Async XLA Ops:
  0.6 17.9 %copy-start = (bf16[1,2,12,128,128]{4,3,2,1,0:T(8,128)(2,1)S(1)}, bf16[1,2,12,128,128]{4,3,2,1,0:T(8,128)(2,1)}, u32[]{:S(2)}) copy-start(bf16[1,2,12,128,128]{4,3,2,1,0:T(8,128)(2,1)} %param.6) | copy-start | bytes 2359300
  0.6 17.8 %copy-start.7 = (s32[2]{0:T(128)S(1)}, s32[2]{0:T(128)}, u32[]{:S(2)}) copy-start(s32[2]{0:T(128)} %param.7) | copy-start | bytes 28
  18.5 1.2 %copy-start.6 = (s32[4]{0:T(128)S(1)}, s32[4]{0:T(128)}, u32[]{:S(2)}) copy-start(s32[4]{0:T(128)} %param.8) | copy-start | bytes 52
  18.5 1.3 %copy-start.4 = (f32[4,3,3,128]{3,0,2,1:T(4,128)S(1)}, f32[4,3,3,128]{3,0,2,1:T(4,128)}, u32[]{:S(2)}) copy-start(f32[4,3,3,128]{3,0,2,1:T(4,128)} %param.9) | copy-start | bytes 55300
  18.5 1.5 %copy-start.1 = (bf16[4,128,128]{2,1,0:T(8,128)(2,1)S(1)}, bf16[4,128,128]{2,1,0:T(8,128)(2,1)}, u32[]{:S(2)}) copy-start(bf16[4,128,128]{2,1,0:T(8,128)(2,1)} %param.10) | copy-start | bytes 393220
  18.5 1.6 %copy-start.5 = (f32[4,128]{1,0:T(4,128)S(1)}, f32[4,128]{1,0:T(4,128)}, u32[]{:S(2)}) copy-start(f32[4,128]{1,0:T(4,128)} %param.11) | copy-start | bytes 6148
  18.5 1.7 %copy-start.2 = (bf16[2,12,8,128]{3,2,1,0:T(8,128)(2,1)S(1)}, bf16[2,12,8,128]{3,2,1,0:T(8,128)(2,1)}, u32[]{:S(2)}) copy-start(bf16[2,12,8,128]{3,2,1,0:T(8,128)(2,1)} %get-tuple-element.7) | copy-start | bytes 147460
  18.5 1.7 %copy-start.3 = (bf16[2,12,8,128]{3,2,1,0:T(8,128)(2,1)S(1)}, bf16[2,12,8,128]{3,2,1,0:T(8,128)(2,1)}, u32[]{:S(2)}) copy-start(bf16[2,12,8,128]{3,2,1,0:T(8,128)(2,1)} %get-tuple-element.9) | copy-start | bytes 147460
  32.9 41.9 %collective-permute-start = (bf16[12,128,128]{2,1,0:T(8,128)(2,1)S(1)}, bf16[12,128,128]{2,1,0:T(8,128)(2,1)S(1)}, u32[]{:S(2)}, u32[]{:S(2)}) collective-permute-start(bf16[12,128,128]{2,1,0:T(8,128)(2,1)S(1)} %get-tuple-element.114), channel_id=1, source_target_pairs={{1,0},{3,2},{5,4},{7,6},{9,8},{11,10},{13,12},{15,14},{17,16},{19,... | collective-permute-start | bytes 1179656 | tf_op jit(solution)/shard_map/ppermute | solution.py:335
  35.2 39.6 %collective-permute-start.1 = (bf16[12,128,128]{2,1,0:T(8,128)(2,1)S(1)}, bf16[12,128,128]{2,1,0:T(8,128)(2,1)S(1)}, u32[]{:S(2)}, u32[]{:S(2)}) collective-permute-start(bf16[12,128,128]{2,1,0:T(8,128)(2,1)S(1)} %get-tuple-element.113), channel_id=1, source_target_pairs={{0,1},{2,3},{4,5},{6,7},{8,9},{10,11},{12,13},{14,15},{16,17},{18,... | collective-permute-start | bytes 1179656 | tf_op jit(solution)/shard_map/ppermute | solution.py:334

commit v19 on v18

--- a/solution.py
+++ b/solution.py
@@ -251,10 +251,17 @@
 
     edges = jnp.stack([held[:, :, :X_HALO], held[:, :, breadth - X_HALO :]])
     body, lo, hi = exchange(held, edges)
-    x_in = jnp.where(core == 0, held[0], body)
-    g_in = jnp.where(core == 0, body, held[1])
-    x_wide = jnp.concatenate([lo[0], x_in, hi[0]], axis=1)
-    g_wide = jnp.concatenate([lo[1][:, X_HALO - G_HALO :], g_in, hi[1][:, :G_HALO]], axis=1)
+    x_wide = jnp.where(
+        core == 0,
+        jnp.concatenate([lo[0], held[0], hi[0]], axis=1),
+        jnp.concatenate([lo[0], body, hi[0]], axis=1),
+    )
+    g_lo, g_hi = lo[1][:, X_HALO - G_HALO :], hi[1][:, :G_HALO]
+    g_wide = jnp.where(
+        core == 0,
+        jnp.concatenate([g_lo, body, g_hi], axis=1),
+        jnp.concatenate([g_lo, held[1], g_hi], axis=1),
+    )
 
     both = (jnp.arange(height, dtype=row_counts.dtype)[:, None] < row_counts[None, :]).astype(jnp.float32)
     live = jnp.where(core == 0, both[:, 0], both[:, 1])[:, None, None]

time: 76 us -> 76.9 us (1.012)
  local copies, waits for them, and re-layouts: 4.98 us -> 6.92 us
  other arithmetic: 17.6 us -> 16.5 us
    squeeze x1 -> x2, local copies, waits for them, and re-layouts: 0.01 us -> 1.98 us  [the longest x1 1.18 us: shards(): held[1]]
    select_n x1 -> x0, other arithmetic: 1.16 us -> none  [shards(): g_in = jnp.where(core == 0, body, held[1])]
  transfers between devices with their start and end apart: 2 -> 2, of which waited for: 0 -> 0; matrix products, arithmetic and copies ran while one was open for 14% -> 14% of each run, Pallas kernels for 36% -> 35%
where the time goes in v19:
time: 76.9 us; the launch traced here: 76.6 us
  Pallas kernels  43.3 us (56%)
  other arithmetic  16.5 us (21%)
  local copies, waits for them, and re-layouts  6.92 us (9%)
  matrix products  5.09 us (7%)
  starting transfers between devices  3.8 us (5%)
  between operations  1.08 us (1%)
    pallas_call x1, Pallas kernels, all_reduce(): pl.pallas_call(reduce_kernel, out_shape=jax.ShapeDtypeStruct(flat.shape,...  27.1 us
    pallas_call x1, Pallas kernels, exchange(): pl.pallas_call(exchange_kernel, out_shape=(jax.ShapeDtypeStruct(grid_shap...  16.2 us
    convert_element_type x3, other arithmetic, shards(): gated = (masked * gelu_pair(preact)[1]).astype(jnp.bfloat16)  4.59 us
    reduce_sum x4, other arithmetic, shards(): jnp.sum(back_in * padded[i:i + height, start:start + breadth].astype(jnp....  3.29 us
    convert_element_type x4, other arithmetic, shards(): mixed = conv_forward(pad_rows(activation), depth).astype(jnp.bfloat16)  2.83 us
    ppermute x1, starting transfers between devices, shards(): got_grad = lax.ppermute(input_grad, 'pipe', [(1, 0)])  2.32 us
    dot_general x4, matrix products, shards(): jnp.dot(mixed.reshape(rows * span, channels), point, preferred_element_ty...  2.24 us
  transfers between devices with their start and end apart: 2, of which 0 were waited for; matrix products, arithmetic and copies ran while one was open for 14% of the time, Pallas kernels for 35%

profile of v19, /device:TPU:1, one launch (start us, length us, event | category | flops | bytes accessed | tf_op | source)
XLA Modules:
  0.0 76.6 jit_solution(707242422526517517)
XLA Ops:
  0.6 1.2 %slice_bitcast_fusion.1 = (bf16[12,128,128]{2,1,0:T(8,128)(2,1)S(1)}, bf16[12,128,128]{2,1,0:T(8,128)(2,1)S(1)}) fusion(bf16[1,2,12,128,128]{4,3,2,1,0:T(8,128)(2,1)} %param.6), kind=kLoop, calls=%fused_computation.207 | loop fusion | bytes 1572864 | tf_op jit(solution)/shard_map/squeeze | solution.py:263
  1.8 0.0 copy-start.5
  1.8 0.0 copy-start.4
  1.8 0.0 copy-start.2
  1.9 0.0 copy-start.1
  1.9 0.0 copy-start.3
  1.9 0.9 %slice_bitcast_fusion.4 = (bf16[1,2,12,8,128]{4,3,2,1,0:T(8,128)(2,1)S(1)}, bf16[1,2,12,8,128]{4,3,2,1,0:T(8,128)(2,1)S(1)}) fusion(bf16[2,12,128,128]{3,2,1,0:T(8,128)(2,1)} %bitcast.230), kind=kLoop, calls=%fused_computation.219 | loop fusion | bytes 196608 | tf_op jit(solution)/shard_map/stack | solution.py:252
  2.8 0.7 pad_maximum_fusion.8.edges_ref
  3.4 16.2 %shard_map.93 = (bf16[12,128,128]{2,1,0:T(8,128)(2,1)}, bf16[2,12,8,128]{3,2,1,0:T(8,128)(2,1)}, bf16[2,12,8,128]{3,2,1,0:T(8,128)(2,1)}) custom-call(bf16[2,12,128,128]{3,2,1,0:T(8,128)(2,1)} %bitcast.231, bf16[2,2,12,8,128]{4,3,2,1,0:T(8,128)(2,1)} %pad_maximum_fusion.8.edges_ref), custom_call_target="tpu_custom_call" | custom-call | tf_op jit(solution)/shard_map/pallas_call | solution.py:128
  19.6 0.0 copy-start
  19.6 0.1 compare_convert_fusion
  19.7 0.1 iota_compare_fusion
  19.8 0.1 select_reduce_fusion.2
  19.9 0.1 select_reduce_fusion.1
  20.1 0.0 copy-done.3
  20.1 0.1 select_reduce_fusion.3
  20.2 0.8 %slice_bitcast_fusion.19 = (bf16[12,8,128]{2,1,0:T(8,128)(2,1)S(1)}, bf16[12,8,128]{2,1,0:T(8,128)(2,1)S(1)}, bf16[12,8,128]{2,1,0:T(8,128)(2,1)S(1)}, bf16[12,8,128]{2,1,0:T(8,128)(2,1)S(1)}) fusion(bf16[2,12,8,128]{3,2,1,0:T(8,128)(2,1)} %get-tuple-element.9, bf16[2,12,8,128]{3,2,1,0:T(8,128)(2,1)} %get-tuple-element.7), kind=kLoop, calls=%fused_computation.226 | loop fusion | bytes 196608 | tf_op jit(solution)/shard_map/squeeze | solution.py:259
  21.1 0.0 copy-done
  21.1 0.2 multiply_convert_fusion
  21.3 0.7 fusion.5
  22.0 0.5 fusion.7
  22.5 0.7 fusion.13
  23.2 0.5 fusion.15
  23.7 0.7 fusion.21
  24.4 0.5 fusion.23
  24.9 0.1 slice_convert_fusion
  25.0 0.7 add_convert_fusion
  25.7 0.8 fusion.29
  26.5 0.4 convolution_convert_fusion.3
  26.8 1.5 %fusion.35 = (bf16[12,134,128]{2,1,0:T(8,128)(2,1)S(1)}, f32[12,134,128]{2,1,0:T(8,128)S(1)}) fusion(f32[12,138,128]{2,1,0:T(8,128)S(1)} %get-tuple-element.120, f32[12]{0:T(128)S(1)} %fusion.114, f32[128]{0:T(128)S(1)} %get-tuple-element.140, f32[128]{0:T(128)S(1)} %get-tuple-element.139, f32[128]{0:T(128)S(1)} %get-tuple-element.138, ...), kind=kLoop, calls=%fused_computation.92 | loop fusion | flops 8438784 | bytes 4582400 | tf_op jit(solution)/shard_map/convert_element_type | solution.py:306
  28.4 0.4 convolution_convert_fusion.2
  28.7 1.5 %fusion.41 = (bf16[12,132,128]{2,1,0:T(8,128)(2,1)S(1)}, f32[12,132,128]{2,1,0:T(8,128)S(1)}) fusion(f32[12,140,128]{2,1,0:T(8,128)S(1)} %get-tuple-element.118, f32[12]{0:T(128)S(1)} %fusion.114, f32[128]{0:T(128)S(1)} %get-tuple-element.81, f32[128]{0:T(128)S(1)} %get-tuple-element.82, f32[128]{0:T(128)S(1)} %get-tuple-element.83, ...), kind=kLoop, calls=%fused_computation.98 | loop fusion | flops 8312832 | bytes 4563968 | tf_op jit(solution)/shard_map/convert_element_type | solution.py:306
  30.3 0.4 convolution_convert_fusion.1
  30.7 1.5 %fusion.47 = (bf16[12,130,128]{2,1,0:T(8,128)(2,1)S(1)}, f32[12,130,128]{2,1,0:T(8,128)S(1)}) fusion(f32[12,142,128]{2,1,0:T(8,128)S(1)} %get-tuple-element.116, f32[12]{0:T(128)S(1)} %fusion.114, f32[128]{0:T(128)S(1)} %get-tuple-element.131, f32[128]{0:T(128)S(1)} %get-tuple-element.130, f32[128]{0:T(128)S(1)} %get-tuple-element.129, ...), kind=kLoop, calls=%fused_computation.104 | loop fusion | flops 8186880 | bytes 4545536 | tf_op jit(solution)/shard_map/convert_element_type | solution.py:306
  32.2 0.4 convolution_convert_fusion
  32.6 1.1 %fusion.99 = (bf16[12,128,128]{2,1,0:T(8,128)(2,1)S(1)}, bf16[12,128,128]{2,1,0:T(8,128)(2,1)S(1)}) fusion(f32[12,136,128]{2,1,0:T(8,128)S(1)} %slice_convert_fusion, f32[12,136,128]{2,1,0:T(8,128)S(1)} %get-tuple-element.57, f32[12,136,128]{2,1,0:T(8,128)S(1)} %get-tuple-element.121, f32[12]{0:T(128)S(1)} %fusion.114, f32[128]{0:T(128)S(1)} %get-tuple-element.99, ...), kind=kLoop, calls=%fused_computation.166 | loop fusion | flops 6488064 | bytes 5534720 | tf_op jit(solution)/shard_map/convert_element_type | solution.py:292
  33.7 2.3 %collective-permute-start = (bf16[12,128,128]{2,1,0:T(8,128)(2,1)S(1)}, bf16[12,128,128]{2,1,0:T(8,128)(2,1)S(1)}, u32[]{:S(2)}, u32[]{:S(2)}) collective-permute-start(bf16[12,128,128]{2,1,0:T(8,128)(2,1)S(1)} %get-tuple-element.114), channel_id=1, source_target_pairs={{1,0},{3,2},{5,4},{7,6},{9,8},{11,10},{13,12},{15,14},{17,16},{19,... | collective-permute-start | bytes 1179656 | tf_op jit(solution)/shard_map/ppermute | solution.py:342
  36.0 1.5 %collective-permute-start.1 = (bf16[12,128,128]{2,1,0:T(8,128)(2,1)S(1)}, bf16[12,128,128]{2,1,0:T(8,128)(2,1)S(1)}, u32[]{:S(2)}, u32[]{:S(2)}) collective-permute-start(bf16[12,128,128]{2,1,0:T(8,128)(2,1)S(1)} %get-tuple-element.113), channel_id=1, source_target_pairs={{0,1},{2,3},{4,5},{6,7},{8,9},{10,11},{12,13},{14,15},{16,17},{18,... | collective-permute-start | bytes 1179656 | tf_op jit(solution)/shard_map/ppermute | solution.py:341
  37.5 0.9 %fusion.89 = (f32[128]{0:T(128)S(1)}, f32[128]{0:T(128)S(1)}, f32[128]{0:T(128)S(1)}, f32[128]{0:T(128)S(1)}, f32[128]{0:T(128)S(1)}, /*index=5*/f32[128]{0:T(12...) fusion(bf16[12,144,128]{2,1,0:T(8,128)(2,1)S(1)} %multiply_convert_fusion, ...), kind=kLoop, calls=%fused_computation.155 | loop fusion | flops 5503872 | bytes 2019840 | tf_op jit(solution)/shard_map/reduce_sum | solution.py:329
  38.4 0.7 fusion.54
  39.1 0.9 %fusion.63 = (f32[128]{0:T(128)S(1)}, f32[128]{0:T(128)S(1)}, f32[128]{0:T(128)S(1)}, f32[128]{0:T(128)S(1)}, f32[128]{0:T(128)S(1)}, /*index=5*/f32[128]{0:T(12...) fusion(bf16[12,140,128]{2,1,0:T(8,128)(2,1)S(1)} %get-tuple-element.117, ...), kind=kLoop, calls=%fused_computation.129 | loop fusion | flops 5503872 | bytes 2019840 | tf_op jit(solution)/shard_map/reduce_sum | solution.py:329
  40.0 0.9 %fusion.72 = (f32[128]{0:T(128)S(1)}, f32[128]{0:T(128)S(1)}, f32[128]{0:T(128)S(1)}, f32[128]{0:T(128)S(1)}, f32[128]{0:T(128)S(1)}, /*index=5*/f32[128]{0:T(12...) fusion(bf16[12,138,128]{2,1,0:T(8,128)(2,1)S(1)} %get-tuple-element.119, ...), kind=kLoop, calls=%fused_computation.138 | loop fusion | flops 5503872 | bytes 2019840 | tf_op jit(solution)/shard_map/reduce_sum | solution.py:329
  40.8 0.3 fusion.104
  41.2 0.3 fusion.102
  41.5 0.3 fusion.106
  41.9 0.3 fusion.108
  42.2 0.2 convert_reduce_fusion.3
  42.4 0.2 convert_reduce_fusion.2
  42.7 0.2 convert_reduce_fusion.1
  42.9 0.2 convert_reduce_fusion
  43.4 0.3 maximum_maximum_fusion
  43.7 0.1 reshape.244
  43.8 0.8 %pad.48 = f32[98304]{0:T(1024)} pad(f32[70656]{0:T(1024)S(1)} %reshape.244, f32[]{:T(128)} %constant.12.clone.1), padding=0_27648 | pad | bytes 675844 | tf_op jit(solution)/shard_map/jit(_pad)/pad | solution.py:353
  44.6 27.1 %shard_map.94 = f32[32,24,128]{2,1,0:T(8,128)} custom-call(f32[32,24,128]{2,1,0:T(8,128)} %bitcast.232), custom_call_target="tpu_custom_call" | custom-call | tf_op jit(solution)/shard_map/pallas_call | solution.py:225
  71.7 1.0 %slice.842 = f32[23,24,128]{2,1,0:T(8,128)S(1)} slice(f32[32,24,128]{2,1,0:T(8,128)} %shard_map.94), slice={[0:23], [0:24], [0:128]} | slice | bytes 565248 | tf_op jit(solution)/shard_map/slice | solution.py:354
  72.6 0.1 broadcast_in_dim.104
  72.8 0.8 %select_reduce_fusion = f32[4,17664]{1,0:T(4,128)S(1)} fusion(f32[4,17664]{1,0:T(4,128)S(1)} %broadcast_in_dim.104, pred[4,4]{1,0:T(4,128)(4,1)S(1)} %get-tuple-element.111), kind=kLoop, calls=%fused_computation.49 | loop fusion | flops 494592 | bytes 565264 | tf_op jit(solution)/shard_map/reduce_sum | solution.py:357
  73.6 0.1 broadcast_multiply_fusion
  73.7 0.6 slice.951
  74.3 0.6 slice.953
  74.9 0.7 copy.30
  75.6 0.0 collective-permute-done
  75.6 0.0 collective-permute-done.1
  75.6 1.0 %maximum_select_fusion = bf16[1,2,12,128,128]{4,3,2,1,0:T(8,128)(2,1)} fusion(bf16[1,1,12,128,128]{4,3,2,1,0:T(8,128)(2,1)S(1)} %bitcast.235, bf16[1,1,12,128,128]{4,3,2,1,0:T(8,128)(2,1)S(1)} %bitcast.234, bf16[1,1,12,128,128]{4,3,2,1,0:T(8,128)(2,1)S(1)} %bitcast.233, bf16[1,1,12,128,128]{4,3,2,1,0:T(8,128)(2,1)S(1)} %bitcast.236, pred[]{:T(512)S(6)} %eq.48), kind=kLoop, calls=%fused_computation.168 | loop fusion | flops 1179648 | bytes 2359297 | tf_op jit(solution)/shard_map/jit(_where)/select_n | solution.py:343
  (32 shorter events, 0.3 us)
Async XLA Ops:
  1.8 17.8 %copy-start.5 = (s32[2]{0:T(128)S(1)}, s32[2]{0:T(128)}, u32[]{:S(2)}) copy-start(s32[2]{0:T(128)} %param.7) | copy-start | bytes 28
  1.8 17.9 %copy-start.4 = (s32[4]{0:T(128)S(1)}, s32[4]{0:T(128)}, u32[]{:S(2)}) copy-start(s32[4]{0:T(128)} %param.8) | copy-start | bytes 52
  1.8 17.9 %copy-start.2 = (f32[4,3,3,128]{3,0,2,1:T(4,128)S(1)}, f32[4,3,3,128]{3,0,2,1:T(4,128)}, u32[]{:S(2)}) copy-start(f32[4,3,3,128]{3,0,2,1:T(4,128)} %param.9) | copy-start | bytes 55300
  1.9 18.1 %copy-start.1 = (bf16[4,128,128]{2,1,0:T(8,128)(2,1)S(1)}, bf16[4,128,128]{2,1,0:T(8,128)(2,1)}, u32[]{:S(2)}) copy-start(bf16[4,128,128]{2,1,0:T(8,128)(2,1)} %param.10) | copy-start | bytes 393220
  1.9 18.2 %copy-start.3 = (f32[4,128]{1,0:T(4,128)S(1)}, f32[4,128]{1,0:T(4,128)}, u32[]{:S(2)}) copy-start(f32[4,128]{1,0:T(4,128)} %param.11) | copy-start | bytes 6148
  19.6 1.5 %copy-start = (bf16[12,128,128]{2,1,0:T(8,128)(2,1)S(1)}, bf16[12,128,128]{2,1,0:T(8,128)(2,1)}, u32[]{:S(2)}) copy-start(bf16[12,128,128]{2,1,0:T(8,128)(2,1)} %get-tuple-element.8) | copy-start | bytes 1179652
  33.7 41.9 %collective-permute-start = (bf16[12,128,128]{2,1,0:T(8,128)(2,1)S(1)}, bf16[12,128,128]{2,1,0:T(8,128)(2,1)S(1)}, u32[]{:S(2)}, u32[]{:S(2)}) collective-permute-start(bf16[12,128,128]{2,1,0:T(8,128)(2,1)S(1)} %get-tuple-element.114), channel_id=1, source_target_pairs={{1,0},{3,2},{5,4},{7,6},{9,8},{11,10},{13,12},{15,14},{17,16},{19,... | collective-permute-start | bytes 1179656 | tf_op jit(solution)/shard_map/ppermute | solution.py:342
  36.0 39.6 %collective-permute-start.1 = (bf16[12,128,128]{2,1,0:T(8,128)(2,1)S(1)}, bf16[12,128,128]{2,1,0:T(8,128)(2,1)S(1)}, u32[]{:S(2)}, u32[]{:S(2)}) collective-permute-start(bf16[12,128,128]{2,1,0:T(8,128)(2,1)S(1)} %get-tuple-element.113), channel_id=1, source_target_pairs={{0,1},{2,3},{4,5},{6,7},{8,9},{10,11},{12,13},{14,15},{16,17},{18,... | collective-permute-start | bytes 1179656 | tf_op jit(solution)/shard_map/ppermute | solution.py:341

commit v20 on v18

--- a/solution.py
+++ b/solution.py
@@ -339,6 +339,8 @@
 
     pieces = (jnp.stack(depth_terms), jnp.stack(point_terms), jnp.stack(bias_terms))
     flat = jnp.concatenate([piece.reshape(layers, -1) for piece in pieces], axis=1)
+    chosen = layer_order[None, :] == jnp.arange(layers, dtype=layer_order.dtype)[:, None]
+    flat = jnp.sum(jnp.where(chosen[:, :, None], flat[None, :, :], 0.0), axis=1)
     chunks = 2 * lax.axis_size("y") * lax.axis_size("x")
     size = flat.size
     rows = -(-size // (chunks * 128))
@@ -346,8 +348,7 @@
     packed = jnp.pad(flat.reshape(-1), (0, chunks * rows * 128 - size)).reshape(chunks, rows, 128)
     flat = all_reduce(packed).reshape(-1)[:size].reshape(flat.shape)
     factor = 1.0 / math.sqrt(held.shape[0] * height * breadth * blk_count())
-    chosen = layer_order[None, :] == jnp.arange(layers, dtype=layer_order.dtype)[:, None]
-    flat = jnp.sum(jnp.where(chosen[:, :, None], flat[None, :, :], 0.0), axis=1) * factor
+    flat = flat * factor
     ordered, at = [], 0
     for piece in pieces:
         width = piece[0].size

time: 76 us -> 76 us (level)
  local copies, waits for them, and re-layouts: 4.98 us -> 4.01 us
  other arithmetic: 17.6 us -> 18.5 us
    slice x1 -> x0, local copies, waits for them, and re-layouts: 0.98 us -> none  [shards(): flat = all_reduce(packed).reshape(-1)[:size].reshape(flat.shape)]
    mul x1, other arithmetic: 0.07 us -> 0.98 us  [shards(): flat = flat * factor]
where the time goes in v20:
time: 76 us; the launch traced here: 75.7 us
  Pallas kernels  43.2 us (57%)
  other arithmetic  18.5 us (24%)
  matrix products  5 us (7%)
  local copies, waits for them, and re-layouts  4.01 us (5%)
  starting transfers between devices  3.81 us (5%)
  between operations  1.09 us (1%)
    pallas_call x1, Pallas kernels, all_reduce(): pl.pallas_call(reduce_kernel, out_shape=jax.ShapeDtypeStruct(flat.shape,...  27.1 us
    pallas_call x1, Pallas kernels, exchange(): pl.pallas_call(exchange_kernel, out_shape=(jax.ShapeDtypeStruct(grid_shap...  16.2 us
    convert_element_type x3, other arithmetic, shards(): gated = (masked * gelu_pair(preact)[1]).astype(jnp.bfloat16)  4.6 us
    reduce_sum x4, other arithmetic, shards(): jnp.sum(back_in * padded[i:i + height, start:start + breadth].astype(jnp....  3.28 us
    convert_element_type x4, other arithmetic, shards(): mixed = conv_forward(pad_rows(activation), depth).astype(jnp.bfloat16)  2.83 us
    ppermute x1, starting transfers between devices, shards(): got_grad = lax.ppermute(input_grad, 'pipe', [(1, 0)])  2.33 us
    dot_general x4, matrix products, shards(): jnp.dot(mixed.reshape(rows * span, channels), point, preferred_element_ty...  2.15 us
  transfers between devices with their start and end apart: 2, of which 0 were waited for; matrix products, arithmetic and copies ran while one was open for 14% of the time, Pallas kernels for 36%

profile of v20, /device:TPU:1, one launch (start us, length us, event | category | flops | bytes accessed | tf_op | source)
XLA Modules:
  0.0 75.7 jit_solution(14673120575257031586)
XLA Ops:
  0.6 0.0 copy-start
  0.6 0.0 copy-start.7
  0.7 0.9 %slice_bitcast_fusion.2 = (bf16[1,2,12,8,128]{4,3,2,1,0:T(8,128)(2,1)S(1)}, bf16[1,2,12,8,128]{4,3,2,1,0:T(8,128)(2,1)S(1)}) fusion(bf16[2,12,128,128]{3,2,1,0:T(8,128)(2,1)} %bitcast.230), kind=kLoop, calls=%fused_computation.209 | loop fusion | bytes 196608 | tf_op jit(solution)/shard_map/stack | solution.py:252
  1.6 0.7 pad_maximum_fusion.edges_ref
  2.2 16.2 %shard_map.93 = (bf16[12,128,128]{2,1,0:T(8,128)(2,1)}, bf16[2,12,8,128]{3,2,1,0:T(8,128)(2,1)}, bf16[2,12,8,128]{3,2,1,0:T(8,128)(2,1)}) custom-call(bf16[2,12,128,128]{3,2,1,0:T(8,128)(2,1)} %bitcast.231, bf16[2,2,12,8,128]{4,3,2,1,0:T(8,128)(2,1)} %pad_maximum_fusion.edges_ref), custom_call_target="tpu_custom_call" | custom-call | tf_op jit(solution)/shard_map/pallas_call | solution.py:128
  18.4 0.0 copy-done.7
  18.4 0.1 compare_convert_fusion
  18.5 0.0 copy-done
  18.5 0.0 copy-start.5
  18.5 0.0 copy-start.2
  18.5 0.0 copy-start.3
  18.5 1.2 %bitcast_select_fusion.1 = (bf16[12,128,128]{2,1,0:T(8,128)(2,1)S(1)}, bf16[12,128,128]{2,1,0:T(8,128)(2,1)S(1)}) fusion(bf16[12,128,128]{2,1,0:T(8,128)(2,1)} %get-tuple-element.8, bf16[1,2,12,128,128]{4,3,2,1,0:T(8,128)(2,1)S(1)} %copy-done, pred[]{:T(512)S(6)} %eq.48), kind=kLoop, calls=%fused_computation.193 | loop fusion | flops 393216 | bytes 1966081 | tf_op jit(solution)/shard_map/jit(_where)/select_n | solution.py:255
  19.7 0.0 copy-done.6
  19.7 0.1 iota_compare_fusion
  19.8 0.0 copy-done.4
  19.8 0.1 select_reduce_fusion.2
  19.9 0.1 select_reduce_fusion.1
  20.1 0.0 copy-done.5
  20.1 0.1 select_reduce_fusion.3
  20.3 0.2 multiply_convert_fusion
  20.5 0.7 fusion.5
  21.2 0.5 fusion.7
  21.7 0.7 fusion.13
  22.4 0.5 fusion.15
  22.9 0.7 fusion.21
  23.6 0.5 fusion.23
  24.2 0.1 slice_convert_fusion
  24.2 0.7 add_convert_fusion
  24.9 0.7 fusion.29
  25.6 0.4 convolution_convert_fusion.3
  26.0 1.5 %fusion.35 = (bf16[12,134,128]{2,1,0:T(8,128)(2,1)S(1)}, f32[12,134,128]{2,1,0:T(8,128)S(1)}) fusion(f32[12,138,128]{2,1,0:T(8,128)S(1)} %get-tuple-element.116, f32[12]{0:T(128)S(1)} %fusion.112, f32[128]{0:T(128)S(1)} %get-tuple-element.136, f32[128]{0:T(128)S(1)} %get-tuple-element.135, f32[128]{0:T(128)S(1)} %get-tuple-element.134, ...), kind=kLoop, calls=%fused_computation.92 | loop fusion | flops 8438784 | bytes 4582400 | tf_op jit(solution)/shard_map/convert_element_type | solution.py:299
  27.5 0.4 convolution_convert_fusion.2
  27.9 1.5 %fusion.41 = (bf16[12,132,128]{2,1,0:T(8,128)(2,1)S(1)}, f32[12,132,128]{2,1,0:T(8,128)S(1)}) fusion(f32[12,140,128]{2,1,0:T(8,128)S(1)} %get-tuple-element.114, f32[12]{0:T(128)S(1)} %fusion.112, f32[128]{0:T(128)S(1)} %get-tuple-element.77, f32[128]{0:T(128)S(1)} %get-tuple-element.78, f32[128]{0:T(128)S(1)} %get-tuple-element.79, ...), kind=kLoop, calls=%fused_computation.98 | loop fusion | flops 8312832 | bytes 4563968 | tf_op jit(solution)/shard_map/convert_element_type | solution.py:299
  29.4 0.4 convolution_convert_fusion.1
  29.8 1.5 %fusion.47 = (bf16[12,130,128]{2,1,0:T(8,128)(2,1)S(1)}, f32[12,130,128]{2,1,0:T(8,128)S(1)}) fusion(f32[12,142,128]{2,1,0:T(8,128)S(1)} %get-tuple-element.112, f32[12]{0:T(128)S(1)} %fusion.112, f32[128]{0:T(128)S(1)} %get-tuple-element.127, f32[128]{0:T(128)S(1)} %get-tuple-element.126, f32[128]{0:T(128)S(1)} %get-tuple-element.125, ...), kind=kLoop, calls=%fused_computation.104 | loop fusion | flops 8186880 | bytes 4545536 | tf_op jit(solution)/shard_map/convert_element_type | solution.py:299
  31.3 0.4 convolution_convert_fusion
  31.7 1.1 %fusion.99 = (bf16[12,128,128]{2,1,0:T(8,128)(2,1)S(1)}, bf16[12,128,128]{2,1,0:T(8,128)(2,1)S(1)}) fusion(f32[12,136,128]{2,1,0:T(8,128)S(1)} %slice_convert_fusion, f32[12,136,128]{2,1,0:T(8,128)S(1)} %get-tuple-element.53, f32[12,136,128]{2,1,0:T(8,128)S(1)} %get-tuple-element.117, f32[12]{0:T(128)S(1)} %fusion.112, f32[128]{0:T(128)S(1)} %get-tuple-element.95, ...), kind=kLoop, calls=%fused_computation.166 | loop fusion | flops 6488064 | bytes 5534720 | tf_op jit(solution)/shard_map/convert_element_type | solution.py:285
  32.9 2.3 %collective-permute-start = (bf16[12,128,128]{2,1,0:T(8,128)(2,1)S(1)}, bf16[12,128,128]{2,1,0:T(8,128)(2,1)S(1)}, u32[]{:S(2)}, u32[]{:S(2)}) collective-permute-start(bf16[12,128,128]{2,1,0:T(8,128)(2,1)S(1)} %get-tuple-element.110), channel_id=1, source_target_pairs={{1,0},{3,2},{5,4},{7,6},{9,8},{11,10},{13,12},{15,14},{17,16},{19,... | collective-permute-start | bytes 1179656 | tf_op jit(solution)/shard_map/ppermute | solution.py:335
  35.2 1.5 %collective-permute-start.1 = (bf16[12,128,128]{2,1,0:T(8,128)(2,1)S(1)}, bf16[12,128,128]{2,1,0:T(8,128)(2,1)S(1)}, u32[]{:S(2)}, u32[]{:S(2)}) collective-permute-start(bf16[12,128,128]{2,1,0:T(8,128)(2,1)S(1)} %get-tuple-element.109), channel_id=1, source_target_pairs={{0,1},{2,3},{4,5},{6,7},{8,9},{10,11},{12,13},{14,15},{16,17},{18,... | collective-permute-start | bytes 1179656 | tf_op jit(solution)/shard_map/ppermute | solution.py:334
  36.7 0.8 %fusion.89 = (f32[128]{0:T(128)S(1)}, f32[128]{0:T(128)S(1)}, f32[128]{0:T(128)S(1)}, f32[128]{0:T(128)S(1)}, f32[128]{0:T(128)S(1)}, /*index=5*/f32[128]{0:T(12...) fusion(bf16[12,144,128]{2,1,0:T(8,128)(2,1)S(1)} %multiply_convert_fusion, ...), kind=kLoop, calls=%fused_computation.155 | loop fusion | flops 5503872 | bytes 2019840 | tf_op jit(solution)/shard_map/reduce_sum | solution.py:322
  37.5 0.7 fusion.54
  38.2 0.9 %fusion.63 = (f32[128]{0:T(128)S(1)}, f32[128]{0:T(128)S(1)}, f32[128]{0:T(128)S(1)}, f32[128]{0:T(128)S(1)}, f32[128]{0:T(128)S(1)}, /*index=5*/f32[128]{0:T(12...) fusion(bf16[12,140,128]{2,1,0:T(8,128)(2,1)S(1)} %get-tuple-element.113, ...), kind=kLoop, calls=%fused_computation.129 | loop fusion | flops 5503872 | bytes 2019840 | tf_op jit(solution)/shard_map/reduce_sum | solution.py:322
  39.1 0.9 %fusion.72 = (f32[128]{0:T(128)S(1)}, f32[128]{0:T(128)S(1)}, f32[128]{0:T(128)S(1)}, f32[128]{0:T(128)S(1)}, f32[128]{0:T(128)S(1)}, /*index=5*/f32[128]{0:T(12...) fusion(bf16[12,138,128]{2,1,0:T(8,128)(2,1)S(1)} %get-tuple-element.115, ...), kind=kLoop, calls=%fused_computation.138 | loop fusion | flops 5503872 | bytes 2019840 | tf_op jit(solution)/shard_map/reduce_sum | solution.py:322
  40.0 0.3 fusion.102
  40.3 0.3 fusion.100
  40.7 0.3 fusion.104
  41.0 0.3 fusion.106
  41.4 0.2 convert_reduce_fusion.3
  41.6 0.2 convert_reduce_fusion.2
  41.8 0.2 convert_reduce_fusion.1
  42.0 0.2 convert_reduce_fusion
  42.6 0.3 maximum_maximum_fusion
  42.8 0.8 %select_reduce_fusion = f32[4,17664]{1,0:T(4,128)S(1)} fusion(f32[4,17664]{1,0:T(4,128)S(1)} %maximum_maximum_fusion, pred[4,4]{1,0:T(4,128)(4,1)S(1)} %get-tuple-element.107), kind=kLoop, calls=%fused_computation.49 | loop fusion | flops 494592 | bytes 565264 | tf_op jit(solution)/shard_map/reduce_sum | solution.py:343
  43.7 0.1 reshape.247
  43.8 0.8 %pad.48 = f32[98304]{0:T(1024)} pad(f32[70656]{0:T(1024)S(1)} %reshape.247, f32[]{:T(128)} %constant.12.clone.1), padding=0_27648 | pad | bytes 675844 | tf_op jit(solution)/shard_map/jit(_pad)/pad | solution.py:348
  44.6 27.1 %shard_map.94 = f32[32,24,128]{2,1,0:T(8,128)} custom-call(f32[32,24,128]{2,1,0:T(8,128)} %bitcast.232), custom_call_target="tpu_custom_call" | custom-call | tf_op jit(solution)/shard_map/pallas_call | solution.py:225
  71.6 1.0 %slice_multiply_fusion.1 = f32[23,24,128]{2,1,0:T(8,128)S(1)} fusion(f32[32,24,128]{2,1,0:T(8,128)} %shard_map.94), kind=kLoop, calls=%fused_computation.203 | loop fusion | flops 70656 | bytes 565248 | tf_op jit(solution)/shard_map/mul | solution.py:351
  72.6 0.1 mul.1335
  72.7 0.6 slice.949
  73.4 0.6 slice.951
  74.0 0.7 copy.25
  74.7 0.0 collective-permute-done
  74.7 0.0 collective-permute-done.1
  74.7 1.0 %maximum_select_fusion = bf16[1,2,12,128,128]{4,3,2,1,0:T(8,128)(2,1)} fusion(bf16[1,1,12,128,128]{4,3,2,1,0:T(8,128)(2,1)S(1)} %bitcast.235, bf16[1,1,12,128,128]{4,3,2,1,0:T(8,128)(2,1)S(1)} %bitcast.234, bf16[1,1,12,128,128]{4,3,2,1,0:T(8,128)(2,1)S(1)} %bitcast.233, bf16[1,1,12,128,128]{4,3,2,1,0:T(8,128)(2,1)S(1)} %bitcast.236, pred[]{:T(512)S(6)} %eq.48), kind=kLoop, calls=%fused_computation.168 | loop fusion | flops 1179648 | bytes 2359297 | tf_op jit(solution)/shard_map/jit(_where)/select_n | solution.py:336
  (35 shorter events, 0.3 us)
Async XLA Ops:
  0.6 17.9 %copy-start = (bf16[1,2,12,128,128]{4,3,2,1,0:T(8,128)(2,1)S(1)}, bf16[1,2,12,128,128]{4,3,2,1,0:T(8,128)(2,1)}, u32[]{:S(2)}) copy-start(bf16[1,2,12,128,128]{4,3,2,1,0:T(8,128)(2,1)} %param.6) | copy-start | bytes 2359300
  0.6 17.8 %copy-start.7 = (s32[2]{0:T(128)S(1)}, s32[2]{0:T(128)}, u32[]{:S(2)}) copy-start(s32[2]{0:T(128)} %param.7) | copy-start | bytes 28
  18.5 1.2 %copy-start.6 = (s32[4]{0:T(128)S(1)}, s32[4]{0:T(128)}, u32[]{:S(2)}) copy-start(s32[4]{0:T(128)} %param.8) | copy-start | bytes 52
  18.5 1.3 %copy-start.4 = (f32[4,3,3,128]{3,0,2,1:T(4,128)S(1)}, f32[4,3,3,128]{3,0,2,1:T(4,128)}, u32[]{:S(2)}) copy-start(f32[4,3,3,128]{3,0,2,1:T(4,128)} %param.9) | copy-start | bytes 55300
  18.5 1.5 %copy-start.1 = (bf16[4,128,128]{2,1,0:T(8,128)(2,1)S(1)}, bf16[4,128,128]{2,1,0:T(8,128)(2,1)}, u32[]{:S(2)}) copy-start(bf16[4,128,128]{2,1,0:T(8,128)(2,1)} %param.10) | copy-start | bytes 393220
  18.5 1.6 %copy-start.5 = (f32[4,128]{1,0:T(4,128)S(1)}, f32[4,128]{1,0:T(4,128)}, u32[]{:S(2)}) copy-start(f32[4,128]{1,0:T(4,128)} %param.11) | copy-start | bytes 6148
  18.5 1.7 %copy-start.2 = (bf16[2,12,8,128]{3,2,1,0:T(8,128)(2,1)S(1)}, bf16[2,12,8,128]{3,2,1,0:T(8,128)(2,1)}, u32[]{:S(2)}) copy-start(bf16[2,12,8,128]{3,2,1,0:T(8,128)(2,1)} %get-tuple-element.7) | copy-start | bytes 147460
  18.5 1.7 %copy-start.3 = (bf16[2,12,8,128]{3,2,1,0:T(8,128)(2,1)S(1)}, bf16[2,12,8,128]{3,2,1,0:T(8,128)(2,1)}, u32[]{:S(2)}) copy-start(bf16[2,12,8,128]{3,2,1,0:T(8,128)(2,1)} %get-tuple-element.9) | copy-start | bytes 147460
  32.9 41.8 %collective-permute-start = (bf16[12,128,128]{2,1,0:T(8,128)(2,1)S(1)}, bf16[12,128,128]{2,1,0:T(8,128)(2,1)S(1)}, u32[]{:S(2)}, u32[]{:S(2)}) collective-permute-start(bf16[12,128,128]{2,1,0:T(8,128)(2,1)S(1)} %get-tuple-element.110), channel_id=1, source_target_pairs={{1,0},{3,2},{5,4},{7,6},{9,8},{11,10},{13,12},{15,14},{17,16},{19,... | collective-permute-start | bytes 1179656 | tf_op jit(solution)/shard_map/ppermute | solution.py:335
  35.2 39.5 %collective-permute-start.1 = (bf16[12,128,128]{2,1,0:T(8,128)(2,1)S(1)}, bf16[12,128,128]{2,1,0:T(8,128)(2,1)S(1)}, u32[]{:S(2)}, u32[]{:S(2)}) collective-permute-start(bf16[12,128,128]{2,1,0:T(8,128)(2,1)S(1)} %get-tuple-element.109), channel_id=1, source_target_pairs={{0,1},{2,3},{4,5},{6,7},{8,9},{10,11},{12,13},{14,15},{16,17},{18,... | collective-permute-start | bytes 1179656 | tf_op jit(solution)/shard_map/ppermute | solution.py:334
